TPU v7x, 32 devices: a whole 2x2x4 slice. The times are simulated.
32 devices in a mesh: rep: 4 (over x, core), shard: 8 (over z, y).
Axes of the slice: x: 2, y: 2, z: 4, core: 2. Of those that a mesh axis runs over, the one named last changes fastest.
Arguments:
- tokens: bfloat16 [4096, 768], P(('rep', 'shard')), may hold values from -6 to 6
- segment_ids: int32 [4096], P(('rep', 'shard')), may hold values from 0 to 3, as said below
- cotangent: bfloat16 [4096, 768], P(('rep', 'shard')), may hold values from -6 to 6
- ln1_gain: bfloat16 [1, 768], P(None, 'shard'), may hold values from 0.25 to 1.75
- ln1_bias: bfloat16 [1, 768], P(None, 'shard'), may hold values from -3 to 3
- qkv_weight: bfloat16 [1, 768, 2304], P(None, 'shard'), may hold values from -0.21875 to 0.21875
- qv_bias: bfloat16 [1, 1536], P(None, 'shard'), may hold values from -3 to 3
- out_weight: bfloat16 [1, 768, 768], P(None, 'shard'), may hold values from -0.875 to 0.875
- out_bias: bfloat16 [1, 768], P(None, 'shard'), may hold values from -3 to 3
- ln2_gain: bfloat16 [1, 768], P(None, 'shard'), may hold values from 0.25 to 1.75
- ln2_bias: bfloat16 [1, 768], P(None, 'shard'), may hold values from -3 to 3
- fc_weight: bfloat16 [1, 768, 3072], P(None, 'shard'), may hold values from -0.21875 to 0.21875
- fc_bias: bfloat16 [1, 3072], P(None, 'shard'), may hold values from -3 to 3
- proj_weight: bfloat16 [1, 3072, 768], P(None, 'shard'), may hold values from -0.109375 to 0.109375
- proj_bias: bfloat16 [1, 768], P(None, 'shard'), may hold values from -3 to 3
Outputs:
- out_tokens: bfloat16 [4096, 768], P(('rep', 'shard'))
- input_grad: float32 [4096, 768], P(('rep', 'shard'))
- grad_ln1_gain: float32 [1, 768], P(None, 'shard')
- grad_ln1_bias: float32 [1, 768], P(None, 'shard')
- grad_qkv_weight: float32 [1, 768, 2304], P(None, 'shard')
- grad_qv_bias: float32 [1, 1536], P(None, 'shard')
- grad_out_weight: float32 [1, 768, 768], P(None, 'shard')
- grad_out_bias: float32 [1, 768], P(None, 'shard')
- grad_ln2_gain: float32 [1, 768], P(None, 'shard')
- grad_ln2_bias: float32 [1, 768], P(None, 'shard')
- grad_fc_weight: float32 [1, 768, 3072], P(None, 'shard')
- grad_fc_bias: float32 [1, 3072], P(None, 'shard')
- grad_proj_weight: float32 [1, 3072, 768], P(None, 'shard')
- grad_proj_bias: float32 [1, 768], P(None, 'shard')
Inputs may be any that keep to these rules, and one draw needn't show every extreme that they name: `segment_ids`: each aligned block of 128 rows (one device's rows) holds three documents with ids 0, 1, 2 in this order, each of one row or more, followed by padding rows of id 3, which attend among themselves; the first block has no padding and the last block is half padding.
All inputs are finite; a program needn't handle non-finite values.
Results may differ from a plain program's by a relative error of at most 0.0098.
Values may be sent and summed in bfloat16 or wider, within the bound.
A program may use at most 128 MiB of HBM per device.

v0:
```python
import jax
import jax.numpy as jnp
from jax import lax
from jax.sharding import PartitionSpec as P

HEADS = 12
HEAD = 64
LAYERS = 1


epsilon = 1e-05


def to_float(value):
    return value.astype(jnp.float32)


def layer_norm(inputs, norm_gain, norm_shift):
    center = inputs - jnp.mean(inputs, axis=-1, keepdims=True)
    inverse_std = lax.rsqrt(jnp.mean(center * center, axis=-1, keepdims=True) + epsilon)
    normed = center * inverse_std
    return (normed * norm_gain + norm_shift, normed, inverse_std)


def norm_back(upstream, normed, inverse_std, norm_gain):
    scaled = upstream * norm_gain
    inner_term = scaled - jnp.mean(scaled, axis=-1, keepdims=True)
    inner_term = inner_term - normed * jnp.mean(scaled * normed, axis=-1, keepdims=True)
    return (inverse_std * inner_term, jnp.sum(upstream * normed, axis=0), jnp.sum(upstream, axis=0))


def layer_forward(inputs, allowed, weights, kept_lse):
    (
        ln1_gain,
        ln1_bias,
        qkv_weight,
        qv_bias,
        out_weight,
        out_bias,
        ln2_gain,
        ln2_bias,
        fc_weight,
        fc_bias,
        proj_weight,
        proj_bias,
    ) = weights
    row_count = inputs.shape[0]
    width_all = inputs.shape[1]
    first_norm, normed_one, inverse_one = layer_norm(inputs, to_float(ln1_gain), to_float(ln1_bias))
    first_low = first_norm.astype(jnp.bfloat16)
    offset = jnp.concatenate(
        [
            to_float(qv_bias[:width_all]),
            jnp.zeros((width_all,), jnp.float32),
            to_float(qv_bias[width_all:]),
        ]
    )
    projected = (
        jnp.dot(first_low, qkv_weight, preferred_element_type=jnp.float32) + offset
    ).astype(jnp.bfloat16)
    queries = projected[:, :width_all].reshape(row_count, HEADS, HEAD)
    keys_all = projected[:, width_all : 2 * width_all].reshape(row_count, HEADS, HEAD)
    values_all = projected[:, 2 * width_all :].reshape(row_count, HEADS, HEAD)
    scores = jnp.einsum(
        "qhd,khd->hqk", queries, keys_all, preferred_element_type=jnp.float32
    ) * HEAD ** (-0.5)
    scores = jnp.where(allowed[None], scores, -1e30)
    if kept_lse is None:
        row_max = jnp.max(scores, axis=-1, keepdims=True)
        log_total = row_max + jnp.log(jnp.sum(jnp.exp(scores - row_max), axis=-1, keepdims=True))
    else:
        log_total = kept_lse
    attn_probs = jnp.exp(scores - log_total)
    probs_low = attn_probs.astype(jnp.bfloat16)
    attn_mixed = jnp.einsum(
        "hqk,khd->qhd", probs_low, values_all, preferred_element_type=jnp.float32
    )
    attn_mixed = attn_mixed.reshape(row_count, width_all).astype(jnp.bfloat16)
    after_attn = (
        inputs
        + jnp.dot(attn_mixed, out_weight, preferred_element_type=jnp.float32)
        + to_float(out_bias)
    )
    second_norm, normed_two, inverse_two = layer_norm(
        after_attn, to_float(ln2_gain), to_float(ln2_bias)
    )
    second_low = second_norm.astype(jnp.bfloat16)
    hidden_pre = jnp.dot(second_low, fc_weight, preferred_element_type=jnp.float32) + to_float(
        fc_bias
    )
    hidden_low = jax.nn.gelu(hidden_pre, approximate=True).astype(jnp.bfloat16)
    result = (
        after_attn
        + jnp.dot(hidden_low, proj_weight, preferred_element_type=jnp.float32)
        + to_float(proj_bias)
    )
    return dict(
        normed_one=normed_one,
        inverse_one=inverse_one,
        first_low=first_low,
        queries=queries,
        keys_all=keys_all,
        values_all=values_all,
        attn_probs=attn_probs,
        probs_low=probs_low,
        attn_mixed=attn_mixed,
        normed_two=normed_two,
        inverse_two=inverse_two,
        second_low=second_low,
        hidden_pre=hidden_pre,
        hidden_low=hidden_low,
        result=result,
        log_total=log_total,
    )


def layer_backward(upstream, saved, weights):
    (
        ln1_gain,
        ln1_bias,
        qkv_weight,
        qv_bias,
        out_weight,
        out_bias,
        ln2_gain,
        ln2_bias,
        fc_weight,
        fc_bias,
        proj_weight,
        proj_bias,
    ) = weights
    row_count = upstream.shape[0]
    width_all = upstream.shape[1]
    proj_in = upstream.astype(jnp.bfloat16)
    grad_proj = jnp.einsum(
        "tf,td->fd", saved["hidden_low"], proj_in, preferred_element_type=jnp.float32
    )
    grad_proj_b = jnp.sum(to_float(proj_in), axis=0)
    hidden_grad = jnp.einsum("td,fd->tf", proj_in, proj_weight, preferred_element_type=jnp.float32)
    _, gelu_pull = jax.vjp(lambda value: jax.nn.gelu(value, approximate=True), saved["hidden_pre"])
    pre_grad = gelu_pull(hidden_grad)[0].astype(jnp.bfloat16)
    grad_fc = jnp.einsum(
        "td,tf->df", saved["second_low"], pre_grad, preferred_element_type=jnp.float32
    )
    grad_fc_b = jnp.sum(to_float(pre_grad), axis=0)
    second_grad = jnp.einsum("tf,df->td", pre_grad, fc_weight, preferred_element_type=jnp.float32)
    norm_part, grad_ln2_g, grad_ln2_b = norm_back(
        second_grad, saved["normed_two"], saved["inverse_two"], to_float(ln2_gain)
    )
    residual_grad = upstream + norm_part
    branch_in = residual_grad.astype(jnp.bfloat16)
    grad_out = jnp.einsum(
        "tc,td->cd", saved["attn_mixed"], branch_in, preferred_element_type=jnp.float32
    )
    grad_out_b = jnp.sum(to_float(branch_in), axis=0)
    mixed_grad = jnp.einsum("td,cd->tc", branch_in, out_weight, preferred_element_type=jnp.float32)
    mixed_grad = mixed_grad.astype(jnp.bfloat16).reshape(row_count, HEADS, HEAD)
    prob_grad = jnp.einsum(
        "qhd,khd->hqk", mixed_grad, saved["values_all"], preferred_element_type=jnp.float32
    )
    value_grad = jnp.einsum(
        "hqk,qhd->khd", saved["probs_low"], mixed_grad, preferred_element_type=jnp.float32
    )
    attn_probs = saved["attn_probs"]
    row_delta = jnp.sum(attn_probs * prob_grad, axis=-1, keepdims=True)
    score_grad = (attn_probs * (prob_grad - row_delta)).astype(jnp.bfloat16)
    query_grad = jnp.einsum(
        "hqk,khd->qhd", score_grad, saved["keys_all"], preferred_element_type=jnp.float32
    ) * HEAD ** (-0.5)
    key_grad = jnp.einsum(
        "hqk,qhd->khd", score_grad, saved["queries"], preferred_element_type=jnp.float32
    ) * HEAD ** (-0.5)
    joined_grad = jnp.concatenate(
        [
            query_grad.reshape(row_count, width_all),
            key_grad.reshape(row_count, width_all),
            value_grad.reshape(row_count, width_all),
        ],
        axis=1,
    ).astype(jnp.bfloat16)
    grad_qkv = jnp.einsum(
        "tc,te->ce", saved["first_low"], joined_grad, preferred_element_type=jnp.float32
    )
    column_sums = jnp.sum(to_float(joined_grad), axis=0)
    grad_qv_b = jnp.concatenate([column_sums[:width_all], column_sums[2 * width_all :]])
    first_grad = jnp.einsum(
        "te,ce->tc", joined_grad, qkv_weight, preferred_element_type=jnp.float32
    )
    norm_first, grad_ln1_g, grad_ln1_b = norm_back(
        first_grad, saved["normed_one"], saved["inverse_one"], to_float(ln1_gain)
    )
    gradients = (
        grad_ln1_g,
        grad_ln1_b,
        grad_qkv,
        grad_qv_b,
        grad_out,
        grad_out_b,
        grad_ln2_g,
        grad_ln2_b,
        grad_fc,
        grad_fc_b,
        grad_proj,
        grad_proj_b,
    )
    return (residual_grad + norm_first, gradients)


def own_grads(gradients):
    shares = (
        lax.psum_scatter(gradients[0], "shard", scatter_dimension=0, tiled=True),
        lax.psum_scatter(gradients[1], "shard", scatter_dimension=0, tiled=True),
        lax.psum_scatter(gradients[2], "shard", scatter_dimension=0, tiled=True),
        lax.psum_scatter(gradients[3], "shard", scatter_dimension=0, tiled=True),
        lax.psum_scatter(gradients[4], "shard", scatter_dimension=0, tiled=True),
        lax.psum_scatter(gradients[5], "shard", scatter_dimension=0, tiled=True),
        lax.psum_scatter(gradients[6], "shard", scatter_dimension=0, tiled=True),
        lax.psum_scatter(gradients[7], "shard", scatter_dimension=0, tiled=True),
        lax.psum_scatter(gradients[8], "shard", scatter_dimension=0, tiled=True),
        lax.psum_scatter(gradients[9], "shard", scatter_dimension=0, tiled=True),
        lax.psum_scatter(gradients[10], "shard", scatter_dimension=0, tiled=True),
        lax.psum_scatter(gradients[11], "shard", scatter_dimension=0, tiled=True),
    )
    owned = lax.psum(
        (
            shares[0],
            shares[1],
            shares[2],
            shares[3],
            shares[4],
            shares[5],
            shares[6],
            shares[7],
            shares[8],
            shares[9],
            shares[10],
            shares[11],
        ),
        "rep",
    )
    return owned


def per_device(
    tokens,
    segment_ids,
    cotangent,
    ln1_gain,
    ln1_bias,
    qkv_weight,
    qv_bias,
    out_weight,
    out_bias,
    ln2_gain,
    ln2_bias,
    fc_weight,
    fc_bias,
    proj_weight,
    proj_bias,
):
    row_count = tokens.shape[0]
    positions = jnp.arange(row_count)
    allowed = (segment_ids[:, None] == segment_ids[None, :]) & (
        positions[None, :] <= positions[:, None]
    )
    residual = to_float(tokens)
    layer_index = 0
    gathered = (
        lax.all_gather(ln1_gain[layer_index], "shard", axis=0, tiled=True),
        lax.all_gather(ln1_bias[layer_index], "shard", axis=0, tiled=True),
        lax.all_gather(qkv_weight[layer_index], "shard", axis=0, tiled=True),
        lax.all_gather(qv_bias[layer_index], "shard", axis=0, tiled=True),
        lax.all_gather(out_weight[layer_index], "shard", axis=0, tiled=True),
        lax.all_gather(out_bias[layer_index], "shard", axis=0, tiled=True),
        lax.all_gather(ln2_gain[layer_index], "shard", axis=0, tiled=True),
        lax.all_gather(ln2_bias[layer_index], "shard", axis=0, tiled=True),
        lax.all_gather(fc_weight[layer_index], "shard", axis=0, tiled=True),
        lax.all_gather(fc_bias[layer_index], "shard", axis=0, tiled=True),
        lax.all_gather(proj_weight[layer_index], "shard", axis=0, tiled=True),
        lax.all_gather(proj_bias[layer_index], "shard", axis=0, tiled=True),
    )
    saved = layer_forward(residual, allowed, gathered, None)
    kept_inputs = [residual]
    kept_lse = [saved["log_total"]]
    residual = saved["result"]
    out_tokens = residual.astype(jnp.bfloat16)
    upstream = to_float(cotangent)
    owned_grads = [None] * LAYERS
    for layer_index in reversed(range(LAYERS)):
        gathered = (
            lax.all_gather(ln1_gain[layer_index], "shard", axis=0, tiled=True),
            lax.all_gather(ln1_bias[layer_index], "shard", axis=0, tiled=True),
            lax.all_gather(qkv_weight[layer_index], "shard", axis=0, tiled=True),
            lax.all_gather(qv_bias[layer_index], "shard", axis=0, tiled=True),
            lax.all_gather(out_weight[layer_index], "shard", axis=0, tiled=True),
            lax.all_gather(out_bias[layer_index], "shard", axis=0, tiled=True),
            lax.all_gather(ln2_gain[layer_index], "shard", axis=0, tiled=True),
            lax.all_gather(ln2_bias[layer_index], "shard", axis=0, tiled=True),
            lax.all_gather(fc_weight[layer_index], "shard", axis=0, tiled=True),
            lax.all_gather(fc_bias[layer_index], "shard", axis=0, tiled=True),
            lax.all_gather(proj_weight[layer_index], "shard", axis=0, tiled=True),
            lax.all_gather(proj_bias[layer_index], "shard", axis=0, tiled=True),
        )
        saved = layer_forward(kept_inputs[layer_index], allowed, gathered, kept_lse[layer_index])
        upstream, gradients = layer_backward(upstream, saved, gathered)
        owned_grads[layer_index] = own_grads(gradients)
    stacked = tuple((jnp.stack([owned_grads[0][member]]) for member in range(12)))
    return (out_tokens, upstream) + stacked


def solution(mesh):
    placed = (
        P(("rep", "shard"), None),
        P(("rep", "shard")),
        P(("rep", "shard"), None),
        P(None, "shard"),
        P(None, "shard"),
        P(None, "shard", None),
        P(None, "shard"),
        P(None, "shard", None),
        P(None, "shard"),
        P(None, "shard"),
        P(None, "shard"),
        P(None, "shard", None),
        P(None, "shard"),
        P(None, "shard", None),
        P(None, "shard"),
    )
    return jax.shard_map(
        per_device,
        mesh=mesh,
        in_specs=placed,
        out_specs=(
            P(("rep", "shard"), None),
            P(("rep", "shard"), None),
            P(None, "shard"),
            P(None, "shard"),
            P(None, "shard", None),
            P(None, "shard"),
            P(None, "shard", None),
            P(None, "shard"),
            P(None, "shard"),
            P(None, "shard"),
            P(None, "shard", None),
            P(None, "shard"),
            P(None, "shard", None),
            P(None, "shard"),
        ),
        check_vma=False,
    )
```

profile of v0, /device:TPU:0, one launch (start us, length us, event | category | flops | bytes accessed | tf_op | source)
XLA Modules:
  0.0 913.5 jit_solution(14599363228877090021)
XLA Ops:
  7.3 0.7 all-gather.17.cloned.1.call-update
  8.1 0.7 all-gather.19.cloned.1.call-update
  8.8 0.7 all-gather.21.cloned.1.call-update
  9.6 0.5 all-gather.23.cloned.1.call-update
  10.2 0.6 fusion.73
  12.1 0.2 dynamic-update-slice.1
  13.7 39.5 %all-reduce.18 = (bf16[1536]{0:T(1024)(128)(2,1)S(1)}, bf16[768]{0:T(1024)(128)(2,1)S(1)}, bf16[768]{0:T(1024)(128)(2,1)S(1)}, bf16[768]{0:T(1024)(128)(2,1)S(1)...) all-reduce(bf16[1536]{0:T(1024)(128)(2,1)S(1)} %dynamic-update-slic, ...), channel_id=5, replica_groups=mesh['rep'=4,'shard'=8] {'shard'}, use_global_device_ids=true, to_apply=%add.2 | all-reduce | flops 6144 | bytes 24576
  53.3 26.1 %all-gather.9 = bf16[1,3072]{1,0:T(2,128)(2,1)S(1)} all-gather(bf16[1,384]{1,0:T(2,128)(2,1)S(1)} %copy-done.39), channel_id=11, replica_groups=mesh['rep'=4,'shard'=8] {'shard'}, dimensions={1}, use_global_device_ids=true | all-gather | bytes 6912 | tf_op jit(solution)/shard_map/all_gather | solution.py:278
  80.0 2.7 fusion.11
  83.3 0.3 fusion.74
  83.7 0.2 convolution_convert_fusion.1
  84.0 36.8 %all-gather.19.cloned.1.call-done = bf16[1,768,768]{2,1,0:T(8,128)(2,1)} async-done(((bf16[1,96,768]{2,1,0:T(8,128)(2,1)}), bf16[1,768,768]{2,1,0:T(8,128)(2,1)}) %all-gather.19.cloned.1.call-update) | async-done | bytes 1179664 | tf_op jit(solution)/shard_map/all_gather | solution.py:273
  120.8 1.7 fusion.75
  122.8 78.9 %all-gather.21.cloned.1.call-done = bf16[1,768,3072]{2,1,0:T(8,128)(2,1)} async-done(((bf16[1,96,3072]{2,1,0:T(8,128)(2,1)}), bf16[1,768,3072]{2,1,0:T(8,128)(2,1)}) %all-gather.21.cloned.1.call-update) | async-done | bytes 4718608 | tf_op jit(solution)/shard_map/all_gather | solution.py:277
  201.7 3.2 fusion.8
  204.9 76.8 %all-gather.23.cloned.1.call-done = bf16[1,3072,768]{2,1,0:T(8,128)(2,1)} async-done(((bf16[1,384,768]{2,1,0:T(8,128)(2,1)}), bf16[1,3072,768]{2,1,0:T(8,128)(2,1)}) %all-gather.23.cloned.1.call-update) | async-done | bytes 4718608 | tf_op jit(solution)/shard_map/all_gather | solution.py:279
  281.8 5.0 convert_reduce_fusion
  286.9 2.3 multiply_reduce_fusion.1
  289.2 1.5 convert_reduce_fusion.4
  290.7 1.8 fusion.63
  292.8 2.5 fusion.35
  295.3 1.7 copy.53
  297.0 1.3 multiply_reduce_fusion
  298.6 0.4 fusion.42
  299.0 0.3 copy-done.7
  299.5 0.4 convolution_convert_fusion
  300.0 0.3 copy-done.13
  300.2 4.1 fusion.66
  304.4 1.1 copy-done.3
  305.5 5.8 fusion.69
  311.4 0.9 copy-done.19
  312.2 5.2 fusion.70
  317.5 0.5 copy-done.36
  318.0 0.6 convert_element_type.141
  320.6 0.2 convert_reduce_fusion.1
  320.9 4.1 fusion.56
  324.9 35.8 %all-reduce.15 = (f32[768]{0:T(1024)S(1)}, f32[768]{0:T(1024)S(1)}, f32[1536]{0:T(1024)S(1)}, f32[768]{0:T(1024)S(1)}, f32[768]{0:T(1024)S(1)}, /*index=5*/f32[7...) all-reduce(f32[768]{0:T(1024)} %get-tuple-element.16, ...), channel_id=14, replica_groups=mesh['rep'=4,'shard'=8] {'shard'}, use_global_device_ids=true, to_apply=%region_12.13.clone | all-reduce | flops 9216 | bytes 73728
  360.8 130.8 %reduce-scatter.5.cloned.1.call-done = f32[96,2304]{1,0:T(8,128)} async-done(((f32[768,2304]{1,0:T(8,128)}), f32[96,2304]{1,0:T(8,128)}) %reduce-scatter.5.cloned.1.call-update) | async-done | bytes 884752 | tf_op jit(solution)/shard_map/reduce_scatter | solution.py:213
  491.5 166.6 %reduce-scatter.9.cloned.1.call-done = f32[96,3072]{1,0:T(8,128)} async-done(((f32[768,3072]{1,0:T(8,128)}), f32[96,3072]{1,0:T(8,128)}) %reduce-scatter.9.cloned.1.call-update) | async-done | bytes 1179664 | tf_op jit(solution)/shard_map/reduce_scatter | solution.py:219
  658.1 166.6 %reduce-scatter.11.cloned.1.call-done = f32[384,768]{1,0:T(8,128)} async-done(((f32[3072,768]{1,0:T(8,128)}), f32[384,768]{1,0:T(8,128)}) %reduce-scatter.11.cloned.1.call-update) | async-done | bytes 1179664 | tf_op jit(solution)/shard_map/reduce_scatter | solution.py:221
  825.3 7.5 all-reduce.16
  832.9 0.9 fusion.55
  833.8 4.1 fusion.38
  837.9 64.1 %all-reduce.21.cloned.1.call-done = (f32[1,96,2304]{2,1,0:T(8,128)}, f32[1,96,768]{2,1,0:T(8,128)}, f32[1,96,3072]{2,1,0:T(8,128)}, f32[1,384,768]{2,1,0:T(8,128)}) async-done(((f32[1,96,2304]{2,1,0:T(8,128)}, f32[1,96,768]{2,1,0:T(8,128)}, f32[1,96,3072]{2,1,0:T(8,128)}, f32[1,384,768]{2,1,0:T(8,128)}), (f32[1,96,2304]{2,1,0:T(8,128)}, f32[1,96,768]{2,1,0:T(8,128)}, f32[1,96,3072]{2,1,0:T(8,128)}, ...) | async-done | bytes 3538960 | tf_op jit(solution)/shard_map/psum | solution.py:224
  902.0 2.2 copy.72
  904.2 0.7 copy.73
  905.0 1.0 copy.74
  906.0 1.0 copy.75
  (163 shorter events, 4.7 us)
Async XLA Ops:
  7.2 3.0 copy-start.38
  7.2 4.8 copy-start.40
  7.2 4.9 copy-start.41
  7.2 5.1 copy-start.42
  7.2 5.3 copy-start.43
  7.2 5.6 copy-start.44
  7.2 5.8 copy-start.45
  7.3 6.0 copy-start.46
  7.3 46.0 %copy-start.39 = (bf16[1,384]{1,0:T(2,128)(2,1)S(1)}, bf16[1,384]{1,0:T(2,128)(2,1)}, u32[]{:S(2)}) copy-start(bf16[1,384]{1,0:T(2,128)(2,1)} %param.27) | copy-start | bytes 2308
  7.3 72.2 %copy-start.1 = (bf16[128,768]{1,0:T(8,128)(2,1)S(1)}, bf16[128,768]{1,0:T(8,128)(2,1)}, u32[]{:S(2)}) copy-start(bf16[128,768]{1,0:T(8,128)(2,1)} %param.15) | copy-start | bytes 589828
  7.3 72.5 %copy-start.37 = (s32[128]{0:T(128)S(1)}, s32[128]{0:T(128)}, u32[]{:S(2)}) copy-start(s32[128]{0:T(128)} %param.16) | copy-start | bytes 1540
  7.3 72.7 %all-gather.17.cloned.1.call-start = ((), (), s32[]{:S(2)}) async-start(), calls=%async_computation.8 | async-start | bytes 3981312 | tf_op jit(solution)/shard_map/all_gather | solution.py:271
  8.0 112.8 %all-gather.19.cloned.1.call-start = ((), (), s32[]{:S(2)}) async-start(), calls=%async_computation.9 | async-start | bytes 1327104 | tf_op jit(solution)/shard_map/all_gather | solution.py:273
  8.8 192.9 %all-gather.21.cloned.1.call-start = ((), (), s32[]{:S(2)}) async-start(), calls=%async_computation.10 | async-start | bytes 5308416 | tf_op jit(solution)/shard_map/all_gather | solution.py:277
  9.5 272.3 %all-gather.23.cloned.1.call-start = ((), (), s32[]{:S(2)}) async-start(), calls=%async_computation.11 | async-start | bytes 5308416 | tf_op jit(solution)/shard_map/all_gather | solution.py:279
  10.1 350.7 %reduce-scatter.7.cloned.1.call-start = ((), (), s32[]{:S(2)}) async-start(), calls=%async_computation.5 | async-start | bytes 2654208 | tf_op jit(solution)/shard_map/reduce_scatter | solution.py:215
  53.3 29.4 %copy-start.23 = (f32[768]{0:T(1024)}, f32[768]{0:T(1024)S(1)}, u32[]{:S(2)}) copy-start(f32[768]{0:T(1024)S(1)} %convert_element_type.137) | copy-start | bytes 9220
  79.4 122.3 %copy-start.21 = (f32[768]{0:T(1024)}, f32[768]{0:T(1024)S(1)}, u32[]{:S(2)}) copy-start(f32[768]{0:T(1024)S(1)} %convert_element_type.140) | copy-start | bytes 9220
  79.6 3.1 copy-start.28
  79.8 2.9 copy-start.32
  122.6 164.3 %copy-start.25 = (f32[128]{0:T(128)}, f32[128]{0:T(128)S(1)}, u32[]{:S(2)}) copy-start(f32[128]{0:T(128)S(1)} %broadcast_multiply_fusion.4) | copy-start | bytes 1540
  122.8 164.1 %copy-start.31 = (f32[128]{0:T(128)}, f32[128]{0:T(128)S(1)}, u32[]{:S(2)}) copy-start(f32[128]{0:T(128)S(1)} %add_rsqrt_fusion) | copy-start | bytes 1540
  201.7 80.1 %copy-start.17 = (bf16[128,768]{1,0:T(8,128)(2,1)S(1)}, bf16[128,768]{1,0:T(8,128)(2,1)}, u32[]{:S(2)}) copy-start(bf16[128,768]{1,0:T(8,128)(2,1)} %param.17) | copy-start | bytes 589828
  281.8 5.0 copy-start
  286.8 2.4 copy-start.2
  286.8 2.3 copy-start.18
  292.5 4.5 copy-start.9
  292.5 199.0 %reduce-scatter.5.cloned.1.call-start = ((), (), s32[]{:S(2)}) async-start(), calls=%async_computation.4 | async-start | bytes 7962624 | tf_op jit(solution)/shard_map/reduce_scatter | solution.py:213
  297.0 1.5 copy-start.5
  298.4 1.2 copy-start.10
  298.6 1.7 copy-start.24
  298.6 1.6 copy-start.29
  298.6 1.6 copy-start.33
  304.4 1.1 copy-start.26
  304.4 353.7 %reduce-scatter.9.cloned.1.call-start = ((), (), s32[]{:S(2)}) async-start(), calls=%async_computation.6 | async-start | bytes 10616832 | tf_op jit(solution)/shard_map/reduce_scatter | solution.py:219
  311.3 513.4 %reduce-scatter.11.cloned.1.call-start = ((), (), s32[]{:S(2)}) async-start(), calls=%async_computation.7 | async-start | bytes 10616832 | tf_op jit(solution)/shard_map/reduce_scatter | solution.py:221
  317.4 3.2 copy-start.12
  317.4 3.2 copy-start.14
  317.4 584.5 %all-reduce.21.cloned.1.call-start = ((), (), s32[]{:S(2)}) async-start(), calls=%async_computation.12 | async-start | bytes 7077888 | tf_op jit(solution)/shard_map/psum | solution.py:224
  320.9 4.1 copy-start.27
  824.7 8.2 copy-start.48
  824.7 8.2 copy-start.47
  824.7 8.2 copy-start.30
  824.7 8.2 copy-start.34
  824.7 9.1 copy-start.35
  902.0 2.3 copy-start.20
  902.0 3.0 copy-start.16
  904.2 1.7 copy-start.15
  (10 other events, 8.9 us)
Sparse Core Ops, SparseCore 0:
  10.3 68.5 all-gather.16
  81.1 39.6 all-gather.18
  123.0 78.6 all-gather.20
  203.7 78.0 all-gather.22
  292.6 67.2 reduce-scatter.6
  363.5 128.0 reduce-scatter.4
  495.5 162.4 reduce-scatter.8
  662.1 162.5 reduce-scatter.10
  827.4 74.4 all-reduce.20
where the time goes:
time: 914 us
  waiting for transfers between devices  723 us (79%)
  blocking collectives  109 us (12%)
  matrix products  45.5 us (5%)
  between operations  17.8 us (2%)
  local copies, waits for them, and re-layouts  13.4 us (1%)
    reduce_scatter x1, waiting for transfers between devices, own_grads(): lax.psum_scatter(gradients[10], 'shard', scatter_dimension=0, tiled=True)  167 us
    reduce_scatter x1, waiting for transfers between devices, own_grads(): lax.psum_scatter(gradients[8], 'shard', scatter_dimension=0, tiled=True)  167 us
    reduce_scatter x1, waiting for transfers between devices, own_grads(): lax.psum_scatter(gradients[2], 'shard', scatter_dimension=0, tiled=True)  131 us
    all_gather x1, waiting for transfers between devices, per_device(): lax.all_gather(fc_weight[layer_index], 'shard', axis=0, tiled=True)  78.9 us
    all_gather x1, waiting for transfers between devices, per_device(): lax.all_gather(proj_weight[layer_index], 'shard', axis=0, tiled=True)  76.8 us
    unnamed x2, blocking collectives  75.3 us
    psum x1, waiting for transfers between devices, own_grads(): lax.psum((shares[0], shares[1], shares[2], shares[3], shares[4], shares[5...  64.1 us
    all_gather x1, waiting for transfers between devices, per_device(): lax.all_gather(out_weight[layer_index], 'shard', axis=0, tiled=True)  36.8 us
  transfers between devices with their start and end apart: 9, of which 7 were waited for; matrix products, arithmetic and copies ran while one was open for 5% of the time, Pallas kernels for 0%

commit v1 on v0

v1 whole, which is shorter than its diff:
```python
import jax
import jax.numpy as jnp
from jax import lax
from jax.sharding import PartitionSpec as P

HEADS = 12
HEAD = 64
LAYERS = 1

epsilon = 1e-05

def to_float(value):
    return value.astype(jnp.float32)


def layer_norm(inputs, norm_gain, norm_shift):
    center = inputs - jnp.mean(inputs, axis=-1, keepdims=True)
    inverse_std = lax.rsqrt(jnp.mean(center * center, axis=-1, keepdims=True) + epsilon)
    normed = center * inverse_std
    return (normed * norm_gain + norm_shift, normed, inverse_std)


def norm_back(upstream, normed, inverse_std, norm_gain):
    scaled = upstream * norm_gain
    inner_term = scaled - jnp.mean(scaled, axis=-1, keepdims=True)
    inner_term = inner_term - normed * jnp.mean(scaled * normed, axis=-1, keepdims=True)
    return (inverse_std * inner_term, jnp.sum(upstream * normed, axis=0), jnp.sum(upstream, axis=0))


def layer_forward(inputs, allowed, small, weights):
    ln1_gain, ln1_bias, qv_bias, out_bias, ln2_gain, ln2_bias, fc_bias, proj_bias = small
    qkv_weight, out_weight, fc_weight, proj_weight = weights
    row_count = inputs.shape[0]
    width_all = inputs.shape[1]
    first_norm, normed_one, inverse_one = layer_norm(inputs, ln1_gain, ln1_bias)
    first_low = first_norm.astype(jnp.bfloat16)
    offset = jnp.concatenate(
        [qv_bias[:width_all], jnp.zeros((width_all,), jnp.float32), qv_bias[width_all:]]
    )
    projected = (
        jnp.dot(first_low, qkv_weight, preferred_element_type=jnp.float32) + offset
    ).astype(jnp.bfloat16)
    queries = projected[:, :width_all].reshape(row_count, HEADS, HEAD)
    keys_all = projected[:, width_all : 2 * width_all].reshape(row_count, HEADS, HEAD)
    values_all = projected[:, 2 * width_all :].reshape(row_count, HEADS, HEAD)
    scores = jnp.einsum(
        "qhd,khd->hqk", queries, keys_all, preferred_element_type=jnp.float32
    ) * HEAD ** (-0.5)
    scores = jnp.where(allowed[None], scores, -1e30)
    row_max = jnp.max(scores, axis=-1, keepdims=True)
    log_total = row_max + jnp.log(jnp.sum(jnp.exp(scores - row_max), axis=-1, keepdims=True))
    attn_probs = jnp.exp(scores - log_total)
    probs_low = attn_probs.astype(jnp.bfloat16)
    attn_mixed = jnp.einsum(
        "hqk,khd->qhd", probs_low, values_all, preferred_element_type=jnp.float32
    )
    attn_mixed = attn_mixed.reshape(row_count, width_all).astype(jnp.bfloat16)
    after_attn = (
        inputs + jnp.dot(attn_mixed, out_weight, preferred_element_type=jnp.float32) + out_bias
    )
    second_norm, normed_two, inverse_two = layer_norm(after_attn, ln2_gain, ln2_bias)
    second_low = second_norm.astype(jnp.bfloat16)
    hidden_pre = jnp.dot(second_low, fc_weight, preferred_element_type=jnp.float32) + fc_bias
    hidden_low = jax.nn.gelu(hidden_pre, approximate=True).astype(jnp.bfloat16)
    result = (
        after_attn + jnp.dot(hidden_low, proj_weight, preferred_element_type=jnp.float32) + proj_bias
    )
    return dict(
        normed_one=normed_one,
        inverse_one=inverse_one,
        first_low=first_low,
        queries=queries,
        keys_all=keys_all,
        values_all=values_all,
        attn_probs=attn_probs,
        probs_low=probs_low,
        attn_mixed=attn_mixed,
        normed_two=normed_two,
        inverse_two=inverse_two,
        second_low=second_low,
        hidden_pre=hidden_pre,
        hidden_low=hidden_low,
        result=result,
    )


def layer_backward(upstream, saved, small, weights):
    ln1_gain, ln1_bias, qv_bias, out_bias, ln2_gain, ln2_bias, fc_bias, proj_bias = small
    qkv_weight, out_weight, fc_weight, proj_weight = weights
    row_count = upstream.shape[0]
    width_all = upstream.shape[1]
    proj_in = upstream.astype(jnp.bfloat16)
    grad_proj_b = jnp.sum(to_float(proj_in), axis=0)
    hidden_grad = jnp.einsum("td,fd->tf", proj_in, proj_weight, preferred_element_type=jnp.float32)
    _, gelu_pull = jax.vjp(lambda value: jax.nn.gelu(value, approximate=True), saved["hidden_pre"])
    pre_grad = gelu_pull(hidden_grad)[0].astype(jnp.bfloat16)
    grad_fc_b = jnp.sum(to_float(pre_grad), axis=0)
    second_grad = jnp.einsum("tf,df->td", pre_grad, fc_weight, preferred_element_type=jnp.float32)
    norm_part, grad_ln2_g, grad_ln2_b = norm_back(
        second_grad, saved["normed_two"], saved["inverse_two"], ln2_gain
    )
    residual_grad = upstream + norm_part
    branch_in = residual_grad.astype(jnp.bfloat16)
    grad_out_b = jnp.sum(to_float(branch_in), axis=0)
    mixed_grad = jnp.einsum("td,cd->tc", branch_in, out_weight, preferred_element_type=jnp.float32)
    mixed_grad = mixed_grad.astype(jnp.bfloat16).reshape(row_count, HEADS, HEAD)
    prob_grad = jnp.einsum(
        "qhd,khd->hqk", mixed_grad, saved["values_all"], preferred_element_type=jnp.float32
    )
    value_grad = jnp.einsum(
        "hqk,qhd->khd", saved["probs_low"], mixed_grad, preferred_element_type=jnp.float32
    )
    attn_probs = saved["attn_probs"]
    row_delta = jnp.sum(attn_probs * prob_grad, axis=-1, keepdims=True)
    score_grad = (attn_probs * (prob_grad - row_delta)).astype(jnp.bfloat16)
    query_grad = jnp.einsum(
        "hqk,khd->qhd", score_grad, saved["keys_all"], preferred_element_type=jnp.float32
    ) * HEAD ** (-0.5)
    key_grad = jnp.einsum(
        "hqk,qhd->khd", score_grad, saved["queries"], preferred_element_type=jnp.float32
    ) * HEAD ** (-0.5)
    joined_grad = jnp.concatenate(
        [
            query_grad.reshape(row_count, width_all),
            key_grad.reshape(row_count, width_all),
            value_grad.reshape(row_count, width_all),
        ],
        axis=1,
    ).astype(jnp.bfloat16)
    column_sums = jnp.sum(to_float(joined_grad), axis=0)
    grad_qv_b = jnp.concatenate([column_sums[:width_all], column_sums[2 * width_all :]])
    first_grad = jnp.einsum(
        "te,ce->tc", joined_grad, qkv_weight, preferred_element_type=jnp.float32
    )
    norm_first, grad_ln1_g, grad_ln1_b = norm_back(
        first_grad, saved["normed_one"], saved["inverse_one"], ln1_gain
    )
    small_grads = (
        grad_ln1_g,
        grad_ln1_b,
        grad_qv_b,
        grad_out_b,
        grad_ln2_g,
        grad_ln2_b,
        grad_fc_b,
        grad_proj_b,
    )
    pairs = (
        (saved["first_low"], joined_grad),
        (saved["attn_mixed"], branch_in),
        (saved["second_low"], pre_grad),
        (saved["hidden_low"], proj_in),
    )
    return (residual_grad + norm_first, small_grads, pairs)


def swap_core(value):
    rep = lax.axis_size("rep")
    return lax.ppermute(value, "rep", perm=[(i, i ^ 1) for i in range(rep)])


def swap_x(value):
    rep = lax.axis_size("rep")
    return lax.ppermute(value, "rep", perm=[(i, i ^ 2) for i in range(rep)])


def join_halves(mine, theirs, core, axis):
    first = jnp.where(core == 0, mine, theirs)
    second = jnp.where(core == 0, theirs, mine)
    return jnp.concatenate([first, second], axis=axis)


def take_half(value, core, axis):
    half = value.shape[axis] // 2
    return lax.dynamic_slice_in_dim(value, core * half, half, axis=axis)


def per_device(
    tokens,
    segment_ids,
    cotangent,
    ln1_gain,
    ln1_bias,
    qkv_weight,
    qv_bias,
    out_weight,
    out_bias,
    ln2_gain,
    ln2_bias,
    fc_weight,
    fc_bias,
    proj_weight,
    proj_bias,
):
    rep = lax.axis_size("rep")
    assert rep == 4
    core = lax.axis_index("rep") % 2
    row_count = tokens.shape[0]
    positions = jnp.arange(row_count)
    allowed = (segment_ids[:, None] == segment_ids[None, :]) & (
        positions[None, :] <= positions[:, None]
    )
    layer_index = 0
    small_local = (ln1_gain, ln1_bias, qv_bias, out_bias, ln2_gain, ln2_bias, fc_bias, proj_bias)
    small_local = [v[layer_index] for v in small_local]
    widths = [v.shape[0] for v in small_local]
    packed = jnp.concatenate(small_local)
    packed_all = lax.all_gather(packed, "shard", axis=0, tiled=False)
    small = []
    start = 0
    for width in widths:
        small.append(to_float(packed_all[:, start : start + width].reshape(-1)))
        start += width
    small = tuple(small)

    local_weights = (
        qkv_weight[layer_index],
        out_weight[layer_index],
        fc_weight[layer_index],
        proj_weight[layer_index],
    )
    weights = []
    for local in local_weights:
        mine = lax.all_gather(take_half(local, core, 1), "shard", axis=0, tiled=True)
        theirs = swap_core(mine)
        weights.append(join_halves(mine, theirs, core, 1))
    weights = tuple(weights)

    residual = to_float(tokens)
    saved = layer_forward(residual, allowed, small, weights)
    out_tokens = saved["result"].astype(jnp.bfloat16)
    upstream = to_float(cotangent)
    input_grad, small_grads, pairs = layer_backward(upstream, saved, small, weights)

    outgoing = jnp.concatenate(
        [x for x, _ in pairs] + [take_half(dy, 1 - core, 1) for _, dy in pairs], axis=1
    )
    incoming = swap_core(outgoing)
    start = 0
    partner_x = []
    for x, _ in pairs:
        partner_x.append(incoming[:, start : start + x.shape[1]])
        start += x.shape[1]
    partner_dy = []
    for _, dy in pairs:
        partner_dy.append(incoming[:, start : start + dy.shape[1] // 2])
        start += dy.shape[1] // 2

    owned = []
    for (x, dy), px, pdy in zip(pairs, partner_x, partner_dy):
        rows = jnp.concatenate([x, px], axis=0)
        grads = jnp.concatenate([take_half(dy, core, 1), pdy], axis=0)
        half_grad = jnp.einsum("tc,te->ce", rows, grads, preferred_element_type=jnp.float32)
        share = lax.psum_scatter(half_grad, "shard", scatter_dimension=0, tiled=True)
        share = share + swap_x(share)
        owned.append(join_halves(share, swap_core(share), core, 1)[None])

    shard = lax.axis_size("shard")
    small_split = jnp.concatenate(
        [g.reshape(shard, -1) for g in small_grads], axis=1
    )
    small_share = lax.psum_scatter(small_split, "shard", scatter_dimension=0, tiled=True)
    small_share = lax.psum(small_share, "rep")
    small_owned = []
    start = 0
    for g in small_grads:
        width = g.shape[0] // shard
        small_owned.append(small_share[:, start : start + width])
        start += width

    (g_ln1_g, g_ln1_b, g_qv_b, g_out_b, g_ln2_g, g_ln2_b, g_fc_b, g_proj_b) = small_owned
    g_qkv, g_out, g_fc, g_proj = owned
    return (
        out_tokens,
        input_grad,
        g_ln1_g,
        g_ln1_b,
        g_qkv,
        g_qv_b,
        g_out,
        g_out_b,
        g_ln2_g,
        g_ln2_b,
        g_fc,
        g_fc_b,
        g_proj,
        g_proj_b,
    )


def solution(mesh):
    placed = (
        P(("rep", "shard"), None),
        P(("rep", "shard")),
        P(("rep", "shard"), None),
        P(None, "shard"),
        P(None, "shard"),
        P(None, "shard", None),
        P(None, "shard"),
        P(None, "shard", None),
        P(None, "shard"),
        P(None, "shard"),
        P(None, "shard"),
        P(None, "shard", None),
        P(None, "shard"),
        P(None, "shard", None),
        P(None, "shard"),
    )
    return jax.shard_map(
        per_device,
        mesh=mesh,
        in_specs=placed,
        out_specs=(
            P(("rep", "shard"), None),
            P(("rep", "shard"), None),
            P(None, "shard"),
            P(None, "shard"),
            P(None, "shard", None),
            P(None, "shard"),
            P(None, "shard", None),
            P(None, "shard"),
            P(None, "shard"),
            P(None, "shard"),
            P(None, "shard", None),
            P(None, "shard"),
            P(None, "shard", None),
            P(None, "shard"),
        ),
        check_vma=False,
    )
```

time: 914 us -> 578 us (0.63)
  waiting for transfers between devices: 723 us -> 362 us
  other arithmetic: 4.24 us -> 20.6 us
  matrix products: 45.5 us -> 30.8 us
  local copies, waits for them, and re-layouts: 13.4 us -> 24.4 us
    reduce_scatter x4, waiting for transfers between devices: 464 us -> 260 us  [per_device(): lax.psum_scatter(half_grad, 'shard', scatter_dimension=0, tiled=True)]
    all_gather x4 -> x3, waiting for transfers between devices: 193 us -> 85.2 us  [per_device(): lax.all_gather(take_half(local, core, 1), 'shard', axis=0, tiled=True)]
    psum x1 -> x0, waiting for transfers between devices: 64.1 us -> none  [own_grads(): lax.psum((shares[0], shares[1], shares[2], shares[3], shares[4], shares[5...]
    unnamed x2 -> x1, blocking collectives: 75.3 us -> 36 us
    all_gather x1 -> x2, blocking collectives: 26.1 us -> 64.5 us  [the longest x1 33.8 us: per_device(): lax.all_gather(take_half(local, core, 1), 'shard', axis=0, tiled=True)]
    ppermute x0 -> x13, waiting for transfers between devices: none -> 17.1 us  [the longest x4 12.8 us: swap_x(): return lax.ppermute(value, 'rep', perm=[(i, i ^ 2) for i in range(rep)])]
    select_n x0 -> x8, other arithmetic: none -> 9.24 us  [join_halves(): first = jnp.where(core == 0, mine, theirs)]
  transfers between devices with their start and end apart: 9 -> 20, of which waited for: 7 -> 8; matrix products, arithmetic and copies ran while one was open for 5% -> 9% of each run, Pallas kernels for 0% -> 0%
where the time goes in v1:
time: 578 us; the launch traced here: 577 us
  waiting for transfers between devices  362 us (63%)
  blocking collectives  116 us (20%)
  matrix products  30.8 us (5%)
  local copies, waits for them, and re-layouts  24.4 us (4%)
  other arithmetic  20.6 us (4%)
  between operations  15 us (3%)
  starting transfers between devices  7.69 us (1%)
    reduce_scatter x4, waiting for transfers between devices, per_device(): lax.psum_scatter(half_grad, 'shard', scatter_dimension=0, tiled=True)  260 us
    all_gather x3, waiting for transfers between devices, per_device(): lax.all_gather(take_half(local, core, 1), 'shard', axis=0, tiled=True)  85.2 us
    unnamed x1, blocking collectives  36 us
    all_gather x1, blocking collectives, per_device(): lax.all_gather(take_half(local, core, 1), 'shard', axis=0, tiled=True)  33.8 us
    all_gather x1, blocking collectives, per_device(): packed_all = lax.all_gather(packed, 'shard', axis=0, tiled=False)  30.8 us
    psum x1, blocking collectives, per_device(): small_share = lax.psum(small_share, 'rep')  15.9 us
    ppermute x4, waiting for transfers between devices, swap_x(): return lax.ppermute(value, 'rep', perm=[(i, i ^ 2) for i in range(rep)])  12.8 us
  transfers between devices with their start and end apart: 20, of which 8 were waited for; matrix products, arithmetic and copies ran while one was open for 9% of the time, Pallas kernels for 0%

profile of v1, /device:TPU:0, one launch (start us, length us, event | category | flops | bytes accessed | tf_op | source)
XLA Modules:
  0.0 576.9 jit_solution(5192218940658444994)
XLA Ops:
  7.4 1.8 constant_dynamic-slice_fusion.7
  9.3 0.8 constant_dynamic-slice_fusion.4
  10.1 1.7 constant_dynamic-slice_fusion.5
  11.9 33.8 %all-gather.2 = bf16[1,768,384]{2,1,0:T(8,128)(2,1)S(1)} all-gather(bf16[1,96,384]{2,1,0:T(8,128)(2,1)S(1)} %constant_dynamic-slice_fusion.6), channel_id=4, replica_groups=mesh['rep'=4,'shard'=8] {'shard'}, dimensions={1}, use_global_device_ids=true | all-gather | bytes 663552 | tf_op jit(solution)/shard_map/all_gather | solution.py:224
  45.9 30.8 %all-gather.5 = bf16[8,1,1152]{2,1,0:T(2,128)(2,1)S(1)} all-gather(bf16[1,1,1152]{2,1,0:T(2,128)(2,1)S(1)} %reshape.273), channel_id=2, replica_groups=mesh['rep'=4,'shard'=8] {'shard'}, dimensions={0}, use_global_device_ids=true | all-gather | bytes 20736 | tf_op jit(solution)/shard_map/all_gather | solution.py:208
  80.9 0.8 constant_dynamic-update-slice_fusion.3
  81.8 2.3 broadcast_select_fusion.7
  84.1 31.8 %all-gather.14.cloned.1.call-done = bf16[1,3072,384]{2,1,0:T(8,128)(2,1)} async-done(((bf16[1,384,384]{2,1,0:T(8,128)(2,1)}), bf16[1,3072,384]{2,1,0:T(8,128)(2,1)}) %all-gather.14.cloned.1.call-update) | async-done | bytes 2359312 | tf_op jit(solution)/shard_map/all_gather | solution.py:224
  115.8 53.4 %all-gather.12.cloned.1.call-done = bf16[1,768,1536]{2,1,0:T(8,128)(2,1)} async-done(((bf16[1,96,1536]{2,1,0:T(8,128)(2,1)}), bf16[1,768,1536]{2,1,0:T(8,128)(2,1)}) %all-gather.12.cloned.1.call-update) | async-done | bytes 2359312 | tf_op jit(solution)/shard_map/all_gather | solution.py:224
  169.2 1.8 broadcast_select_fusion.5
  175.0 1.1 fusion.84
  176.4 0.8 constant_dynamic-update-slice_fusion.1
  177.2 2.8 broadcast_select_fusion.3
  180.0 3.6 constant_dynamic-update-slice_fusion
  183.7 2.1 broadcast_select_fusion.1
  185.8 2.9 convert_reduce_fusion
  188.7 2.3 multiply_reduce_fusion.1
  191.0 0.8 convert_reduce_fusion.4
  194.6 0.8 constant_dynamic-slice_fusion.3
  196.1 1.9 constant_dynamic-slice_fusion.1
  199.2 4.2 collective-permute-done.4
  203.4 1.4 copy-done.6
  205.5 2.6 fusion.27
  208.3 1.0 fusion.77
  209.3 1.4 fusion.48
  210.8 1.2 slice.174
  212.0 3.2 fusion.11
  215.3 0.9 slice-done
  216.4 2.9 fusion.22
  221.1 3.5 fusion.43
  224.9 36.0 %all-reduce = f32[8,1152]{1,0:T(8,128)S(1)} all-reduce(f32[8,1152]{1,0:T(8,128)S(1)} %concatenate.82), channel_id=7, replica_groups=mesh['rep'=4,'shard'=8] {'shard'}, use_global_device_ids=true, to_apply=%region_19.20.clone | all-reduce | flops 9216 | bytes 73728
  260.9 4.2 fusion.19
  265.1 22.2 %reduce-scatter.5.cloned.1.call-done = f32[96,1152]{1,0:T(8,128)} async-done(((f32[768,1152]{1,0:T(8,128)}), f32[96,1152]{1,0:T(8,128)}) %reduce-scatter.5.cloned.1.call-update) | async-done | bytes 442384 | tf_op jit(solution)/shard_map/reduce_scatter | solution.py:254
  287.3 1.5 collective-permute-start.5
  288.8 0.9 fusion.42
  289.7 65.2 %reduce-scatter.7.cloned.1.call-done = f32[96,384]{1,0:T(8,128)} async-done(((f32[768,384]{1,0:T(8,128)}), f32[96,384]{1,0:T(8,128)}) %reduce-scatter.7.cloned.1.call-update) | async-done | bytes 147472 | tf_op jit(solution)/shard_map/reduce_scatter | solution.py:254
  354.9 1.5 collective-permute-start.7
  356.4 96.3 %reduce-scatter.11.cloned.1.call-done = f32[384,384]{1,0:T(8,128)} async-done(((f32[3072,384]{1,0:T(8,128)}), f32[384,384]{1,0:T(8,128)}) %reduce-scatter.11.cloned.1.call-update) | async-done | bytes 589840 | tf_op jit(solution)/shard_map/reduce_scatter | solution.py:254
  452.7 1.5 collective-permute-start.11
  454.8 15.9 %psum.7 = f32[1,1152]{1,0:T(1,128)S(1)} all-reduce(f32[1,1152]{1,0:T(1,128)S(1)} %constant_dynamic-slice_fusion.8), channel_id=1, replica_groups=mesh['rep'=4,'shard'=8] {'rep'}, use_global_device_ids=true, to_apply=%region_20.21 | all-reduce | flops 1152 | bytes 9216 | tf_op jit(solution)/shard_map/psum | solution.py:263
  470.7 0.9 add.174
  471.8 1.1 add.173
  475.3 76.0 %reduce-scatter.9.cloned.1.call-done = f32[96,1536]{1,0:T(8,128)} async-done(((f32[768,1536]{1,0:T(8,128)}), f32[96,1536]{1,0:T(8,128)}) %reduce-scatter.9.cloned.1.call-update) | async-done | bytes 589840 | tf_op jit(solution)/shard_map/reduce_scatter | solution.py:254
  551.3 1.5 collective-permute-start.9
  553.8 12.8 %collective-permute-done.9 = f32[96,1536]{1,0:T(8,128)S(1)} collective-permute-done((f32[96,1536]{1,0:T(8,128)}, f32[96,1536]{1,0:T(8,128)S(1)}, u32[]{:S(2)}, u32[]{:S(2)}) %collective-permute-start.9) | collective-permute-done | bytes 589856 | tf_op jit(solution)/shard_map/ppermute | solution.py:164
  566.7 1.0 maximum_bitcast_fusion.2
  567.8 1.1 maximum_bitcast_fusion.1
  569.0 1.1 maximum_bitcast_fusion
  (219 shorter events, 21.0 us)
Async XLA Ops:
  7.2 4.7 copy-start.29
  7.2 38.5 %copy-start.43 = (bf16[1,192]{1,0:T(2,128)(2,1)S(1)}, bf16[1,192]{1,0:T(2,128)(2,1)}, u32[]{:S(2)}) copy-start(bf16[1,192]{1,0:T(2,128)(2,1)} %param.21) | copy-start | bytes 1156
  7.2 38.5 %copy-start.42 = (bf16[1,384]{1,0:T(2,128)(2,1)S(1)}, bf16[1,384]{1,0:T(2,128)(2,1)}, u32[]{:S(2)}) copy-start(bf16[1,384]{1,0:T(2,128)(2,1)} %param.27) | copy-start | bytes 2308
  7.2 38.5 %copy-start.49 = (bf16[1,96]{1,0:T(2,128)(2,1)S(1)}, bf16[1,96]{1,0:T(2,128)(2,1)}, u32[]{:S(2)}) copy-start(bf16[1,96]{1,0:T(2,128)(2,1)} %param.29) | copy-start | bytes 580
  7.2 38.5 %copy-start.48 = (bf16[1,96]{1,0:T(2,128)(2,1)S(1)}, bf16[1,96]{1,0:T(2,128)(2,1)}, u32[]{:S(2)}) copy-start(bf16[1,96]{1,0:T(2,128)(2,1)} %param.25) | copy-start | bytes 580
  7.3 38.5 %copy-start.47 = (bf16[1,96]{1,0:T(2,128)(2,1)S(1)}, bf16[1,96]{1,0:T(2,128)(2,1)}, u32[]{:S(2)}) copy-start(bf16[1,96]{1,0:T(2,128)(2,1)} %param.24) | copy-start | bytes 580
  7.3 38.5 %copy-start.46 = (bf16[1,96]{1,0:T(2,128)(2,1)S(1)}, bf16[1,96]{1,0:T(2,128)(2,1)}, u32[]{:S(2)}) copy-start(bf16[1,96]{1,0:T(2,128)(2,1)} %param.23) | copy-start | bytes 580
  7.3 38.5 %copy-start.45 = (bf16[1,96]{1,0:T(2,128)(2,1)S(1)}, bf16[1,96]{1,0:T(2,128)(2,1)}, u32[]{:S(2)}) copy-start(bf16[1,96]{1,0:T(2,128)(2,1)} %param.19) | copy-start | bytes 580
  7.3 38.5 %copy-start.44 = (bf16[1,96]{1,0:T(2,128)(2,1)S(1)}, bf16[1,96]{1,0:T(2,128)(2,1)}, u32[]{:S(2)}) copy-start(bf16[1,96]{1,0:T(2,128)(2,1)} %param.18) | copy-start | bytes 580
  7.3 69.4 %copy-start.2 = (bf16[128,768]{1,0:T(8,128)(2,1)S(1)}, bf16[128,768]{1,0:T(8,128)(2,1)}, u32[]{:S(2)}) copy-start(bf16[128,768]{1,0:T(8,128)(2,1)} %param.15) | copy-start | bytes 589828
  7.3 73.5 %copy-start.41 = (s32[128]{0:T(128)S(1)}, s32[128]{0:T(128)}, u32[]{:S(2)}) copy-start(s32[128]{0:T(128)} %param.16) | copy-start | bytes 1540
  7.3 69.6 %all-gather.10.cloned.1.call-start = ((), (), s32[]{:S(2)}) async-start(), calls=%async_computation.8 | async-start | bytes 1990656 | tf_op jit(solution)/shard_map/all_gather | solution.py:224
  9.2 106.6 %all-gather.14.cloned.1.call-start = ((), (), s32[]{:S(2)}) async-start(), calls=%async_computation.10 | async-start | bytes 2654208 | tf_op jit(solution)/shard_map/all_gather | solution.py:224
  10.1 159.1 %all-gather.12.cloned.1.call-start = ((), (), s32[]{:S(2)}) async-start(), calls=%async_computation.9 | async-start | bytes 2654208 | tf_op jit(solution)/shard_map/all_gather | solution.py:224
  11.9 275.5 %reduce-scatter.5.cloned.1.call-start = ((), (), s32[]{:S(2)}) async-start(), calls=%async_computation.4 | async-start | bytes 3981312 | tf_op jit(solution)/shard_map/reduce_scatter | solution.py:254
  45.7 36.1 %collective-permute-start.1 = (bf16[768,384]{1,0:T(8,128)(2,1)S(1)}, bf16[768,384]{1,0:T(8,128)(2,1)}, u32[]{:S(2)}, u32[]{:S(2)}) collective-permute-start(bf16[768,384]{1,0:T(8,128)(2,1)S(1)} %bitcast.68), channel_id=1, source_target_pairs={{0,8},{8,0},{16,24},{24,16},{1,9},{9,1},{17,25},{25,17},{2,10},{10... | collective-permute-start | bytes 1769480 | tf_op jit(solution)/shard_map/ppermute | solution.py:159
  76.8 94.2 %copy-start.35 = (f32[128]{0:T(128)}, f32[128]{0:T(128)S(1)}, u32[]{:S(2)}) copy-start(f32[128]{0:T(128)S(1)} %broadcast_multiply_fusion.5) | copy-start | bytes 1540
  76.9 92.3 %copy-start.10 = (bf16[1,768,1152]{2,1,0:T(8,128)(2,1)S(1)}, bf16[1,768,1152]{2,1,0:T(8,128)(2,1)}, u32[]{:S(2)}) copy-start(bf16[1,768,1152]{2,1,0:T(8,128)(2,1)} %all-gather.10.cloned.1.call-done) | copy-start | bytes 5308420
  76.9 92.3 %collective-permute-start = (bf16[768,1152]{1,0:T(8,128)(2,1)}, bf16[768,1152]{1,0:T(8,128)(2,1)}, u32[]{:S(2)}, u32[]{:S(2)}) collective-permute-start(bf16[768,1152]{1,0:T(8,128)(2,1)} %bitcast.71), channel_id=1, source_target_pairs={{0,8},{8,0},{16,24},{24,16},{1,9},{9,1},{17,25},{25,17},{2,10},{10... | collective-permute-start | bytes 5308424 | tf_op jit(solution)/shard_map/ppermute | solution.py:159
  77.9 93.1 %copy-start.39 = (f32[128]{0:T(128)}, f32[128]{0:T(128)S(1)}, u32[]{:S(2)}) copy-start(f32[128]{0:T(128)S(1)} %add_rsqrt_fusion.1) | copy-start | bytes 1540
  79.4 91.6 %copy-start.26 = (f32[768]{0:T(1024)}, f32[768]{0:T(1024)S(1)}, u32[]{:S(2)}) copy-start(f32[768]{0:T(1024)S(1)} %reshape.261) | copy-start | bytes 9220
  81.8 89.3 %copy-start.15 = (bf16[128,768]{1,0:T(8,128)(2,1)}, bf16[128,768]{1,0:T(8,128)(2,1)S(1)}, u32[]{:S(2)}) copy-start(bf16[128,768]{1,0:T(8,128)(2,1)S(1)} %get-tuple-element.27) | copy-start | bytes 589828
  115.8 67.8 %collective-permute-start.3 = (bf16[3072,384]{1,0:T(8,128)(2,1)}, bf16[3072,384]{1,0:T(8,128)(2,1)}, u32[]{:S(2)}, u32[]{:S(2)}) collective-permute-start(bf16[3072,384]{1,0:T(8,128)(2,1)} %bitcast.69), channel_id=1, source_target_pairs={{0,8},{8,0},{16,24},{24,16},{1,9},{9,1},{17,25},{25,17},{2,10},{10... | collective-permute-start | bytes 7077896 | tf_op jit(solution)/shard_map/ppermute | solution.py:159
  169.2 8.0 %collective-permute-start.2 = (bf16[768,1536]{1,0:T(8,128)(2,1)}, bf16[768,1536]{1,0:T(8,128)(2,1)}, u32[]{:S(2)}, u32[]{:S(2)}) collective-permute-start(bf16[768,1536]{1,0:T(8,128)(2,1)} %bitcast.70), channel_id=1, source_target_pairs={{0,8},{8,0},{16,24},{24,16},{1,9},{9,1},{17,25},{25,17},{2,10},{10... | collective-permute-start | bytes 7077896 | tf_op jit(solution)/shard_map/ppermute | solution.py:159
  177.2 2.8 copy-start.17
  177.2 2.8 copy-start.34
  180.0 3.6 copy-start.5
  185.8 2.9 copy-start.3
  185.8 2.9 copy-start.4
  188.7 3.1 copy-start.22
  188.7 3.1 copy-start.24
  195.4 10.1 %copy-start.16 = (bf16[128,768]{1,0:T(8,128)(2,1)S(1)}, bf16[128,768]{1,0:T(8,128)(2,1)}, u32[]{:S(2)}) copy-start(bf16[128,768]{1,0:T(8,128)(2,1)} %copy-done.15) | copy-start | bytes 589828
  198.7 4.7 collective-permute-start.4
  208.1 146.8 %reduce-scatter.7.cloned.1.call-start = ((), (), s32[]{:S(2)}) async-start(), calls=%async_computation.5 | async-start | bytes 1327104 | tf_op jit(solution)/shard_map/reduce_scatter | solution.py:254
  209.3 2.7 copy-start.11
  210.8 241.9 %reduce-scatter.11.cloned.1.call-start = ((), (), s32[]{:S(2)}) async-start(), calls=%async_computation.7 | async-start | bytes 5308416 | tf_op jit(solution)/shard_map/reduce_scatter | solution.py:254
  215.3 336.1 %reduce-scatter.9.cloned.1.call-start = ((), (), s32[]{:S(2)}) async-start(), calls=%async_computation.6 | async-start | bytes 5308416 | tf_op jit(solution)/shard_map/reduce_scatter | solution.py:254
  260.9 27.9 %copy-start.25 = (f32[128,768]{1,0:T(8,128)S(1)}, f32[128,768]{1,0:T(8,128)}, u32[]{:S(2)}) copy-start(f32[128,768]{1,0:T(8,128)} %get-tuple-element.90) | copy-start | bytes 1179652
  287.3 184.4 %collective-permute-start.5 = (f32[96,1152]{1,0:T(8,128)}, f32[96,1152]{1,0:T(8,128)S(1)}, u32[]{:S(2)}, u32[]{:S(2)}) collective-permute-start(f32[96,1152]{1,0:T(8,128)} %reduce-scatter.5.cloned.1.call-done), channel_id=1, source_target_pairs={{0,16},{8,24},{16,0},{24,8},{1,17},{9,25},{17,1},{25,9},{2,18},{10... | collective-permute-start | bytes 1327112 | tf_op jit(solution)/shard_map/ppermute | solution.py:164
  354.9 115.9 %collective-permute-start.7 = (f32[96,384]{1,0:T(8,128)}, f32[96,384]{1,0:T(8,128)S(1)}, u32[]{:S(2)}, u32[]{:S(2)}) collective-permute-start(f32[96,384]{1,0:T(8,128)} %reduce-scatter.7.cloned.1.call-done), channel_id=1, source_target_pairs={{0,16},{8,24},{16,0},{24,8},{1,17},{9,25},{17,1},{25,9},{2,18},{10... | collective-permute-start | bytes 442376 | tf_op jit(solution)/shard_map/ppermute | solution.py:164
  452.7 100.9 %copy-start.19 = (f32[384,384]{1,0:T(8,128)S(1)}, f32[384,384]{1,0:T(8,128)}, u32[]{:S(2)}) copy-start(f32[384,384]{1,0:T(8,128)} %reduce-scatter.11.cloned.1.call-done) | copy-start | bytes 1769476
  452.7 100.9 %collective-permute-start.11 = (f32[384,384]{1,0:T(8,128)}, f32[384,384]{1,0:T(8,128)S(1)}, u32[]{:S(2)}, u32[]{:S(2)}) collective-permute-start(f32[384,384]{1,0:T(8,128)} %reduce-scatter.11.cloned.1.call-done), channel_id=1, source_target_pairs={{0,16},{8,24},{16,0},{24,8},{1,17},{9,25},{17,1},{25,9},{2,18},{10... | collective-permute-start | bytes 1769480 | tf_op jit(solution)/shard_map/ppermute | solution.py:164
  471.7 3.6 collective-permute-start.8
  472.8 80.8 %collective-permute-start.6 = (f32[96,1152]{1,0:T(8,128)S(1)}, f32[96,1152]{1,0:T(8,128)S(1)}, u32[]{:S(2)}, u32[]{:S(2)}) collective-permute-start(f32[96,1152]{1,0:T(8,128)S(1)} %add.173), channel_id=1, source_target_pairs={{0,8},{8,0},{16,24},{24,16},{1,9},{9,1},{17,25},{25,17},{2,10},{10... | collective-permute-start | bytes 1327112 | tf_op jit(solution)/shard_map/ppermute | solution.py:159
  551.3 15.3 %copy-start.20 = (f32[96,1536]{1,0:T(8,128)S(1)}, f32[96,1536]{1,0:T(8,128)}, u32[]{:S(2)}) copy-start(f32[96,1536]{1,0:T(8,128)} %reduce-scatter.9.cloned.1.call-done) | copy-start | bytes 1769476
  551.3 15.3 %collective-permute-start.9 = (f32[96,1536]{1,0:T(8,128)}, f32[96,1536]{1,0:T(8,128)S(1)}, u32[]{:S(2)}, u32[]{:S(2)}) collective-permute-start(f32[96,1536]{1,0:T(8,128)} %reduce-scatter.9.cloned.1.call-done), channel_id=1, source_target_pairs={{0,16},{8,24},{16,0},{24,8},{1,17},{9,25},{17,1},{25,9},{2,18},{10... | collective-permute-start | bytes 1769480 | tf_op jit(solution)/shard_map/ppermute | solution.py:164
  553.6 14.1 %collective-permute-start.12 = (f32[384,384]{1,0:T(8,128)S(1)}, f32[384,384]{1,0:T(8,128)S(1)}, u32[]{:S(2)}, u32[]{:S(2)}) collective-permute-start(f32[384,384]{1,0:T(8,128)S(1)} %add.176), channel_id=1, source_target_pairs={{0,8},{8,0},{16,24},{24,16},{1,9},{9,1},{17,25},{25,17},{2,10},{10... | collective-permute-start | bytes 1769480 | tf_op jit(solution)/shard_map/ppermute | solution.py:159
  566.7 2.2 collective-permute-start.10
  (24 other events, 38.9 us)
Sparse Core Ops, SparseCore 0:
  10.9 50.0 all-gather.9
  63.7 52.0 all-gather.13
  118.6 50.5 all-gather.11
  208.2 79.0 reduce-scatter.4
  291.1 63.6 reduce-scatter.6
  358.4 94.2 reduce-scatter.10
  456.3 94.9 reduce-scatter.8

commit v2 on v1

--- a/solution.py
+++ b/solution.py
@@ -201,30 +201,44 @@
         positions[None, :] <= positions[:, None]
     )
     layer_index = 0
+    shard = lax.axis_size("shard")
     small_local = (ln1_gain, ln1_bias, qv_bias, out_bias, ln2_gain, ln2_bias, fc_bias, proj_bias)
     small_local = [v[layer_index] for v in small_local]
     widths = [v.shape[0] for v in small_local]
-    packed = jnp.concatenate(small_local)
-    packed_all = lax.all_gather(packed, "shard", axis=0, tiled=False)
-    small = []
-    start = 0
-    for width in widths:
-        small.append(to_float(packed_all[:, start : start + width].reshape(-1)))
-        start += width
-    small = tuple(small)
-
     local_weights = (
         qkv_weight[layer_index],
         out_weight[layer_index],
         fc_weight[layer_index],
         proj_weight[layer_index],
     )
+    rows_local = local_weights[0].shape[0]
+    halves = [take_half(w, core, 1) for w in local_weights]
+    half_widths = [h.size // rows_local for h in halves]
+    slab = jnp.concatenate(
+        [h.reshape(rows_local, -1) for h in halves]
+        + [jnp.concatenate(small_local).reshape(rows_local, -1)],
+        axis=1,
+    )
+    gathered = lax.all_gather(slab, "shard", axis=0, tiled=True)
+    weight_cols = sum(half_widths)
+    theirs_all = swap_core(gathered[:, :weight_cols])
     weights = []
-    for local in local_weights:
-        mine = lax.all_gather(take_half(local, core, 1), "shard", axis=0, tiled=True)
-        theirs = swap_core(mine)
+    start = 0
+    for local, h, width in zip(local_weights, halves, half_widths):
+        def unslab(block):
+            return block.reshape(shard, rows_local, width).reshape(shard * h.shape[0], h.shape[1])
+        mine = unslab(gathered[:, start : start + width])
+        theirs = unslab(theirs_all[:, start : start + width])
         weights.append(join_halves(mine, theirs, core, 1))
+        start += width
     weights = tuple(weights)
+    packed_all = gathered[:, weight_cols:].reshape(shard, -1)
+    small = []
+    start = 0
+    for width in widths:
+        small.append(to_float(packed_all[:, start : start + width].reshape(-1)))
+        start += width
+    small = tuple(small)
 
     residual = to_float(tokens)
     saved = layer_forward(residual, allowed, small, weights)
@@ -246,21 +260,27 @@
         partner_dy.append(incoming[:, start : start + dy.shape[1] // 2])
         start += dy.shape[1] // 2
 
-    owned = []
+    grad_slabs = []
     for (x, dy), px, pdy in zip(pairs, partner_x, partner_dy):
         rows = jnp.concatenate([x, px], axis=0)
         grads = jnp.concatenate([take_half(dy, core, 1), pdy], axis=0)
         half_grad = jnp.einsum("tc,te->ce", rows, grads, preferred_element_type=jnp.float32)
-        share = lax.psum_scatter(half_grad, "shard", scatter_dimension=0, tiled=True)
-        share = share + swap_x(share)
-        owned.append(join_halves(share, swap_core(share), core, 1)[None])
-
-    shard = lax.axis_size("shard")
-    small_split = jnp.concatenate(
-        [g.reshape(shard, -1) for g in small_grads], axis=1
-    )
-    small_share = lax.psum_scatter(small_split, "shard", scatter_dimension=0, tiled=True)
-    small_share = lax.psum(small_share, "rep")
+        grad_slabs.append(half_grad.reshape(shard, -1, half_grad.shape[1]).reshape(shard * rows_local, -1))
+    small_split = jnp.concatenate([g.reshape(shard, -1) for g in small_grads], axis=1)
+    grad_slabs.append(small_split.reshape(shard * rows_local, -1))
+    share = lax.psum_scatter(jnp.concatenate(grad_slabs, axis=1), "shard", scatter_dimension=0, tiled=True)
+    share = share + swap_x(share)
+    partner_share = swap_core(share)
+    owned = []
+    start = 0
+    for h, width in zip(halves, half_widths):
+        def unslab(block):
+            return block.reshape(h.shape[0], h.shape[1])
+        mine = unslab(share[:, start : start + width])
+        theirs = unslab(partner_share[:, start : start + width])
+        owned.append(join_halves(mine, theirs, core, 1)[None])
+        start += width
+    small_share = (share[:, start:] + partner_share[:, start:]).reshape(1, -1)
     small_owned = []
     start = 0
     for g in small_grads:

time: 578 us -> 533 us (0.922)
  blocking collectives: 116 us -> 0 us
  local copies, waits for them, and re-layouts: 24.4 us -> 61.5 us
  waiting for transfers between devices: 362 us -> 398 us
  other arithmetic: 20.6 us -> 29.1 us
  starting transfers between devices: 7.69 us -> 1.74 us
    all_gather x2 -> x0, blocking collectives: 64.5 us -> none  [the longest x1 33.8 us: per_device(): lax.all_gather(take_half(local, core, 1), 'shard', axis=0, tiled=True)]
    unnamed x1 -> x0, blocking collectives: 36 us -> none
    all_gather x3 -> x1, waiting for transfers between devices: 85.2 us -> 114 us  [per_device(): gathered = lax.all_gather(slab, 'shard', axis=0, tiled=True)]
    ppermute x4 -> x1, waiting for transfers between devices: 12.8 us -> 40.2 us  [swap_x(): return lax.ppermute(value, 'rep', perm=[(i, i ^ 2) for i in range(rep)])]
    reduce_scatter x4 -> x1, waiting for transfers between devices: 260 us -> 233 us  [per_device(): lax.psum_scatter(jnp.concatenate(grad_slabs, axis=1), 'shard', scatter_di...]
    psum x1 -> x0, blocking collectives: 15.9 us -> none  [per_device(): small_share = lax.psum(small_share, 'rep')]
    select_n x0 -> x4, local copies, waits for them, and re-layouts: none -> 10.9 us  [the longest x2 5.88 us: join_halves(): second = jnp.where(core == 0, theirs, mine)]
    concatenate x1 -> x4, local copies, waits for them, and re-layouts: 0.1 us -> 8.42 us  [the longest x1 4.09 us: per_device(): jnp.concatenate(small_local).reshape(rows_local, -1)]
  transfers between devices with their start and end apart: 20 -> 6, of which waited for: 8 -> 5; matrix products, arithmetic and copies ran while one was open for 9% -> 2% of each run, Pallas kernels for 0% -> 0%
where the time goes in v2:
time: 533 us; the launch traced here: 532 us
  waiting for transfers between devices  398 us (75%)
  local copies, waits for them, and re-layouts  61.5 us (12%)
  other arithmetic  29.1 us (5%)
  matrix products  27.2 us (5%)
  between operations  14.7 us (3%)
    reduce_scatter x1, waiting for transfers between devices, per_device(): lax.psum_scatter(jnp.concatenate(grad_slabs, axis=1), 'shard', scatter_di...  233 us
    all_gather x1, waiting for transfers between devices, per_device(): gathered = lax.all_gather(slab, 'shard', axis=0, tiled=True)  114 us
    ppermute x1, waiting for transfers between devices, swap_x(): return lax.ppermute(value, 'rep', perm=[(i, i ^ 2) for i in range(rep)])  40.2 us
    unnamed x79, local copies, waits for them, and re-layouts  13.3 us
    ppermute x3, waiting for transfers between devices, swap_core(): return lax.ppermute(value, 'rep', perm=[(i, i ^ 1) for i in range(rep)])  10.7 us
  transfers between devices with their start and end apart: 6, of which 5 were waited for; matrix products, arithmetic and copies ran while one was open for 2% of the time, Pallas kernels for 0%

profile of v2, /device:TPU:0, one launch (start us, length us, event | category | flops | bytes accessed | tf_op | source)
XLA Modules:
  0.0 532.3 jit_solution(13321480627081432139)
XLA Ops:
  7.3 1.0 copy-done
  9.9 4.1 concatenate.78
  14.1 1.0 bitcast_dynamic-update-slice_fusion.1
  16.0 1.0 bitcast_dynamic-update-slice_fusion
  18.0 114.0 %all-gather.2.cloned.1.call-done = bf16[768,4620]{1,0:T(8,128)(2,1)} async-done(((bf16[96,4620]{1,0:T(8,128)(2,1)}), bf16[768,4620]{1,0:T(8,128)(2,1)}) %all-gather.2.cloned.1.call-update) | async-done | bytes 7096336 | tf_op jit(solution)/shard_map/all_gather | solution.py:222
  132.0 6.4 %slice.230 = bf16[768,4608]{1,0:T(8,128)(2,1)} slice(bf16[768,4620]{1,0:T(8,128)(2,1)} %all-gather.2.cloned.1.call-done), slice={[0:768], [0:4608]} | slice | bytes 14155776 | tf_op jit(solution)/shard_map/slice | solution.py:224
  140.8 9.3 %collective-permute-done = bf16[768,4608]{1,0:T(8,128)(2,1)} collective-permute-done((bf16[768,4608]{1,0:T(8,128)(2,1)}, bf16[768,4608]{1,0:T(8,128)(2,1)}, u32[]{:S(2)}, u32[]{:S(2)}) %collective-permute-start) | collective-permute-done | bytes 7077920 | tf_op jit(solution)/shard_map/ppermute | solution.py:159
  150.1 2.3 broadcast_select_fusion.5
  155.7 1.4 broadcast_select_fusion.7
  157.8 7.0 %broadcast_select_fusion = (bf16[768,1536]{1,0:T(8,128)(2,1)}, bf16[768,1536]{1,0:T(8,128)(2,1)}, bf16[768,1536]{1,0:T(8,128)(2,1)}, bf16[768,1536]{1,0:T(8,128)(2,1)}) fusion(pred[]{:T(512)S(6)} %eq.14, bf16[768,4608]{1,0:T(8,128)(2,1)} %collective-permute-done, bf16[768,4620]{1,0:T(8,128)(2,1)} %all-gather.2.cloned.1.call-done), kind=kLoop, calls=%fused_computation.9 | loop fusion | flops 4718592 | bytes 18874368 | tf_op jit(solution)/shard_map/jit(_where)/select_n | solution.py:169
  164.8 4.9 select_n.154
  169.7 3.3 constant_dynamic-update-slice_fusion.3
  173.0 4.9 select_n.156
  178.6 3.5 constant_dynamic-update-slice_fusion.2
  183.0 2.1 constant_dynamic-update-slice_fusion.4
  185.1 2.0 convert_reduce_fusion
  187.2 1.8 multiply_reduce_fusion.1
  189.0 1.0 convert_reduce_fusion.4
  191.3 1.1 convolution_convert_fusion
  192.4 1.4 multiply_reduce_fusion
  194.6 1.1 copy.57
  197.6 2.0 constant_dynamic-slice_fusion.1
  200.4 2.0 fusion.39
  203.6 1.4 collective-permute-done.1
  205.0 1.6 fusion.70
  206.6 1.2 slice.255
  207.8 3.2 fusion.10
  211.0 5.9 %reshape_reshape.2 = f32[768,1536]{1,0:T(8,128)} reshape(f32[3072,384]{1,0:T(8,128)} %fusion.10) | data formatting | bytes 9437184 | tf_op jit(solution)/shard_map/reshape;reshape | solution.py:268
  216.9 1.0 slice.250
  217.9 1.2 fusion.71
  219.1 2.5 convolution_dynamic-update-slice_fusion.1
  221.6 1.5 convolution_dynamic-update-slice_fusion.2
  223.1 1.0 slice.254
  224.1 3.0 convolution_dynamic-update-slice_fusion
  227.1 2.5 constant_dynamic-update-slice_fusion.9
  230.4 233.0 %reduce-scatter.2.cloned.1.call-done = f32[96,4620]{1,0:T(8,128)} async-done(((f32[768,4620]{1,0:T(8,128)}), f32[96,4620]{1,0:T(8,128)}) %reduce-scatter.2.cloned.1.call-update) | async-done | bytes 1774096 | tf_op jit(solution)/shard_map/reduce_scatter | solution.py:271
  463.4 1.5 collective-permute-start.2
  464.9 40.2 %collective-permute-done.2 = f32[96,4620]{1,0:T(8,128)S(1)} collective-permute-done((f32[96,4620]{1,0:T(8,128)}, f32[96,4620]{1,0:T(8,128)S(1)}, u32[]{:S(2)}, u32[]{:S(2)}) %collective-permute-start.2) | collective-permute-done | bytes 1774112 | tf_op jit(solution)/shard_map/ppermute | solution.py:164
  505.1 1.7 add.157
  507.0 2.0 fusion.38
  509.0 3.8 fusion.17
  515.6 2.6 slice_select_fusion.1
  518.2 1.0 select_n.172
  519.4 1.2 slice_select_fusion.5
  520.6 1.0 maximum_bitcast_fusion.2
  521.5 0.9 slice_select_fusion.7
  523.2 1.1 maximum_bitcast_fusion
  524.3 1.1 maximum_bitcast_fusion.1
  (164 shorter events, 22.1 us)
Async XLA Ops:
  7.2 1.1 copy-start
  7.2 124.8 %all-gather.2.cloned.1.call-start = ((), (), s32[]{:S(2)}) async-start(), calls=%async_computation.1 | async-start | bytes 8183808 | tf_op jit(solution)/shard_map/all_gather | solution.py:222
  17.0 0.9 copy-start.16
  17.9 120.5 %copy-start.2 = (bf16[128,768]{1,0:T(8,128)(2,1)S(1)}, bf16[128,768]{1,0:T(8,128)(2,1)}, u32[]{:S(2)}) copy-start(bf16[128,768]{1,0:T(8,128)(2,1)} %param.15) | copy-start | bytes 589828
  18.0 120.8 %copy-start.31 = (s32[128]{0:T(128)S(1)}, s32[128]{0:T(128)}, u32[]{:S(2)}) copy-start(s32[128]{0:T(128)} %param.16) | copy-start | bytes 1540
  18.0 445.5 %reduce-scatter.2.cloned.1.call-start = ((), (), s32[]{:S(2)}) async-start(), calls=%async_computation.2 | async-start | bytes 16367616 | tf_op jit(solution)/shard_map/reduce_scatter | solution.py:271
  132.0 6.9 %slice-start = ((bf16[768,4620]{1,0:T(8,128)(2,1)}), bf16[768,12]{1,0:T(8,128)(2,1)S(1)}, s32[]{:S(2)}) async-start(bf16[768,4620]{1,0:T(8,128)(2,1)} %all-gather.2.cloned.1.call-done), calls=%async_computation.3 | async-start | bytes 393216 | tf_op jit(solution)/shard_map/slice | solution.py:235
  138.4 11.6 %collective-permute-start = (bf16[768,4608]{1,0:T(8,128)(2,1)}, bf16[768,4608]{1,0:T(8,128)(2,1)}, u32[]{:S(2)}, u32[]{:S(2)}) collective-permute-start(bf16[768,4608]{1,0:T(8,128)(2,1)} %slice.230), channel_id=1, source_target_pairs={{0,8},{8,0},{16,24},{24,16},{1,9},{9,1},{17,25},{25,17},{2,10},{10... | collective-permute-start | bytes 21233672 | tf_op jit(solution)/shard_map/ppermute | solution.py:159
  140.8 11.7 %copy-start.22 = (bf16[128,768]{1,0:T(8,128)(2,1)}, bf16[128,768]{1,0:T(8,128)(2,1)S(1)}, u32[]{:S(2)}) copy-start(bf16[128,768]{1,0:T(8,128)(2,1)S(1)} %get-tuple-element.32) | copy-start | bytes 589828
  152.4 1.2 copy-start.8
  152.4 1.8 copy-start.10
  154.5 2.6 copy-start.14
  154.8 2.3 copy-start.12
  157.1 7.7 %copy-start.26 = (bf16[768,384]{1,0:T(8,128)(2,1)}, bf16[768,384]{1,0:T(8,128)(2,1)S(1)}, u32[]{:S(2)}) copy-start(bf16[768,384]{1,0:T(8,128)(2,1)S(1)} %get-tuple-element.37) | copy-start | bytes 1769476
  157.1 7.6 %copy-start.28 = (bf16[768,384]{1,0:T(8,128)(2,1)}, bf16[768,384]{1,0:T(8,128)(2,1)S(1)}, u32[]{:S(2)}) copy-start(bf16[768,384]{1,0:T(8,128)(2,1)S(1)} %get-tuple-element.38) | copy-start | bytes 1769476
  178.6 4.4 copy-start.6
  178.6 4.4 copy-start.7
  182.1 3.0 slice-start.3
  183.0 2.1 copy-start.24
  183.0 2.1 slice-start.4
  183.0 2.1 copy-start.17
  187.2 1.8 copy-start.21
  187.2 2.8 copy-start.27
  187.2 2.8 copy-start.29
  189.9 0.7 copy-start.19
  190.6 0.7 copy-start.15
  192.4 1.9 copy-start.13
  194.3 2.6 copy-start.20
  196.0 3.6 copy-start.18
  196.0 4.4 copy-start.9
  196.0 4.4 copy-start.11
  200.3 4.7 collective-permute-start.1
  211.0 8.0 %copy-start.23 = (bf16[128,768]{1,0:T(8,128)(2,1)S(1)}, bf16[128,768]{1,0:T(8,128)(2,1)}, u32[]{:S(2)}) copy-start(bf16[128,768]{1,0:T(8,128)(2,1)} %copy-done.22) | copy-start | bytes 589828
  219.0 2.5 copy-start.30
  219.0 8.1 %slice-start.1 = ((s8[4718592]{0:T(1024)(128)(4,1)}), s8[4194304]{0:T(1024)(128)(4,1)S(1)}, s32[]{:S(2)}) async-start(s8[4718592]{0:T(1024)(128)(4,1)} %bitcast.60), calls=%async_computation.4 | async-start | bytes 8388608
  221.6 2.6 copy-start.25
  221.6 5.5 %slice-start.2 = ((s8[4718592]{0:T(1024)(128)(4,1)}), s8[524288]{0:T(1024)(128)(4,1)S(1)}, s32[]{:S(2)}) async-start(s8[4718592]{0:T(1024)(128)(4,1)} %bitcast.60), calls=%async_computation.5 | async-start | bytes 1048576
  463.4 41.7 %collective-permute-start.2 = (f32[96,4620]{1,0:T(8,128)}, f32[96,4620]{1,0:T(8,128)S(1)}, u32[]{:S(2)}, u32[]{:S(2)}) collective-permute-start(f32[96,4620]{1,0:T(8,128)} %reduce-scatter.2.cloned.1.call-done), channel_id=1, source_target_pairs={{0,16},{8,24},{16,0},{24,8},{1,17},{9,25},{17,1},{25,9},{2,18},{10... | collective-permute-start | bytes 5322248 | tf_op jit(solution)/shard_map/ppermute | solution.py:164
  506.8 6.0 %collective-permute-start.3 = (f32[96,4620]{1,0:T(8,128)S(1)}, f32[96,4620]{1,0:T(8,128)}, u32[]{:S(2)}, u32[]{:S(2)}) collective-permute-start(f32[96,4620]{1,0:T(8,128)S(1)} %add.157), channel_id=1, source_target_pairs={{0,8},{8,0},{16,24},{24,16},{1,9},{9,1},{17,25},{25,17},{2,10},{10... | collective-permute-start | bytes 5322248 | tf_op jit(solution)/shard_map/ppermute | solution.py:159
  519.4 3.8 copy-start.3
  519.4 3.8 copy-start.4
  520.6 3.8 copy-start.5
  523.2 2.2 copy-start.1
Sparse Core Ops, SparseCore 0:
  18.1 113.8 all-gather.1
  230.6 232.8 reduce-scatter.1

commit v3 on v2

--- a/solution.py
+++ b/solution.py
@@ -1,7 +1,13 @@
+import functools
+
 import jax
 import jax.numpy as jnp
 from jax import lax
+from jax.experimental import pallas as pl
+from jax.experimental.pallas import tpu as pltpu
 from jax.sharding import PartitionSpec as P
+
+MESH = pl.DeviceIdType.MESH
 
 HEADS = 12
 HEAD = 64
@@ -152,6 +158,141 @@
         (saved["hidden_low"], proj_in),
     )
     return (residual_grad + norm_first, small_grads, pairs)
+
+
+def ring_position(shard_index, n):
+    if n != 8:
+        return shard_index
+    y = shard_index % 2
+    z = shard_index // 2
+    return z * (1 - 2 * y) + 7 * y
+
+
+def ring_shard(position, n):
+    position = position % n
+    if n != 8:
+        return position
+    y = position // 4
+    z = (position % 4) * (1 - 2 * y) + 3 * y
+    return z * 2 + y
+
+
+FIRST_CORE_HALF = (0, 3)
+
+
+def gather_kernel(n, count, *refs):
+    local = refs[:count]
+    full = refs[count : 2 * count]
+    ring_send, ring_recv, pair_send, pair_recv = refs[2 * count :]
+    rep = lax.axis_index("rep")
+    shard = lax.axis_index("shard")
+    core = rep % 2
+    step_dir = 1 - 2 * core
+    partner = (rep + step_dir, shard)
+    here = ring_position(shard, n)
+    target = (rep, ring_shard(here + step_dir, n))
+    source = (rep, ring_shard(here - step_dir, n))
+    steps = n // 2
+    split_last = n % 2 == 0
+
+    barrier = pltpu.get_barrier_semaphore()
+    for peer in (target, source, partner):
+        pl.semaphore_signal(barrier, inc=1, device_id=peer, device_id_type=MESH)
+    pl.semaphore_wait(barrier, 3)
+
+    def mine_at(k, w):
+        if split_last and k == steps:
+            return (core == 0) == (w in FIRST_CORE_HALF)
+        return True
+
+    def guarded(cond, fn):
+        if cond is True:
+            fn()
+        else:
+            pl.when(cond)(fn)
+
+    def slot(position):
+        return ring_shard(position, n)
+
+    def ring_copy(k, w):
+        src_pos = here - step_dir * (k - 1)
+        src = local[w] if k == 1 else full[w].at[slot(src_pos)]
+        return pltpu.make_async_remote_copy(
+            src_ref=src,
+            dst_ref=full[w].at[slot(src_pos)],
+            send_sem=ring_send.at[k - 1, w],
+            recv_sem=ring_recv.at[k - 1, w],
+            device_id=target,
+            device_id_type=MESH,
+        )
+
+    def incoming_ring(k, w):
+        pos = here - step_dir * k
+        return pltpu.make_async_remote_copy(
+            src_ref=full[w].at[slot(pos)],
+            dst_ref=full[w].at[slot(pos)],
+            send_sem=ring_send.at[k - 1, w],
+            recv_sem=ring_recv.at[k - 1, w],
+            device_id=source,
+            device_id_type=MESH,
+        )
+
+    def pair_copy(k, w, pos):
+        src = local[w] if k == 0 else full[w].at[slot(pos)]
+        return pltpu.make_async_remote_copy(
+            src_ref=src,
+            dst_ref=full[w].at[slot(pos)],
+            send_sem=pair_send.at[k, w],
+            recv_sem=pair_recv.at[k, w],
+            device_id=partner,
+            device_id_type=MESH,
+        )
+
+    for w in range(count):
+        pair_copy(0, w, here).start()
+    for w in range(count):
+        guarded(mine_at(1, w), lambda w=w: ring_copy(1, w).start())
+    for k in range(1, steps + 1):
+        for w in range(count):
+            def arrived(k=k, w=w):
+                incoming_ring(k, w).wait_recv()
+                if k < steps:
+                    guarded(mine_at(k + 1, w), lambda: ring_copy(k + 1, w).start())
+                pair_copy(k, w, here - step_dir * k).start()
+            guarded(mine_at(k, w), arrived)
+    for w in range(count):
+        pair_copy(0, w, here).wait_recv()
+    for k in range(1, steps + 1):
+        for w in range(count):
+            theirs = mine_at(k, w)
+            theirs = True if theirs is True else jnp.logical_not(theirs)
+            guarded(theirs, lambda k=k, w=w: pair_copy(k, w, here + step_dir * k).wait_recv())
+    for w in range(count):
+        pair_copy(0, w, here).wait_send()
+    for k in range(1, steps + 1):
+        for w in range(count):
+            def sent(k=k, w=w):
+                ring_copy(k, w).wait_send()
+                pair_copy(k, w, here - step_dir * k).wait_send()
+            guarded(mine_at(k, w), sent)
+
+
+def gather_weights(locals_, n):
+    count = len(locals_)
+    steps = n // 2
+    return pl.pallas_call(
+        functools.partial(gather_kernel, n, count),
+        out_shape=[jax.ShapeDtypeStruct((n,) + a.shape, a.dtype) for a in locals_],
+        in_specs=[pl.BlockSpec(memory_space=pl.ANY)] * count,
+        out_specs=[pl.BlockSpec(memory_space=pl.ANY)] * count,
+        scratch_shapes=[
+            pltpu.SemaphoreType.DMA((steps, count)),
+            pltpu.SemaphoreType.DMA((steps, count)),
+            pltpu.SemaphoreType.DMA((steps + 1, count)),
+            pltpu.SemaphoreType.DMA((steps + 1, count)),
+        ],
+        compiler_params=pltpu.CompilerParams(collective_id=0, has_side_effects=True),
+    )(*locals_)
 
 
 def swap_core(value):
@@ -212,27 +353,12 @@
         proj_weight[layer_index],
     )
     rows_local = local_weights[0].shape[0]
+    small_row = jnp.concatenate(small_local).reshape(1, -1)
+    fulls = gather_weights(list(local_weights) + [small_row], shard)
+    weights = tuple(f.reshape(-1, f.shape[-1]) for f in fulls[:4])
     halves = [take_half(w, core, 1) for w in local_weights]
     half_widths = [h.size // rows_local for h in halves]
-    slab = jnp.concatenate(
-        [h.reshape(rows_local, -1) for h in halves]
-        + [jnp.concatenate(small_local).reshape(rows_local, -1)],
-        axis=1,
-    )
-    gathered = lax.all_gather(slab, "shard", axis=0, tiled=True)
-    weight_cols = sum(half_widths)
-    theirs_all = swap_core(gathered[:, :weight_cols])
-    weights = []
-    start = 0
-    for local, h, width in zip(local_weights, halves, half_widths):
-        def unslab(block):
-            return block.reshape(shard, rows_local, width).reshape(shard * h.shape[0], h.shape[1])
-        mine = unslab(gathered[:, start : start + width])
-        theirs = unslab(theirs_all[:, start : start + width])
-        weights.append(join_halves(mine, theirs, core, 1))
-        start += width
-    weights = tuple(weights)
-    packed_all = gathered[:, weight_cols:].reshape(shard, -1)
+    packed_all = fulls[4].reshape(shard, -1)
     small = []
     start = 0
     for width in widths:

time: 533 us -> 459 us (0.86)
  waiting for transfers between devices: 398 us -> 276 us
  Pallas kernels: 0 us -> 77.3 us
  local copies, waits for them, and re-layouts: 61.5 us -> 31.5 us
  other arithmetic: 29.1 us -> 20.3 us
  matrix products: 27.2 us -> 35.8 us
    all_gather x1 -> x0, waiting for transfers between devices: 114 us -> none  [per_device(): gathered = lax.all_gather(slab, 'shard', axis=0, tiled=True)]
    pallas_call x0 -> x1, Pallas kernels: none -> 77.3 us  [gather_weights(): pl.pallas_call(functools.partial(gather_kernel, n, count), out_shape=[jax...]
    ppermute x3 -> x2, waiting for transfers between devices: 10.7 us -> 1.14 us  [swap_core(): return lax.ppermute(value, 'rep', perm=[(i, i ^ 1) for i in range(rep)])]
    unnamed x79 -> x77, local copies, waits for them, and re-layouts: 13.3 us -> 4.78 us
    select_n x1 -> x0, other arithmetic: 6.95 us -> none  [join_halves(): second = jnp.where(core == 0, theirs, mine)]
    slice x3 -> x0, local copies, waits for them, and re-layouts: 6.45 us -> none  [the longest x1 6.44 us: per_device(): theirs_all = swap_core(gathered[:, :weight_cols])]
  transfers between devices with their start and end apart: 6 -> 4, of which waited for: 5 -> 3; matrix products, arithmetic and copies ran while one was open for 2% -> 2% of each run, Pallas kernels for 0% -> 0%
where the time goes in v3:
time: 459 us; the launch traced here: 458 us
  waiting for transfers between devices  276 us (60%)
  Pallas kernels  77.3 us (17%)
  matrix products  35.8 us (8%)
  local copies, waits for them, and re-layouts  31.5 us (7%)
  other arithmetic  20.3 us (4%)
  between operations  14.7 us (3%)
    reduce_scatter x1, waiting for transfers between devices, per_device(): lax.psum_scatter(jnp.concatenate(grad_slabs, axis=1), 'shard', scatter_di...  235 us
    pallas_call x1, Pallas kernels, gather_weights(): pl.pallas_call(functools.partial(gather_kernel, n, count), out_shape=[jax...  77.3 us
    ppermute x1, waiting for transfers between devices, swap_x(): return lax.ppermute(value, 'rep', perm=[(i, i ^ 2) for i in range(rep)])  40.2 us
    dot_general x4, matrix products, per_device(): jnp.einsum('tc,te->ce', rows, grads, preferred_element_type=jnp.float32)  10.5 us
  transfers between devices with their start and end apart: 4, of which 3 were waited for; matrix products, arithmetic and copies ran while one was open for 2% of the time, Pallas kernels for 0%

profile of v3, /device:TPU:0, one launch (start us, length us, event | category | flops | bytes accessed | tf_op | source)
XLA Modules:
  0.0 458.0 jit_solution(2995683405337347279)
XLA Ops:
  7.2 0.7 reduce
  8.0 0.7 reduce.1
  8.7 4.1 concatenate.63
  13.4 77.3 %shard_map.254 = (bf16[8,96,2304]{2,1,0:T(8,128)(2,1)}, bf16[8,96,768]{2,1,0:T(8,128)(2,1)}, bf16[8,96,3072]{2,1,0:T(8,128)(2,1)}, bf16[8,384,768]{2,1,0:T(8,128)(2,1)}, bf16[8,1,1152]{2,1,0:T(2,128)(2,1)}) custom-call(bf16[96,2304]{1,0:T(8,128)(2,1)} %bitcast.98, bf16[96,768]{1,0:T(8,128)(2,1)} %bitcast.99, bf16[96,3072]{1,0:T(8,128)(2,1)} %bitcast.96, ...), custom_call_target="tpu_custom_call" | custom-call | tf_op jit(solution)/shard_map/pallas_call | solution.py:283
  90.6 0.8 copy.68
  93.0 0.8 constant_dynamic-update-slice_fusion.3
  93.8 2.7 fusion
  99.3 0.7 constant_dynamic-update-slice_fusion.2
  100.0 0.8 constant_dynamic-update-slice_fusion.1
  100.8 4.9 %constant_dynamic-update-slice_fusion = (bf16[128,8832]{1,0:T(8,128)(2,1)}, bf16[128,3072]{1,0:T(8,128)(2,1)}, f32[128,3072]{1,0:T(8,128)S(1)}) fusion(bf16[128,8832]{1,0:T(8,128)(2,1)} %get-tuple-element.39, f32[3072]{0:T(1024)S(1)} %reshape.301, bf16[128,768]{1,0:T(8,128)(2,1)S(1)} %get-tuple-element.40, bf16[768,3072]{1,0:T(8,128)(2,1)} %bitcast.75), kind=kOutput, calls=%fused_computation.109 | convolution fusion | flops 607911936 | bytes 8073216 | tf_op jit(solution)/shard_map/dot_general | solution.py:69
  105.8 5.0 %convert_reduce_fusion = (f32[3072]{0:T(1024)}, bf16[128,3072]{1,0:T(8,128)(2,1)S(1)}) fusion(f32[128,3072]{1,0:T(8,128)S(1)} %get-tuple-element.88, bf16[3072,768]{1,0:T(8,128)(2,1)} %bitcast.81, bf16[128,768]{1,0:T(8,128)(2,1)S(1)} %copy-done.16), kind=kOutput, calls=%fused_computation.19 | convolution fusion | flops 612627456 | bytes 7286784 | tf_op jit(solution)/shard_map/td,fd->tf/dot_general | solution.py:100
  110.8 2.3 multiply_reduce_fusion.1
  113.1 2.2 convert_reduce_fusion.4
  115.4 1.2 convolution_convert_fusion.1
  116.6 1.1 copy.51
  118.1 1.3 multiply_reduce_fusion
  121.2 0.8 constant_dynamic-slice_fusion.3
  122.7 0.8 constant_dynamic-slice_fusion.1
  123.6 0.7 constant_dynamic-slice_fusion
  124.8 2.1 fusion.37
  128.0 1.1 collective-permute-done
  129.1 1.0 fusion.62
  130.1 1.2 slice.205
  131.3 3.4 fusion.8
  134.7 5.8 %reshape_reshape.3 = f32[768,1536]{1,0:T(8,128)} reshape(f32[3072,384]{1,0:T(8,128)} %fusion.8) | data formatting | bytes 9437184 | tf_op jit(solution)/shard_map/reshape;reshape | solution.py:394
  140.5 1.0 slice.200
  141.5 1.2 fusion.63
  142.7 2.6 convolution_dynamic-update-slice_fusion.1
  145.4 1.4 convolution_dynamic-update-slice_fusion.2
  146.8 1.0 slice.204
  147.8 3.0 convolution_dynamic-update-slice_fusion
  150.9 2.5 constant_dynamic-update-slice_fusion.5
  153.3 0.8 constant_dynamic-update-slice_fusion.4
  154.2 235.0 %reduce-scatter.2.cloned.1.call-done = f32[96,4620]{1,0:T(8,128)} async-done(((f32[768,4620]{1,0:T(8,128)}), f32[96,4620]{1,0:T(8,128)}) %reduce-scatter.2.cloned.1.call-update) | async-done | bytes 1774096 | tf_op jit(solution)/shard_map/reduce_scatter | solution.py:397
  389.2 1.5 collective-permute-start.1
  390.7 40.2 %collective-permute-done.1 = f32[96,4620]{1,0:T(8,128)S(1)} collective-permute-done((f32[96,4620]{1,0:T(8,128)}, f32[96,4620]{1,0:T(8,128)S(1)}, u32[]{:S(2)}, u32[]{:S(2)}) %collective-permute-start.1) | collective-permute-done | bytes 1774112 | tf_op jit(solution)/shard_map/ppermute | solution.py:305
  430.9 1.7 add.153
  432.8 2.0 fusion.36
  434.8 3.8 fusion.15
  438.6 0.8 slice_add_fusion
  441.4 2.6 slice_select_fusion.1
  444.0 1.0 select_n.103
  445.1 1.1 slice_select_fusion.5
  446.2 1.0 maximum_bitcast_fusion.2
  447.2 1.0 slice_select_fusion.7
  448.2 0.7 maximum_bitcast_fusion.3
  449.0 1.1 maximum_bitcast_fusion
  450.1 1.1 maximum_bitcast_fusion.1
  (145 shorter events, 11.5 us)
Async XLA Ops:
  7.2 85.3 %copy-start.1 = (bf16[128,768]{1,0:T(8,128)(2,1)S(1)}, bf16[128,768]{1,0:T(8,128)(2,1)}, u32[]{:S(2)}) copy-start(bf16[128,768]{1,0:T(8,128)(2,1)} %param.15) | copy-start | bytes 589828
  7.2 382.0 %reduce-scatter.2.cloned.1.call-start = ((), (), s32[]{:S(2)}) async-start(), calls=%async_computation.1 | async-start | bytes 16367616 | tf_op jit(solution)/shard_map/reduce_scatter | solution.py:397
  92.6 4.0 copy-start.26
  92.8 3.8 copy-start.29
  93.8 2.8 copy-start.7
  96.6 0.7 copy-start.32
  96.8 1.3 copy-start.15
  97.0 1.1 copy-start.11
  97.2 1.0 copy-start.13
  97.3 1.3 copy-start.2
  98.2 7.5 %copy-start.9 = (bf16[128,768]{1,0:T(8,128)(2,1)}, bf16[128,768]{1,0:T(8,128)(2,1)S(1)}, u32[]{:S(2)}) copy-start(bf16[128,768]{1,0:T(8,128)(2,1)S(1)} %copy.58) | copy-start | bytes 589828
  99.0 11.7 %copy-start.28 = (f32[128]{0:T(128)}, f32[128]{0:T(128)S(1)}, u32[]{:S(2)}) copy-start(f32[128]{0:T(128)S(1)} %broadcast_multiply_fusion.4) | copy-start | bytes 1540
  99.3 11.5 %copy-start.31 = (f32[128]{0:T(128)}, f32[128]{0:T(128)S(1)}, u32[]{:S(2)}) copy-start(f32[128]{0:T(128)S(1)} %add_rsqrt_fusion) | copy-start | bytes 1540
  100.8 4.9 %copy-start.18 = (bf16[128,768]{1,0:T(8,128)(2,1)}, bf16[128,768]{1,0:T(8,128)(2,1)S(1)}, u32[]{:S(2)}) copy-start(bf16[128,768]{1,0:T(8,128)(2,1)S(1)} %get-tuple-element.40) | copy-start | bytes 589828
  100.8 4.9 %copy-start.16 = (bf16[128,768]{1,0:T(8,128)(2,1)S(1)}, bf16[128,768]{1,0:T(8,128)(2,1)}, u32[]{:S(2)}) copy-start(bf16[128,768]{1,0:T(8,128)(2,1)} %param.17) | copy-start | bytes 589828
  100.8 10.0 %slice-start.2 = ((s8[4718592]{0:T(1024)(128)(4,1)}), s8[4194304]{0:T(1024)(128)(4,1)S(1)}, s32[]{:S(2)}) async-start(s8[4718592]{0:T(1024)(128)(4,1)} %bitcast.76), calls=%async_computation.4 | async-start | bytes 8388608
  105.8 5.0 %slice-start.3 = ((s8[4718592]{0:T(1024)(128)(4,1)}), s8[524288]{0:T(1024)(128)(4,1)S(1)}, s32[]{:S(2)}) async-start(s8[4718592]{0:T(1024)(128)(4,1)} %bitcast.76), calls=%async_computation.5 | async-start | bytes 1048576
  118.0 1.5 copy-start.12
  119.4 0.9 copy-start.14
  121.1 2.5 copy-start.17
  121.2 3.6 copy-start
  121.2 3.6 copy-start.27
  121.2 3.5 copy-start.30
  124.2 2.9 copy-start.23
  124.2 3.0 copy-start.21
  124.3 3.0 copy-start.20
  124.3 3.1 copy-start.25
  124.3 3.1 copy-start.22
  124.3 4.8 %collective-permute-start = (bf16[128,8832]{1,0:T(8,128)(2,1)}, bf16[128,8832]{1,0:T(8,128)(2,1)}, u32[]{:S(2)}, u32[]{:S(2)}) collective-permute-start(bf16[128,8832]{1,0:T(8,128)(2,1)} %get-tuple-element.65), channel_id=1, source_target_pairs={{0,8},{8,0},{16,24},{24,16},{1,9},{9,1},{17,25},{25,17},{2,10},{10... | collective-permute-start | bytes 6782984 | tf_op jit(solution)/shard_map/ppermute | solution.py:300
  126.8 4.5 copy-start.3
  140.5 2.2 copy-start.8
  142.7 2.7 copy-start.10
  142.7 8.1 %slice-start = ((s8[4718592]{0:T(1024)(128)(4,1)}), s8[4194304]{0:T(1024)(128)(4,1)S(1)}, s32[]{:S(2)}) async-start(s8[4718592]{0:T(1024)(128)(4,1)} %bitcast.71), calls=%async_computation.2 | async-start | bytes 8388608
  145.3 2.5 copy-start.19
  145.4 5.5 %slice-start.1 = ((s8[4718592]{0:T(1024)(128)(4,1)}), s8[524288]{0:T(1024)(128)(4,1)S(1)}, s32[]{:S(2)}) async-start(s8[4718592]{0:T(1024)(128)(4,1)} %bitcast.71), calls=%async_computation.3 | async-start | bytes 1048576
  154.2 278.5 %copy-start.24 = (f32[8,96]{1,0:T(8,128)S(1)}, f32[8,96]{1,0:T(8,128)}, u32[]{:S(2)}) copy-start(f32[8,96]{1,0:T(8,128)} %get-tuple-element.68) | copy-start | bytes 9220
  389.2 41.7 %collective-permute-start.1 = (f32[96,4620]{1,0:T(8,128)}, f32[96,4620]{1,0:T(8,128)S(1)}, u32[]{:S(2)}, u32[]{:S(2)}) collective-permute-start(f32[96,4620]{1,0:T(8,128)} %reduce-scatter.2.cloned.1.call-done), channel_id=1, source_target_pairs={{0,16},{8,24},{16,0},{24,8},{1,17},{9,25},{17,1},{25,9},{2,18},{10... | collective-permute-start | bytes 5322248 | tf_op jit(solution)/shard_map/ppermute | solution.py:305
  432.6 6.0 %collective-permute-start.2 = (f32[96,4620]{1,0:T(8,128)S(1)}, f32[96,4620]{1,0:T(8,128)}, u32[]{:S(2)}, u32[]{:S(2)}) collective-permute-start(f32[96,4620]{1,0:T(8,128)S(1)} %add.153), channel_id=1, source_target_pairs={{0,8},{8,0},{16,24},{24,16},{1,9},{9,1},{17,25},{25,17},{2,10},{10... | collective-permute-start | bytes 5322248 | tf_op jit(solution)/shard_map/ppermute | solution.py:300
  446.2 2.7 copy-start.4
  446.2 2.7 copy-start.5
  447.2 2.8 copy-start.6
Sparse Core Ops, SparseCore 0:
  154.3 234.8 reduce-scatter.1

commit v4 on v3

--- a/solution.py
+++ b/solution.py
@@ -293,6 +293,151 @@
         ],
         compiler_params=pltpu.CompilerParams(collective_id=0, has_side_effects=True),
     )(*locals_)
+
+
+def add_rows(dst, parts, rows, chunk):
+    def body(i, carry):
+        window = pl.ds(pl.multiple_of(i * chunk, chunk), chunk)
+        total = parts[0][window, :]
+        for part in parts[1:]:
+            total = total + part[window, :]
+        dst[window, :] = total
+        return carry
+
+    lax.fori_loop(0, rows // chunk, body, 0)
+
+
+def reduce_kernel(n, count, *refs):
+    contrib = refs[:count]
+    out = refs[count : 2 * count]
+    land, send, other, own = (refs[2 * count + i * count : 2 * count + (i + 1) * count] for i in range(4))
+    load_sem, own_sem, ring_send, ring_recv, pair_send, pair_recv = refs[6 * count :]
+    rep = lax.axis_index("rep")
+    shard = lax.axis_index("shard")
+    core = rep % 2
+    step_dir = 1 - 2 * core
+    partner = (rep + step_dir, shard)
+    here = ring_position(shard, n)
+    target = (rep, ring_shard(here + step_dir, n))
+    source = (rep, ring_shard(here - step_dir, n))
+    steps = n // 2
+    split_first = n % 2 == 0
+
+    def carried(k, w):
+        if split_first and k == 1:
+            return (core == 0) == (w in FIRST_CORE_HALF)
+        return True
+
+    def guarded(cond, fn):
+        if cond is True:
+            fn()
+        else:
+            pl.when(cond)(fn)
+
+    def block_at(k):
+        return here + step_dir * (steps - k + 1)
+
+    def load(k, w):
+        return pltpu.make_async_copy(contrib[w].at[ring_shard(block_at(k), n)], send[w].at[k - 1], load_sem.at[k - 1, w])
+
+    def load_own(w):
+        return pltpu.make_async_copy(contrib[w].at[shard], own[w], own_sem.at[w])
+
+    def ring_copy(k, w, device):
+        return pltpu.make_async_remote_copy(
+            src_ref=send[w].at[k - 1],
+            dst_ref=land[w].at[k - 1],
+            send_sem=ring_send.at[k - 1, w],
+            recv_sem=ring_recv.at[k - 1, w],
+            device_id=device,
+            device_id_type=MESH,
+        )
+
+    def pair_copy(w):
+        return pltpu.make_async_remote_copy(
+            src_ref=land[w].at[steps - 1],
+            dst_ref=other[w],
+            send_sem=pair_send.at[w],
+            recv_sem=pair_recv.at[w],
+            device_id=partner,
+            device_id_type=MESH,
+        )
+
+    for w in range(count):
+        load_own(w).start()
+    for k in range(1, steps + 1):
+        for w in range(count):
+            guarded(carried(k, w), lambda k=k, w=w: load(k, w).start())
+
+    barrier = pltpu.get_barrier_semaphore()
+    for peer in (target, source, partner):
+        pl.semaphore_signal(barrier, inc=1, device_id=peer, device_id_type=MESH)
+    pl.semaphore_wait(barrier, 3)
+
+    for k in range(1, steps + 1):
+        for w in range(count):
+            def step(k=k, w=w):
+                load(k, w).wait()
+                if k > 1:
+                    def accumulate():
+                        ring_copy(k - 1, w, source).wait_recv()
+                        rows = send[w].shape[1]
+                        chunk = 8 if rows % 8 == 0 else rows
+                        add_rows(send[w].at[k - 1], [send[w].at[k - 1], land[w].at[k - 2]], rows, chunk)
+                    guarded(carried(k - 1, w), accumulate)
+                ring_copy(k, w, target).start()
+            guarded(carried(k, w), step)
+    for w in range(count):
+        ring_copy(steps, w, source).wait_recv()
+        pair_copy(w).start()
+    for w in range(count):
+        pair_copy(w).wait_recv()
+        load_own(w).wait()
+        rows = own[w].shape[0]
+        chunk = 8 if rows % 8 == 0 else rows
+        mine = land[w].at[steps - 1]
+
+        @pl.when(core == 0)
+        def _():
+            add_rows(out[w], [own[w], mine, other[w]], rows, chunk)
+
+        @pl.when(core == 1)
+        def _():
+            add_rows(out[w], [own[w], other[w], mine], rows, chunk)
+
+    for w in range(count):
+        pair_copy(w).wait_send()
+    for k in range(1, steps + 1):
+        for w in range(count):
+            guarded(carried(k, w), lambda k=k, w=w: ring_copy(k, w, target).wait_send())
+
+
+def reduce_gradients(contribs, n):
+    count = len(contribs)
+    steps = n // 2
+    blocks = [c.shape[1:] for c in contribs]
+    vmem = lambda shape: pltpu.VMEM(shape, jnp.float32)
+    return pl.pallas_call(
+        functools.partial(reduce_kernel, n, count),
+        out_shape=[jax.ShapeDtypeStruct(b, jnp.float32) for b in blocks],
+        in_specs=[pl.BlockSpec(memory_space=pl.ANY)] * count,
+        out_specs=[pl.BlockSpec(memory_space=pltpu.VMEM)] * count,
+        scratch_shapes=[vmem((steps,) + b) for b in blocks]
+        + [vmem((steps,) + b) for b in blocks]
+        + [vmem(b) for b in blocks]
+        + [vmem(b) for b in blocks]
+        + [
+            pltpu.SemaphoreType.DMA((steps, count)),
+            pltpu.SemaphoreType.DMA((count,)),
+            pltpu.SemaphoreType.DMA((steps, count)),
+            pltpu.SemaphoreType.DMA((steps, count)),
+            pltpu.SemaphoreType.DMA((count,)),
+            pltpu.SemaphoreType.DMA((count,)),
+        ],
+        compiler_params=pltpu.CompilerParams(
+            collective_id=1, has_side_effects=True, vmem_limit_bytes=60 * 1024 * 1024
+        ),
+    )(*contribs)
 
 
 def swap_core(value):
@@ -372,41 +517,33 @@
     upstream = to_float(cotangent)
     input_grad, small_grads, pairs = layer_backward(upstream, saved, small, weights)
 
-    outgoing = jnp.concatenate(
-        [x for x, _ in pairs] + [take_half(dy, 1 - core, 1) for _, dy in pairs], axis=1
-    )
+    outgoing = jnp.concatenate([x for x, _ in pairs] + [dy for _, dy in pairs], axis=1)
     incoming = swap_core(outgoing)
+    small_mine = jnp.concatenate([g.reshape(shard, -1) for g in small_grads], axis=1)
+    small_theirs = swap_core(small_mine)
+    small_chip = jnp.where(core == 0, small_mine + small_theirs, small_theirs + small_mine)
+    contribs = []
     start = 0
     partner_x = []
     for x, _ in pairs:
         partner_x.append(incoming[:, start : start + x.shape[1]])
         start += x.shape[1]
-    partner_dy = []
-    for _, dy in pairs:
-        partner_dy.append(incoming[:, start : start + dy.shape[1] // 2])
-        start += dy.shape[1] // 2
-
-    grad_slabs = []
-    for (x, dy), px, pdy in zip(pairs, partner_x, partner_dy):
-        rows = jnp.concatenate([x, px], axis=0)
-        grads = jnp.concatenate([take_half(dy, core, 1), pdy], axis=0)
-        half_grad = jnp.einsum("tc,te->ce", rows, grads, preferred_element_type=jnp.float32)
-        grad_slabs.append(half_grad.reshape(shard, -1, half_grad.shape[1]).reshape(shard * rows_local, -1))
-    small_split = jnp.concatenate([g.reshape(shard, -1) for g in small_grads], axis=1)
-    grad_slabs.append(small_split.reshape(shard * rows_local, -1))
-    share = lax.psum_scatter(jnp.concatenate(grad_slabs, axis=1), "shard", scatter_dimension=0, tiled=True)
-    share = share + swap_x(share)
-    partner_share = swap_core(share)
+    for (x, dy), px in zip(pairs, partner_x):
+        pdy = incoming[:, start : start + dy.shape[1]]
+        start += dy.shape[1]
+        rows = join_halves(x, px, core, 0)
+        grads = join_halves(dy, pdy, core, 0)
+        grad = jnp.einsum("tc,te->ce", rows, grads, preferred_element_type=jnp.float32)
+        contribs.append(grad.reshape(shard, -1, grad.shape[1]))
+    contribs.append(small_chip.reshape(shard, 1, -1))
+    plane = reduce_gradients(contribs, shard)
     owned = []
-    start = 0
-    for h, width in zip(halves, half_widths):
-        def unslab(block):
-            return block.reshape(h.shape[0], h.shape[1])
-        mine = unslab(share[:, start : start + width])
-        theirs = unslab(partner_share[:, start : start + width])
-        owned.append(join_halves(mine, theirs, core, 1)[None])
-        start += width
-    small_share = (share[:, start:] + partner_share[:, start:]).reshape(1, -1)
+    for total in plane:
+        half = take_half(total, core, 1)
+        half = half + swap_x(half)
+        owned.append(join_halves(half, swap_core(half), core, 1))
+    small_share = owned[4]
+    owned = [o[None] for o in owned[:4]]
     small_owned = []
     start = 0
     for g in small_grads:

time: 459 us -> 343 us (0.75)
  waiting for transfers between devices: 276 us -> 30.5 us
  Pallas kernels: 77.3 us -> 223 us
  between operations: 14.7 us -> 1.35 us
  local copies, waits for them, and re-layouts: 31.5 us -> 22.2 us
  starting transfers between devices: 2.06 us -> 7.26 us
  matrix products: 35.8 us -> 40.6 us
    reduce_scatter x1 -> x0, waiting for transfers between devices: 235 us -> none  [per_device(): lax.psum_scatter(jnp.concatenate(grad_slabs, axis=1), 'shard', scatter_di...]
    pallas_call x0 -> x1, Pallas kernels: none -> 146 us  [reduce_gradients(): pl.pallas_call(functools.partial(reduce_kernel, n, count), out_shape=[jax...]
    ppermute x1 -> x5, waiting for transfers between devices: 40.2 us -> 30.4 us  [swap_x(): return lax.ppermute(value, 'rep', perm=[(i, i ^ 2) for i in range(rep)])]
    another operation x1 -> x0, local copies, waits for them, and re-layouts: 5.84 us -> none  [per_device(): half_grad.reshape(shard, -1, half_grad.shape[1])]
    dot_general x4, matrix products: 10.5 us -> 16.1 us  [per_device(): jnp.einsum('tc,te->ce', rows, grads, preferred_element_type=jnp.float32)]
    slice x5 -> x0, local copies, waits for them, and re-layouts: 5.35 us -> none  [the longest x3 3.01 us: per_device(): partner_dy.append(incoming[:, start:start + dy.shape[1] // 2])]
  transfers between devices with their start and end apart: 4 -> 12, of which waited for: 3 -> 3; matrix products, arithmetic and copies ran while one was open for 2% -> 5% of each run, Pallas kernels for 0% -> 0%
where the time goes in v4:
time: 343 us
  Pallas kernels  223 us (65%)
  matrix products  40.6 us (12%)
  waiting for transfers between devices  30.5 us (9%)
  local copies, waits for them, and re-layouts  22.2 us (6%)
  other arithmetic  18 us (5%)
  starting transfers between devices  7.26 us (2%)
    pallas_call x1, Pallas kernels, reduce_gradients(): pl.pallas_call(functools.partial(reduce_kernel, n, count), out_shape=[jax...  146 us
    pallas_call x1, Pallas kernels, gather_weights(): pl.pallas_call(functools.partial(gather_kernel, n, count), out_shape=[jax...  77.3 us
    ppermute x5, waiting for transfers between devices, swap_x(): return lax.ppermute(value, 'rep', perm=[(i, i ^ 2) for i in range(rep)])  30.4 us
    dot_general x4, matrix products, per_device(): jnp.einsum('tc,te->ce', rows, grads, preferred_element_type=jnp.float32)  16.1 us
  transfers between devices with their start and end apart: 12, of which 3 were waited for; matrix products, arithmetic and copies ran while one was open for 5% of the time, Pallas kernels for 0%

profile of v4, /device:TPU:0, one launch (start us, length us, event | category | flops | bytes accessed | tf_op | source)
XLA Modules:
  0.0 342.8 jit_solution(6092812439392757210)
XLA Ops:
  0.7 0.7 reduce
  1.4 0.7 reduce.1
  2.1 4.1 %concatenate.61 = bf16[1152]{0:T(1024)(128)(2,1)S(1)} concatenate(bf16[96]{0:T(256)(128)(2,1)} %bitcast.107, bf16[96]{0:T(256)(128)(2,1)} %bitcast.108, bf16[192]{0:T(256)(128)(2,1)S(1)} %reduce, bf16[96]{0:T(256)(128)(2,1)} %bitcast.109, bf16[96]{0:T(256)(128)(2,1)} %bitcast.110, bf16[96]{0:T(256)(128)(2,1)} %bitcast.111, bf16[384]{0:T(512)(128)(2,1)S(1)} %reduce.1, ...), dimensions={0} | concatenate | bytes 4608 | tf_op jit(solution)/shard_map/concatenate | solution.py:501
  6.8 77.3 %shard_map.254 = (bf16[8,96,2304]{2,1,0:T(8,128)(2,1)}, bf16[8,96,768]{2,1,0:T(8,128)(2,1)}, bf16[8,96,3072]{2,1,0:T(8,128)(2,1)}, bf16[8,384,768]{2,1,0:T(8,128)(2,1)}, bf16[8,1,1152]{2,1,0:T(2,128)(2,1)}) custom-call(bf16[96,2304]{1,0:T(8,128)(2,1)} %bitcast.102, bf16[96,768]{1,0:T(8,128)(2,1)} %bitcast.103, bf16[96,3072]{1,0:T(8,128)(2,1)} %bitcast.100, ...), custom_call_target="tpu_custom_call" | custom-call | tf_op jit(solution)/shard_map/pallas_call | solution.py:283
  84.1 0.8 copy.70
  84.8 0.7 slice_convert_fusion.2
  86.4 0.8 constant_dynamic-update-slice_fusion.9
  87.2 2.7 fusion
  92.7 0.7 constant_dynamic-update-slice_fusion.8
  93.4 0.8 constant_dynamic-update-slice_fusion.7
  94.2 4.9 %constant_dynamic-update-slice_fusion.6 = (bf16[128,12288]{1,0:T(8,128)(2,1)}, bf16[128,3072]{1,0:T(8,128)(2,1)}, f32[128,3072]{1,0:T(8,128)S(1)}) fusion(bf16[128,12288]{1,0:T(8,128)(2,1)} %get-tuple-element.47, f32[3072]{0:T(1024)S(1)} %reshape.307, bf16[128,768]{1,0:T(8,128)(2,1)S(1)} %get-tuple-element.48, bf16[768,3072]{1,0:T(8,128)(2,1)} %bitcast.77), kind=kOutput, calls=%fused_computation.126 | convolution fusion | flops 607911936 | bytes 8073216 | tf_op jit(solution)/shard_map/dot_general | solution.py:69
  99.2 5.0 %convert_reduce_fusion = (f32[3072]{0:T(1024)}, bf16[128,3072]{1,0:T(8,128)(2,1)S(1)}) fusion(f32[128,3072]{1,0:T(8,128)S(1)} %get-tuple-element.107, bf16[3072,768]{1,0:T(8,128)(2,1)} %bitcast.83, bf16[128,768]{1,0:T(8,128)(2,1)S(1)} %copy-done.8), kind=kOutput, calls=%fused_computation.21 | convolution fusion | flops 612627456 | bytes 7286784 | tf_op jit(solution)/shard_map/td,fd->tf/dot_general | solution.py:100
  104.2 2.3 multiply_reduce_fusion.1
  106.5 2.2 convert_reduce_fusion.4
  108.8 1.2 convolution_convert_fusion.1
  110.0 1.1 copy.51
  113.5 0.7 constant_dynamic-update-slice_fusion.5
  114.2 0.7 constant_dynamic-update-slice_fusion.4
  114.9 0.7 constant_dynamic-update-slice_fusion.3
  115.7 0.7 constant_dynamic-update-slice_fusion.2
  116.4 1.0 constant_dynamic-update-slice_fusion.1
  117.3 0.7 constant_dynamic-update-slice_fusion
  118.6 2.1 fusion.39
  121.8 3.9 %fusion.23 = bf16[128,768]{1,0:T(8,128)(2,1)} fusion(f32[128,768]{1,0:T(8,128)S(1)} %get-tuple-element.106, bf16[128,3072]{1,0:T(8,128)(2,1)S(1)} %copy-done.3, bf16[3072,768]{1,0:T(8,128)(2,1)} %bitcast.84, f32[768]{0:T(1024)S(1)} %reshape.308), kind=kOutput, calls=%fused_computation.38 | convolution fusion | flops 604274688 | bytes 6097920 | tf_op jit(solution)/shard_map/dot_general | solution.py:72
  125.7 1.1 fusion.38
  127.4 1.3 broadcast_select_fusion.5
  128.7 1.1 broadcast_select_fusion.21
  129.9 4.0 %fusion.19 = f32[768,2304]{1,0:T(8,128)} fusion(bf16[128,2304]{1,0:T(8,128)(2,1)S(1)} %get-tuple-element.54, bf16[128,2304]{1,0:T(8,128)(2,1)S(1)} %get-tuple-element.53, bf16[128,768]{1,0:T(8,128)(2,1)S(1)} %get-tuple-element.56, bf16[128,768]{1,0:T(8,128)(2,1)S(1)} %get-tuple-element.55), kind=kOutput, calls=%fused_computation.31 | convolution fusion | flops 909115392 | bytes 8650752 | tf_op jit(solution)/shard_map/tc,te->ce/dot_general | solution.py:536
  133.9 1.3 broadcast_select_fusion.13
  135.3 1.9 fusion.44
  137.2 1.6 broadcast_select_fusion.1
  138.8 5.1 %fusion.8 = f32[768,3072]{1,0:T(8,128)} fusion(bf16[128,3072]{1,0:T(8,128)(2,1)S(1)} %get-tuple-element.71, bf16[128,3072]{1,0:T(8,128)(2,1)S(1)} %get-tuple-element.72, bf16[128,768]{1,0:T(8,128)(2,1)S(1)} %get-tuple-element.69, bf16[128,768]{1,0:T(8,128)(2,1)S(1)} %get-tuple-element.70), kind=kOutput, calls=%fused_computation.13 | convolution fusion | flops 1211891712 | bytes 11403264 | tf_op jit(solution)/shard_map/tc,te->ce/dot_general | solution.py:536
  143.8 5.1 %fusion.12 = f32[3072,768]{1,0:T(8,128)} fusion(bf16[128,3072]{1,0:T(8,128)(2,1)S(1)} %get-tuple-element.50, bf16[128,3072]{1,0:T(8,128)(2,1)S(1)} %get-tuple-element.49, bf16[128,768]{1,0:T(8,128)(2,1)S(1)} %get-tuple-element.58, bf16[128,768]{1,0:T(8,128)(2,1)S(1)} %get-tuple-element.57), kind=kOutput, calls=%fused_computation.17 | convolution fusion | flops 1211891712 | bytes 11403264 | tf_op jit(solution)/shard_map/tc,te->ce/dot_general | solution.py:536
  149.0 145.7 %shard_map.255 = (f32[96,2304]{1,0:T(8,128)}, f32[96,768]{1,0:T(8,128)}, f32[96,3072]{1,0:T(8,128)}, f32[384,768]{1,0:T(8,128)}, f32[1,1152]{1,0:T(1,128)}) custom-call(f32[8,96,2304]{2,1,0:T(8,128)} %bitcast.75, f32[8,96,768]{2,1,0:T(8,128)} %bitcast.76, f32[8,96,3072]{2,1,0:T(8,128)} %bitcast.74, f32[8,384,768]{2,1,0:T(8,128)} %bitcast.73, ...), custom_call_target="tpu_custom_call" | custom-call | tf_op jit(solution)/shard_map/pallas_call | solution.py:420
  294.7 0.9 constant_dynamic-slice_fusion.4
  295.6 1.5 collective-permute-start.2
  297.1 1.1 constant_dynamic-slice_fusion.3
  298.8 0.9 constant_dynamic-slice_fusion.2
  299.7 1.6 collective-permute-start.6
  301.3 1.1 constant_dynamic-slice_fusion.1
  303.1 1.6 collective-permute-start.10
  305.3 9.1 %collective-permute-done.6 = f32[96,384]{1,0:T(8,128)S(1)} collective-permute-done((f32[96,384]{1,0:T(8,128)S(1)}, f32[96,384]{1,0:T(8,128)S(1)}, u32[]{:S(2)}, u32[]{:S(2)}) %collective-permute-start.6) | collective-permute-done | bytes 147488 | tf_op jit(solution)/shard_map/ppermute | solution.py:450
  316.4 0.7 maximum_bitcast_fusion.3
  317.7 9.3 %collective-permute-done.8 = f32[96,1536]{1,0:T(8,128)S(1)} collective-permute-done((f32[96,1536]{1,0:T(8,128)S(1)}, f32[96,1536]{1,0:T(8,128)S(1)}, u32[]{:S(2)}, u32[]{:S(2)}) %collective-permute-start.8) | collective-permute-done | bytes 589856 | tf_op jit(solution)/shard_map/ppermute | solution.py:450
  327.2 12.1 %collective-permute-done.10 = f32[384,384]{1,0:T(8,128)S(1)} collective-permute-done((f32[384,384]{1,0:T(8,128)S(1)}, f32[384,384]{1,0:T(8,128)S(1)}, u32[]{:S(2)}, u32[]{:S(2)}) %collective-permute-start.10) | collective-permute-done | bytes 589856 | tf_op jit(solution)/shard_map/ppermute | solution.py:450
  339.5 1.0 maximum_bitcast_fusion.2
  340.6 1.1 maximum_bitcast_fusion
  341.7 1.1 maximum_bitcast_fusion.1
  (177 shorter events, 13.7 us)
Async XLA Ops:
  0.6 85.4 %copy-start = (bf16[128,768]{1,0:T(8,128)(2,1)S(1)}, bf16[128,768]{1,0:T(8,128)(2,1)}, u32[]{:S(2)}) copy-start(bf16[128,768]{1,0:T(8,128)(2,1)} %param.15) | copy-start | bytes 589828
  85.9 1.3 copy-start.23
  86.1 3.8 %copy-start.30 = (f32[128]{0:T(128)}, f32[128]{0:T(128)S(1)}, u32[]{:S(2)}) copy-start(f32[128]{0:T(128)S(1)} %broadcast_multiply_fusion.5) | copy-start | bytes 1540
  86.4 3.6 %copy-start.34 = (f32[128]{0:T(128)}, f32[128]{0:T(128)S(1)}, u32[]{:S(2)}) copy-start(f32[128]{0:T(128)S(1)} %add_rsqrt_fusion.1) | copy-start | bytes 1540
  90.2 1.3 copy-start.13
  91.6 2.6 copy-start.11
  92.4 11.7 %copy-start.33 = (f32[128]{0:T(128)}, f32[128]{0:T(128)S(1)}, u32[]{:S(2)}) copy-start(f32[128]{0:T(128)S(1)} %broadcast_multiply_fusion.4) | copy-start | bytes 1540
  92.7 11.5 %copy-start.38 = (f32[128]{0:T(128)}, f32[128]{0:T(128)S(1)}, u32[]{:S(2)}) copy-start(f32[128]{0:T(128)S(1)} %add_rsqrt_fusion) | copy-start | bytes 1540
  94.2 5.0 %copy-start.19 = (bf16[128,768]{1,0:T(8,128)(2,1)}, bf16[128,768]{1,0:T(8,128)(2,1)S(1)}, u32[]{:S(2)}) copy-start(bf16[128,768]{1,0:T(8,128)(2,1)S(1)} %get-tuple-element.48) | copy-start | bytes 589828
  94.2 5.0 %copy-start.8 = (bf16[128,768]{1,0:T(8,128)(2,1)S(1)}, bf16[128,768]{1,0:T(8,128)(2,1)}, u32[]{:S(2)}) copy-start(bf16[128,768]{1,0:T(8,128)(2,1)} %param.17) | copy-start | bytes 589828
  94.2 10.0 %slice-start = ((s8[4718592]{0:T(1024)(128)(4,1)}), s8[4194304]{0:T(1024)(128)(4,1)S(1)}, s32[]{:S(2)}) async-start(s8[4718592]{0:T(1024)(128)(4,1)} %bitcast.78), calls=%async_computation | async-start | bytes 8388608
  99.2 5.0 %slice-start.1 = ((s8[4718592]{0:T(1024)(128)(4,1)}), s8[524288]{0:T(1024)(128)(4,1)S(1)}, s32[]{:S(2)}) async-start(s8[4718592]{0:T(1024)(128)(4,1)} %bitcast.78), calls=%async_computation.1 | async-start | bytes 1048576
  110.0 1.5 copy-start.14
  113.4 4.0 %copy-start.9 = (bf16[128,768]{1,0:T(8,128)(2,1)S(1)}, bf16[128,768]{1,0:T(8,128)(2,1)}, u32[]{:S(2)}) copy-start(bf16[128,768]{1,0:T(8,128)(2,1)} %param.17) | copy-start | bytes 589828
  113.5 5.1 %copy-start.2 = (bf16[8,96,2304]{2,1,0:T(8,128)(2,1)S(1)}, bf16[8,96,2304]{2,1,0:T(8,128)(2,1)}, u32[]{:S(2)}) copy-start(bf16[8,96,2304]{2,1,0:T(8,128)(2,1)} %get-tuple-element.25) | copy-start | bytes 10616836
  114.2 4.4 %copy-start.31 = (f32[128]{0:T(128)S(1)}, f32[128]{0:T(128)}, u32[]{:S(2)}) copy-start(f32[128]{0:T(128)} %copy-done.30) | copy-start | bytes 1540
  114.2 4.4 %copy-start.35 = (f32[128]{0:T(128)S(1)}, f32[128]{0:T(128)}, u32[]{:S(2)}) copy-start(f32[128]{0:T(128)} %copy-done.34) | copy-start | bytes 1540
  118.1 3.0 copy-start.28
  118.1 3.1 copy-start.26
  118.1 3.2 copy-start.25
  118.1 3.2 copy-start.32
  118.1 3.2 copy-start.27
  118.1 3.6 %copy-start.29 = (f32[8,96]{1,0:T(8,128)S(1)}, f32[8,96]{1,0:T(8,128)}, u32[]{:S(2)}) copy-start(f32[8,96]{1,0:T(8,128)} %get-tuple-element.85) | copy-start | bytes 9220
  118.1 3.6 %copy-start.3 = (bf16[128,3072]{1,0:T(8,128)(2,1)S(1)}, bf16[128,3072]{1,0:T(8,128)(2,1)}, u32[]{:S(2)}) copy-start(bf16[128,3072]{1,0:T(8,128)(2,1)} %get-tuple-element.46) | copy-start | bytes 2359300
  118.1 9.3 %collective-permute-start = (bf16[128,12288]{1,0:T(8,128)(2,1)}, bf16[128,12288]{1,0:T(8,128)(2,1)}, u32[]{:S(2)}, u32[]{:S(2)}) collective-permute-start(bf16[128,12288]{1,0:T(8,128)(2,1)} %constant_dynamic-update-slice_fusion), channel_id=1, source_target_pairs={{0,8},{8,0},{16,24},{24,16},{1,9},{9,1},{17,25},{25,17},{2,10},{10... | collective-permute-start | bytes 9437192 | tf_op jit(solution)/shard_map/ppermute | solution.py:445
  121.5 5.3 %collective-permute-start.1 = (f32[8,1152]{1,0:T(8,128)S(1)}, f32[8,1152]{1,0:T(8,128)S(1)}, u32[]{:S(2)}, u32[]{:S(2)}) collective-permute-start(f32[8,1152]{1,0:T(8,128)S(1)} %concatenate.76), channel_id=1, source_target_pairs={{0,8},{8,0},{16,24},{24,16},{1,9},{9,1},{17,25},{25,17},{2,10},{10... | collective-permute-start | bytes 110600 | tf_op jit(solution)/shard_map/ppermute | solution.py:445
  121.8 3.9 %copy-start.15 = (f32[128,768]{1,0:T(8,128)S(1)}, f32[128,768]{1,0:T(8,128)}, u32[]{:S(2)}) copy-start(f32[128,768]{1,0:T(8,128)} %get-tuple-element.44) | copy-start | bytes 1179652
  121.8 3.9 %copy-start.21 = (f32[128,768]{1,0:T(8,128)S(1)}, f32[128,768]{1,0:T(8,128)}, u32[]{:S(2)}) copy-start(f32[128,768]{1,0:T(8,128)} %get-tuple-element.111) | copy-start | bytes 1179652
  126.8 1.9 copy-start.24
  126.8 1.9 copy-start.36
  129.9 4.1 %copy-start.10 = (bf16[128,768]{1,0:T(8,128)(2,1)S(1)}, bf16[128,768]{1,0:T(8,128)(2,1)}, u32[]{:S(2)}) copy-start(bf16[128,768]{1,0:T(8,128)(2,1)} %param.17) | copy-start | bytes 589828
  129.9 4.1 %copy-start.12 = (bf16[128,768]{1,0:T(8,128)(2,1)S(1)}, bf16[128,768]{1,0:T(8,128)(2,1)}, u32[]{:S(2)}) copy-start(bf16[128,768]{1,0:T(8,128)(2,1)} %copy-done.11) | copy-start | bytes 589828
  129.9 4.1 %copy-start.20 = (bf16[128,768]{1,0:T(8,128)(2,1)S(1)}, bf16[128,768]{1,0:T(8,128)(2,1)}, u32[]{:S(2)}) copy-start(bf16[128,768]{1,0:T(8,128)(2,1)} %copy-done.19) | copy-start | bytes 589828
  294.7 8.3 %copy-start.37 = (f32[1,1152]{1,0:T(1,128)S(1)}, f32[1,1152]{1,0:T(1,128)}, u32[]{:S(2)}) copy-start(f32[1,1152]{1,0:T(1,128)} %get-tuple-element.29) | copy-start | bytes 13828
  294.7 8.4 %copy-start.16 = (f32[384,768]{1,0:T(8,128)S(1)}, f32[384,768]{1,0:T(8,128)}, u32[]{:S(2)}) copy-start(f32[384,768]{1,0:T(8,128)} %get-tuple-element.33) | copy-start | bytes 3538948
  295.6 7.4 %collective-permute-start.2 = (f32[1,576]{1,0:T(1,128)S(1)}, f32[1,576]{1,0:T(1,128)S(1)}, u32[]{:S(2)}, u32[]{:S(2)}) collective-permute-start(f32[1,576]{1,0:T(1,128)S(1)} %constant_dynamic-slice_fusion.4), channel_id=1, source_target_pairs={{0,16},{8,24},{16,0},{24,8},{1,17},{9,25},{17,1},{25,9},{2,18},{10... | collective-permute-start | bytes 6920 | tf_op jit(solution)/shard_map/ppermute | solution.py:450
  297.1 17.3 %copy-start.22 = (f32[96,768]{1,0:T(8,128)S(1)}, f32[96,768]{1,0:T(8,128)}, u32[]{:S(2)}) copy-start(f32[96,768]{1,0:T(8,128)} %get-tuple-element.31) | copy-start | bytes 884740
  298.2 18.9 %collective-permute-start.4 = (f32[96,1152]{1,0:T(8,128)S(1)}, f32[96,1152]{1,0:T(8,128)S(1)}, u32[]{:S(2)}, u32[]{:S(2)}) collective-permute-start(f32[96,1152]{1,0:T(8,128)S(1)} %constant_dynamic-slice_fusion.3), channel_id=1, source_target_pairs={{0,16},{8,24},{16,0},{24,8},{1,17},{9,25},{17,1},{25,9},{2,18},{10... | collective-permute-start | bytes 1327112 | tf_op jit(solution)/shard_map/ppermute | solution.py:450
  299.7 14.7 %collective-permute-start.6 = (f32[96,384]{1,0:T(8,128)S(1)}, f32[96,384]{1,0:T(8,128)S(1)}, u32[]{:S(2)}, u32[]{:S(2)}) collective-permute-start(f32[96,384]{1,0:T(8,128)S(1)} %constant_dynamic-slice_fusion.2), channel_id=1, source_target_pairs={{0,16},{8,24},{16,0},{24,8},{1,17},{9,25},{17,1},{25,9},{2,18},{10... | collective-permute-start | bytes 442376 | tf_op jit(solution)/shard_map/ppermute | solution.py:450
  302.4 14.7 %copy-start.18 = (f32[96,2304]{1,0:T(8,128)S(1)}, f32[96,2304]{1,0:T(8,128)}, u32[]{:S(2)}) copy-start(f32[96,2304]{1,0:T(8,128)} %get-tuple-element.30) | copy-start | bytes 2654212
  302.4 24.6 %collective-permute-start.8 = (f32[96,1536]{1,0:T(8,128)S(1)}, f32[96,1536]{1,0:T(8,128)S(1)}, u32[]{:S(2)}, u32[]{:S(2)}) collective-permute-start(f32[96,1536]{1,0:T(8,128)S(1)} %constant_dynamic-slice_fusion.1), channel_id=1, source_target_pairs={{0,16},{8,24},{16,0},{24,8},{1,17},{9,25},{17,1},{25,9},{2,18},{10... | collective-permute-start | bytes 1769480 | tf_op jit(solution)/shard_map/ppermute | solution.py:450
  303.1 1.7 collective-permute-start.3
  303.1 23.9 %copy-start.17 = (f32[96,3072]{1,0:T(8,128)S(1)}, f32[96,3072]{1,0:T(8,128)}, u32[]{:S(2)}) copy-start(f32[96,3072]{1,0:T(8,128)} %get-tuple-element.32) | copy-start | bytes 3538948
  303.1 36.1 %collective-permute-start.10 = (f32[384,384]{1,0:T(8,128)S(1)}, f32[384,384]{1,0:T(8,128)S(1)}, u32[]{:S(2)}, u32[]{:S(2)}) collective-permute-start(f32[384,384]{1,0:T(8,128)S(1)} %constant_dynamic-slice_fusion), channel_id=1, source_target_pairs={{0,16},{8,24},{16,0},{24,8},{1,17},{9,25},{17,1},{25,9},{2,18},{10... | collective-permute-start | bytes 1769480 | tf_op jit(solution)/shard_map/ppermute | solution.py:450
  314.4 1.9 collective-permute-start.7
  317.2 22.3 %collective-permute-start.5 = (f32[96,1152]{1,0:T(8,128)S(1)}, f32[96,1152]{1,0:T(8,128)S(1)}, u32[]{:S(2)}, u32[]{:S(2)}) collective-permute-start(f32[96,1152]{1,0:T(8,128)S(1)} %fusion.100), channel_id=1, source_target_pairs={{0,8},{8,0},{16,24},{24,16},{1,9},{9,1},{17,25},{25,17},{2,10},{10... | collective-permute-start | bytes 1327112 | tf_op jit(solution)/shard_map/ppermute | solution.py:445
  327.1 13.4 %collective-permute-start.9 = (f32[96,1536]{1,0:T(8,128)S(1)}, f32[96,1536]{1,0:T(8,128)S(1)}, u32[]{:S(2)}, u32[]{:S(2)}) collective-permute-start(f32[96,1536]{1,0:T(8,128)S(1)} %fusion.98), channel_id=1, source_target_pairs={{0,8},{8,0},{16,24},{24,16},{1,9},{9,1},{17,25},{25,17},{2,10},{10... | collective-permute-start | bytes 1769480 | tf_op jit(solution)/shard_map/ppermute | solution.py:445
  339.3 2.3 collective-permute-start.11
  (6 other events, 5.5 us)

commit v5 on v4

--- a/solution.py
+++ b/solution.py
@@ -310,13 +310,18 @@
 def reduce_kernel(n, count, *refs):
     contrib = refs[:count]
     out = refs[count : 2 * count]
-    land, send, other, own = (refs[2 * count + i * count : 2 * count + (i + 1) * count] for i in range(4))
-    load_sem, own_sem, ring_send, ring_recv, pair_send, pair_recv = refs[6 * count :]
+    land, send, other, own, xland = (
+        refs[2 * count + i * count : 2 * count + (i + 1) * count] for i in range(5)
+    )
+    (load_sem, own_sem, ring_send, ring_recv, pair_send, pair_recv, x_send, x_recv, back_send, back_recv) = refs[
+        7 * count :
+    ]
     rep = lax.axis_index("rep")
     shard = lax.axis_index("shard")
     core = rep % 2
     step_dir = 1 - 2 * core
     partner = (rep + step_dir, shard)
+    x_partner = ((rep + 2) % 4, shard)
     here = ring_position(shard, n)
     target = (rep, ring_shard(here + step_dir, n))
     source = (rep, ring_shard(here - step_dir, n))
@@ -343,25 +348,25 @@
     def load_own(w):
         return pltpu.make_async_copy(contrib[w].at[shard], own[w], own_sem.at[w])
 
+    def remote(src, dst, ssem, rsem, device):
+        return pltpu.make_async_remote_copy(
+            src_ref=src, dst_ref=dst, send_sem=ssem, recv_sem=rsem, device_id=device, device_id_type=MESH
+        )
+
     def ring_copy(k, w, device):
-        return pltpu.make_async_remote_copy(
-            src_ref=send[w].at[k - 1],
-            dst_ref=land[w].at[k - 1],
-            send_sem=ring_send.at[k - 1, w],
-            recv_sem=ring_recv.at[k - 1, w],
-            device_id=device,
-            device_id_type=MESH,
-        )
+        return remote(send[w].at[k - 1], land[w].at[k - 1], ring_send.at[k - 1, w], ring_recv.at[k - 1, w], device)
 
     def pair_copy(w):
-        return pltpu.make_async_remote_copy(
-            src_ref=land[w].at[steps - 1],
-            dst_ref=other[w],
-            send_sem=pair_send.at[w],
-            recv_sem=pair_recv.at[w],
-            device_id=partner,
-            device_id_type=MESH,
-        )
+        return remote(land[w].at[steps - 1], other[w], pair_send.at[w], pair_recv.at[w], partner)
+
+    def x_copy(w):
+        return remote(own[w], xland[w], x_send.at[w], x_recv.at[w], x_partner)
+
+    def back_copy(w):
+        return remote(out[w], out[w], back_send.at[w], back_recv.at[w], partner)
+
+    def owner(w):
+        return core == w % 2
 
     for w in range(count):
         load_own(w).start()
@@ -370,9 +375,14 @@
             guarded(carried(k, w), lambda k=k, w=w: load(k, w).start())
 
     barrier = pltpu.get_barrier_semaphore()
-    for peer in (target, source, partner):
+    for peer in (target, source, partner, x_partner):
         pl.semaphore_signal(barrier, inc=1, device_id=peer, device_id_type=MESH)
-    pl.semaphore_wait(barrier, 3)
+    pl.semaphore_wait(barrier, 4)
+
+    def add_into(dst, parts):
+        rows = dst.shape[0]
+        chunk = 8 if rows % 8 == 0 else rows
+        add_rows(dst, parts, rows, chunk)
 
     for k in range(1, steps + 1):
         for w in range(count):
@@ -381,32 +391,47 @@
                 if k > 1:
                     def accumulate():
                         ring_copy(k - 1, w, source).wait_recv()
-                        rows = send[w].shape[1]
-                        chunk = 8 if rows % 8 == 0 else rows
-                        add_rows(send[w].at[k - 1], [send[w].at[k - 1], land[w].at[k - 2]], rows, chunk)
+                        add_into(send[w].at[k - 1], [send[w].at[k - 1], land[w].at[k - 2]])
                     guarded(carried(k - 1, w), accumulate)
                 ring_copy(k, w, target).start()
             guarded(carried(k, w), step)
+
     for w in range(count):
         ring_copy(steps, w, source).wait_recv()
-        pair_copy(w).start()
+        pl.when(jnp.logical_not(owner(w)))(lambda w=w: pair_copy(w).start())
+        mine = land[w].at[steps - 1]
+
+        def finish(w=w, mine=mine):
+            pair_copy(w).wait_recv()
+            load_own(w).wait()
+
+            @pl.when(core == 0)
+            def _():
+                add_into(own[w], [own[w], mine, other[w]])
+
+            @pl.when(core == 1)
+            def _():
+                add_into(own[w], [own[w], other[w], mine])
+
+            x_copy(w).start()
+            x_copy(w).wait_recv()
+            add_into(out[w], [own[w], xland[w]])
+            back_copy(w).start()
+
+        pl.when(owner(w))(finish)
+
     for w in range(count):
-        pair_copy(w).wait_recv()
-        load_own(w).wait()
-        rows = own[w].shape[0]
-        chunk = 8 if rows % 8 == 0 else rows
-        mine = land[w].at[steps - 1]
-
-        @pl.when(core == 0)
-        def _():
-            add_rows(out[w], [own[w], mine, other[w]], rows, chunk)
-
-        @pl.when(core == 1)
-        def _():
-            add_rows(out[w], [own[w], other[w], mine], rows, chunk)
-
-    for w in range(count):
-        pair_copy(w).wait_send()
+        def not_owner(w=w):
+            load_own(w).wait()
+            back_copy(w).wait_recv()
+            pair_copy(w).wait_send()
+
+        def was_owner(w=w):
+            x_copy(w).wait_send()
+            back_copy(w).wait_send()
+
+        pl.when(owner(w))(was_owner)
+        pl.when(jnp.logical_not(owner(w)))(not_owner)
     for k in range(1, steps + 1):
         for w in range(count):
             guarded(carried(k, w), lambda k=k, w=w: ring_copy(k, w, target).wait_send())
@@ -417,6 +442,7 @@
     steps = n // 2
     blocks = [c.shape[1:] for c in contribs]
     vmem = lambda shape: pltpu.VMEM(shape, jnp.float32)
+    dma = pltpu.SemaphoreType.DMA
     return pl.pallas_call(
         functools.partial(reduce_kernel, n, count),
         out_shape=[jax.ShapeDtypeStruct(b, jnp.float32) for b in blocks],
@@ -426,13 +452,18 @@
         + [vmem((steps,) + b) for b in blocks]
         + [vmem(b) for b in blocks]
         + [vmem(b) for b in blocks]
+        + [vmem(b) for b in blocks]
         + [
-            pltpu.SemaphoreType.DMA((steps, count)),
-            pltpu.SemaphoreType.DMA((count,)),
-            pltpu.SemaphoreType.DMA((steps, count)),
-            pltpu.SemaphoreType.DMA((steps, count)),
-            pltpu.SemaphoreType.DMA((count,)),
-            pltpu.SemaphoreType.DMA((count,)),
+            dma((steps, count)),
+            dma((count,)),
+            dma((steps, count)),
+            dma((steps, count)),
+            dma((count,)),
+            dma((count,)),
+            dma((count,)),
+            dma((count,)),
+            dma((count,)),
+            dma((count,)),
         ],
         compiler_params=pltpu.CompilerParams(
             collective_id=1, has_side_effects=True, vmem_limit_bytes=60 * 1024 * 1024
@@ -536,14 +567,9 @@
         grad = jnp.einsum("tc,te->ce", rows, grads, preferred_element_type=jnp.float32)
         contribs.append(grad.reshape(shard, -1, grad.shape[1]))
     contribs.append(small_chip.reshape(shard, 1, -1))
-    plane = reduce_gradients(contribs, shard)
-    owned = []
-    for total in plane:
-        half = take_half(total, core, 1)
-        half = half + swap_x(half)
-        owned.append(join_halves(half, swap_core(half), core, 1))
-    small_share = owned[4]
-    owned = [o[None] for o in owned[:4]]
+    totals = reduce_gradients(contribs, shard)
+    small_share = totals[4]
+    owned = [t[None] for t in totals[:4]]
     small_owned = []
     start = 0
     for g in small_grads:

time: 343 us -> 342 us (level)
  Pallas kernels: 223 us -> 257 us
  waiting for transfers between devices: 30.5 us -> 0.01 us
  starting transfers between devices: 7.26 us -> 0.58 us
  other arithmetic: 18 us -> 12.9 us
  local copies, waits for them, and re-layouts: 22.2 us -> 26.5 us
    pallas_call x1, Pallas kernels: 146 us -> 180 us  [reduce_gradients(): pl.pallas_call(functools.partial(reduce_kernel, n, count), out_shape=[jax...]
    ppermute x5 -> x0, waiting for transfers between devices: 30.4 us -> none  [swap_x(): return lax.ppermute(value, 'rep', perm=[(i, i ^ 2) for i in range(rep)])]
    ppermute x5 -> x0, starting transfers between devices: 5.82 us -> none  [swap_x(): return lax.ppermute(value, 'rep', perm=[(i, i ^ 2) for i in range(rep)])]
    unnamed x91 -> x87, local copies, waits for them, and re-layouts: 6.13 us -> 11.1 us
    dynamic_slice x5 -> x0, local copies, waits for them, and re-layouts: 4.02 us -> none  [take_half(): return lax.dynamic_slice_in_dim(value, core * half, half, axis=axis)]
    broadcast_in_dim x4 -> x0, other arithmetic: 3.9 us -> none  [per_device(): owned = [o[None] for o in owned[:4]]]
  transfers between devices with their start and end apart: 12 -> 2, of which waited for: 3 -> 0; matrix products, arithmetic and copies ran while one was open for 5% -> 3% of each run, Pallas kernels for 0% -> 0%
where the time goes in v5:
time: 342 us; the launch traced here: 341 us
  Pallas kernels  257 us (75%)
  matrix products  42.7 us (12%)
  local copies, waits for them, and re-layouts  26.5 us (8%)
  other arithmetic  12.9 us (4%)
    pallas_call x1, Pallas kernels, reduce_gradients(): pl.pallas_call(functools.partial(reduce_kernel, n, count), out_shape=[jax...  180 us
    pallas_call x1, Pallas kernels, gather_weights(): pl.pallas_call(functools.partial(gather_kernel, n, count), out_shape=[jax...  77.3 us
    dot_general x4, matrix products, per_device(): jnp.einsum('tc,te->ce', rows, grads, preferred_element_type=jnp.float32)  16.1 us
    unnamed x87, local copies, waits for them, and re-layouts  11.1 us
  transfers between devices with their start and end apart: 2, of which 0 were waited for; matrix products, arithmetic and copies ran while one was open for 3% of the time, Pallas kernels for 0%

profile of v5, /device:TPU:0, one launch (start us, length us, event | category | flops | bytes accessed | tf_op | source)
XLA Modules:
  0.0 341.0 jit_solution(3711254917149855577)
XLA Ops:
  0.7 0.7 reduce
  1.4 0.7 reduce.1
  2.1 4.1 %concatenate.49 = bf16[1152]{0:T(1024)(128)(2,1)S(1)} concatenate(bf16[96]{0:T(256)(128)(2,1)} %bitcast.107, bf16[96]{0:T(256)(128)(2,1)} %bitcast.108, bf16[192]{0:T(256)(128)(2,1)S(1)} %reduce, bf16[96]{0:T(256)(128)(2,1)} %bitcast.109, bf16[96]{0:T(256)(128)(2,1)} %bitcast.110, bf16[96]{0:T(256)(128)(2,1)} %bitcast.111, bf16[384]{0:T(512)(128)(2,1)S(1)} %reduce.1, ...), dimensions={0} | concatenate | bytes 4608 | tf_op jit(solution)/shard_map/concatenate | solution.py:532
  6.2 0.6 reshape.277.refs_4_
  6.8 77.3 %shard_map.254 = (bf16[8,96,2304]{2,1,0:T(8,128)(2,1)}, bf16[8,96,768]{2,1,0:T(8,128)(2,1)}, bf16[8,96,3072]{2,1,0:T(8,128)(2,1)}, bf16[8,384,768]{2,1,0:T(8,128)(2,1)}, bf16[8,1,1152]{2,1,0:T(2,128)(2,1)}) custom-call(bf16[96,2304]{1,0:T(8,128)(2,1)} %bitcast.101, bf16[96,768]{1,0:T(8,128)(2,1)} %bitcast.103, bf16[96,3072]{1,0:T(8,128)(2,1)} %bitcast.99, ...), custom_call_target="tpu_custom_call" | custom-call | tf_op jit(solution)/shard_map/pallas_call | solution.py:283
  84.1 0.8 copy.70
  85.0 0.7 slice_convert_fusion.2
  86.3 0.6 reshape.307
  87.1 0.7 reshape.306
  87.8 0.7 reshape.304
  88.4 0.8 constant_dynamic-update-slice_fusion.9
  89.3 2.7 fusion
  93.9 0.4 fusion.71
  94.6 0.7 constant_dynamic-update-slice_fusion.8
  95.3 0.8 constant_dynamic-update-slice_fusion.7
  96.2 5.0 %constant_dynamic-update-slice_fusion.6 = (bf16[128,12288]{1,0:T(8,128)(2,1)}, bf16[128,3072]{1,0:T(8,128)(2,1)}, f32[128,3072]{1,0:T(8,128)S(1)}) fusion(bf16[128,12288]{1,0:T(8,128)(2,1)} %get-tuple-element.47, f32[3072]{0:T(1024)S(1)} %copy-done.32, bf16[128,768]{1,0:T(8,128)(2,1)S(1)} %get-tuple-element.48, bf16[768,3072]{1,0:T(8,128)(2,1)} %bitcast.73), kind=kOutput, calls=%fused_computation.114 | convolution fusion | flops 607911936 | bytes 8073216 | tf_op jit(solution)/shard_map/dot_general | solution.py:69
  101.1 5.0 %convert_reduce_fusion = (f32[3072]{0:T(1024)}, bf16[128,3072]{1,0:T(8,128)(2,1)S(1)}) fusion(f32[128,3072]{1,0:T(8,128)S(1)} %get-tuple-element.97, bf16[3072,768]{1,0:T(8,128)(2,1)} %bitcast.79, bf16[128,768]{1,0:T(8,128)(2,1)S(1)} %copy-done.7), kind=kOutput, calls=%fused_computation.21 | convolution fusion | flops 612627456 | bytes 7286784 | tf_op jit(solution)/shard_map/td,fd->tf/dot_general | solution.py:100
  106.2 2.3 multiply_reduce_fusion.1
  108.5 1.5 convert_reduce_fusion.4
  110.0 1.2 convolution_convert_fusion.1
  111.3 1.1 copy.51
  114.8 0.7 constant_dynamic-update-slice_fusion.5
  115.6 0.7 constant_dynamic-update-slice_fusion.4
  116.3 0.7 constant_dynamic-update-slice_fusion.3
  117.0 0.7 constant_dynamic-update-slice_fusion.2
  117.7 1.0 constant_dynamic-update-slice_fusion.1
  118.6 0.7 constant_dynamic-update-slice_fusion
  119.4 0.4 collective-permute-start
  120.1 4.1 %fusion.39 = (f32[768]{0:T(1024)S(1)}, f32[128]{0:T(128)S(1)}, f32[128]{0:T(128)S(1)}, f32[768]{0:T(1024)S(1)}, f32[128,768]{1,0:T(8,128)}) fusion(bf16[128,768]{1,0:T(8,128)(2,1)S(1)} %copy-done, f32[128]{0:T(128)S(1)} %copy-done.34, f32[128]{0:T(128)S(1)} %copy-done.30, f32[768]{0:T(1024)S(1)} %reshape.302, bf16[768,2304]{1,0:T(8,128)(2,1)} %bitcast.82, ...), kind=kOutput, calls=%fused_computation.70 | convolution fusion | flops 455735552 | bytes 4729856 | tf_op jit(solution)/shard_map/te,ce->tc/dot_general | solution.py:138
  125.0 3.9 %fusion.23 = bf16[128,768]{1,0:T(8,128)(2,1)} fusion(f32[128,768]{1,0:T(8,128)S(1)} %get-tuple-element.96, bf16[128,3072]{1,0:T(8,128)(2,1)S(1)} %copy-done.2, bf16[3072,768]{1,0:T(8,128)(2,1)} %bitcast.80, f32[768]{0:T(1024)S(1)} %reshape.308), kind=kOutput, calls=%fused_computation.36 | convolution fusion | flops 604274688 | bytes 6097920 | tf_op jit(solution)/shard_map/dot_general | solution.py:72
  128.9 1.1 fusion.38
  130.1 0.6 reshape.301.refs_4_
  130.7 1.3 broadcast_select_fusion.7
  132.1 2.0 fusion.44
  134.0 1.1 broadcast_select_fusion.15
  135.2 1.3 broadcast_select_fusion.5
  136.4 4.0 %fusion.19 = f32[768,2304]{1,0:T(8,128)} fusion(bf16[128,2304]{1,0:T(8,128)(2,1)S(1)} %get-tuple-element.54, bf16[128,2304]{1,0:T(8,128)(2,1)S(1)} %get-tuple-element.53, bf16[128,768]{1,0:T(8,128)(2,1)S(1)} %get-tuple-element.56, bf16[128,768]{1,0:T(8,128)(2,1)S(1)} %get-tuple-element.55), kind=kOutput, calls=%fused_computation.31 | convolution fusion | flops 909115392 | bytes 8650752 | tf_op jit(solution)/shard_map/tc,te->ce/dot_general | solution.py:567
  140.5 1.6 broadcast_select_fusion.1
  142.1 5.1 %fusion.12 = f32[3072,768]{1,0:T(8,128)} fusion(bf16[128,3072]{1,0:T(8,128)(2,1)S(1)} %get-tuple-element.50, bf16[128,3072]{1,0:T(8,128)(2,1)S(1)} %get-tuple-element.49, bf16[128,768]{1,0:T(8,128)(2,1)S(1)} %get-tuple-element.58, bf16[128,768]{1,0:T(8,128)(2,1)S(1)} %get-tuple-element.57), kind=kOutput, calls=%fused_computation.17 | convolution fusion | flops 1211891712 | bytes 11403264 | tf_op jit(solution)/shard_map/tc,te->ce/dot_general | solution.py:567
  147.2 5.0 %fusion.8 = f32[768,3072]{1,0:T(8,128)} fusion(bf16[128,3072]{1,0:T(8,128)(2,1)S(1)} %get-tuple-element.71, bf16[128,3072]{1,0:T(8,128)(2,1)S(1)} %get-tuple-element.72, bf16[128,768]{1,0:T(8,128)(2,1)S(1)} %get-tuple-element.69, bf16[128,768]{1,0:T(8,128)(2,1)S(1)} %get-tuple-element.70), kind=kOutput, calls=%fused_computation.13 | convolution fusion | flops 1211891712 | bytes 11403264 | tf_op jit(solution)/shard_map/tc,te->ce/dot_general | solution.py:567
  152.2 179.8 %shard_map.255 = (f32[96,2304]{1,0:T(8,128)}, f32[96,768]{1,0:T(8,128)}, f32[96,3072]{1,0:T(8,128)}, f32[384,768]{1,0:T(8,128)}, f32[1,1152]{1,0:T(1,128)}) custom-call(f32[8,96,2304]{2,1,0:T(8,128)} %bitcast.71, f32[8,96,768]{2,1,0:T(8,128)} %bitcast.72, f32[8,96,3072]{2,1,0:T(8,128)} %bitcast.70, f32[8,384,768]{2,1,0:T(8,128)} %bitcast.69, ...), custom_call_target="tpu_custom_call" | custom-call | tf_op jit(solution)/shard_map/pallas_call | solution.py:446
  332.0 1.4 slice.140
  333.4 1.3 slice.144
  334.7 1.3 fusion.69
  336.1 2.1 copy.84
  338.2 0.7 copy.85
  338.9 1.0 copy.86
  339.9 1.0 copy.87
  (133 shorter events, 6.4 us)
Async XLA Ops:
  0.6 85.0 %copy-start = (bf16[128,768]{1,0:T(8,128)(2,1)S(1)}, bf16[128,768]{1,0:T(8,128)(2,1)}, u32[]{:S(2)}) copy-start(bf16[128,768]{1,0:T(8,128)(2,1)} %param.15) | copy-start | bytes 589828
  0.7 85.3 %copy-start.35 = (s32[128]{0:T(128)S(1)}, s32[128]{0:T(128)}, u32[]{:S(2)}) copy-start(s32[128]{0:T(128)} %param.16) | copy-start | bytes 1540
  85.8 6.2 %copy-start.29 = (f32[128]{0:T(128)}, f32[128]{0:T(128)S(1)}, u32[]{:S(2)}) copy-start(f32[128]{0:T(128)S(1)} %broadcast_multiply_fusion.5) | copy-start | bytes 1540
  86.0 6.0 %copy-start.33 = (f32[128]{0:T(128)}, f32[128]{0:T(128)S(1)}, u32[]{:S(2)}) copy-start(f32[128]{0:T(128)S(1)} %add_rsqrt_fusion.1) | copy-start | bytes 1540
  87.1 4.9 %copy-start.20 = (f32[768]{0:T(1024)}, f32[768]{0:T(1024)S(1)}, u32[]{:S(2)}) copy-start(f32[768]{0:T(1024)S(1)} %reshape.303) | copy-start | bytes 9220
  92.2 0.9 copy-start.3
  92.4 1.0 copy-start.5
  92.6 0.8 copy-start.11
  92.6 1.3 copy-start.1
  92.6 1.3 copy-start.27
  93.4 1.9 copy-start.26
  93.5 2.6 copy-start.9
  93.9 2.2 copy-start.32
  96.1 5.0 %copy-start.16 = (bf16[128,768]{1,0:T(8,128)(2,1)}, bf16[128,768]{1,0:T(8,128)(2,1)S(1)}, u32[]{:S(2)}) copy-start(bf16[128,768]{1,0:T(8,128)(2,1)S(1)} %get-tuple-element.48) | copy-start | bytes 589828
  96.1 5.0 %copy-start.7 = (bf16[128,768]{1,0:T(8,128)(2,1)S(1)}, bf16[128,768]{1,0:T(8,128)(2,1)}, u32[]{:S(2)}) copy-start(bf16[128,768]{1,0:T(8,128)(2,1)} %param.17) | copy-start | bytes 589828
  96.2 10.0 %slice-start = ((s8[4718592]{0:T(1024)(128)(4,1)}), s8[4194304]{0:T(1024)(128)(4,1)S(1)}, s32[]{:S(2)}) async-start(s8[4718592]{0:T(1024)(128)(4,1)} %bitcast.74), calls=%async_computation | async-start | bytes 8388608
  101.1 5.0 %slice-start.1 = ((s8[4718592]{0:T(1024)(128)(4,1)}), s8[524288]{0:T(1024)(128)(4,1)S(1)}, s32[]{:S(2)}) async-start(s8[4718592]{0:T(1024)(128)(4,1)} %bitcast.74), calls=%async_computation.1 | async-start | bytes 1048576
  111.3 1.5 copy-start.12
  112.8 0.9 copy-start.6
  113.1 1.0 copy-start.4
  114.8 3.9 %copy-start.8 = (bf16[128,768]{1,0:T(8,128)(2,1)S(1)}, bf16[128,768]{1,0:T(8,128)(2,1)}, u32[]{:S(2)}) copy-start(bf16[128,768]{1,0:T(8,128)(2,1)} %param.17) | copy-start | bytes 589828
  115.5 4.3 %copy-start.31 = (f32[3072]{0:T(1024)S(1)}, f32[3072]{0:T(1024)}, u32[]{:S(2)}) copy-start(f32[3072]{0:T(1024)} %get-tuple-element.102) | copy-start | bytes 36868
  115.5 4.3 %copy-start.23 = (f32[768]{0:T(1024)S(1)}, f32[768]{0:T(1024)}, u32[]{:S(2)}) copy-start(f32[768]{0:T(1024)} %get-tuple-element.34) | copy-start | bytes 9220
  115.5 4.4 %copy-start.25 = (f32[768]{0:T(1024)S(1)}, f32[768]{0:T(1024)}, u32[]{:S(2)}) copy-start(f32[768]{0:T(1024)} %get-tuple-element.42) | copy-start | bytes 9220
  115.5 4.4 %copy-start.24 = (f32[768]{0:T(1024)S(1)}, f32[768]{0:T(1024)}, u32[]{:S(2)}) copy-start(f32[768]{0:T(1024)} %get-tuple-element.76) | copy-start | bytes 9220
  115.5 4.5 %copy-start.22 = (f32[768]{0:T(1024)S(1)}, f32[768]{0:T(1024)}, u32[]{:S(2)}) copy-start(f32[768]{0:T(1024)} %get-tuple-element.40) | copy-start | bytes 9220
  115.5 4.6 %copy-start.30 = (f32[128]{0:T(128)S(1)}, f32[128]{0:T(128)}, u32[]{:S(2)}) copy-start(f32[128]{0:T(128)} %copy-done.29) | copy-start | bytes 1540
  115.6 4.6 %copy-start.34 = (f32[128]{0:T(128)S(1)}, f32[128]{0:T(128)}, u32[]{:S(2)}) copy-start(f32[128]{0:T(128)} %copy-done.33) | copy-start | bytes 1540
  119.4 11.3 %collective-permute-start = (bf16[128,12288]{1,0:T(8,128)(2,1)}, bf16[128,12288]{1,0:T(8,128)(2,1)}, u32[]{:S(2)}, u32[]{:S(2)}) collective-permute-start(bf16[128,12288]{1,0:T(8,128)(2,1)} %constant_dynamic-update-slice_fusion), channel_id=1, source_target_pairs={{0,8},{8,0},{16,24},{24,16},{1,9},{9,1},{17,25},{25,17},{2,10},{10... | collective-permute-start | bytes 9437192 | tf_op jit(solution)/shard_map/ppermute | solution.py:476
  120.1 4.8 %copy-start.28 = (f32[8,96]{1,0:T(8,128)S(1)}, f32[8,96]{1,0:T(8,128)}, u32[]{:S(2)}) copy-start(f32[8,96]{1,0:T(8,128)} %get-tuple-element.77) | copy-start | bytes 9220
  120.1 4.9 %copy-start.2 = (bf16[128,3072]{1,0:T(8,128)(2,1)S(1)}, bf16[128,3072]{1,0:T(8,128)(2,1)}, u32[]{:S(2)}) copy-start(bf16[128,3072]{1,0:T(8,128)(2,1)} %get-tuple-element.46) | copy-start | bytes 2359300
  124.8 5.3 %collective-permute-start.1 = (f32[8,1152]{1,0:T(8,128)S(1)}, f32[8,1152]{1,0:T(8,128)S(1)}, u32[]{:S(2)}, u32[]{:S(2)}) collective-permute-start(f32[8,1152]{1,0:T(8,128)S(1)} %concatenate.64), channel_id=1, source_target_pairs={{0,8},{8,0},{16,24},{24,16},{1,9},{9,1},{17,25},{25,17},{2,10},{10... | collective-permute-start | bytes 110600 | tf_op jit(solution)/shard_map/ppermute | solution.py:476
  125.0 3.9 %copy-start.13 = (f32[128,768]{1,0:T(8,128)S(1)}, f32[128,768]{1,0:T(8,128)}, u32[]{:S(2)}) copy-start(f32[128,768]{1,0:T(8,128)} %get-tuple-element.44) | copy-start | bytes 1179652
  125.0 3.9 %copy-start.18 = (f32[128,768]{1,0:T(8,128)S(1)}, f32[128,768]{1,0:T(8,128)}, u32[]{:S(2)}) copy-start(f32[128,768]{1,0:T(8,128)} %get-tuple-element.101) | copy-start | bytes 1179652
  128.9 1.8 copy-start.10
  128.9 1.8 copy-start.17
  132.1 2.0 copy-start.21
  332.0 6.2 %copy-start.19 = (f32[96,768]{1,0:T(8,128)S(1)}, f32[96,768]{1,0:T(8,128)}, u32[]{:S(2)}) copy-start(f32[96,768]{1,0:T(8,128)} %get-tuple-element.31) | copy-start | bytes 884740
  332.0 6.9 %copy-start.15 = (f32[96,3072]{1,0:T(8,128)S(1)}, f32[96,3072]{1,0:T(8,128)}, u32[]{:S(2)}) copy-start(f32[96,3072]{1,0:T(8,128)} %get-tuple-element.32) | copy-start | bytes 3538948
  338.2 1.7 copy-start.14

commit v6 on v5

--- a/solution.py
+++ b/solution.py
@@ -384,24 +384,21 @@
         chunk = 8 if rows % 8 == 0 else rows
         add_rows(dst, parts, rows, chunk)
 
-    for k in range(1, steps + 1):
-        for w in range(count):
-            def step(k=k, w=w):
-                load(k, w).wait()
-                if k > 1:
-                    def accumulate():
-                        ring_copy(k - 1, w, source).wait_recv()
-                        add_into(send[w].at[k - 1], [send[w].at[k - 1], land[w].at[k - 2]])
-                    guarded(carried(k - 1, w), accumulate)
-                ring_copy(k, w, target).start()
-            guarded(carried(k, w), step)
-
-    for w in range(count):
+    def step(k, w):
+        load(k, w).wait()
+        if k > 1:
+            def accumulate():
+                ring_copy(k - 1, w, source).wait_recv()
+                add_into(send[w].at[k - 1], [send[w].at[k - 1], land[w].at[k - 2]])
+            guarded(carried(k - 1, w), accumulate)
+        ring_copy(k, w, target).start()
+
+    def arrive(w):
         ring_copy(steps, w, source).wait_recv()
-        pl.when(jnp.logical_not(owner(w)))(lambda w=w: pair_copy(w).start())
+        pl.when(jnp.logical_not(owner(w)))(lambda: pair_copy(w).start())
         mine = land[w].at[steps - 1]
 
-        def finish(w=w, mine=mine):
+        def plane():
             pair_copy(w).wait_recv()
             load_own(w).wait()
 
@@ -414,11 +411,25 @@
                 add_into(own[w], [own[w], other[w], mine])
 
             x_copy(w).start()
-            x_copy(w).wait_recv()
-            add_into(out[w], [own[w], xland[w]])
-            back_copy(w).start()
-
-        pl.when(owner(w))(finish)
+
+        pl.when(owner(w))(plane)
+
+    def total(w):
+        x_copy(w).wait_recv()
+        add_into(out[w], [own[w], xland[w]])
+        back_copy(w).start()
+
+    slots = steps + count - 1
+    for t in range(slots + 1):
+        for w in range(count):
+            k = t - w + 1
+            if 1 <= k <= steps:
+                guarded(carried(k, w), lambda k=k, w=w: step(k, w))
+        for w in range(count):
+            if steps + w == t:
+                arrive(w)
+    for w in range(count):
+        pl.when(owner(w))(lambda w=w: total(w))
 
     for w in range(count):
         def not_owner(w=w):

time: 342 us -> 334 us (0.977)
  Pallas kernels: 257 us -> 250 us
    pallas_call x1, Pallas kernels: 180 us -> 173 us  [reduce_gradients(): pl.pallas_call(functools.partial(reduce_kernel, n, count), out_shape=[jax...]
where the time goes in v6:
time: 334 us
  Pallas kernels  250 us (75%)
  matrix products  42.7 us (13%)
  local copies, waits for them, and re-layouts  26.5 us (8%)
  other arithmetic  12.9 us (4%)
    pallas_call x1, Pallas kernels, reduce_gradients(): pl.pallas_call(functools.partial(reduce_kernel, n, count), out_shape=[jax...  173 us
    pallas_call x1, Pallas kernels, gather_weights(): pl.pallas_call(functools.partial(gather_kernel, n, count), out_shape=[jax...  77.3 us
    dot_general x4, matrix products, per_device(): jnp.einsum('tc,te->ce', rows, grads, preferred_element_type=jnp.float32)  16.1 us
    unnamed x87, local copies, waits for them, and re-layouts  11.1 us
  transfers between devices with their start and end apart: 2, of which 0 were waited for; matrix products, arithmetic and copies ran while one was open for 3% of the time, Pallas kernels for 0%

profile of v6, /device:TPU:0, one launch (start us, length us, event | category | flops | bytes accessed | tf_op | source)
XLA Modules:
  0.0 333.8 jit_solution(10670567879028957795)
XLA Ops:
  0.7 0.7 reduce
  1.4 0.7 reduce.1
  2.1 4.1 %concatenate.49 = bf16[1152]{0:T(1024)(128)(2,1)S(1)} concatenate(bf16[96]{0:T(256)(128)(2,1)} %bitcast.107, bf16[96]{0:T(256)(128)(2,1)} %bitcast.108, bf16[192]{0:T(256)(128)(2,1)S(1)} %reduce, bf16[96]{0:T(256)(128)(2,1)} %bitcast.109, bf16[96]{0:T(256)(128)(2,1)} %bitcast.110, bf16[96]{0:T(256)(128)(2,1)} %bitcast.111, bf16[384]{0:T(512)(128)(2,1)S(1)} %reduce.1, ...), dimensions={0} | concatenate | bytes 4608 | tf_op jit(solution)/shard_map/concatenate | solution.py:543
  6.2 0.6 reshape.277.refs_4_
  6.8 77.3 %shard_map.254 = (bf16[8,96,2304]{2,1,0:T(8,128)(2,1)}, bf16[8,96,768]{2,1,0:T(8,128)(2,1)}, bf16[8,96,3072]{2,1,0:T(8,128)(2,1)}, bf16[8,384,768]{2,1,0:T(8,128)(2,1)}, bf16[8,1,1152]{2,1,0:T(2,128)(2,1)}) custom-call(bf16[96,2304]{1,0:T(8,128)(2,1)} %bitcast.101, bf16[96,768]{1,0:T(8,128)(2,1)} %bitcast.103, bf16[96,3072]{1,0:T(8,128)(2,1)} %bitcast.99, ...), custom_call_target="tpu_custom_call" | custom-call | tf_op jit(solution)/shard_map/pallas_call | solution.py:283
  84.1 0.8 copy.70
  85.0 0.7 slice_convert_fusion.2
  86.3 0.6 reshape.307
  87.1 0.7 reshape.306
  87.8 0.7 reshape.304
  88.4 0.8 constant_dynamic-update-slice_fusion.9
  89.3 2.7 fusion
  93.9 0.4 fusion.71
  94.6 0.7 constant_dynamic-update-slice_fusion.8
  95.3 0.8 constant_dynamic-update-slice_fusion.7
  96.2 5.0 %constant_dynamic-update-slice_fusion.6 = (bf16[128,12288]{1,0:T(8,128)(2,1)}, bf16[128,3072]{1,0:T(8,128)(2,1)}, f32[128,3072]{1,0:T(8,128)S(1)}) fusion(bf16[128,12288]{1,0:T(8,128)(2,1)} %get-tuple-element.47, f32[3072]{0:T(1024)S(1)} %copy-done.32, bf16[128,768]{1,0:T(8,128)(2,1)S(1)} %get-tuple-element.48, bf16[768,3072]{1,0:T(8,128)(2,1)} %bitcast.73), kind=kOutput, calls=%fused_computation.114 | convolution fusion | flops 607911936 | bytes 8073216 | tf_op jit(solution)/shard_map/dot_general | solution.py:69
  101.1 5.0 %convert_reduce_fusion = (f32[3072]{0:T(1024)}, bf16[128,3072]{1,0:T(8,128)(2,1)S(1)}) fusion(f32[128,3072]{1,0:T(8,128)S(1)} %get-tuple-element.97, bf16[3072,768]{1,0:T(8,128)(2,1)} %bitcast.79, bf16[128,768]{1,0:T(8,128)(2,1)S(1)} %copy-done.7), kind=kOutput, calls=%fused_computation.21 | convolution fusion | flops 612627456 | bytes 7286784 | tf_op jit(solution)/shard_map/td,fd->tf/dot_general | solution.py:100
  106.2 2.3 multiply_reduce_fusion.1
  108.5 1.5 convert_reduce_fusion.4
  110.0 1.2 convolution_convert_fusion.1
  111.3 1.1 copy.51
  114.8 0.7 constant_dynamic-update-slice_fusion.5
  115.6 0.7 constant_dynamic-update-slice_fusion.4
  116.3 0.7 constant_dynamic-update-slice_fusion.3
  117.0 0.7 constant_dynamic-update-slice_fusion.2
  117.7 1.0 constant_dynamic-update-slice_fusion.1
  118.6 0.7 constant_dynamic-update-slice_fusion
  119.4 0.4 collective-permute-start
  120.1 4.1 %fusion.39 = (f32[768]{0:T(1024)S(1)}, f32[128]{0:T(128)S(1)}, f32[128]{0:T(128)S(1)}, f32[768]{0:T(1024)S(1)}, f32[128,768]{1,0:T(8,128)}) fusion(bf16[128,768]{1,0:T(8,128)(2,1)S(1)} %copy-done, f32[128]{0:T(128)S(1)} %copy-done.34, f32[128]{0:T(128)S(1)} %copy-done.30, f32[768]{0:T(1024)S(1)} %reshape.302, bf16[768,2304]{1,0:T(8,128)(2,1)} %bitcast.82, ...), kind=kOutput, calls=%fused_computation.70 | convolution fusion | flops 455735552 | bytes 4729856 | tf_op jit(solution)/shard_map/te,ce->tc/dot_general | solution.py:138
  125.0 3.9 %fusion.23 = bf16[128,768]{1,0:T(8,128)(2,1)} fusion(f32[128,768]{1,0:T(8,128)S(1)} %get-tuple-element.96, bf16[128,3072]{1,0:T(8,128)(2,1)S(1)} %copy-done.2, bf16[3072,768]{1,0:T(8,128)(2,1)} %bitcast.80, f32[768]{0:T(1024)S(1)} %reshape.308), kind=kOutput, calls=%fused_computation.36 | convolution fusion | flops 604274688 | bytes 6097920 | tf_op jit(solution)/shard_map/dot_general | solution.py:72
  128.9 1.1 fusion.38
  130.1 0.6 reshape.301.refs_4_
  130.7 1.3 broadcast_select_fusion.7
  132.1 2.0 fusion.44
  134.0 1.1 broadcast_select_fusion.15
  135.2 1.3 broadcast_select_fusion.5
  136.4 4.0 %fusion.19 = f32[768,2304]{1,0:T(8,128)} fusion(bf16[128,2304]{1,0:T(8,128)(2,1)S(1)} %get-tuple-element.54, bf16[128,2304]{1,0:T(8,128)(2,1)S(1)} %get-tuple-element.53, bf16[128,768]{1,0:T(8,128)(2,1)S(1)} %get-tuple-element.56, bf16[128,768]{1,0:T(8,128)(2,1)S(1)} %get-tuple-element.55), kind=kOutput, calls=%fused_computation.31 | convolution fusion | flops 909115392 | bytes 8650752 | tf_op jit(solution)/shard_map/tc,te->ce/dot_general | solution.py:578
  140.5 1.6 broadcast_select_fusion.1
  142.1 5.1 %fusion.12 = f32[3072,768]{1,0:T(8,128)} fusion(bf16[128,3072]{1,0:T(8,128)(2,1)S(1)} %get-tuple-element.50, bf16[128,3072]{1,0:T(8,128)(2,1)S(1)} %get-tuple-element.49, bf16[128,768]{1,0:T(8,128)(2,1)S(1)} %get-tuple-element.58, bf16[128,768]{1,0:T(8,128)(2,1)S(1)} %get-tuple-element.57), kind=kOutput, calls=%fused_computation.17 | convolution fusion | flops 1211891712 | bytes 11403264 | tf_op jit(solution)/shard_map/tc,te->ce/dot_general | solution.py:578
  147.2 5.0 %fusion.8 = f32[768,3072]{1,0:T(8,128)} fusion(bf16[128,3072]{1,0:T(8,128)(2,1)S(1)} %get-tuple-element.71, bf16[128,3072]{1,0:T(8,128)(2,1)S(1)} %get-tuple-element.72, bf16[128,768]{1,0:T(8,128)(2,1)S(1)} %get-tuple-element.69, bf16[128,768]{1,0:T(8,128)(2,1)S(1)} %get-tuple-element.70), kind=kOutput, calls=%fused_computation.13 | convolution fusion | flops 1211891712 | bytes 11403264 | tf_op jit(solution)/shard_map/tc,te->ce/dot_general | solution.py:578
  152.2 172.6 %shard_map.255 = (f32[96,2304]{1,0:T(8,128)}, f32[96,768]{1,0:T(8,128)}, f32[96,3072]{1,0:T(8,128)}, f32[384,768]{1,0:T(8,128)}, f32[1,1152]{1,0:T(1,128)}) custom-call(f32[8,96,2304]{2,1,0:T(8,128)} %bitcast.71, f32[8,96,768]{2,1,0:T(8,128)} %bitcast.72, f32[8,96,3072]{2,1,0:T(8,128)} %bitcast.70, f32[8,384,768]{2,1,0:T(8,128)} %bitcast.69, ...), custom_call_target="tpu_custom_call" | custom-call | tf_op jit(solution)/shard_map/pallas_call | solution.py:457
  324.8 1.4 slice.140
  326.2 1.3 slice.144
  327.5 1.3 fusion.69
  328.9 2.1 copy.84
  331.0 0.7 copy.85
  331.7 1.0 copy.86
  332.8 1.0 copy.87
  (133 shorter events, 6.4 us)
Async XLA Ops:
  0.6 85.0 %copy-start = (bf16[128,768]{1,0:T(8,128)(2,1)S(1)}, bf16[128,768]{1,0:T(8,128)(2,1)}, u32[]{:S(2)}) copy-start(bf16[128,768]{1,0:T(8,128)(2,1)} %param.15) | copy-start | bytes 589828
  0.7 85.3 %copy-start.35 = (s32[128]{0:T(128)S(1)}, s32[128]{0:T(128)}, u32[]{:S(2)}) copy-start(s32[128]{0:T(128)} %param.16) | copy-start | bytes 1540
  85.8 6.2 %copy-start.29 = (f32[128]{0:T(128)}, f32[128]{0:T(128)S(1)}, u32[]{:S(2)}) copy-start(f32[128]{0:T(128)S(1)} %broadcast_multiply_fusion.5) | copy-start | bytes 1540
  86.0 6.0 %copy-start.33 = (f32[128]{0:T(128)}, f32[128]{0:T(128)S(1)}, u32[]{:S(2)}) copy-start(f32[128]{0:T(128)S(1)} %add_rsqrt_fusion.1) | copy-start | bytes 1540
  87.1 4.9 %copy-start.20 = (f32[768]{0:T(1024)}, f32[768]{0:T(1024)S(1)}, u32[]{:S(2)}) copy-start(f32[768]{0:T(1024)S(1)} %reshape.303) | copy-start | bytes 9220
  92.2 0.9 copy-start.3
  92.4 1.0 copy-start.5
  92.6 0.8 copy-start.11
  92.6 1.3 copy-start.1
  92.6 1.3 copy-start.27
  93.4 1.9 copy-start.26
  93.5 2.6 copy-start.9
  93.9 2.2 copy-start.32
  96.1 5.0 %copy-start.16 = (bf16[128,768]{1,0:T(8,128)(2,1)}, bf16[128,768]{1,0:T(8,128)(2,1)S(1)}, u32[]{:S(2)}) copy-start(bf16[128,768]{1,0:T(8,128)(2,1)S(1)} %get-tuple-element.48) | copy-start | bytes 589828
  96.1 5.0 %copy-start.7 = (bf16[128,768]{1,0:T(8,128)(2,1)S(1)}, bf16[128,768]{1,0:T(8,128)(2,1)}, u32[]{:S(2)}) copy-start(bf16[128,768]{1,0:T(8,128)(2,1)} %param.17) | copy-start | bytes 589828
  96.2 10.0 %slice-start = ((s8[4718592]{0:T(1024)(128)(4,1)}), s8[4194304]{0:T(1024)(128)(4,1)S(1)}, s32[]{:S(2)}) async-start(s8[4718592]{0:T(1024)(128)(4,1)} %bitcast.74), calls=%async_computation | async-start | bytes 8388608
  101.1 5.0 %slice-start.1 = ((s8[4718592]{0:T(1024)(128)(4,1)}), s8[524288]{0:T(1024)(128)(4,1)S(1)}, s32[]{:S(2)}) async-start(s8[4718592]{0:T(1024)(128)(4,1)} %bitcast.74), calls=%async_computation.1 | async-start | bytes 1048576
  111.3 1.5 copy-start.12
  112.8 0.9 copy-start.6
  113.1 1.0 copy-start.4
  114.8 3.9 %copy-start.8 = (bf16[128,768]{1,0:T(8,128)(2,1)S(1)}, bf16[128,768]{1,0:T(8,128)(2,1)}, u32[]{:S(2)}) copy-start(bf16[128,768]{1,0:T(8,128)(2,1)} %param.17) | copy-start | bytes 589828
  115.5 4.3 %copy-start.31 = (f32[3072]{0:T(1024)S(1)}, f32[3072]{0:T(1024)}, u32[]{:S(2)}) copy-start(f32[3072]{0:T(1024)} %get-tuple-element.102) | copy-start | bytes 36868
  115.5 4.3 %copy-start.23 = (f32[768]{0:T(1024)S(1)}, f32[768]{0:T(1024)}, u32[]{:S(2)}) copy-start(f32[768]{0:T(1024)} %get-tuple-element.34) | copy-start | bytes 9220
  115.5 4.4 %copy-start.25 = (f32[768]{0:T(1024)S(1)}, f32[768]{0:T(1024)}, u32[]{:S(2)}) copy-start(f32[768]{0:T(1024)} %get-tuple-element.42) | copy-start | bytes 9220
  115.5 4.4 %copy-start.24 = (f32[768]{0:T(1024)S(1)}, f32[768]{0:T(1024)}, u32[]{:S(2)}) copy-start(f32[768]{0:T(1024)} %get-tuple-element.76) | copy-start | bytes 9220
  115.5 4.5 %copy-start.22 = (f32[768]{0:T(1024)S(1)}, f32[768]{0:T(1024)}, u32[]{:S(2)}) copy-start(f32[768]{0:T(1024)} %get-tuple-element.40) | copy-start | bytes 9220
  115.5 4.6 %copy-start.30 = (f32[128]{0:T(128)S(1)}, f32[128]{0:T(128)}, u32[]{:S(2)}) copy-start(f32[128]{0:T(128)} %copy-done.29) | copy-start | bytes 1540
  115.6 4.6 %copy-start.34 = (f32[128]{0:T(128)S(1)}, f32[128]{0:T(128)}, u32[]{:S(2)}) copy-start(f32[128]{0:T(128)} %copy-done.33) | copy-start | bytes 1540
  119.4 11.3 %collective-permute-start = (bf16[128,12288]{1,0:T(8,128)(2,1)}, bf16[128,12288]{1,0:T(8,128)(2,1)}, u32[]{:S(2)}, u32[]{:S(2)}) collective-permute-start(bf16[128,12288]{1,0:T(8,128)(2,1)} %constant_dynamic-update-slice_fusion), channel_id=1, source_target_pairs={{0,8},{8,0},{16,24},{24,16},{1,9},{9,1},{17,25},{25,17},{2,10},{10... | collective-permute-start | bytes 9437192 | tf_op jit(solution)/shard_map/ppermute | solution.py:487
  120.1 4.8 %copy-start.28 = (f32[8,96]{1,0:T(8,128)S(1)}, f32[8,96]{1,0:T(8,128)}, u32[]{:S(2)}) copy-start(f32[8,96]{1,0:T(8,128)} %get-tuple-element.77) | copy-start | bytes 9220
  120.1 4.9 %copy-start.2 = (bf16[128,3072]{1,0:T(8,128)(2,1)S(1)}, bf16[128,3072]{1,0:T(8,128)(2,1)}, u32[]{:S(2)}) copy-start(bf16[128,3072]{1,0:T(8,128)(2,1)} %get-tuple-element.46) | copy-start | bytes 2359300
  124.8 5.3 %collective-permute-start.1 = (f32[8,1152]{1,0:T(8,128)S(1)}, f32[8,1152]{1,0:T(8,128)S(1)}, u32[]{:S(2)}, u32[]{:S(2)}) collective-permute-start(f32[8,1152]{1,0:T(8,128)S(1)} %concatenate.64), channel_id=1, source_target_pairs={{0,8},{8,0},{16,24},{24,16},{1,9},{9,1},{17,25},{25,17},{2,10},{10... | collective-permute-start | bytes 110600 | tf_op jit(solution)/shard_map/ppermute | solution.py:487
  125.0 3.9 %copy-start.13 = (f32[128,768]{1,0:T(8,128)S(1)}, f32[128,768]{1,0:T(8,128)}, u32[]{:S(2)}) copy-start(f32[128,768]{1,0:T(8,128)} %get-tuple-element.44) | copy-start | bytes 1179652
  125.0 3.9 %copy-start.18 = (f32[128,768]{1,0:T(8,128)S(1)}, f32[128,768]{1,0:T(8,128)}, u32[]{:S(2)}) copy-start(f32[128,768]{1,0:T(8,128)} %get-tuple-element.101) | copy-start | bytes 1179652
  128.9 1.8 copy-start.10
  128.9 1.8 copy-start.17
  132.1 2.0 copy-start.21
  324.8 6.2 %copy-start.19 = (f32[96,768]{1,0:T(8,128)S(1)}, f32[96,768]{1,0:T(8,128)}, u32[]{:S(2)}) copy-start(f32[96,768]{1,0:T(8,128)} %get-tuple-element.31) | copy-start | bytes 884740
  324.8 6.9 %copy-start.15 = (f32[96,3072]{1,0:T(8,128)S(1)}, f32[96,3072]{1,0:T(8,128)}, u32[]{:S(2)}) copy-start(f32[96,3072]{1,0:T(8,128)} %get-tuple-element.32) | copy-start | bytes 3538948
  331.0 1.7 copy-start.14

commit v7 on v6

--- a/solution.py
+++ b/solution.py
@@ -180,15 +180,20 @@
 FIRST_CORE_HALF = (0, 3)
 
 
+X_ONLY = (2, 3)
+
+
 def gather_kernel(n, count, *refs):
     local = refs[:count]
     full = refs[count : 2 * count]
-    ring_send, ring_recv, pair_send, pair_recv = refs[2 * count :]
+    ring_send, ring_recv, pair_send, pair_recv, x_send, x_recv, relay_send, relay_recv = refs[2 * count :]
     rep = lax.axis_index("rep")
     shard = lax.axis_index("shard")
     core = rep % 2
+    plane = rep // 2
     step_dir = 1 - 2 * core
     partner = (rep + step_dir, shard)
+    x_partner = ((rep + 2) % 4, shard)
     here = ring_position(shard, n)
     target = (rep, ring_shard(here + step_dir, n))
     source = (rep, ring_shard(here - step_dir, n))
@@ -196,16 +201,53 @@
     split_last = n % 2 == 0
 
     barrier = pltpu.get_barrier_semaphore()
-    for peer in (target, source, partner):
+    for peer in (target, source, partner, x_partner):
         pl.semaphore_signal(barrier, inc=1, device_id=peer, device_id_type=MESH)
-    pl.semaphore_wait(barrier, 3)
-
-    def mine_at(k, w):
+    pl.semaphore_wait(barrier, 4)
+
+    def both(a, b):
+        if a is True:
+            return b
+        if b is True:
+            return a
+        return jnp.logical_and(a, b)
+
+    def core_carries(k, w, which_core):
         if split_last and k == steps:
-            return (core == 0) == (w in FIRST_CORE_HALF)
+            return (which_core == 0) == (w in FIRST_CORE_HALF)
         return True
 
+    def plane_carries(w, which_plane):
+        if w == X_ONLY[0]:
+            return which_plane == 0
+        if w == X_ONLY[1]:
+            return which_plane == 1
+        return True
+
+    def ring_in(k, w):
+        return both(plane_carries(w, plane), core_carries(k, w, core))
+
+    def x_out(k, w):
+        if w not in X_ONLY:
+            return False
+        return both(plane_carries(w, plane), core_carries(k, w, core))
+
+    def x_in(k, w):
+        if w not in X_ONLY:
+            return False
+        return both(plane_carries(w, 1 - plane), core_carries(k, w, core))
+
+    def partner_ring_in(k, w):
+        return both(plane_carries(w, plane), core_carries(k, w, 1 - core))
+
+    def partner_x_in(k, w):
+        if w not in X_ONLY:
+            return False
+        return both(plane_carries(w, 1 - plane), core_carries(k, w, 1 - core))
+
     def guarded(cond, fn):
+        if cond is False:
+            return
         if cond is True:
             fn()
         else:
@@ -214,59 +256,56 @@
     def slot(position):
         return ring_shard(position, n)
 
+    def remote(src, dst, ssem, rsem, device):
+        return pltpu.make_async_remote_copy(
+            src_ref=src, dst_ref=dst, send_sem=ssem, recv_sem=rsem, device_id=device, device_id_type=MESH
+        )
+
     def ring_copy(k, w):
         src_pos = here - step_dir * (k - 1)
         src = local[w] if k == 1 else full[w].at[slot(src_pos)]
-        return pltpu.make_async_remote_copy(
-            src_ref=src,
-            dst_ref=full[w].at[slot(src_pos)],
-            send_sem=ring_send.at[k - 1, w],
-            recv_sem=ring_recv.at[k - 1, w],
-            device_id=target,
-            device_id_type=MESH,
-        )
+        return remote(src, full[w].at[slot(src_pos)], ring_send.at[k - 1, w], ring_recv.at[k - 1, w], target)
 
     def incoming_ring(k, w):
-        pos = here - step_dir * k
-        return pltpu.make_async_remote_copy(
-            src_ref=full[w].at[slot(pos)],
-            dst_ref=full[w].at[slot(pos)],
-            send_sem=ring_send.at[k - 1, w],
-            recv_sem=ring_recv.at[k - 1, w],
-            device_id=source,
-            device_id_type=MESH,
-        )
+        pos = slot(here - step_dir * k)
+        return remote(full[w].at[pos], full[w].at[pos], ring_send.at[k - 1, w], ring_recv.at[k - 1, w], source)
 
     def pair_copy(k, w, pos):
         src = local[w] if k == 0 else full[w].at[slot(pos)]
-        return pltpu.make_async_remote_copy(
-            src_ref=src,
-            dst_ref=full[w].at[slot(pos)],
-            send_sem=pair_send.at[k, w],
-            recv_sem=pair_recv.at[k, w],
-            device_id=partner,
-            device_id_type=MESH,
-        )
+        return remote(src, full[w].at[slot(pos)], pair_send.at[k, w], pair_recv.at[k, w], partner)
+
+    def x_copy(k, w):
+        pos = slot(here - step_dir * k)
+        return remote(full[w].at[pos], full[w].at[pos], x_send.at[k - 1, w], x_recv.at[k - 1, w], x_partner)
+
+    def relay_copy(k, w, pos):
+        pos = slot(pos)
+        return remote(full[w].at[pos], full[w].at[pos], relay_send.at[k - 1, w], relay_recv.at[k - 1, w], partner)
 
     for w in range(count):
         pair_copy(0, w, here).start()
     for w in range(count):
-        guarded(mine_at(1, w), lambda w=w: ring_copy(1, w).start())
+        guarded(ring_in(1, w), lambda w=w: ring_copy(1, w).start())
     for k in range(1, steps + 1):
         for w in range(count):
             def arrived(k=k, w=w):
                 incoming_ring(k, w).wait_recv()
                 if k < steps:
-                    guarded(mine_at(k + 1, w), lambda: ring_copy(k + 1, w).start())
+                    guarded(ring_in(k + 1, w), lambda: ring_copy(k + 1, w).start())
+                guarded(x_out(k, w), lambda: x_copy(k, w).start())
                 pair_copy(k, w, here - step_dir * k).start()
-            guarded(mine_at(k, w), arrived)
+            guarded(ring_in(k, w), arrived)
+        for w in range(count):
+            def crossed(k=k, w=w):
+                x_copy(k, w).wait_recv()
+                relay_copy(k, w, here - step_dir * k).start()
+            guarded(x_in(k, w), crossed)
     for w in range(count):
         pair_copy(0, w, here).wait_recv()
     for k in range(1, steps + 1):
         for w in range(count):
-            theirs = mine_at(k, w)
-            theirs = True if theirs is True else jnp.logical_not(theirs)
-            guarded(theirs, lambda k=k, w=w: pair_copy(k, w, here + step_dir * k).wait_recv())
+            guarded(partner_ring_in(k, w), lambda k=k, w=w: pair_copy(k, w, here + step_dir * k).wait_recv())
+            guarded(partner_x_in(k, w), lambda k=k, w=w: relay_copy(k, w, here + step_dir * k).wait_recv())
     for w in range(count):
         pair_copy(0, w, here).wait_send()
     for k in range(1, steps + 1):
@@ -274,22 +313,29 @@
             def sent(k=k, w=w):
                 ring_copy(k, w).wait_send()
                 pair_copy(k, w, here - step_dir * k).wait_send()
-            guarded(mine_at(k, w), sent)
+            guarded(ring_in(k, w), sent)
+            guarded(x_out(k, w), lambda k=k, w=w: x_copy(k, w).wait_send())
+            guarded(x_in(k, w), lambda k=k, w=w: relay_copy(k, w, here - step_dir * k).wait_send())
 
 
 def gather_weights(locals_, n):
     count = len(locals_)
     steps = n // 2
+    dma = pltpu.SemaphoreType.DMA
     return pl.pallas_call(
         functools.partial(gather_kernel, n, count),
         out_shape=[jax.ShapeDtypeStruct((n,) + a.shape, a.dtype) for a in locals_],
         in_specs=[pl.BlockSpec(memory_space=pl.ANY)] * count,
         out_specs=[pl.BlockSpec(memory_space=pl.ANY)] * count,
         scratch_shapes=[
-            pltpu.SemaphoreType.DMA((steps, count)),
-            pltpu.SemaphoreType.DMA((steps, count)),
-            pltpu.SemaphoreType.DMA((steps + 1, count)),
-            pltpu.SemaphoreType.DMA((steps + 1, count)),
+            dma((steps, count)),
+            dma((steps, count)),
+            dma((steps + 1, count)),
+            dma((steps + 1, count)),
+            dma((steps, count)),
+            dma((steps, count)),
+            dma((steps, count)),
+            dma((steps, count)),
         ],
         compiler_params=pltpu.CompilerParams(collective_id=0, has_side_effects=True),
     )(*locals_)

time: 334 us -> 334 us (level)
  no operation moved by 1% of the time
where the time goes in v7:
time: 334 us; the launch traced here: 333 us
  Pallas kernels  249 us (75%)
  matrix products  42.9 us (13%)
  local copies, waits for them, and re-layouts  26.5 us (8%)
  other arithmetic  12.7 us (4%)
    pallas_call x1, Pallas kernels, reduce_gradients(): pl.pallas_call(functools.partial(reduce_kernel, n, count), out_shape=[jax...  173 us
    pallas_call x1, Pallas kernels, gather_weights(): pl.pallas_call(functools.partial(gather_kernel, n, count), out_shape=[jax...  76 us
    dot_general x4, matrix products, per_device(): jnp.einsum('tc,te->ce', rows, grads, preferred_element_type=jnp.float32)  16.1 us
    unnamed x87, local copies, waits for them, and re-layouts  11.1 us
  transfers between devices with their start and end apart: 2, of which 0 were waited for; matrix products, arithmetic and copies ran while one was open for 3% of the time, Pallas kernels for 0%

profile of v7, /device:TPU:0, one launch (start us, length us, event | category | flops | bytes accessed | tf_op | source)
XLA Modules:
  0.0 333.0 jit_solution(2587623702525901266)
XLA Ops:
  0.7 0.7 reduce
  1.4 0.7 reduce.1
  2.1 4.1 %concatenate.49 = bf16[1152]{0:T(1024)(128)(2,1)S(1)} concatenate(bf16[96]{0:T(256)(128)(2,1)} %bitcast.107, bf16[96]{0:T(256)(128)(2,1)} %bitcast.108, bf16[192]{0:T(256)(128)(2,1)S(1)} %reduce, bf16[96]{0:T(256)(128)(2,1)} %bitcast.109, bf16[96]{0:T(256)(128)(2,1)} %bitcast.110, bf16[96]{0:T(256)(128)(2,1)} %bitcast.111, bf16[384]{0:T(512)(128)(2,1)S(1)} %reduce.1, ...), dimensions={0} | concatenate | bytes 4608 | tf_op jit(solution)/shard_map/concatenate | solution.py:589
  6.2 0.6 reshape.277.refs_4_
  6.8 76.0 %shard_map.254 = (bf16[8,96,2304]{2,1,0:T(8,128)(2,1)}, bf16[8,96,768]{2,1,0:T(8,128)(2,1)}, bf16[8,96,3072]{2,1,0:T(8,128)(2,1)}, bf16[8,384,768]{2,1,0:T(8,128)(2,1)}, bf16[8,1,1152]{2,1,0:T(2,128)(2,1)}) custom-call(bf16[96,2304]{1,0:T(8,128)(2,1)} %bitcast.101, bf16[96,768]{1,0:T(8,128)(2,1)} %bitcast.103, bf16[96,3072]{1,0:T(8,128)(2,1)} %bitcast.99, ...), custom_call_target="tpu_custom_call" | custom-call | tf_op jit(solution)/shard_map/pallas_call | solution.py:325
  82.8 0.8 copy.70
  83.7 0.7 slice_convert_fusion.2
  85.0 0.6 reshape.307
  85.9 0.7 reshape.306
  86.5 0.7 reshape.304
  87.2 0.8 constant_dynamic-update-slice_fusion.9
  88.0 2.7 fusion
  92.7 0.4 fusion.71
  93.4 0.7 constant_dynamic-update-slice_fusion.8
  94.1 0.8 constant_dynamic-update-slice_fusion.7
  94.9 5.0 %constant_dynamic-update-slice_fusion.6 = (bf16[128,12288]{1,0:T(8,128)(2,1)}, bf16[128,3072]{1,0:T(8,128)(2,1)}, f32[128,3072]{1,0:T(8,128)S(1)}) fusion(bf16[128,12288]{1,0:T(8,128)(2,1)} %get-tuple-element.47, f32[3072]{0:T(1024)S(1)} %copy-done.32, bf16[128,768]{1,0:T(8,128)(2,1)S(1)} %get-tuple-element.48, bf16[768,3072]{1,0:T(8,128)(2,1)} %bitcast.73), kind=kOutput, calls=%fused_computation.114 | convolution fusion | flops 607911936 | bytes 8073216 | tf_op jit(solution)/shard_map/dot_general | solution.py:69
  99.9 5.0 %convert_reduce_fusion = (f32[3072]{0:T(1024)}, bf16[128,3072]{1,0:T(8,128)(2,1)S(1)}) fusion(f32[128,3072]{1,0:T(8,128)S(1)} %get-tuple-element.97, bf16[3072,768]{1,0:T(8,128)(2,1)} %bitcast.79, bf16[128,768]{1,0:T(8,128)(2,1)S(1)} %copy-done.7), kind=kOutput, calls=%fused_computation.21 | convolution fusion | flops 612627456 | bytes 7286784 | tf_op jit(solution)/shard_map/td,fd->tf/dot_general | solution.py:100
  104.9 2.3 multiply_reduce_fusion.1
  107.2 1.5 convert_reduce_fusion.4
  108.8 1.2 convolution_convert_fusion.1
  110.0 1.1 copy.51
  113.6 0.7 constant_dynamic-update-slice_fusion.5
  114.3 0.7 constant_dynamic-update-slice_fusion.4
  115.0 0.7 constant_dynamic-update-slice_fusion.3
  115.7 0.7 constant_dynamic-update-slice_fusion.2
  116.4 1.0 constant_dynamic-update-slice_fusion.1
  117.4 0.7 constant_dynamic-update-slice_fusion
  118.1 0.4 collective-permute-start
  118.9 4.1 %fusion.39 = (f32[768]{0:T(1024)S(1)}, f32[128]{0:T(128)S(1)}, f32[128]{0:T(128)S(1)}, f32[768]{0:T(1024)S(1)}, f32[128,768]{1,0:T(8,128)}) fusion(bf16[128,768]{1,0:T(8,128)(2,1)S(1)} %copy-done, f32[128]{0:T(128)S(1)} %copy-done.34, f32[128]{0:T(128)S(1)} %copy-done.30, f32[768]{0:T(1024)S(1)} %reshape.302, bf16[768,2304]{1,0:T(8,128)(2,1)} %bitcast.82, ...), kind=kOutput, calls=%fused_computation.70 | convolution fusion | flops 455735552 | bytes 4729856 | tf_op jit(solution)/shard_map/te,ce->tc/dot_general | solution.py:138
  123.8 4.1 %fusion.23 = bf16[128,768]{1,0:T(8,128)(2,1)} fusion(f32[128,768]{1,0:T(8,128)S(1)} %get-tuple-element.96, bf16[128,3072]{1,0:T(8,128)(2,1)S(1)} %copy-done.2, bf16[3072,768]{1,0:T(8,128)(2,1)} %bitcast.80, f32[768]{0:T(1024)S(1)} %reshape.308), kind=kOutput, calls=%fused_computation.36 | convolution fusion | flops 604274688 | bytes 6097920 | tf_op jit(solution)/shard_map/dot_general | solution.py:72
  127.9 0.9 fusion.38
  128.8 0.6 reshape.301.refs_4_
  129.5 1.3 broadcast_select_fusion.7
  130.8 2.0 fusion.44
  132.8 1.1 broadcast_select_fusion.15
  134.0 1.3 broadcast_select_fusion.5
  135.2 4.0 %fusion.19 = f32[768,2304]{1,0:T(8,128)} fusion(bf16[128,2304]{1,0:T(8,128)(2,1)S(1)} %get-tuple-element.54, bf16[128,2304]{1,0:T(8,128)(2,1)S(1)} %get-tuple-element.53, bf16[128,768]{1,0:T(8,128)(2,1)S(1)} %get-tuple-element.56, bf16[128,768]{1,0:T(8,128)(2,1)S(1)} %get-tuple-element.55), kind=kOutput, calls=%fused_computation.31 | convolution fusion | flops 909115392 | bytes 8650752 | tf_op jit(solution)/shard_map/tc,te->ce/dot_general | solution.py:624
  139.3 1.6 broadcast_select_fusion.1
  140.8 5.1 %fusion.12 = f32[3072,768]{1,0:T(8,128)} fusion(bf16[128,3072]{1,0:T(8,128)(2,1)S(1)} %get-tuple-element.50, bf16[128,3072]{1,0:T(8,128)(2,1)S(1)} %get-tuple-element.49, bf16[128,768]{1,0:T(8,128)(2,1)S(1)} %get-tuple-element.58, bf16[128,768]{1,0:T(8,128)(2,1)S(1)} %get-tuple-element.57), kind=kOutput, calls=%fused_computation.17 | convolution fusion | flops 1211891712 | bytes 11403264 | tf_op jit(solution)/shard_map/tc,te->ce/dot_general | solution.py:624
  145.9 5.0 %fusion.8 = f32[768,3072]{1,0:T(8,128)} fusion(bf16[128,3072]{1,0:T(8,128)(2,1)S(1)} %get-tuple-element.71, bf16[128,3072]{1,0:T(8,128)(2,1)S(1)} %get-tuple-element.72, bf16[128,768]{1,0:T(8,128)(2,1)S(1)} %get-tuple-element.69, bf16[128,768]{1,0:T(8,128)(2,1)S(1)} %get-tuple-element.70), kind=kOutput, calls=%fused_computation.13 | convolution fusion | flops 1211891712 | bytes 11403264 | tf_op jit(solution)/shard_map/tc,te->ce/dot_general | solution.py:624
  151.0 173.0 %shard_map.255 = (f32[96,2304]{1,0:T(8,128)}, f32[96,768]{1,0:T(8,128)}, f32[96,3072]{1,0:T(8,128)}, f32[384,768]{1,0:T(8,128)}, f32[1,1152]{1,0:T(1,128)}) custom-call(f32[8,96,2304]{2,1,0:T(8,128)} %bitcast.71, f32[8,96,768]{2,1,0:T(8,128)} %bitcast.72, f32[8,96,3072]{2,1,0:T(8,128)} %bitcast.70, f32[8,384,768]{2,1,0:T(8,128)} %bitcast.69, ...), custom_call_target="tpu_custom_call" | custom-call | tf_op jit(solution)/shard_map/pallas_call | solution.py:503
  324.1 1.4 slice.140
  325.5 1.3 slice.144
  326.8 1.3 fusion.69
  328.1 2.1 copy.84
  330.3 0.7 copy.85
  331.0 1.0 copy.86
  332.0 1.0 copy.87
  (133 shorter events, 6.4 us)
Async XLA Ops:
  0.6 83.8 %copy-start = (bf16[128,768]{1,0:T(8,128)(2,1)S(1)}, bf16[128,768]{1,0:T(8,128)(2,1)}, u32[]{:S(2)}) copy-start(bf16[128,768]{1,0:T(8,128)(2,1)} %param.15) | copy-start | bytes 589828
  0.7 84.1 %copy-start.35 = (s32[128]{0:T(128)S(1)}, s32[128]{0:T(128)}, u32[]{:S(2)}) copy-start(s32[128]{0:T(128)} %param.16) | copy-start | bytes 1540
  84.5 6.2 %copy-start.29 = (f32[128]{0:T(128)}, f32[128]{0:T(128)S(1)}, u32[]{:S(2)}) copy-start(f32[128]{0:T(128)S(1)} %broadcast_multiply_fusion.5) | copy-start | bytes 1540
  84.8 6.0 %copy-start.33 = (f32[128]{0:T(128)}, f32[128]{0:T(128)S(1)}, u32[]{:S(2)}) copy-start(f32[128]{0:T(128)S(1)} %add_rsqrt_fusion.1) | copy-start | bytes 1540
  85.9 4.9 %copy-start.20 = (f32[768]{0:T(1024)}, f32[768]{0:T(1024)S(1)}, u32[]{:S(2)}) copy-start(f32[768]{0:T(1024)S(1)} %reshape.303) | copy-start | bytes 9220
  91.0 0.9 copy-start.3
  91.2 1.0 copy-start.5
  91.3 0.8 copy-start.11
  91.3 1.3 copy-start.1
  91.4 1.3 copy-start.27
  92.1 2.0 copy-start.26
  92.3 2.6 copy-start.9
  92.7 2.2 copy-start.32
  94.9 5.0 %copy-start.16 = (bf16[128,768]{1,0:T(8,128)(2,1)}, bf16[128,768]{1,0:T(8,128)(2,1)S(1)}, u32[]{:S(2)}) copy-start(bf16[128,768]{1,0:T(8,128)(2,1)S(1)} %get-tuple-element.48) | copy-start | bytes 589828
  94.9 5.0 %copy-start.7 = (bf16[128,768]{1,0:T(8,128)(2,1)S(1)}, bf16[128,768]{1,0:T(8,128)(2,1)}, u32[]{:S(2)}) copy-start(bf16[128,768]{1,0:T(8,128)(2,1)} %param.17) | copy-start | bytes 589828
  94.9 10.0 %slice-start = ((s8[4718592]{0:T(1024)(128)(4,1)}), s8[4194304]{0:T(1024)(128)(4,1)S(1)}, s32[]{:S(2)}) async-start(s8[4718592]{0:T(1024)(128)(4,1)} %bitcast.74), calls=%async_computation | async-start | bytes 8388608
  99.9 5.0 %slice-start.1 = ((s8[4718592]{0:T(1024)(128)(4,1)}), s8[524288]{0:T(1024)(128)(4,1)S(1)}, s32[]{:S(2)}) async-start(s8[4718592]{0:T(1024)(128)(4,1)} %bitcast.74), calls=%async_computation.1 | async-start | bytes 1048576
  110.0 1.5 copy-start.12
  111.6 0.9 copy-start.6
  111.9 1.0 copy-start.4
  113.5 3.9 %copy-start.8 = (bf16[128,768]{1,0:T(8,128)(2,1)S(1)}, bf16[128,768]{1,0:T(8,128)(2,1)}, u32[]{:S(2)}) copy-start(bf16[128,768]{1,0:T(8,128)(2,1)} %param.17) | copy-start | bytes 589828
  114.3 4.3 %copy-start.31 = (f32[3072]{0:T(1024)S(1)}, f32[3072]{0:T(1024)}, u32[]{:S(2)}) copy-start(f32[3072]{0:T(1024)} %get-tuple-element.102) | copy-start | bytes 36868
  114.3 4.3 %copy-start.23 = (f32[768]{0:T(1024)S(1)}, f32[768]{0:T(1024)}, u32[]{:S(2)}) copy-start(f32[768]{0:T(1024)} %get-tuple-element.34) | copy-start | bytes 9220
  114.3 4.4 %copy-start.25 = (f32[768]{0:T(1024)S(1)}, f32[768]{0:T(1024)}, u32[]{:S(2)}) copy-start(f32[768]{0:T(1024)} %get-tuple-element.42) | copy-start | bytes 9220
  114.3 4.4 %copy-start.24 = (f32[768]{0:T(1024)S(1)}, f32[768]{0:T(1024)}, u32[]{:S(2)}) copy-start(f32[768]{0:T(1024)} %get-tuple-element.76) | copy-start | bytes 9220
  114.3 4.5 %copy-start.22 = (f32[768]{0:T(1024)S(1)}, f32[768]{0:T(1024)}, u32[]{:S(2)}) copy-start(f32[768]{0:T(1024)} %get-tuple-element.40) | copy-start | bytes 9220
  114.3 4.6 %copy-start.30 = (f32[128]{0:T(128)S(1)}, f32[128]{0:T(128)}, u32[]{:S(2)}) copy-start(f32[128]{0:T(128)} %copy-done.29) | copy-start | bytes 1540
  114.3 4.6 %copy-start.34 = (f32[128]{0:T(128)S(1)}, f32[128]{0:T(128)}, u32[]{:S(2)}) copy-start(f32[128]{0:T(128)} %copy-done.33) | copy-start | bytes 1540
  118.1 11.4 %collective-permute-start = (bf16[128,12288]{1,0:T(8,128)(2,1)}, bf16[128,12288]{1,0:T(8,128)(2,1)}, u32[]{:S(2)}, u32[]{:S(2)}) collective-permute-start(bf16[128,12288]{1,0:T(8,128)(2,1)} %constant_dynamic-update-slice_fusion), channel_id=1, source_target_pairs={{0,8},{8,0},{16,24},{24,16},{1,9},{9,1},{17,25},{25,17},{2,10},{10... | collective-permute-start | bytes 9437192 | tf_op jit(solution)/shard_map/ppermute | solution.py:533
  118.9 4.8 %copy-start.28 = (f32[8,96]{1,0:T(8,128)S(1)}, f32[8,96]{1,0:T(8,128)}, u32[]{:S(2)}) copy-start(f32[8,96]{1,0:T(8,128)} %get-tuple-element.77) | copy-start | bytes 9220
  118.9 4.9 %copy-start.2 = (bf16[128,3072]{1,0:T(8,128)(2,1)S(1)}, bf16[128,3072]{1,0:T(8,128)(2,1)}, u32[]{:S(2)}) copy-start(bf16[128,3072]{1,0:T(8,128)(2,1)} %get-tuple-element.46) | copy-start | bytes 2359300
  123.6 5.3 %collective-permute-start.1 = (f32[8,1152]{1,0:T(8,128)S(1)}, f32[8,1152]{1,0:T(8,128)S(1)}, u32[]{:S(2)}, u32[]{:S(2)}) collective-permute-start(f32[8,1152]{1,0:T(8,128)S(1)} %concatenate.64), channel_id=1, source_target_pairs={{0,8},{8,0},{16,24},{24,16},{1,9},{9,1},{17,25},{25,17},{2,10},{10... | collective-permute-start | bytes 110600 | tf_op jit(solution)/shard_map/ppermute | solution.py:533
  123.8 4.1 %copy-start.13 = (f32[128,768]{1,0:T(8,128)S(1)}, f32[128,768]{1,0:T(8,128)}, u32[]{:S(2)}) copy-start(f32[128,768]{1,0:T(8,128)} %get-tuple-element.44) | copy-start | bytes 1179652
  123.8 4.1 %copy-start.18 = (f32[128,768]{1,0:T(8,128)S(1)}, f32[128,768]{1,0:T(8,128)}, u32[]{:S(2)}) copy-start(f32[128,768]{1,0:T(8,128)} %get-tuple-element.101) | copy-start | bytes 1179652
  127.9 1.6 copy-start.10
  127.9 1.6 copy-start.17
  130.8 2.0 copy-start.21
  324.0 6.2 %copy-start.19 = (f32[96,768]{1,0:T(8,128)S(1)}, f32[96,768]{1,0:T(8,128)}, u32[]{:S(2)}) copy-start(f32[96,768]{1,0:T(8,128)} %get-tuple-element.31) | copy-start | bytes 884740
  324.0 6.9 %copy-start.15 = (f32[96,3072]{1,0:T(8,128)S(1)}, f32[96,3072]{1,0:T(8,128)}, u32[]{:S(2)}) copy-start(f32[96,3072]{1,0:T(8,128)} %get-tuple-element.32) | copy-start | bytes 3538948
  330.3 1.7 copy-start.14

commit v8 on v7

--- a/solution.py
+++ b/solution.py
@@ -353,14 +353,15 @@
     lax.fori_loop(0, rows // chunk, body, 0)
 
 
-def reduce_kernel(n, count, *refs):
-    contrib = refs[:count]
-    out = refs[count : 2 * count]
-    land, send, other, own, xland = (
-        refs[2 * count + i * count : 2 * count + (i + 1) * count] for i in range(5)
-    )
+def reduce_kernel(n, count, mm, *refs):
+    xt = refs[:mm]
+    dy = refs[mm : 2 * mm]
+    contrib = (None,) * mm + refs[2 * mm : mm + count]
+    refs = refs[mm + count :]
+    out = refs[:count]
+    land, send, other, own, xland = (refs[count + i * count : count + (i + 1) * count] for i in range(5))
     (load_sem, own_sem, ring_send, ring_recv, pair_send, pair_recv, x_send, x_recv, back_send, back_recv) = refs[
-        7 * count :
+        6 * count :
     ]
     rep = lax.axis_index("rep")
     shard = lax.axis_index("shard")
@@ -414,10 +415,21 @@
     def owner(w):
         return core == w % 2
 
-    for w in range(count):
+    def contribute(dst, w, position):
+        block = ring_shard(position, n)
+        width = 256
+
+        def body(i, carry):
+            window = pl.ds(pl.multiple_of(i * width, width), width)
+            dst[:, window] = jnp.dot(xt[w][block], dy[w][:, window], preferred_element_type=jnp.float32)
+            return carry
+
+        lax.fori_loop(0, dy[w].shape[1] // width, body, 0)
+
+    for w in range(mm, count):
         load_own(w).start()
     for k in range(1, steps + 1):
-        for w in range(count):
+        for w in range(mm, count):
             guarded(carried(k, w), lambda k=k, w=w: load(k, w).start())
 
     barrier = pltpu.get_barrier_semaphore()
@@ -431,7 +443,10 @@
         add_rows(dst, parts, rows, chunk)
 
     def step(k, w):
-        load(k, w).wait()
+        if w < mm:
+            contribute(send[w].at[k - 1], w, block_at(k))
+        else:
+            load(k, w).wait()
         if k > 1:
             def accumulate():
                 ring_copy(k - 1, w, source).wait_recv()
@@ -445,8 +460,11 @@
         mine = land[w].at[steps - 1]
 
         def plane():
+            if w < mm:
+                contribute(own[w], w, here)
+            else:
+                load_own(w).wait()
             pair_copy(w).wait_recv()
-            load_own(w).wait()
 
             @pl.when(core == 0)
             def _():
@@ -479,7 +497,8 @@
 
     for w in range(count):
         def not_owner(w=w):
-            load_own(w).wait()
+            if w >= mm:
+                load_own(w).wait()
             back_copy(w).wait_recv()
             pair_copy(w).wait_send()
 
@@ -494,16 +513,18 @@
             guarded(carried(k, w), lambda k=k, w=w: ring_copy(k, w, target).wait_send())
 
 
-def reduce_gradients(contribs, n):
-    count = len(contribs)
+def reduce_gradients(pairs_t, contribs, n):
+    mm = len(pairs_t)
+    count = mm + len(contribs)
     steps = n // 2
-    blocks = [c.shape[1:] for c in contribs]
+    blocks = [(xt.shape[1], dy.shape[1]) for xt, dy in pairs_t] + [c.shape[1:] for c in contribs]
     vmem = lambda shape: pltpu.VMEM(shape, jnp.float32)
     dma = pltpu.SemaphoreType.DMA
     return pl.pallas_call(
-        functools.partial(reduce_kernel, n, count),
+        functools.partial(reduce_kernel, n, count, mm),
         out_shape=[jax.ShapeDtypeStruct(b, jnp.float32) for b in blocks],
-        in_specs=[pl.BlockSpec(memory_space=pl.ANY)] * count,
+        in_specs=[pl.BlockSpec(memory_space=pltpu.VMEM)] * (2 * mm)
+        + [pl.BlockSpec(memory_space=pl.ANY)] * len(contribs),
         out_specs=[pl.BlockSpec(memory_space=pltpu.VMEM)] * count,
         scratch_shapes=[vmem((steps,) + b) for b in blocks]
         + [vmem((steps,) + b) for b in blocks]
@@ -523,9 +544,9 @@
             dma((count,)),
         ],
         compiler_params=pltpu.CompilerParams(
-            collective_id=1, has_side_effects=True, vmem_limit_bytes=60 * 1024 * 1024
+            collective_id=1, has_side_effects=True, vmem_limit_bytes=62 * 1024 * 1024
         ),
-    )(*contribs)
+    )(*[xt for xt, _ in pairs_t], *[dy for _, dy in pairs_t], *contribs)
 
 
 def swap_core(value):
@@ -610,21 +631,18 @@
     small_mine = jnp.concatenate([g.reshape(shard, -1) for g in small_grads], axis=1)
     small_theirs = swap_core(small_mine)
     small_chip = jnp.where(core == 0, small_mine + small_theirs, small_theirs + small_mine)
-    contribs = []
     start = 0
     partner_x = []
     for x, _ in pairs:
         partner_x.append(incoming[:, start : start + x.shape[1]])
         start += x.shape[1]
+    pairs_t = []
     for (x, dy), px in zip(pairs, partner_x):
         pdy = incoming[:, start : start + dy.shape[1]]
         start += dy.shape[1]
-        rows = join_halves(x, px, core, 0)
-        grads = join_halves(dy, pdy, core, 0)
-        grad = jnp.einsum("tc,te->ce", rows, grads, preferred_element_type=jnp.float32)
-        contribs.append(grad.reshape(shard, -1, grad.shape[1]))
-    contribs.append(small_chip.reshape(shard, 1, -1))
-    totals = reduce_gradients(contribs, shard)
+        rows_t = jnp.concatenate([x, px], axis=0).T
+        pairs_t.append((rows_t.reshape(shard, -1, rows_t.shape[1]), jnp.concatenate([dy, pdy], axis=0)))
+    totals = reduce_gradients(pairs_t, [small_chip.reshape(shard, 1, -1)], shard)
     small_share = totals[4]
     owned = [t[None] for t in totals[:4]]
     small_owned = []

time: 334 us -> 331 us (level)
  matrix products: 42.9 us -> 29.3 us
  local copies, waits for them, and re-layouts: 26.5 us -> 34.2 us
  Pallas kernels: 249 us -> 253 us
    dot_general x4 -> x0, matrix products: 16.1 us -> none  [per_device(): jnp.einsum('tc,te->ce', rows, grads, preferred_element_type=jnp.float32)]
    select_n x4 -> x0, other arithmetic: 5.31 us -> none  [join_halves(): first = jnp.where(core == 0, mine, theirs)]
    pallas_call x1, Pallas kernels: 173 us -> 177 us  [reduce_gradients(): pl.pallas_call(functools.partial(reduce_kernel, n, count, mm), out_shape=...]
    slice x0 -> x3, local copies, waits for them, and re-layouts: none -> 3.95 us  [per_device(): pdy = incoming[:, start:start + dy.shape[1]]]
    concatenate x0 -> x4, other arithmetic: none -> 3.9 us  [per_device(): jnp.concatenate([dy, pdy], axis=0)]
    unnamed x87 -> x89, local copies, waits for them, and re-layouts: 11.1 us -> 11.1 us
  transfers between devices with their start and end apart: 2 -> 2, of which waited for: 0 -> 0; matrix products, arithmetic and copies ran while one was open for 3% -> 4% of each run, Pallas kernels for 0% -> 0%
where the time goes in v8:
time: 331 us
  Pallas kernels  253 us (76%)
  local copies, waits for them, and re-layouts  34.2 us (10%)
  matrix products  29.3 us (9%)
  other arithmetic  12.3 us (4%)
    pallas_call x1, Pallas kernels, reduce_gradients(): pl.pallas_call(functools.partial(reduce_kernel, n, count, mm), out_shape=...  177 us
    pallas_call x1, Pallas kernels, gather_weights(): pl.pallas_call(functools.partial(gather_kernel, n, count), out_shape=[jax...  76 us
    unnamed x89, local copies, waits for them, and re-layouts  11.1 us
  transfers between devices with their start and end apart: 2, of which 0 were waited for; matrix products, arithmetic and copies ran while one was open for 4% of the time, Pallas kernels for 0%

profile of v8, /device:TPU:0, one launch (start us, length us, event | category | flops | bytes accessed | tf_op | source)
XLA Modules:
  0.0 330.7 jit_solution(14139225802835222625)
XLA Ops:
  0.7 0.7 reduce
  1.4 0.7 reduce.1
  2.1 4.1 %concatenate.49 = bf16[1152]{0:T(1024)(128)(2,1)S(1)} concatenate(bf16[96]{0:T(256)(128)(2,1)} %bitcast.114, bf16[96]{0:T(256)(128)(2,1)} %bitcast.115, bf16[192]{0:T(256)(128)(2,1)S(1)} %reduce, bf16[96]{0:T(256)(128)(2,1)} %bitcast.116, bf16[96]{0:T(256)(128)(2,1)} %bitcast.117, bf16[96]{0:T(256)(128)(2,1)} %bitcast.118, bf16[384]{0:T(512)(128)(2,1)S(1)} %reduce.1, ...), dimensions={0} | concatenate | bytes 4608 | tf_op jit(solution)/shard_map/concatenate | solution.py:610
  6.8 76.0 %shard_map.254 = (bf16[8,96,2304]{2,1,0:T(8,128)(2,1)}, bf16[8,96,768]{2,1,0:T(8,128)(2,1)}, bf16[8,96,3072]{2,1,0:T(8,128)(2,1)}, bf16[8,384,768]{2,1,0:T(8,128)(2,1)}, bf16[8,1,1152]{2,1,0:T(2,128)(2,1)}) custom-call(bf16[96,2304]{1,0:T(8,128)(2,1)} %bitcast.108, bf16[96,768]{1,0:T(8,128)(2,1)} %bitcast.110, bf16[96,3072]{1,0:T(8,128)(2,1)} %bitcast.106, ...), custom_call_target="tpu_custom_call" | custom-call | tf_op jit(solution)/shard_map/pallas_call | solution.py:325
  82.8 0.8 copy.76
  83.7 0.7 slice_convert_fusion.2
  85.4 0.9 constant_dynamic-update-slice_fusion.9
  86.3 2.7 fusion
  91.6 0.7 constant_dynamic-update-slice_fusion.8
  92.3 0.8 constant_dynamic-update-slice_fusion.7
  93.2 5.0 %constant_dynamic-update-slice_fusion.6 = (bf16[128,12288]{1,0:T(8,128)(2,1)}, bf16[128,3072]{1,0:T(8,128)(2,1)}, f32[128,3072]{1,0:T(8,128)S(1)}) fusion(bf16[128,12288]{1,0:T(8,128)(2,1)} %get-tuple-element.47, f32[3072]{0:T(1024)S(1)} %reshape.307, bf16[128,768]{1,0:T(8,128)(2,1)S(1)} %get-tuple-element.48, bf16[768,3072]{1,0:T(8,128)(2,1)} %bitcast.79), kind=kOutput, calls=%fused_computation.79 | convolution fusion | flops 607911936 | bytes 8073216 | tf_op jit(solution)/shard_map/dot_general | solution.py:69
  98.1 5.0 %convert_reduce_fusion = (f32[3072]{0:T(1024)}, bf16[128,3072]{1,0:T(8,128)(2,1)S(1)}) fusion(f32[128,3072]{1,0:T(8,128)S(1)} %get-tuple-element.82, bf16[3072,768]{1,0:T(8,128)(2,1)} %bitcast.85, bf16[128,768]{1,0:T(8,128)(2,1)S(1)} %copy-done.6), kind=kOutput, calls=%fused_computation.15 | convolution fusion | flops 612627456 | bytes 7286784 | tf_op jit(solution)/shard_map/td,fd->tf/dot_general | solution.py:100
  103.2 2.3 multiply_reduce_fusion.1
  105.5 1.5 convert_reduce_fusion.4
  107.0 1.2 convolution_convert_fusion.1
  108.2 1.8 copy.53
  110.0 2.0 convolution_convert_fusion
  112.0 1.3 multiply_reduce_fusion
  115.0 0.7 constant_dynamic-update-slice_fusion.5
  115.7 0.7 constant_dynamic-update-slice_fusion.4
  116.4 0.7 constant_dynamic-update-slice_fusion.3
  117.1 0.7 constant_dynamic-update-slice_fusion.2
  117.8 1.0 constant_dynamic-update-slice_fusion.1
  118.8 0.7 constant_dynamic-update-slice_fusion
  120.3 4.1 %fusion.27 = (f32[768]{0:T(1024)S(1)}, f32[128]{0:T(128)S(1)}, f32[128]{0:T(128)S(1)}, f32[768]{0:T(1024)S(1)}, f32[128,768]{1,0:T(8,128)}) fusion(bf16[128,768]{1,0:T(8,128)(2,1)S(1)} %copy-done, f32[128]{0:T(128)S(1)} %copy-done.34, f32[128]{0:T(128)S(1)} %copy-done.31, f32[768]{0:T(1024)S(1)} %reshape.302, bf16[768,2304]{1,0:T(8,128)(2,1)} %bitcast.88, ...), kind=kOutput, calls=%fused_computation.55 | convolution fusion | flops 455735552 | bytes 4729856 | tf_op jit(solution)/shard_map/te,ce->tc/dot_general | solution.py:138
  124.9 0.7 concatenate.64
  125.8 4.1 %fusion.11 = bf16[128,768]{1,0:T(8,128)(2,1)} fusion(f32[128,768]{1,0:T(8,128)S(1)} %get-tuple-element.81, bf16[128,3072]{1,0:T(8,128)(2,1)S(1)} %copy-done.2, bf16[3072,768]{1,0:T(8,128)(2,1)} %bitcast.86, f32[768]{0:T(1024)S(1)} %reshape.308), kind=kOutput, calls=%fused_computation.27 | convolution fusion | flops 604274688 | bytes 6097920 | tf_op jit(solution)/shard_map/dot_general | solution.py:72
  129.9 0.9 fusion.26
  130.8 0.8 add.120
  132.2 1.1 slice.163
  133.3 1.1 pad_maximum_fusion.1.refs_4_
  134.4 1.5 fusion.36
  135.9 1.3 pad_maximum_fusion.refs_6_
  137.2 1.4 fusion.35
  138.6 0.8 pad_maximum_fusion.4.refs_7_
  139.3 0.8 pad_maximum_fusion.3.refs_5_
  140.1 0.9 copy.67
  141.1 0.9 copy.66
  142.1 0.9 copy.64
  143.1 1.6 copy.73
  144.7 177.1 %shard_map.255 = (f32[96,2304]{1,0:T(8,128)}, f32[96,768]{1,0:T(8,128)}, f32[96,3072]{1,0:T(8,128)}, f32[384,768]{1,0:T(8,128)}, f32[1,1152]{1,0:T(1,128)}) custom-call(bf16[8,96,256]{2,1,0:T(8,128)(2,1)} %bitcast.99, bf16[8,96,256]{2,1,0:T(8,128)(2,1)} %bitcast.98, bf16[8,96,256]{2,1,0:T(8,128)(2,1)} %bitcast.97, bf16[8,384,256]{2,1,0:T(8,128)(2,1)} %bitcast.78, ...), custom_call_target="tpu_custom_call" | custom-call | tf_op jit(solution)/shard_map/pallas_call | solution.py:523
  321.8 1.4 slice.140
  323.2 1.3 slice.144
  324.5 1.4 fusion.40
  325.8 2.1 copy.90
  328.0 0.7 copy.91
  328.7 1.0 copy.92
  329.7 1.0 copy.93
  (142 shorter events, 8.0 us)
Async XLA Ops:
  0.6 83.8 %copy-start = (bf16[128,768]{1,0:T(8,128)(2,1)S(1)}, bf16[128,768]{1,0:T(8,128)(2,1)}, u32[]{:S(2)}) copy-start(bf16[128,768]{1,0:T(8,128)(2,1)} %param.15) | copy-start | bytes 589828
  0.7 84.1 %copy-start.36 = (s32[128]{0:T(128)S(1)}, s32[128]{0:T(128)}, u32[]{:S(2)}) copy-start(s32[128]{0:T(128)} %param.16) | copy-start | bytes 1540
  84.5 4.5 %copy-start.30 = (f32[128]{0:T(128)}, f32[128]{0:T(128)S(1)}, u32[]{:S(2)}) copy-start(f32[128]{0:T(128)S(1)} %broadcast_multiply_fusion.5) | copy-start | bytes 1540
  84.8 4.3 %copy-start.33 = (f32[128]{0:T(128)}, f32[128]{0:T(128)S(1)}, u32[]{:S(2)}) copy-start(f32[128]{0:T(128)S(1)} %add_rsqrt_fusion.1) | copy-start | bytes 1540
  86.3 2.8 copy-start.4
  89.2 1.1 copy-start.8
  89.4 0.9 copy-start.10
  89.6 0.8 copy-start.14
  89.6 1.3 copy-start.1
  90.5 2.6 copy-start.12
  93.1 5.0 %copy-start.20 = (bf16[128,768]{1,0:T(8,128)(2,1)}, bf16[128,768]{1,0:T(8,128)(2,1)S(1)}, u32[]{:S(2)}) copy-start(bf16[128,768]{1,0:T(8,128)(2,1)S(1)} %get-tuple-element.48) | copy-start | bytes 589828
  93.2 5.0 %copy-start.6 = (bf16[128,768]{1,0:T(8,128)(2,1)S(1)}, bf16[128,768]{1,0:T(8,128)(2,1)}, u32[]{:S(2)}) copy-start(bf16[128,768]{1,0:T(8,128)(2,1)} %param.17) | copy-start | bytes 589828
  93.2 10.0 %slice-start = ((s8[4718592]{0:T(1024)(128)(4,1)}), s8[4194304]{0:T(1024)(128)(4,1)S(1)}, s32[]{:S(2)}) async-start(s8[4718592]{0:T(1024)(128)(4,1)} %bitcast.80), calls=%async_computation | async-start | bytes 8388608
  98.1 5.0 %slice-start.1 = ((s8[4718592]{0:T(1024)(128)(4,1)}), s8[524288]{0:T(1024)(128)(4,1)S(1)}, s32[]{:S(2)}) async-start(s8[4718592]{0:T(1024)(128)(4,1)} %bitcast.80), calls=%async_computation.1 | async-start | bytes 1048576
  108.2 3.8 %copy-start.15 = (bf16[128,768]{0,1:T(8,128)(2,1)S(1)}, bf16[128,768]{0,1:T(8,128)(2,1)}, u32[]{:S(2)}) copy-start(bf16[128,768]{0,1:T(8,128)(2,1)} %copy-done.14) | copy-start | bytes 589828
  112.0 1.5 copy-start.11
  113.3 0.9 copy-start.9
  113.5 1.0 copy-start.19
  115.0 3.9 %copy-start.7 = (bf16[128,768]{1,0:T(8,128)(2,1)S(1)}, bf16[128,768]{1,0:T(8,128)(2,1)}, u32[]{:S(2)}) copy-start(bf16[128,768]{1,0:T(8,128)(2,1)} %param.17) | copy-start | bytes 589828
  115.7 4.3 %copy-start.29 = (f32[3072]{0:T(1024)S(1)}, f32[3072]{0:T(1024)}, u32[]{:S(2)}) copy-start(f32[3072]{0:T(1024)} %get-tuple-element.87) | copy-start | bytes 36868
  115.7 4.3 %copy-start.25 = (f32[768]{0:T(1024)S(1)}, f32[768]{0:T(1024)}, u32[]{:S(2)}) copy-start(f32[768]{0:T(1024)} %get-tuple-element.34) | copy-start | bytes 9220
  115.7 4.4 %copy-start.27 = (f32[768]{0:T(1024)S(1)}, f32[768]{0:T(1024)}, u32[]{:S(2)}) copy-start(f32[768]{0:T(1024)} %get-tuple-element.42) | copy-start | bytes 9220
  115.7 4.4 %copy-start.26 = (f32[768]{0:T(1024)S(1)}, f32[768]{0:T(1024)}, u32[]{:S(2)}) copy-start(f32[768]{0:T(1024)} %get-tuple-element.61) | copy-start | bytes 9220
  115.7 4.5 %copy-start.24 = (f32[768]{0:T(1024)S(1)}, f32[768]{0:T(1024)}, u32[]{:S(2)}) copy-start(f32[768]{0:T(1024)} %get-tuple-element.40) | copy-start | bytes 9220
  115.7 4.6 %copy-start.31 = (f32[128]{0:T(128)S(1)}, f32[128]{0:T(128)}, u32[]{:S(2)}) copy-start(f32[128]{0:T(128)} %copy-done.30) | copy-start | bytes 1540
  115.7 4.6 %copy-start.34 = (f32[128]{0:T(128)S(1)}, f32[128]{0:T(128)}, u32[]{:S(2)}) copy-start(f32[128]{0:T(128)} %copy-done.33) | copy-start | bytes 1540
  119.5 12.7 %collective-permute-start = (bf16[128,12288]{1,0:T(8,128)(2,1)}, bf16[128,12288]{1,0:T(8,128)(2,1)}, u32[]{:S(2)}, u32[]{:S(2)}) collective-permute-start(bf16[128,12288]{1,0:T(8,128)(2,1)} %constant_dynamic-update-slice_fusion), channel_id=1, source_target_pairs={{0,8},{8,0},{16,24},{24,16},{1,9},{9,1},{17,25},{25,17},{2,10},{10... | collective-permute-start | bytes 9437192 | tf_op jit(solution)/shard_map/ppermute | solution.py:554
  120.3 5.3 %copy-start.28 = (f32[8,96]{1,0:T(8,128)S(1)}, f32[8,96]{1,0:T(8,128)}, u32[]{:S(2)}) copy-start(f32[8,96]{1,0:T(8,128)} %get-tuple-element.62) | copy-start | bytes 9220
  120.3 5.4 %copy-start.2 = (bf16[128,3072]{1,0:T(8,128)(2,1)S(1)}, bf16[128,3072]{1,0:T(8,128)(2,1)}, u32[]{:S(2)}) copy-start(bf16[128,3072]{1,0:T(8,128)(2,1)} %get-tuple-element.46) | copy-start | bytes 2359300
  125.6 5.2 %collective-permute-start.1 = (f32[8,1152]{1,0:T(8,128)}, f32[8,1152]{1,0:T(8,128)}, u32[]{:S(2)}, u32[]{:S(2)}) collective-permute-start(f32[8,1152]{1,0:T(8,128)} %concatenate.64), channel_id=1, source_target_pairs={{0,8},{8,0},{16,24},{24,16},{1,9},{9,1},{17,25},{25,17},{2,10},{10... | collective-permute-start | bytes 110600 | tf_op jit(solution)/shard_map/ppermute | solution.py:554
  125.7 4.1 %copy-start.16 = (f32[128,768]{1,0:T(8,128)S(1)}, f32[128,768]{1,0:T(8,128)}, u32[]{:S(2)}) copy-start(f32[128,768]{1,0:T(8,128)} %get-tuple-element.44) | copy-start | bytes 1179652
  125.7 4.1 %copy-start.22 = (f32[128,768]{1,0:T(8,128)S(1)}, f32[128,768]{1,0:T(8,128)}, u32[]{:S(2)}) copy-start(f32[128,768]{1,0:T(8,128)} %get-tuple-element.86) | copy-start | bytes 1179652
  125.7 4.1 %copy-start.32 = (f32[128]{0:T(128)S(1)}, f32[128]{0:T(128)}, u32[]{:S(2)}) copy-start(f32[128]{0:T(128)} %copy-done.30) | copy-start | bytes 1540
  125.8 4.1 %copy-start.35 = (f32[128]{0:T(128)S(1)}, f32[128]{0:T(128)}, u32[]{:S(2)}) copy-start(f32[128]{0:T(128)} %copy-done.33) | copy-start | bytes 1540
  137.2 2.9 copy-start.21
  138.5 2.5 copy-start.13
  140.1 1.9 copy-start.5
  141.1 1.9 copy-start.3
  321.8 6.2 %copy-start.23 = (f32[96,768]{1,0:T(8,128)S(1)}, f32[96,768]{1,0:T(8,128)}, u32[]{:S(2)}) copy-start(f32[96,768]{1,0:T(8,128)} %get-tuple-element.31) | copy-start | bytes 884740
  321.8 6.9 %copy-start.18 = (f32[96,3072]{1,0:T(8,128)S(1)}, f32[96,3072]{1,0:T(8,128)}, u32[]{:S(2)}) copy-start(f32[96,3072]{1,0:T(8,128)} %get-tuple-element.32) | copy-start | bytes 3538948
  328.0 1.7 copy-start.17

commit v9 on v8

--- a/solution.py
+++ b/solution.py
@@ -344,10 +344,10 @@
 def add_rows(dst, parts, rows, chunk):
     def body(i, carry):
         window = pl.ds(pl.multiple_of(i * chunk, chunk), chunk)
-        total = parts[0][window, :]
+        total = parts[0][window, :].astype(jnp.float32)
         for part in parts[1:]:
-            total = total + part[window, :]
-        dst[window, :] = total
+            total = total + part[window, :].astype(jnp.float32)
+        dst[window, :] = total.astype(dst.dtype)
         return carry
 
     lax.fori_loop(0, rows // chunk, body, 0)
@@ -359,9 +359,9 @@
     contrib = (None,) * mm + refs[2 * mm : mm + count]
     refs = refs[mm + count :]
     out = refs[:count]
-    land, send, other, own, xland = (refs[count + i * count : count + (i + 1) * count] for i in range(5))
+    land, send, other, own, xland, stage = (refs[count + i * count : count + (i + 1) * count] for i in range(6))
     (load_sem, own_sem, ring_send, ring_recv, pair_send, pair_recv, x_send, x_recv, back_send, back_recv) = refs[
-        6 * count :
+        7 * count :
     ]
     rep = lax.axis_index("rep")
     shard = lax.axis_index("shard")
@@ -439,19 +439,35 @@
 
     def add_into(dst, parts):
         rows = dst.shape[0]
-        chunk = 8 if rows % 8 == 0 else rows
+        chunk = 16 if rows % 16 == 0 else rows
         add_rows(dst, parts, rows, chunk)
 
     def step(k, w):
         if w < mm:
-            contribute(send[w].at[k - 1], w, block_at(k))
+            contribute(stage[w], w, block_at(k))
+            if k > 1:
+                def accumulate():
+                    ring_copy(k - 1, w, source).wait_recv()
+                    add_into(send[w].at[k - 1], [stage[w], land[w].at[k - 2]])
+
+                def start_chain():
+                    add_into(send[w].at[k - 1], [stage[w]])
+
+                cond = carried(k - 1, w)
+                if cond is True:
+                    accumulate()
+                else:
+                    pl.when(cond)(accumulate)
+                    pl.when(jnp.logical_not(cond))(start_chain)
+            else:
+                add_into(send[w].at[k - 1], [stage[w]])
         else:
             load(k, w).wait()
-        if k > 1:
-            def accumulate():
-                ring_copy(k - 1, w, source).wait_recv()
-                add_into(send[w].at[k - 1], [send[w].at[k - 1], land[w].at[k - 2]])
-            guarded(carried(k - 1, w), accumulate)
+            if k > 1:
+                def accumulate():
+                    ring_copy(k - 1, w, source).wait_recv()
+                    add_into(send[w].at[k - 1], [send[w].at[k - 1], land[w].at[k - 2]])
+                guarded(carried(k - 1, w), accumulate)
         ring_copy(k, w, target).start()
 
     def arrive(w):
@@ -518,7 +534,8 @@
     count = mm + len(contribs)
     steps = n // 2
     blocks = [(xt.shape[1], dy.shape[1]) for xt, dy in pairs_t] + [c.shape[1:] for c in contribs]
-    vmem = lambda shape: pltpu.VMEM(shape, jnp.float32)
+    ring_types = [jnp.bfloat16] * mm + [jnp.float32] * len(contribs)
+    vmem = lambda shape, dtype=jnp.float32: pltpu.VMEM(shape, dtype)
     dma = pltpu.SemaphoreType.DMA
     return pl.pallas_call(
         functools.partial(reduce_kernel, n, count, mm),
@@ -526,8 +543,9 @@
         in_specs=[pl.BlockSpec(memory_space=pltpu.VMEM)] * (2 * mm)
         + [pl.BlockSpec(memory_space=pl.ANY)] * len(contribs),
         out_specs=[pl.BlockSpec(memory_space=pltpu.VMEM)] * count,
-        scratch_shapes=[vmem((steps,) + b) for b in blocks]
-        + [vmem((steps,) + b) for b in blocks]
+        scratch_shapes=[vmem((steps,) + b, t) for b, t in zip(blocks, ring_types)]
+        + [vmem((steps,) + b, t) for b, t in zip(blocks, ring_types)]
+        + [vmem(b, t) for b, t in zip(blocks, ring_types)]
         + [vmem(b) for b in blocks]
         + [vmem(b) for b in blocks]
         + [vmem(b) for b in blocks]

time: 331 us -> 268 us (0.81)
  Pallas kernels: 253 us -> 190 us
    pallas_call x1, Pallas kernels: 177 us -> 113 us  [reduce_gradients(): pl.pallas_call(functools.partial(reduce_kernel, n, count, mm), out_shape=...]
  transfers between devices with their start and end apart: 2 -> 2, of which waited for: 0 -> 0; matrix products, arithmetic and copies ran while one was open for 4% -> 5% of each run, Pallas kernels for 0% -> 0%
where the time goes in v9:
time: 268 us; the launch traced here: 267 us
  Pallas kernels  190 us (71%)
  local copies, waits for them, and re-layouts  34.2 us (13%)
  matrix products  29.3 us (11%)
  other arithmetic  12.3 us (5%)
    pallas_call x1, Pallas kernels, reduce_gradients(): pl.pallas_call(functools.partial(reduce_kernel, n, count, mm), out_shape=...  113 us
    pallas_call x1, Pallas kernels, gather_weights(): pl.pallas_call(functools.partial(gather_kernel, n, count), out_shape=[jax...  76 us
    unnamed x89, local copies, waits for them, and re-layouts  11.1 us
  transfers between devices with their start and end apart: 2, of which 0 were waited for; matrix products, arithmetic and copies ran while one was open for 5% of the time, Pallas kernels for 0%

profile of v9, /device:TPU:0, one launch (start us, length us, event | category | flops | bytes accessed | tf_op | source)
XLA Modules:
  0.0 267.1 jit_solution(12274613790293173944)
XLA Ops:
  0.7 0.7 reduce
  1.4 0.7 reduce.1
  2.1 4.1 %concatenate.49 = bf16[1152]{0:T(1024)(128)(2,1)S(1)} concatenate(bf16[96]{0:T(256)(128)(2,1)} %bitcast.114, bf16[96]{0:T(256)(128)(2,1)} %bitcast.115, bf16[192]{0:T(256)(128)(2,1)S(1)} %reduce, bf16[96]{0:T(256)(128)(2,1)} %bitcast.116, bf16[96]{0:T(256)(128)(2,1)} %bitcast.117, bf16[96]{0:T(256)(128)(2,1)} %bitcast.118, bf16[384]{0:T(512)(128)(2,1)S(1)} %reduce.1, ...), dimensions={0} | concatenate | bytes 4608 | tf_op jit(solution)/shard_map/concatenate | solution.py:628
  6.8 76.0 %shard_map.254 = (bf16[8,96,2304]{2,1,0:T(8,128)(2,1)}, bf16[8,96,768]{2,1,0:T(8,128)(2,1)}, bf16[8,96,3072]{2,1,0:T(8,128)(2,1)}, bf16[8,384,768]{2,1,0:T(8,128)(2,1)}, bf16[8,1,1152]{2,1,0:T(2,128)(2,1)}) custom-call(bf16[96,2304]{1,0:T(8,128)(2,1)} %bitcast.108, bf16[96,768]{1,0:T(8,128)(2,1)} %bitcast.110, bf16[96,3072]{1,0:T(8,128)(2,1)} %bitcast.106, ...), custom_call_target="tpu_custom_call" | custom-call | tf_op jit(solution)/shard_map/pallas_call | solution.py:325
  82.8 0.8 copy.76
  83.7 0.7 slice_convert_fusion.2
  85.4 0.9 constant_dynamic-update-slice_fusion.9
  86.3 2.7 %fusion = bf16[128,2304]{1,0:T(8,128)(2,1)S(1)} fusion(bf16[128,768]{1,0:T(8,128)(2,1)S(1)} %get-tuple-element.50, bf16[768,2304]{1,0:T(8,128)(2,1)} %bitcast.87, f32[2304]{0:T(1024)S(1)} %pad_maximum_fusion.6), kind=kOutput, calls=%fused_computation.3 | convolution fusion | flops 453574656 | bytes 4334592 | tf_op jit(solution)/shard_map/dot_general | solution.py:47
  91.6 0.7 constant_dynamic-update-slice_fusion.8
  92.3 0.8 constant_dynamic-update-slice_fusion.7
  93.2 5.0 %constant_dynamic-update-slice_fusion.6 = (bf16[128,12288]{1,0:T(8,128)(2,1)}, bf16[128,3072]{1,0:T(8,128)(2,1)}, f32[128,3072]{1,0:T(8,128)S(1)}) fusion(bf16[128,12288]{1,0:T(8,128)(2,1)} %get-tuple-element.47, f32[3072]{0:T(1024)S(1)} %reshape.307, bf16[128,768]{1,0:T(8,128)(2,1)S(1)} %get-tuple-element.48, bf16[768,3072]{1,0:T(8,128)(2,1)} %bitcast.79), kind=kOutput, calls=%fused_computation.79 | convolution fusion | flops 607911936 | bytes 8073216 | tf_op jit(solution)/shard_map/dot_general | solution.py:69
  98.1 5.0 %convert_reduce_fusion = (f32[3072]{0:T(1024)}, bf16[128,3072]{1,0:T(8,128)(2,1)S(1)}) fusion(f32[128,3072]{1,0:T(8,128)S(1)} %get-tuple-element.82, bf16[3072,768]{1,0:T(8,128)(2,1)} %bitcast.85, bf16[128,768]{1,0:T(8,128)(2,1)S(1)} %copy-done.6), kind=kOutput, calls=%fused_computation.15 | convolution fusion | flops 612627456 | bytes 7286784 | tf_op jit(solution)/shard_map/td,fd->tf/dot_general | solution.py:100
  103.2 2.3 multiply_reduce_fusion.1
  105.5 1.5 convert_reduce_fusion.4
  107.0 1.2 convolution_convert_fusion.1
  108.2 1.8 copy.53
  110.0 2.0 convolution_convert_fusion
  112.0 1.3 multiply_reduce_fusion
  115.0 0.7 constant_dynamic-update-slice_fusion.5
  115.7 0.7 constant_dynamic-update-slice_fusion.4
  116.4 0.7 constant_dynamic-update-slice_fusion.3
  117.1 0.7 constant_dynamic-update-slice_fusion.2
  117.8 1.0 constant_dynamic-update-slice_fusion.1
  118.8 0.7 constant_dynamic-update-slice_fusion
  120.3 4.1 %fusion.27 = (f32[768]{0:T(1024)S(1)}, f32[128]{0:T(128)S(1)}, f32[128]{0:T(128)S(1)}, f32[768]{0:T(1024)S(1)}, f32[128,768]{1,0:T(8,128)}) fusion(bf16[128,768]{1,0:T(8,128)(2,1)S(1)} %copy-done, f32[128]{0:T(128)S(1)} %copy-done.34, f32[128]{0:T(128)S(1)} %copy-done.31, f32[768]{0:T(1024)S(1)} %reshape.302, bf16[768,2304]{1,0:T(8,128)(2,1)} %bitcast.88, ...), kind=kOutput, calls=%fused_computation.55 | convolution fusion | flops 455735552 | bytes 4729856 | tf_op jit(solution)/shard_map/te,ce->tc/dot_general | solution.py:138
  124.9 0.7 concatenate.64
  125.8 4.1 %fusion.11 = bf16[128,768]{1,0:T(8,128)(2,1)} fusion(f32[128,768]{1,0:T(8,128)S(1)} %get-tuple-element.81, bf16[128,3072]{1,0:T(8,128)(2,1)S(1)} %copy-done.2, bf16[3072,768]{1,0:T(8,128)(2,1)} %bitcast.86, f32[768]{0:T(1024)S(1)} %reshape.308), kind=kOutput, calls=%fused_computation.27 | convolution fusion | flops 604274688 | bytes 6097920 | tf_op jit(solution)/shard_map/dot_general | solution.py:72
  129.9 0.9 fusion.26
  130.8 0.8 add.120
  132.2 1.1 slice.163
  133.3 1.1 pad_maximum_fusion.1.refs_4_
  134.4 1.5 fusion.36
  135.9 1.3 pad_maximum_fusion.refs_6_
  137.2 1.4 fusion.35
  138.6 0.8 pad_maximum_fusion.4.refs_7_
  139.3 0.8 pad_maximum_fusion.3.refs_5_
  140.1 0.9 copy.67
  141.1 0.9 copy.66
  142.1 0.9 copy.64
  143.1 1.6 copy.73
  144.7 113.5 %shard_map.255 = (f32[96,2304]{1,0:T(8,128)}, f32[96,768]{1,0:T(8,128)}, f32[96,3072]{1,0:T(8,128)}, f32[384,768]{1,0:T(8,128)}, f32[1,1152]{1,0:T(1,128)}) custom-call(bf16[8,96,256]{2,1,0:T(8,128)(2,1)} %bitcast.99, bf16[8,96,256]{2,1,0:T(8,128)(2,1)} %bitcast.98, bf16[8,96,256]{2,1,0:T(8,128)(2,1)} %bitcast.97, bf16[8,384,256]{2,1,0:T(8,128)(2,1)} %bitcast.78, ...), custom_call_target="tpu_custom_call" | custom-call | tf_op jit(solution)/shard_map/pallas_call | solution.py:540
  258.2 1.4 slice.140
  259.5 1.3 slice.144
  260.8 1.4 fusion.40
  262.2 2.1 copy.90
  264.3 0.7 copy.91
  265.0 1.0 copy.92
  266.1 1.0 copy.93
  (142 shorter events, 8.0 us)
Async XLA Ops:
  0.6 83.8 %copy-start = (bf16[128,768]{1,0:T(8,128)(2,1)S(1)}, bf16[128,768]{1,0:T(8,128)(2,1)}, u32[]{:S(2)}) copy-start(bf16[128,768]{1,0:T(8,128)(2,1)} %param.15) | copy-start | bytes 589828
  0.7 84.1 %copy-start.36 = (s32[128]{0:T(128)S(1)}, s32[128]{0:T(128)}, u32[]{:S(2)}) copy-start(s32[128]{0:T(128)} %param.16) | copy-start | bytes 1540
  84.5 4.5 %copy-start.30 = (f32[128]{0:T(128)}, f32[128]{0:T(128)S(1)}, u32[]{:S(2)}) copy-start(f32[128]{0:T(128)S(1)} %broadcast_multiply_fusion.5) | copy-start | bytes 1540
  84.8 4.3 %copy-start.33 = (f32[128]{0:T(128)}, f32[128]{0:T(128)S(1)}, u32[]{:S(2)}) copy-start(f32[128]{0:T(128)S(1)} %add_rsqrt_fusion.1) | copy-start | bytes 1540
  86.3 2.8 %copy-start.4 = (bf16[128,768]{1,0:T(8,128)(2,1)}, bf16[128,768]{1,0:T(8,128)(2,1)S(1)}, u32[]{:S(2)}) copy-start(bf16[128,768]{1,0:T(8,128)(2,1)S(1)} %get-tuple-element.50) | copy-start | bytes 589828
  89.2 1.1 copy-start.8
  89.4 0.9 copy-start.10
  89.6 0.8 copy-start.14
  89.6 1.3 copy-start.1
  90.5 2.6 copy-start.12
  93.1 5.0 %copy-start.20 = (bf16[128,768]{1,0:T(8,128)(2,1)}, bf16[128,768]{1,0:T(8,128)(2,1)S(1)}, u32[]{:S(2)}) copy-start(bf16[128,768]{1,0:T(8,128)(2,1)S(1)} %get-tuple-element.48) | copy-start | bytes 589828
  93.2 5.0 %copy-start.6 = (bf16[128,768]{1,0:T(8,128)(2,1)S(1)}, bf16[128,768]{1,0:T(8,128)(2,1)}, u32[]{:S(2)}) copy-start(bf16[128,768]{1,0:T(8,128)(2,1)} %param.17) | copy-start | bytes 589828
  93.2 10.0 %slice-start = ((s8[4718592]{0:T(1024)(128)(4,1)}), s8[4194304]{0:T(1024)(128)(4,1)S(1)}, s32[]{:S(2)}) async-start(s8[4718592]{0:T(1024)(128)(4,1)} %bitcast.80), calls=%async_computation | async-start | bytes 8388608
  98.1 5.0 %slice-start.1 = ((s8[4718592]{0:T(1024)(128)(4,1)}), s8[524288]{0:T(1024)(128)(4,1)S(1)}, s32[]{:S(2)}) async-start(s8[4718592]{0:T(1024)(128)(4,1)} %bitcast.80), calls=%async_computation.1 | async-start | bytes 1048576
  108.2 3.8 %copy-start.15 = (bf16[128,768]{0,1:T(8,128)(2,1)S(1)}, bf16[128,768]{0,1:T(8,128)(2,1)}, u32[]{:S(2)}) copy-start(bf16[128,768]{0,1:T(8,128)(2,1)} %copy-done.14) | copy-start | bytes 589828
  112.0 1.5 copy-start.11
  113.3 0.9 copy-start.9
  113.5 1.0 copy-start.19
  115.0 3.9 %copy-start.7 = (bf16[128,768]{1,0:T(8,128)(2,1)S(1)}, bf16[128,768]{1,0:T(8,128)(2,1)}, u32[]{:S(2)}) copy-start(bf16[128,768]{1,0:T(8,128)(2,1)} %param.17) | copy-start | bytes 589828
  115.7 4.3 %copy-start.29 = (f32[3072]{0:T(1024)S(1)}, f32[3072]{0:T(1024)}, u32[]{:S(2)}) copy-start(f32[3072]{0:T(1024)} %get-tuple-element.87) | copy-start | bytes 36868
  115.7 4.3 %copy-start.25 = (f32[768]{0:T(1024)S(1)}, f32[768]{0:T(1024)}, u32[]{:S(2)}) copy-start(f32[768]{0:T(1024)} %get-tuple-element.34) | copy-start | bytes 9220
  115.7 4.4 %copy-start.27 = (f32[768]{0:T(1024)S(1)}, f32[768]{0:T(1024)}, u32[]{:S(2)}) copy-start(f32[768]{0:T(1024)} %get-tuple-element.42) | copy-start | bytes 9220
  115.7 4.4 %copy-start.26 = (f32[768]{0:T(1024)S(1)}, f32[768]{0:T(1024)}, u32[]{:S(2)}) copy-start(f32[768]{0:T(1024)} %get-tuple-element.61) | copy-start | bytes 9220
  115.7 4.5 %copy-start.24 = (f32[768]{0:T(1024)S(1)}, f32[768]{0:T(1024)}, u32[]{:S(2)}) copy-start(f32[768]{0:T(1024)} %get-tuple-element.40) | copy-start | bytes 9220
  115.7 4.6 %copy-start.31 = (f32[128]{0:T(128)S(1)}, f32[128]{0:T(128)}, u32[]{:S(2)}) copy-start(f32[128]{0:T(128)} %copy-done.30) | copy-start | bytes 1540
  115.7 4.6 %copy-start.34 = (f32[128]{0:T(128)S(1)}, f32[128]{0:T(128)}, u32[]{:S(2)}) copy-start(f32[128]{0:T(128)} %copy-done.33) | copy-start | bytes 1540
  119.5 12.7 %collective-permute-start = (bf16[128,12288]{1,0:T(8,128)(2,1)}, bf16[128,12288]{1,0:T(8,128)(2,1)}, u32[]{:S(2)}, u32[]{:S(2)}) collective-permute-start(bf16[128,12288]{1,0:T(8,128)(2,1)} %constant_dynamic-update-slice_fusion), channel_id=1, source_target_pairs={{0,8},{8,0},{16,24},{24,16},{1,9},{9,1},{17,25},{25,17},{2,10},{10... | collective-permute-start | bytes 9437192 | tf_op jit(solution)/shard_map/ppermute | solution.py:572
  120.3 5.3 %copy-start.28 = (f32[8,96]{1,0:T(8,128)S(1)}, f32[8,96]{1,0:T(8,128)}, u32[]{:S(2)}) copy-start(f32[8,96]{1,0:T(8,128)} %get-tuple-element.62) | copy-start | bytes 9220
  120.3 5.4 %copy-start.2 = (bf16[128,3072]{1,0:T(8,128)(2,1)S(1)}, bf16[128,3072]{1,0:T(8,128)(2,1)}, u32[]{:S(2)}) copy-start(bf16[128,3072]{1,0:T(8,128)(2,1)} %get-tuple-element.46) | copy-start | bytes 2359300
  125.6 5.2 %collective-permute-start.1 = (f32[8,1152]{1,0:T(8,128)}, f32[8,1152]{1,0:T(8,128)}, u32[]{:S(2)}, u32[]{:S(2)}) collective-permute-start(f32[8,1152]{1,0:T(8,128)} %concatenate.64), channel_id=1, source_target_pairs={{0,8},{8,0},{16,24},{24,16},{1,9},{9,1},{17,25},{25,17},{2,10},{10... | collective-permute-start | bytes 110600 | tf_op jit(solution)/shard_map/ppermute | solution.py:572
  125.7 4.1 %copy-start.16 = (f32[128,768]{1,0:T(8,128)S(1)}, f32[128,768]{1,0:T(8,128)}, u32[]{:S(2)}) copy-start(f32[128,768]{1,0:T(8,128)} %get-tuple-element.44) | copy-start | bytes 1179652
  125.7 4.1 %copy-start.22 = (f32[128,768]{1,0:T(8,128)S(1)}, f32[128,768]{1,0:T(8,128)}, u32[]{:S(2)}) copy-start(f32[128,768]{1,0:T(8,128)} %get-tuple-element.86) | copy-start | bytes 1179652
  125.7 4.1 %copy-start.32 = (f32[128]{0:T(128)S(1)}, f32[128]{0:T(128)}, u32[]{:S(2)}) copy-start(f32[128]{0:T(128)} %copy-done.30) | copy-start | bytes 1540
  125.8 4.1 %copy-start.35 = (f32[128]{0:T(128)S(1)}, f32[128]{0:T(128)}, u32[]{:S(2)}) copy-start(f32[128]{0:T(128)} %copy-done.33) | copy-start | bytes 1540
  137.2 2.9 %copy-start.21 = (bf16[128,768]{1,0:T(8,128)(2,1)S(1)}, bf16[128,768]{1,0:T(8,128)(2,1)}, u32[]{:S(2)}) copy-start(bf16[128,768]{1,0:T(8,128)(2,1)} %copy-done.20) | copy-start | bytes 589828
  138.5 2.5 copy-start.13
  140.1 1.9 copy-start.5
  141.1 1.9 copy-start.3
  258.2 6.2 %copy-start.23 = (f32[96,768]{1,0:T(8,128)S(1)}, f32[96,768]{1,0:T(8,128)}, u32[]{:S(2)}) copy-start(f32[96,768]{1,0:T(8,128)} %get-tuple-element.31) | copy-start | bytes 884740
  258.2 6.9 %copy-start.18 = (f32[96,3072]{1,0:T(8,128)S(1)}, f32[96,3072]{1,0:T(8,128)}, u32[]{:S(2)}) copy-start(f32[96,3072]{1,0:T(8,128)} %get-tuple-element.32) | copy-start | bytes 3538948
  264.3 1.7 copy-start.17

commit v10 on v9

--- a/solution.py
+++ b/solution.py
@@ -178,6 +178,10 @@
 
 
 FIRST_CORE_HALF = (0, 3)
+
+
+CHAIN_RANK = (2, 3, 0, 1, 4)
+CHAIN_LAG = 2
 
 
 X_ONLY = (2, 3)
@@ -499,14 +503,16 @@
         add_into(out[w], [own[w], xland[w]])
         back_copy(w).start()
 
-    slots = steps + count - 1
+    rank = [CHAIN_RANK[w] if w < len(CHAIN_RANK) else w for w in range(count)]
+    slots = steps + CHAIN_LAG * (count - 1)
+    by_rank = sorted(range(count), key=lambda w: rank[w])
     for t in range(slots + 1):
-        for w in range(count):
-            k = t - w + 1
+        for w in by_rank:
+            k = t - CHAIN_LAG * rank[w] + 1
             if 1 <= k <= steps:
                 guarded(carried(k, w), lambda k=k, w=w: step(k, w))
-        for w in range(count):
-            if steps + w == t:
+        for w in by_rank:
+            if steps + CHAIN_LAG * rank[w] == t:
                 arrive(w)
     for w in range(count):
         pl.when(owner(w))(lambda w=w: total(w))

time: 268 us -> 263 us (0.981)
  Pallas kernels: 190 us -> 183 us
    pallas_call x1, Pallas kernels: 113 us -> 107 us  [reduce_gradients(): pl.pallas_call(functools.partial(reduce_kernel, n, count, mm), out_shape=...]
where the time goes in v10:
time: 263 us; the launch traced here: 260 us
  Pallas kernels  183 us (70%)
  local copies, waits for them, and re-layouts  34.2 us (13%)
  matrix products  29.3 us (11%)
  other arithmetic  12.3 us (5%)
    pallas_call x1, Pallas kernels, reduce_gradients(): pl.pallas_call(functools.partial(reduce_kernel, n, count, mm), out_shape=...  107 us
    pallas_call x1, Pallas kernels, gather_weights(): pl.pallas_call(functools.partial(gather_kernel, n, count), out_shape=[jax...  76 us
    unnamed x89, local copies, waits for them, and re-layouts  11.1 us
  transfers between devices with their start and end apart: 2, of which 0 were waited for; matrix products, arithmetic and copies ran while one was open for 5% of the time, Pallas kernels for 0%

profile of v10, /device:TPU:0, one launch (start us, length us, event | category | flops | bytes accessed | tf_op | source)
XLA Modules:
  0.0 260.3 jit_solution(513575016665983231)
XLA Ops:
  0.7 0.7 reduce
  1.4 0.7 reduce.1
  2.1 4.1 %concatenate.49 = bf16[1152]{0:T(1024)(128)(2,1)S(1)} concatenate(bf16[96]{0:T(256)(128)(2,1)} %bitcast.114, bf16[96]{0:T(256)(128)(2,1)} %bitcast.115, bf16[192]{0:T(256)(128)(2,1)S(1)} %reduce, bf16[96]{0:T(256)(128)(2,1)} %bitcast.116, bf16[96]{0:T(256)(128)(2,1)} %bitcast.117, bf16[96]{0:T(256)(128)(2,1)} %bitcast.118, bf16[384]{0:T(512)(128)(2,1)S(1)} %reduce.1, ...), dimensions={0} | concatenate | bytes 4608 | tf_op jit(solution)/shard_map/concatenate | solution.py:634
  6.8 76.0 %shard_map.254 = (bf16[8,96,2304]{2,1,0:T(8,128)(2,1)}, bf16[8,96,768]{2,1,0:T(8,128)(2,1)}, bf16[8,96,3072]{2,1,0:T(8,128)(2,1)}, bf16[8,384,768]{2,1,0:T(8,128)(2,1)}, bf16[8,1,1152]{2,1,0:T(2,128)(2,1)}) custom-call(bf16[96,2304]{1,0:T(8,128)(2,1)} %bitcast.108, bf16[96,768]{1,0:T(8,128)(2,1)} %bitcast.110, bf16[96,3072]{1,0:T(8,128)(2,1)} %bitcast.106, ...), custom_call_target="tpu_custom_call" | custom-call | tf_op jit(solution)/shard_map/pallas_call | solution.py:329
  82.8 0.8 copy.76
  83.7 0.7 slice_convert_fusion.2
  85.4 0.9 constant_dynamic-update-slice_fusion.9
  86.3 2.7 %fusion = bf16[128,2304]{1,0:T(8,128)(2,1)S(1)} fusion(bf16[128,768]{1,0:T(8,128)(2,1)S(1)} %get-tuple-element.50, bf16[768,2304]{1,0:T(8,128)(2,1)} %bitcast.87, f32[2304]{0:T(1024)S(1)} %pad_maximum_fusion.6), kind=kOutput, calls=%fused_computation.3 | convolution fusion | flops 453574656 | bytes 4334592 | tf_op jit(solution)/shard_map/dot_general | solution.py:47
  91.6 0.7 constant_dynamic-update-slice_fusion.8
  92.3 0.8 constant_dynamic-update-slice_fusion.7
  93.2 5.0 %constant_dynamic-update-slice_fusion.6 = (bf16[128,12288]{1,0:T(8,128)(2,1)}, bf16[128,3072]{1,0:T(8,128)(2,1)}, f32[128,3072]{1,0:T(8,128)S(1)}) fusion(bf16[128,12288]{1,0:T(8,128)(2,1)} %get-tuple-element.47, f32[3072]{0:T(1024)S(1)} %reshape.307, bf16[128,768]{1,0:T(8,128)(2,1)S(1)} %get-tuple-element.48, bf16[768,3072]{1,0:T(8,128)(2,1)} %bitcast.79), kind=kOutput, calls=%fused_computation.79 | convolution fusion | flops 607911936 | bytes 8073216 | tf_op jit(solution)/shard_map/dot_general | solution.py:69
  98.1 5.0 %convert_reduce_fusion = (f32[3072]{0:T(1024)}, bf16[128,3072]{1,0:T(8,128)(2,1)S(1)}) fusion(f32[128,3072]{1,0:T(8,128)S(1)} %get-tuple-element.82, bf16[3072,768]{1,0:T(8,128)(2,1)} %bitcast.85, bf16[128,768]{1,0:T(8,128)(2,1)S(1)} %copy-done.6), kind=kOutput, calls=%fused_computation.15 | convolution fusion | flops 612627456 | bytes 7286784 | tf_op jit(solution)/shard_map/td,fd->tf/dot_general | solution.py:100
  103.2 2.3 multiply_reduce_fusion.1
  105.5 1.5 convert_reduce_fusion.4
  107.0 1.2 convolution_convert_fusion.1
  108.2 1.8 copy.53
  110.0 2.0 convolution_convert_fusion
  112.0 1.3 multiply_reduce_fusion
  115.0 0.7 constant_dynamic-update-slice_fusion.5
  115.7 0.7 constant_dynamic-update-slice_fusion.4
  116.4 0.7 constant_dynamic-update-slice_fusion.3
  117.1 0.7 constant_dynamic-update-slice_fusion.2
  117.8 1.0 constant_dynamic-update-slice_fusion.1
  118.8 0.7 constant_dynamic-update-slice_fusion
  120.3 4.1 %fusion.27 = (f32[768]{0:T(1024)S(1)}, f32[128]{0:T(128)S(1)}, f32[128]{0:T(128)S(1)}, f32[768]{0:T(1024)S(1)}, f32[128,768]{1,0:T(8,128)}) fusion(bf16[128,768]{1,0:T(8,128)(2,1)S(1)} %copy-done, f32[128]{0:T(128)S(1)} %copy-done.34, f32[128]{0:T(128)S(1)} %copy-done.31, f32[768]{0:T(1024)S(1)} %reshape.302, bf16[768,2304]{1,0:T(8,128)(2,1)} %bitcast.88, ...), kind=kOutput, calls=%fused_computation.55 | convolution fusion | flops 455735552 | bytes 4729856 | tf_op jit(solution)/shard_map/te,ce->tc/dot_general | solution.py:138
  124.9 0.7 concatenate.64
  125.8 4.1 %fusion.11 = bf16[128,768]{1,0:T(8,128)(2,1)} fusion(f32[128,768]{1,0:T(8,128)S(1)} %get-tuple-element.81, bf16[128,3072]{1,0:T(8,128)(2,1)S(1)} %copy-done.2, bf16[3072,768]{1,0:T(8,128)(2,1)} %bitcast.86, f32[768]{0:T(1024)S(1)} %reshape.308), kind=kOutput, calls=%fused_computation.27 | convolution fusion | flops 604274688 | bytes 6097920 | tf_op jit(solution)/shard_map/dot_general | solution.py:72
  129.9 0.9 fusion.26
  130.8 0.8 add.120
  132.2 1.1 slice.163
  133.3 1.1 pad_maximum_fusion.1.refs_4_
  134.4 1.5 fusion.36
  135.9 1.3 pad_maximum_fusion.refs_6_
  137.2 1.4 fusion.35
  138.6 0.8 pad_maximum_fusion.4.refs_7_
  139.3 0.8 pad_maximum_fusion.3.refs_5_
  140.1 0.9 copy.67
  141.1 0.9 copy.66
  142.1 0.9 copy.64
  143.1 1.6 copy.73
  144.7 106.7 %shard_map.255 = (f32[96,2304]{1,0:T(8,128)}, f32[96,768]{1,0:T(8,128)}, f32[96,3072]{1,0:T(8,128)}, f32[384,768]{1,0:T(8,128)}, f32[1,1152]{1,0:T(1,128)}) custom-call(bf16[8,96,256]{2,1,0:T(8,128)(2,1)} %bitcast.99, bf16[8,96,256]{2,1,0:T(8,128)(2,1)} %bitcast.98, bf16[8,96,256]{2,1,0:T(8,128)(2,1)} %bitcast.97, bf16[8,384,256]{2,1,0:T(8,128)(2,1)} %bitcast.78, ...), custom_call_target="tpu_custom_call" | custom-call | tf_op jit(solution)/shard_map/pallas_call | solution.py:546
  251.4 1.4 slice.140
  252.7 1.3 slice.144
  254.0 1.4 fusion.40
  255.4 2.1 copy.90
  257.5 0.7 copy.91
  258.3 1.0 copy.92
  259.3 1.0 copy.93
  (142 shorter events, 8.0 us)
Async XLA Ops:
  0.6 83.8 %copy-start = (bf16[128,768]{1,0:T(8,128)(2,1)S(1)}, bf16[128,768]{1,0:T(8,128)(2,1)}, u32[]{:S(2)}) copy-start(bf16[128,768]{1,0:T(8,128)(2,1)} %param.15) | copy-start | bytes 589828
  0.7 84.1 %copy-start.36 = (s32[128]{0:T(128)S(1)}, s32[128]{0:T(128)}, u32[]{:S(2)}) copy-start(s32[128]{0:T(128)} %param.16) | copy-start | bytes 1540
  84.5 4.5 %copy-start.30 = (f32[128]{0:T(128)}, f32[128]{0:T(128)S(1)}, u32[]{:S(2)}) copy-start(f32[128]{0:T(128)S(1)} %broadcast_multiply_fusion.5) | copy-start | bytes 1540
  84.8 4.3 %copy-start.33 = (f32[128]{0:T(128)}, f32[128]{0:T(128)S(1)}, u32[]{:S(2)}) copy-start(f32[128]{0:T(128)S(1)} %add_rsqrt_fusion.1) | copy-start | bytes 1540
  86.3 2.8 %copy-start.4 = (bf16[128,768]{1,0:T(8,128)(2,1)}, bf16[128,768]{1,0:T(8,128)(2,1)S(1)}, u32[]{:S(2)}) copy-start(bf16[128,768]{1,0:T(8,128)(2,1)S(1)} %get-tuple-element.50) | copy-start | bytes 589828
  89.2 1.1 copy-start.8
  89.4 0.9 copy-start.10
  89.6 0.8 copy-start.14
  89.6 1.3 copy-start.1
  90.5 2.6 %copy-start.12 = (bf16[128,768]{1,0:T(8,128)(2,1)}, bf16[128,768]{1,0:T(8,128)(2,1)S(1)}, u32[]{:S(2)}) copy-start(bf16[128,768]{1,0:T(8,128)(2,1)S(1)} %copy.60) | copy-start | bytes 589828
  93.1 5.0 %copy-start.20 = (bf16[128,768]{1,0:T(8,128)(2,1)}, bf16[128,768]{1,0:T(8,128)(2,1)S(1)}, u32[]{:S(2)}) copy-start(bf16[128,768]{1,0:T(8,128)(2,1)S(1)} %get-tuple-element.48) | copy-start | bytes 589828
  93.2 5.0 %copy-start.6 = (bf16[128,768]{1,0:T(8,128)(2,1)S(1)}, bf16[128,768]{1,0:T(8,128)(2,1)}, u32[]{:S(2)}) copy-start(bf16[128,768]{1,0:T(8,128)(2,1)} %param.17) | copy-start | bytes 589828
  93.2 10.0 %slice-start = ((s8[4718592]{0:T(1024)(128)(4,1)}), s8[4194304]{0:T(1024)(128)(4,1)S(1)}, s32[]{:S(2)}) async-start(s8[4718592]{0:T(1024)(128)(4,1)} %bitcast.80), calls=%async_computation | async-start | bytes 8388608
  98.1 5.0 %slice-start.1 = ((s8[4718592]{0:T(1024)(128)(4,1)}), s8[524288]{0:T(1024)(128)(4,1)S(1)}, s32[]{:S(2)}) async-start(s8[4718592]{0:T(1024)(128)(4,1)} %bitcast.80), calls=%async_computation.1 | async-start | bytes 1048576
  108.2 3.8 %copy-start.15 = (bf16[128,768]{0,1:T(8,128)(2,1)S(1)}, bf16[128,768]{0,1:T(8,128)(2,1)}, u32[]{:S(2)}) copy-start(bf16[128,768]{0,1:T(8,128)(2,1)} %copy-done.14) | copy-start | bytes 589828
  112.0 1.5 copy-start.11
  113.3 0.9 copy-start.9
  113.5 1.0 copy-start.19
  115.0 3.9 %copy-start.7 = (bf16[128,768]{1,0:T(8,128)(2,1)S(1)}, bf16[128,768]{1,0:T(8,128)(2,1)}, u32[]{:S(2)}) copy-start(bf16[128,768]{1,0:T(8,128)(2,1)} %param.17) | copy-start | bytes 589828
  115.7 4.3 %copy-start.29 = (f32[3072]{0:T(1024)S(1)}, f32[3072]{0:T(1024)}, u32[]{:S(2)}) copy-start(f32[3072]{0:T(1024)} %get-tuple-element.87) | copy-start | bytes 36868
  115.7 4.3 %copy-start.25 = (f32[768]{0:T(1024)S(1)}, f32[768]{0:T(1024)}, u32[]{:S(2)}) copy-start(f32[768]{0:T(1024)} %get-tuple-element.34) | copy-start | bytes 9220
  115.7 4.4 %copy-start.27 = (f32[768]{0:T(1024)S(1)}, f32[768]{0:T(1024)}, u32[]{:S(2)}) copy-start(f32[768]{0:T(1024)} %get-tuple-element.42) | copy-start | bytes 9220
  115.7 4.4 %copy-start.26 = (f32[768]{0:T(1024)S(1)}, f32[768]{0:T(1024)}, u32[]{:S(2)}) copy-start(f32[768]{0:T(1024)} %get-tuple-element.61) | copy-start | bytes 9220
  115.7 4.5 %copy-start.24 = (f32[768]{0:T(1024)S(1)}, f32[768]{0:T(1024)}, u32[]{:S(2)}) copy-start(f32[768]{0:T(1024)} %get-tuple-element.40) | copy-start | bytes 9220
  115.7 4.6 %copy-start.31 = (f32[128]{0:T(128)S(1)}, f32[128]{0:T(128)}, u32[]{:S(2)}) copy-start(f32[128]{0:T(128)} %copy-done.30) | copy-start | bytes 1540
  115.7 4.6 %copy-start.34 = (f32[128]{0:T(128)S(1)}, f32[128]{0:T(128)}, u32[]{:S(2)}) copy-start(f32[128]{0:T(128)} %copy-done.33) | copy-start | bytes 1540
  119.5 12.7 %collective-permute-start = (bf16[128,12288]{1,0:T(8,128)(2,1)}, bf16[128,12288]{1,0:T(8,128)(2,1)}, u32[]{:S(2)}, u32[]{:S(2)}) collective-permute-start(bf16[128,12288]{1,0:T(8,128)(2,1)} %constant_dynamic-update-slice_fusion), channel_id=1, source_target_pairs={{0,8},{8,0},{16,24},{24,16},{1,9},{9,1},{17,25},{25,17},{2,10},{10... | collective-permute-start | bytes 9437192 | tf_op jit(solution)/shard_map/ppermute | solution.py:578
  120.3 5.3 %copy-start.28 = (f32[8,96]{1,0:T(8,128)S(1)}, f32[8,96]{1,0:T(8,128)}, u32[]{:S(2)}) copy-start(f32[8,96]{1,0:T(8,128)} %get-tuple-element.62) | copy-start | bytes 9220
  120.3 5.4 %copy-start.2 = (bf16[128,3072]{1,0:T(8,128)(2,1)S(1)}, bf16[128,3072]{1,0:T(8,128)(2,1)}, u32[]{:S(2)}) copy-start(bf16[128,3072]{1,0:T(8,128)(2,1)} %get-tuple-element.46) | copy-start | bytes 2359300
  125.6 5.2 %collective-permute-start.1 = (f32[8,1152]{1,0:T(8,128)}, f32[8,1152]{1,0:T(8,128)}, u32[]{:S(2)}, u32[]{:S(2)}) collective-permute-start(f32[8,1152]{1,0:T(8,128)} %concatenate.64), channel_id=1, source_target_pairs={{0,8},{8,0},{16,24},{24,16},{1,9},{9,1},{17,25},{25,17},{2,10},{10... | collective-permute-start | bytes 110600 | tf_op jit(solution)/shard_map/ppermute | solution.py:578
  125.7 4.1 %copy-start.16 = (f32[128,768]{1,0:T(8,128)S(1)}, f32[128,768]{1,0:T(8,128)}, u32[]{:S(2)}) copy-start(f32[128,768]{1,0:T(8,128)} %get-tuple-element.44) | copy-start | bytes 1179652
  125.7 4.1 %copy-start.22 = (f32[128,768]{1,0:T(8,128)S(1)}, f32[128,768]{1,0:T(8,128)}, u32[]{:S(2)}) copy-start(f32[128,768]{1,0:T(8,128)} %get-tuple-element.86) | copy-start | bytes 1179652
  125.7 4.1 %copy-start.32 = (f32[128]{0:T(128)S(1)}, f32[128]{0:T(128)}, u32[]{:S(2)}) copy-start(f32[128]{0:T(128)} %copy-done.30) | copy-start | bytes 1540
  125.8 4.1 %copy-start.35 = (f32[128]{0:T(128)S(1)}, f32[128]{0:T(128)}, u32[]{:S(2)}) copy-start(f32[128]{0:T(128)} %copy-done.33) | copy-start | bytes 1540
  137.2 2.9 %copy-start.21 = (bf16[128,768]{1,0:T(8,128)(2,1)S(1)}, bf16[128,768]{1,0:T(8,128)(2,1)}, u32[]{:S(2)}) copy-start(bf16[128,768]{1,0:T(8,128)(2,1)} %copy-done.20) | copy-start | bytes 589828
  138.5 2.5 copy-start.13
  140.1 1.9 copy-start.5
  141.1 1.9 copy-start.3
  251.4 6.2 %copy-start.23 = (f32[96,768]{1,0:T(8,128)S(1)}, f32[96,768]{1,0:T(8,128)}, u32[]{:S(2)}) copy-start(f32[96,768]{1,0:T(8,128)} %get-tuple-element.31) | copy-start | bytes 884740
  251.4 6.9 %copy-start.18 = (f32[96,3072]{1,0:T(8,128)S(1)}, f32[96,3072]{1,0:T(8,128)}, u32[]{:S(2)}) copy-start(f32[96,3072]{1,0:T(8,128)} %get-tuple-element.32) | copy-start | bytes 3538948
  257.5 1.7 copy-start.17

commit v11 on v10

--- a/solution.py
+++ b/solution.py
@@ -363,13 +363,14 @@
     contrib = (None,) * mm + refs[2 * mm : mm + count]
     refs = refs[mm + count :]
     out = refs[:count]
-    land, send, other, own, xland, stage = (refs[count + i * count : count + (i + 1) * count] for i in range(6))
+    land, send, other, own, xland, stage, xsend = (refs[count + i * count : count + (i + 1) * count] for i in range(7))
     (load_sem, own_sem, ring_send, ring_recv, pair_send, pair_recv, x_send, x_recv, back_send, back_recv) = refs[
-        7 * count :
+        8 * count :
     ]
     rep = lax.axis_index("rep")
     shard = lax.axis_index("shard")
     core = rep % 2
+    plane = rep // 2
     step_dir = 1 - 2 * core
     partner = (rep + step_dir, shard)
     x_partner = ((rep + 2) % 4, shard)
@@ -411,7 +412,7 @@
         return remote(land[w].at[steps - 1], other[w], pair_send.at[w], pair_recv.at[w], partner)
 
     def x_copy(w):
-        return remote(own[w], xland[w], x_send.at[w], x_recv.at[w], x_partner)
+        return remote(xsend[w], xland[w], x_send.at[w], x_recv.at[w], x_partner)
 
     def back_copy(w):
         return remote(out[w], out[w], back_send.at[w], back_recv.at[w], partner)
@@ -494,13 +495,21 @@
             def _():
                 add_into(own[w], [own[w], other[w], mine])
 
+            add_into(xsend[w], [own[w]])
             x_copy(w).start()
 
         pl.when(owner(w))(plane)
 
     def total(w):
         x_copy(w).wait_recv()
-        add_into(out[w], [own[w], xland[w]])
+
+        @pl.when(plane == 0)
+        def _():
+            add_into(out[w], [xsend[w], xland[w]])
+
+        @pl.when(plane == 1)
+        def _():
+            add_into(out[w], [xland[w], xsend[w]])
         back_copy(w).start()
 
     rank = [CHAIN_RANK[w] if w < len(CHAIN_RANK) else w for w in range(count)]
@@ -553,8 +562,9 @@
         + [vmem((steps,) + b, t) for b, t in zip(blocks, ring_types)]
         + [vmem(b, t) for b, t in zip(blocks, ring_types)]
         + [vmem(b) for b in blocks]
+        + [vmem(b, t) for b, t in zip(blocks, ring_types)]
         + [vmem(b) for b in blocks]
-        + [vmem(b) for b in blocks]
+        + [vmem(b, t) for b, t in zip(blocks, ring_types)]
         + [
             dma((steps, count)),
             dma((count,)),
@@ -622,8 +632,7 @@
     layer_index = 0
     shard = lax.axis_size("shard")
     small_local = (ln1_gain, ln1_bias, qv_bias, out_bias, ln2_gain, ln2_bias, fc_bias, proj_bias)
-    small_local = [v[layer_index] for v in small_local]
-    widths = [v.shape[0] for v in small_local]
+    widths = [v.shape[1] for v in small_local]
     local_weights = (
         qkv_weight[layer_index],
         out_weight[layer_index],
@@ -631,7 +640,7 @@
         proj_weight[layer_index],
     )
     rows_local = local_weights[0].shape[0]
-    small_row = jnp.concatenate(small_local).reshape(1, -1)
+    small_row = jnp.concatenate(small_local, axis=1)
     fulls = gather_weights(list(local_weights) + [small_row], shard)
     weights = tuple(f.reshape(-1, f.shape[-1]) for f in fulls[:4])
     halves = [take_half(w, core, 1) for w in local_weights]

time: 263 us -> 253 us (0.962)
  local copies, waits for them, and re-layouts: 34.2 us -> 30.5 us
  Pallas kernels: 183 us -> 180 us
    unnamed x89 -> x87, local copies, waits for them, and re-layouts: 11.1 us -> 11.1 us
  transfers between devices with their start and end apart: 2 -> 2, of which waited for: 0 -> 0; matrix products, arithmetic and copies ran while one was open for 5% -> 4% of each run, Pallas kernels for 0% -> 0%
where the time goes in v11:
time: 253 us; the launch traced here: 252 us
  Pallas kernels  180 us (71%)
  local copies, waits for them, and re-layouts  30.5 us (12%)
  matrix products  29.3 us (12%)
  other arithmetic  10.1 us (4%)
    pallas_call x1, Pallas kernels, reduce_gradients(): pl.pallas_call(functools.partial(reduce_kernel, n, count, mm), out_shape=...  104 us
    pallas_call x1, Pallas kernels, gather_weights(): pl.pallas_call(functools.partial(gather_kernel, n, count), out_shape=[jax...  76 us
    unnamed x87, local copies, waits for them, and re-layouts  11.1 us
  transfers between devices with their start and end apart: 2, of which 0 were waited for; matrix products, arithmetic and copies ran while one was open for 4% of the time, Pallas kernels for 0%

profile of v11, /device:TPU:0, one launch (start us, length us, event | category | flops | bytes accessed | tf_op | source)
XLA Modules:
  0.0 251.9 jit_solution(13800673718566232851)
XLA Ops:
  0.7 1.5 concatenate.49.refs_4_
  2.2 76.0 %shard_map.254 = (bf16[8,96,2304]{2,1,0:T(8,128)(2,1)}, bf16[8,96,768]{2,1,0:T(8,128)(2,1)}, bf16[8,96,3072]{2,1,0:T(8,128)(2,1)}, bf16[8,384,768]{2,1,0:T(8,128)(2,1)}, bf16[8,1,1152]{2,1,0:T(2,128)(2,1)}) custom-call(bf16[96,2304]{1,0:T(8,128)(2,1)} %bitcast.102, bf16[96,768]{1,0:T(8,128)(2,1)} %bitcast.104, bf16[96,3072]{1,0:T(8,128)(2,1)} %bitcast.100, ...), custom_call_target="tpu_custom_call" | custom-call | tf_op jit(solution)/shard_map/pallas_call | solution.py:329
  78.2 0.8 copy.76
  79.1 0.7 slice_convert_fusion.2
  80.8 0.9 constant_dynamic-update-slice_fusion.9
  81.7 2.7 %fusion = bf16[128,2304]{1,0:T(8,128)(2,1)S(1)} fusion(bf16[128,768]{1,0:T(8,128)(2,1)S(1)} %get-tuple-element.50, bf16[768,2304]{1,0:T(8,128)(2,1)} %bitcast.81, f32[2304]{0:T(1024)S(1)} %pad_maximum_fusion.6), kind=kOutput, calls=%fused_computation.3 | convolution fusion | flops 453574656 | bytes 4334592 | tf_op jit(solution)/shard_map/dot_general | solution.py:47
  85.9 0.4 copy-done.1
  86.3 0.4 fusion.42
  87.0 0.7 constant_dynamic-update-slice_fusion.8
  87.7 0.8 constant_dynamic-update-slice_fusion.7
  88.6 4.9 %constant_dynamic-update-slice_fusion.6 = (bf16[128,12288]{1,0:T(8,128)(2,1)}, bf16[128,3072]{1,0:T(8,128)(2,1)}, f32[128,3072]{1,0:T(8,128)S(1)}) fusion(bf16[128,12288]{1,0:T(8,128)(2,1)} %get-tuple-element.47, f32[3072]{0:T(1024)S(1)} %reshape.303, bf16[128,768]{1,0:T(8,128)(2,1)S(1)} %get-tuple-element.48, bf16[768,3072]{1,0:T(8,128)(2,1)} %bitcast.73), kind=kOutput, calls=%fused_computation.79 | convolution fusion | flops 607911936 | bytes 8073216 | tf_op jit(solution)/shard_map/dot_general | solution.py:69
  93.5 5.0 %convert_reduce_fusion = (f32[3072]{0:T(1024)}, bf16[128,3072]{1,0:T(8,128)(2,1)S(1)}) fusion(f32[128,3072]{1,0:T(8,128)S(1)} %get-tuple-element.82, bf16[3072,768]{1,0:T(8,128)(2,1)} %bitcast.79, bf16[128,768]{1,0:T(8,128)(2,1)S(1)} %copy-done.6), kind=kOutput, calls=%fused_computation.15 | convolution fusion | flops 612627456 | bytes 7286784 | tf_op jit(solution)/shard_map/td,fd->tf/dot_general | solution.py:100
  98.6 2.3 multiply_reduce_fusion.1
  100.9 1.5 convert_reduce_fusion.4
  102.4 1.2 convolution_convert_fusion.1
  103.6 1.8 copy.53
  105.4 2.0 convolution_convert_fusion
  107.4 1.3 multiply_reduce_fusion
  110.4 0.7 constant_dynamic-update-slice_fusion.5
  111.1 0.7 constant_dynamic-update-slice_fusion.4
  111.8 0.7 constant_dynamic-update-slice_fusion.3
  112.5 0.7 constant_dynamic-update-slice_fusion.2
  113.3 1.0 constant_dynamic-update-slice_fusion.1
  114.2 0.7 constant_dynamic-update-slice_fusion
  115.0 0.4 collective-permute-start
  115.7 4.1 %fusion.27 = (f32[768]{0:T(1024)S(1)}, f32[128]{0:T(128)S(1)}, f32[128]{0:T(128)S(1)}, f32[768]{0:T(1024)S(1)}, f32[128,768]{1,0:T(8,128)}) fusion(bf16[128,768]{1,0:T(8,128)(2,1)S(1)} %copy-done, f32[128]{0:T(128)S(1)} %copy-done.34, f32[128]{0:T(128)S(1)} %copy-done.32, f32[768]{0:T(1024)S(1)} %reshape.298, bf16[768,2304]{1,0:T(8,128)(2,1)} %bitcast.82, ...), kind=kOutput, calls=%fused_computation.55 | convolution fusion | flops 455735552 | bytes 4729856 | tf_op jit(solution)/shard_map/te,ce->tc/dot_general | solution.py:138
  120.6 4.1 %fusion.11 = bf16[128,768]{1,0:T(8,128)(2,1)} fusion(f32[128,768]{1,0:T(8,128)S(1)} %get-tuple-element.81, bf16[128,3072]{1,0:T(8,128)(2,1)S(1)} %copy-done.2, bf16[3072,768]{1,0:T(8,128)(2,1)} %bitcast.80, f32[768]{0:T(1024)S(1)} %reshape.304), kind=kOutput, calls=%fused_computation.27 | convolution fusion | flops 604274688 | bytes 6097920 | tf_op jit(solution)/shard_map/dot_general | solution.py:72
  124.7 0.9 fusion.26
  125.7 0.6 reshape.297.refs_8_
  126.3 1.1 slice.163
  127.4 1.1 pad_maximum_fusion.1.refs_4_
  128.5 1.5 fusion.36
  130.0 1.3 pad_maximum_fusion.refs_6_
  131.2 1.4 fusion.35
  132.6 0.8 pad_maximum_fusion.4.refs_7_
  133.4 0.8 pad_maximum_fusion.3.refs_5_
  134.3 0.9 copy.67
  135.2 0.9 copy.66
  136.2 0.9 copy.64
  137.2 1.6 copy.73
  138.8 104.2 %shard_map.255 = (f32[96,2304]{1,0:T(8,128)}, f32[96,768]{1,0:T(8,128)}, f32[96,3072]{1,0:T(8,128)}, f32[384,768]{1,0:T(8,128)}, f32[1,1152]{1,0:T(1,128)}) custom-call(bf16[8,96,256]{2,1,0:T(8,128)(2,1)} %bitcast.93, bf16[8,96,256]{2,1,0:T(8,128)(2,1)} %bitcast.92, bf16[8,96,256]{2,1,0:T(8,128)(2,1)} %bitcast.91, bf16[8,384,256]{2,1,0:T(8,128)(2,1)} %bitcast.72, ...), custom_call_target="tpu_custom_call" | custom-call | tf_op jit(solution)/shard_map/pallas_call | solution.py:555
  243.0 1.4 slice.140
  244.4 1.3 slice.144
  245.7 1.4 fusion.40
  247.0 2.1 copy.90
  249.2 0.7 copy.91
  249.9 1.0 copy.92
  250.9 1.0 copy.93
  (137 shorter events, 5.6 us)
Async XLA Ops:
  0.6 79.2 %copy-start = (bf16[128,768]{1,0:T(8,128)(2,1)S(1)}, bf16[128,768]{1,0:T(8,128)(2,1)}, u32[]{:S(2)}) copy-start(bf16[128,768]{1,0:T(8,128)(2,1)} %param.15) | copy-start | bytes 589828
  0.7 79.5 %copy-start.35 = (s32[128]{0:T(128)S(1)}, s32[128]{0:T(128)}, u32[]{:S(2)}) copy-start(s32[128]{0:T(128)} %param.16) | copy-start | bytes 1540
  79.9 4.5 %copy-start.31 = (f32[128]{0:T(128)}, f32[128]{0:T(128)S(1)}, u32[]{:S(2)}) copy-start(f32[128]{0:T(128)S(1)} %broadcast_multiply_fusion.5) | copy-start | bytes 1540
  80.2 4.3 %copy-start.33 = (f32[128]{0:T(128)}, f32[128]{0:T(128)S(1)}, u32[]{:S(2)}) copy-start(f32[128]{0:T(128)S(1)} %add_rsqrt_fusion.1) | copy-start | bytes 1540
  81.7 2.8 %copy-start.4 = (bf16[128,768]{1,0:T(8,128)(2,1)}, bf16[128,768]{1,0:T(8,128)(2,1)S(1)}, u32[]{:S(2)}) copy-start(bf16[128,768]{1,0:T(8,128)(2,1)S(1)} %get-tuple-element.50) | copy-start | bytes 589828
  84.6 1.1 copy-start.9
  84.8 0.9 copy-start.11
  85.0 0.8 copy-start.15
  85.0 1.3 copy-start.1
  85.9 2.7 %copy-start.13 = (bf16[128,768]{1,0:T(8,128)(2,1)}, bf16[128,768]{1,0:T(8,128)(2,1)S(1)}, u32[]{:S(2)}) copy-start(bf16[128,768]{1,0:T(8,128)(2,1)S(1)} %copy.60) | copy-start | bytes 589828
  88.6 5.0 %copy-start.21 = (bf16[128,768]{1,0:T(8,128)(2,1)}, bf16[128,768]{1,0:T(8,128)(2,1)S(1)}, u32[]{:S(2)}) copy-start(bf16[128,768]{1,0:T(8,128)(2,1)S(1)} %get-tuple-element.48) | copy-start | bytes 589828
  88.6 5.0 %copy-start.6 = (bf16[128,768]{1,0:T(8,128)(2,1)S(1)}, bf16[128,768]{1,0:T(8,128)(2,1)}, u32[]{:S(2)}) copy-start(bf16[128,768]{1,0:T(8,128)(2,1)} %param.17) | copy-start | bytes 589828
  88.6 10.0 %slice-start = ((s8[4718592]{0:T(1024)(128)(4,1)}), s8[4194304]{0:T(1024)(128)(4,1)S(1)}, s32[]{:S(2)}) async-start(s8[4718592]{0:T(1024)(128)(4,1)} %bitcast.74), calls=%async_computation | async-start | bytes 8388608
  93.5 5.0 %slice-start.1 = ((s8[4718592]{0:T(1024)(128)(4,1)}), s8[524288]{0:T(1024)(128)(4,1)S(1)}, s32[]{:S(2)}) async-start(s8[4718592]{0:T(1024)(128)(4,1)} %bitcast.74), calls=%async_computation.1 | async-start | bytes 1048576
  103.6 3.8 %copy-start.16 = (bf16[128,768]{0,1:T(8,128)(2,1)S(1)}, bf16[128,768]{0,1:T(8,128)(2,1)}, u32[]{:S(2)}) copy-start(bf16[128,768]{0,1:T(8,128)(2,1)} %copy-done.15) | copy-start | bytes 589828
  107.4 1.5 copy-start.12
  108.7 0.9 copy-start.10
  108.9 1.0 copy-start.20
  110.3 3.9 %copy-start.7 = (bf16[128,768]{1,0:T(8,128)(2,1)S(1)}, bf16[128,768]{1,0:T(8,128)(2,1)}, u32[]{:S(2)}) copy-start(bf16[128,768]{1,0:T(8,128)(2,1)} %param.17) | copy-start | bytes 589828
  111.1 4.3 %copy-start.30 = (f32[3072]{0:T(1024)S(1)}, f32[3072]{0:T(1024)}, u32[]{:S(2)}) copy-start(f32[3072]{0:T(1024)} %get-tuple-element.87) | copy-start | bytes 36868
  111.1 4.3 %copy-start.26 = (f32[768]{0:T(1024)S(1)}, f32[768]{0:T(1024)}, u32[]{:S(2)}) copy-start(f32[768]{0:T(1024)} %get-tuple-element.34) | copy-start | bytes 9220
  111.1 4.4 %copy-start.28 = (f32[768]{0:T(1024)S(1)}, f32[768]{0:T(1024)}, u32[]{:S(2)}) copy-start(f32[768]{0:T(1024)} %get-tuple-element.42) | copy-start | bytes 9220
  111.1 4.5 %copy-start.27 = (f32[768]{0:T(1024)S(1)}, f32[768]{0:T(1024)}, u32[]{:S(2)}) copy-start(f32[768]{0:T(1024)} %get-tuple-element.61) | copy-start | bytes 9220
  111.1 4.6 %copy-start.25 = (f32[768]{0:T(1024)S(1)}, f32[768]{0:T(1024)}, u32[]{:S(2)}) copy-start(f32[768]{0:T(1024)} %get-tuple-element.40) | copy-start | bytes 9220
  111.1 4.6 %copy-start.32 = (f32[128]{0:T(128)S(1)}, f32[128]{0:T(128)}, u32[]{:S(2)}) copy-start(f32[128]{0:T(128)} %copy-done.31) | copy-start | bytes 1540
  111.1 4.6 %copy-start.34 = (f32[128]{0:T(128)S(1)}, f32[128]{0:T(128)}, u32[]{:S(2)}) copy-start(f32[128]{0:T(128)} %copy-done.33) | copy-start | bytes 1540
  115.0 11.3 %collective-permute-start = (bf16[128,12288]{1,0:T(8,128)(2,1)}, bf16[128,12288]{1,0:T(8,128)(2,1)}, u32[]{:S(2)}, u32[]{:S(2)}) collective-permute-start(bf16[128,12288]{1,0:T(8,128)(2,1)} %constant_dynamic-update-slice_fusion), channel_id=1, source_target_pairs={{0,8},{8,0},{16,24},{24,16},{1,9},{9,1},{17,25},{25,17},{2,10},{10... | collective-permute-start | bytes 9437192 | tf_op jit(solution)/shard_map/ppermute | solution.py:588
  115.7 4.8 %copy-start.29 = (f32[8,96]{1,0:T(8,128)S(1)}, f32[8,96]{1,0:T(8,128)}, u32[]{:S(2)}) copy-start(f32[8,96]{1,0:T(8,128)} %get-tuple-element.62) | copy-start | bytes 9220
  115.7 4.9 %copy-start.2 = (bf16[128,3072]{1,0:T(8,128)(2,1)S(1)}, bf16[128,3072]{1,0:T(8,128)(2,1)}, u32[]{:S(2)}) copy-start(bf16[128,3072]{1,0:T(8,128)(2,1)} %get-tuple-element.46) | copy-start | bytes 2359300
  120.4 5.3 %collective-permute-start.1 = (f32[8,1152]{1,0:T(8,128)S(1)}, f32[8,1152]{1,0:T(8,128)S(1)}, u32[]{:S(2)}, u32[]{:S(2)}) collective-permute-start(f32[8,1152]{1,0:T(8,128)S(1)} %concatenate.64), channel_id=1, source_target_pairs={{0,8},{8,0},{16,24},{24,16},{1,9},{9,1},{17,25},{25,17},{2,10},{10... | collective-permute-start | bytes 110600 | tf_op jit(solution)/shard_map/ppermute | solution.py:588
  120.6 4.1 %copy-start.17 = (f32[128,768]{1,0:T(8,128)S(1)}, f32[128,768]{1,0:T(8,128)}, u32[]{:S(2)}) copy-start(f32[128,768]{1,0:T(8,128)} %get-tuple-element.44) | copy-start | bytes 1179652
  120.6 4.1 %copy-start.23 = (f32[128,768]{1,0:T(8,128)S(1)}, f32[128,768]{1,0:T(8,128)}, u32[]{:S(2)}) copy-start(f32[128,768]{1,0:T(8,128)} %get-tuple-element.86) | copy-start | bytes 1179652
  131.2 1.4 copy-start.8
  131.2 3.0 %copy-start.22 = (bf16[128,768]{1,0:T(8,128)(2,1)S(1)}, bf16[128,768]{1,0:T(8,128)(2,1)}, u32[]{:S(2)}) copy-start(bf16[128,768]{1,0:T(8,128)(2,1)} %copy-done.21) | copy-start | bytes 589828
  132.6 2.5 %copy-start.14 = (bf16[128,768]{1,0:T(8,128)(2,1)S(1)}, bf16[128,768]{1,0:T(8,128)(2,1)}, u32[]{:S(2)}) copy-start(bf16[128,768]{1,0:T(8,128)(2,1)} %copy-done.13) | copy-start | bytes 589828
  134.2 1.9 copy-start.5
  135.2 1.9 copy-start.3
  242.9 6.2 %copy-start.24 = (f32[96,768]{1,0:T(8,128)S(1)}, f32[96,768]{1,0:T(8,128)}, u32[]{:S(2)}) copy-start(f32[96,768]{1,0:T(8,128)} %get-tuple-element.31) | copy-start | bytes 884740
  243.0 6.9 %copy-start.19 = (f32[96,3072]{1,0:T(8,128)S(1)}, f32[96,3072]{1,0:T(8,128)}, u32[]{:S(2)}) copy-start(f32[96,3072]{1,0:T(8,128)} %get-tuple-element.32) | copy-start | bytes 3538948
  249.2 1.7 copy-start.18

commit v12 on v11

--- a/solution.py
+++ b/solution.py
@@ -449,13 +449,15 @@
 
     def step(k, w):
         if w < mm:
-            contribute(stage[w], w, block_at(k))
+            if k == 1:
+                contribute(stage[w], w, block_at(k))
             if k > 1:
                 def accumulate():
                     ring_copy(k - 1, w, source).wait_recv()
                     add_into(send[w].at[k - 1], [stage[w], land[w].at[k - 2]])
 
                 def start_chain():
+                    contribute(stage[w], w, block_at(k))
                     add_into(send[w].at[k - 1], [stage[w]])
 
                 cond = carried(k - 1, w)
@@ -466,6 +468,11 @@
                     pl.when(jnp.logical_not(cond))(start_chain)
             else:
                 add_into(send[w].at[k - 1], [stage[w]])
+            ring_copy(k, w, target).start()
+            if k < steps:
+                contribute(stage[w], w, block_at(k + 1))
+            else:
+                pl.when(owner(w))(lambda: contribute(own[w], w, here))
         else:
             load(k, w).wait()
             if k > 1:
@@ -473,7 +480,7 @@
                     ring_copy(k - 1, w, source).wait_recv()
                     add_into(send[w].at[k - 1], [send[w].at[k - 1], land[w].at[k - 2]])
                 guarded(carried(k - 1, w), accumulate)
-        ring_copy(k, w, target).start()
+            ring_copy(k, w, target).start()
 
     def arrive(w):
         ring_copy(steps, w, source).wait_recv()
@@ -481,9 +488,7 @@
         mine = land[w].at[steps - 1]
 
         def plane():
-            if w < mm:
-                contribute(own[w], w, here)
-            else:
+            if w >= mm:
                 load_own(w).wait()
             pair_copy(w).wait_recv()
 

time: 253 us -> 253 us (level)
  no operation moved by 1% of the time
where the time goes in v12:
time: 253 us; the launch traced here: 252 us
  Pallas kernels  180 us (71%)
  local copies, waits for them, and re-layouts  30.5 us (12%)
  matrix products  29.3 us (12%)
  other arithmetic  10.1 us (4%)
    pallas_call x1, Pallas kernels, reduce_gradients(): pl.pallas_call(functools.partial(reduce_kernel, n, count, mm), out_shape=...  104 us
    pallas_call x1, Pallas kernels, gather_weights(): pl.pallas_call(functools.partial(gather_kernel, n, count), out_shape=[jax...  76 us
    unnamed x87, local copies, waits for them, and re-layouts  11.1 us
  transfers between devices with their start and end apart: 2, of which 0 were waited for; matrix products, arithmetic and copies ran while one was open for 4% of the time, Pallas kernels for 0%

profile of v12, /device:TPU:0, one launch (start us, length us, event | category | flops | bytes accessed | tf_op | source)
XLA Modules:
  0.0 251.9 jit_solution(7171767484378605968)
XLA Ops:
  0.7 1.5 concatenate.49.refs_4_
  2.2 76.0 %shard_map.254 = (bf16[8,96,2304]{2,1,0:T(8,128)(2,1)}, bf16[8,96,768]{2,1,0:T(8,128)(2,1)}, bf16[8,96,3072]{2,1,0:T(8,128)(2,1)}, bf16[8,384,768]{2,1,0:T(8,128)(2,1)}, bf16[8,1,1152]{2,1,0:T(2,128)(2,1)}) custom-call(bf16[96,2304]{1,0:T(8,128)(2,1)} %bitcast.102, bf16[96,768]{1,0:T(8,128)(2,1)} %bitcast.104, bf16[96,3072]{1,0:T(8,128)(2,1)} %bitcast.100, ...), custom_call_target="tpu_custom_call" | custom-call | tf_op jit(solution)/shard_map/pallas_call | solution.py:329
  78.2 0.8 copy.76
  79.1 0.7 slice_convert_fusion.2
  80.8 0.9 constant_dynamic-update-slice_fusion.9
  81.7 2.7 %fusion = bf16[128,2304]{1,0:T(8,128)(2,1)S(1)} fusion(bf16[128,768]{1,0:T(8,128)(2,1)S(1)} %get-tuple-element.50, bf16[768,2304]{1,0:T(8,128)(2,1)} %bitcast.81, f32[2304]{0:T(1024)S(1)} %pad_maximum_fusion.6), kind=kOutput, calls=%fused_computation.3 | convolution fusion | flops 453574656 | bytes 4334592 | tf_op jit(solution)/shard_map/dot_general | solution.py:47
  85.9 0.4 copy-done.1
  86.3 0.4 fusion.42
  87.0 0.7 constant_dynamic-update-slice_fusion.8
  87.7 0.8 constant_dynamic-update-slice_fusion.7
  88.6 4.9 %constant_dynamic-update-slice_fusion.6 = (bf16[128,12288]{1,0:T(8,128)(2,1)}, bf16[128,3072]{1,0:T(8,128)(2,1)}, f32[128,3072]{1,0:T(8,128)S(1)}) fusion(bf16[128,12288]{1,0:T(8,128)(2,1)} %get-tuple-element.47, f32[3072]{0:T(1024)S(1)} %reshape.303, bf16[128,768]{1,0:T(8,128)(2,1)S(1)} %get-tuple-element.48, bf16[768,3072]{1,0:T(8,128)(2,1)} %bitcast.73), kind=kOutput, calls=%fused_computation.79 | convolution fusion | flops 607911936 | bytes 8073216 | tf_op jit(solution)/shard_map/dot_general | solution.py:69
  93.5 5.0 %convert_reduce_fusion = (f32[3072]{0:T(1024)}, bf16[128,3072]{1,0:T(8,128)(2,1)S(1)}) fusion(f32[128,3072]{1,0:T(8,128)S(1)} %get-tuple-element.82, bf16[3072,768]{1,0:T(8,128)(2,1)} %bitcast.79, bf16[128,768]{1,0:T(8,128)(2,1)S(1)} %copy-done.6), kind=kOutput, calls=%fused_computation.15 | convolution fusion | flops 612627456 | bytes 7286784 | tf_op jit(solution)/shard_map/td,fd->tf/dot_general | solution.py:100
  98.6 2.3 multiply_reduce_fusion.1
  100.9 1.5 convert_reduce_fusion.4
  102.4 1.2 convolution_convert_fusion.1
  103.6 1.8 copy.53
  105.4 2.0 convolution_convert_fusion
  107.4 1.3 multiply_reduce_fusion
  110.4 0.7 constant_dynamic-update-slice_fusion.5
  111.1 0.7 constant_dynamic-update-slice_fusion.4
  111.8 0.7 constant_dynamic-update-slice_fusion.3
  112.5 0.7 constant_dynamic-update-slice_fusion.2
  113.3 1.0 constant_dynamic-update-slice_fusion.1
  114.2 0.7 constant_dynamic-update-slice_fusion
  115.0 0.4 collective-permute-start
  115.7 4.1 %fusion.27 = (f32[768]{0:T(1024)S(1)}, f32[128]{0:T(128)S(1)}, f32[128]{0:T(128)S(1)}, f32[768]{0:T(1024)S(1)}, f32[128,768]{1,0:T(8,128)}) fusion(bf16[128,768]{1,0:T(8,128)(2,1)S(1)} %copy-done, f32[128]{0:T(128)S(1)} %copy-done.34, f32[128]{0:T(128)S(1)} %copy-done.32, f32[768]{0:T(1024)S(1)} %reshape.298, bf16[768,2304]{1,0:T(8,128)(2,1)} %bitcast.82, ...), kind=kOutput, calls=%fused_computation.55 | convolution fusion | flops 455735552 | bytes 4729856 | tf_op jit(solution)/shard_map/te,ce->tc/dot_general | solution.py:138
  120.6 4.1 %fusion.11 = bf16[128,768]{1,0:T(8,128)(2,1)} fusion(f32[128,768]{1,0:T(8,128)S(1)} %get-tuple-element.81, bf16[128,3072]{1,0:T(8,128)(2,1)S(1)} %copy-done.2, bf16[3072,768]{1,0:T(8,128)(2,1)} %bitcast.80, f32[768]{0:T(1024)S(1)} %reshape.304), kind=kOutput, calls=%fused_computation.27 | convolution fusion | flops 604274688 | bytes 6097920 | tf_op jit(solution)/shard_map/dot_general | solution.py:72
  124.7 0.9 fusion.26
  125.7 0.6 reshape.297.refs_8_
  126.3 1.1 slice.163
  127.4 1.1 pad_maximum_fusion.1.refs_4_
  128.5 1.5 fusion.36
  130.0 1.3 pad_maximum_fusion.refs_6_
  131.2 1.4 fusion.35
  132.6 0.8 pad_maximum_fusion.4.refs_7_
  133.4 0.8 pad_maximum_fusion.3.refs_5_
  134.3 0.9 copy.67
  135.2 0.9 copy.66
  136.2 0.9 copy.64
  137.2 1.6 copy.73
  138.8 104.2 %shard_map.255 = (f32[96,2304]{1,0:T(8,128)}, f32[96,768]{1,0:T(8,128)}, f32[96,3072]{1,0:T(8,128)}, f32[384,768]{1,0:T(8,128)}, f32[1,1152]{1,0:T(1,128)}) custom-call(bf16[8,96,256]{2,1,0:T(8,128)(2,1)} %bitcast.93, bf16[8,96,256]{2,1,0:T(8,128)(2,1)} %bitcast.92, bf16[8,96,256]{2,1,0:T(8,128)(2,1)} %bitcast.91, bf16[8,384,256]{2,1,0:T(8,128)(2,1)} %bitcast.72, ...), custom_call_target="tpu_custom_call" | custom-call | tf_op jit(solution)/shard_map/pallas_call | solution.py:560
  243.0 1.4 slice.140
  244.4 1.3 slice.144
  245.7 1.4 fusion.40
  247.0 2.1 copy.90
  249.2 0.7 copy.91
  249.9 1.0 copy.92
  250.9 1.0 copy.93
  (137 shorter events, 5.6 us)
Async XLA Ops:
  0.6 79.2 %copy-start = (bf16[128,768]{1,0:T(8,128)(2,1)S(1)}, bf16[128,768]{1,0:T(8,128)(2,1)}, u32[]{:S(2)}) copy-start(bf16[128,768]{1,0:T(8,128)(2,1)} %param.15) | copy-start | bytes 589828
  0.7 79.5 %copy-start.35 = (s32[128]{0:T(128)S(1)}, s32[128]{0:T(128)}, u32[]{:S(2)}) copy-start(s32[128]{0:T(128)} %param.16) | copy-start | bytes 1540
  79.9 4.5 %copy-start.31 = (f32[128]{0:T(128)}, f32[128]{0:T(128)S(1)}, u32[]{:S(2)}) copy-start(f32[128]{0:T(128)S(1)} %broadcast_multiply_fusion.5) | copy-start | bytes 1540
  80.2 4.3 %copy-start.33 = (f32[128]{0:T(128)}, f32[128]{0:T(128)S(1)}, u32[]{:S(2)}) copy-start(f32[128]{0:T(128)S(1)} %add_rsqrt_fusion.1) | copy-start | bytes 1540
  81.7 2.8 %copy-start.4 = (bf16[128,768]{1,0:T(8,128)(2,1)}, bf16[128,768]{1,0:T(8,128)(2,1)S(1)}, u32[]{:S(2)}) copy-start(bf16[128,768]{1,0:T(8,128)(2,1)S(1)} %get-tuple-element.50) | copy-start | bytes 589828
  84.6 1.1 copy-start.9
  84.8 0.9 copy-start.11
  85.0 0.8 copy-start.15
  85.0 1.3 copy-start.1
  85.9 2.7 %copy-start.13 = (bf16[128,768]{1,0:T(8,128)(2,1)}, bf16[128,768]{1,0:T(8,128)(2,1)S(1)}, u32[]{:S(2)}) copy-start(bf16[128,768]{1,0:T(8,128)(2,1)S(1)} %copy.60) | copy-start | bytes 589828
  88.6 5.0 %copy-start.21 = (bf16[128,768]{1,0:T(8,128)(2,1)}, bf16[128,768]{1,0:T(8,128)(2,1)S(1)}, u32[]{:S(2)}) copy-start(bf16[128,768]{1,0:T(8,128)(2,1)S(1)} %get-tuple-element.48) | copy-start | bytes 589828
  88.6 5.0 %copy-start.6 = (bf16[128,768]{1,0:T(8,128)(2,1)S(1)}, bf16[128,768]{1,0:T(8,128)(2,1)}, u32[]{:S(2)}) copy-start(bf16[128,768]{1,0:T(8,128)(2,1)} %param.17) | copy-start | bytes 589828
  88.6 10.0 %slice-start = ((s8[4718592]{0:T(1024)(128)(4,1)}), s8[4194304]{0:T(1024)(128)(4,1)S(1)}, s32[]{:S(2)}) async-start(s8[4718592]{0:T(1024)(128)(4,1)} %bitcast.74), calls=%async_computation | async-start | bytes 8388608
  93.5 5.0 %slice-start.1 = ((s8[4718592]{0:T(1024)(128)(4,1)}), s8[524288]{0:T(1024)(128)(4,1)S(1)}, s32[]{:S(2)}) async-start(s8[4718592]{0:T(1024)(128)(4,1)} %bitcast.74), calls=%async_computation.1 | async-start | bytes 1048576
  103.6 3.8 %copy-start.16 = (bf16[128,768]{0,1:T(8,128)(2,1)S(1)}, bf16[128,768]{0,1:T(8,128)(2,1)}, u32[]{:S(2)}) copy-start(bf16[128,768]{0,1:T(8,128)(2,1)} %copy-done.15) | copy-start | bytes 589828
  107.4 1.5 copy-start.12
  108.7 0.9 copy-start.10
  108.9 1.0 copy-start.20
  110.3 3.9 %copy-start.7 = (bf16[128,768]{1,0:T(8,128)(2,1)S(1)}, bf16[128,768]{1,0:T(8,128)(2,1)}, u32[]{:S(2)}) copy-start(bf16[128,768]{1,0:T(8,128)(2,1)} %param.17) | copy-start | bytes 589828
  111.1 4.3 %copy-start.30 = (f32[3072]{0:T(1024)S(1)}, f32[3072]{0:T(1024)}, u32[]{:S(2)}) copy-start(f32[3072]{0:T(1024)} %get-tuple-element.87) | copy-start | bytes 36868
  111.1 4.3 %copy-start.26 = (f32[768]{0:T(1024)S(1)}, f32[768]{0:T(1024)}, u32[]{:S(2)}) copy-start(f32[768]{0:T(1024)} %get-tuple-element.34) | copy-start | bytes 9220
  111.1 4.4 %copy-start.28 = (f32[768]{0:T(1024)S(1)}, f32[768]{0:T(1024)}, u32[]{:S(2)}) copy-start(f32[768]{0:T(1024)} %get-tuple-element.42) | copy-start | bytes 9220
  111.1 4.5 %copy-start.27 = (f32[768]{0:T(1024)S(1)}, f32[768]{0:T(1024)}, u32[]{:S(2)}) copy-start(f32[768]{0:T(1024)} %get-tuple-element.61) | copy-start | bytes 9220
  111.1 4.6 %copy-start.25 = (f32[768]{0:T(1024)S(1)}, f32[768]{0:T(1024)}, u32[]{:S(2)}) copy-start(f32[768]{0:T(1024)} %get-tuple-element.40) | copy-start | bytes 9220
  111.1 4.6 %copy-start.32 = (f32[128]{0:T(128)S(1)}, f32[128]{0:T(128)}, u32[]{:S(2)}) copy-start(f32[128]{0:T(128)} %copy-done.31) | copy-start | bytes 1540
  111.1 4.6 %copy-start.34 = (f32[128]{0:T(128)S(1)}, f32[128]{0:T(128)}, u32[]{:S(2)}) copy-start(f32[128]{0:T(128)} %copy-done.33) | copy-start | bytes 1540
  115.0 11.3 %collective-permute-start = (bf16[128,12288]{1,0:T(8,128)(2,1)}, bf16[128,12288]{1,0:T(8,128)(2,1)}, u32[]{:S(2)}, u32[]{:S(2)}) collective-permute-start(bf16[128,12288]{1,0:T(8,128)(2,1)} %constant_dynamic-update-slice_fusion), channel_id=1, source_target_pairs={{0,8},{8,0},{16,24},{24,16},{1,9},{9,1},{17,25},{25,17},{2,10},{10... | collective-permute-start | bytes 9437192 | tf_op jit(solution)/shard_map/ppermute | solution.py:593
  115.7 4.8 %copy-start.29 = (f32[8,96]{1,0:T(8,128)S(1)}, f32[8,96]{1,0:T(8,128)}, u32[]{:S(2)}) copy-start(f32[8,96]{1,0:T(8,128)} %get-tuple-element.62) | copy-start | bytes 9220
  115.7 4.9 %copy-start.2 = (bf16[128,3072]{1,0:T(8,128)(2,1)S(1)}, bf16[128,3072]{1,0:T(8,128)(2,1)}, u32[]{:S(2)}) copy-start(bf16[128,3072]{1,0:T(8,128)(2,1)} %get-tuple-element.46) | copy-start | bytes 2359300
  120.4 5.3 %collective-permute-start.1 = (f32[8,1152]{1,0:T(8,128)S(1)}, f32[8,1152]{1,0:T(8,128)S(1)}, u32[]{:S(2)}, u32[]{:S(2)}) collective-permute-start(f32[8,1152]{1,0:T(8,128)S(1)} %concatenate.64), channel_id=1, source_target_pairs={{0,8},{8,0},{16,24},{24,16},{1,9},{9,1},{17,25},{25,17},{2,10},{10... | collective-permute-start | bytes 110600 | tf_op jit(solution)/shard_map/ppermute | solution.py:593
  120.6 4.1 %copy-start.17 = (f32[128,768]{1,0:T(8,128)S(1)}, f32[128,768]{1,0:T(8,128)}, u32[]{:S(2)}) copy-start(f32[128,768]{1,0:T(8,128)} %get-tuple-element.44) | copy-start | bytes 1179652
  120.6 4.1 %copy-start.23 = (f32[128,768]{1,0:T(8,128)S(1)}, f32[128,768]{1,0:T(8,128)}, u32[]{:S(2)}) copy-start(f32[128,768]{1,0:T(8,128)} %get-tuple-element.86) | copy-start | bytes 1179652
  131.2 1.4 copy-start.8
  131.2 3.0 %copy-start.22 = (bf16[128,768]{1,0:T(8,128)(2,1)S(1)}, bf16[128,768]{1,0:T(8,128)(2,1)}, u32[]{:S(2)}) copy-start(bf16[128,768]{1,0:T(8,128)(2,1)} %copy-done.21) | copy-start | bytes 589828
  132.6 2.5 %copy-start.14 = (bf16[128,768]{1,0:T(8,128)(2,1)S(1)}, bf16[128,768]{1,0:T(8,128)(2,1)}, u32[]{:S(2)}) copy-start(bf16[128,768]{1,0:T(8,128)(2,1)} %copy-done.13) | copy-start | bytes 589828
  134.2 1.9 copy-start.5
  135.2 1.9 copy-start.3
  242.9 6.2 %copy-start.24 = (f32[96,768]{1,0:T(8,128)S(1)}, f32[96,768]{1,0:T(8,128)}, u32[]{:S(2)}) copy-start(f32[96,768]{1,0:T(8,128)} %get-tuple-element.31) | copy-start | bytes 884740
  243.0 6.9 %copy-start.19 = (f32[96,3072]{1,0:T(8,128)S(1)}, f32[96,3072]{1,0:T(8,128)}, u32[]{:S(2)}) copy-start(f32[96,3072]{1,0:T(8,128)} %get-tuple-element.32) | copy-start | bytes 3538948
  249.2 1.7 copy-start.18

commit v13 on v12

--- a/solution.py
+++ b/solution.py
@@ -181,7 +181,7 @@
 
 
 CHAIN_RANK = (2, 3, 0, 1, 4)
-CHAIN_LAG = 2
+CHAIN_LAG = 0
 
 
 X_ONLY = (2, 3)

time: 253 us -> 240 us (0.949)
  Pallas kernels: 180 us -> 168 us
    pallas_call x1, Pallas kernels: 104 us -> 91.7 us  [reduce_gradients(): pl.pallas_call(functools.partial(reduce_kernel, n, count, mm), out_shape=...]
where the time goes in v13:
time: 240 us; the launch traced here: 239 us
  Pallas kernels  168 us (70%)
  local copies, waits for them, and re-layouts  30.5 us (13%)
  matrix products  29.3 us (12%)
  other arithmetic  10.1 us (4%)
    pallas_call x1, Pallas kernels, reduce_gradients(): pl.pallas_call(functools.partial(reduce_kernel, n, count, mm), out_shape=...  91.7 us
    pallas_call x1, Pallas kernels, gather_weights(): pl.pallas_call(functools.partial(gather_kernel, n, count), out_shape=[jax...  76 us
    unnamed x87, local copies, waits for them, and re-layouts  11.1 us
    dot_general x1, matrix products, layer_backward(): jnp.einsum('td,fd->tf', proj_in, proj_weight, preferred_element_type=jnp....  5.01 us
    dot_general x1, matrix products, layer_forward(): jnp.dot(second_low, fc_weight, preferred_element_type=jnp.float32) + fc_bias  4.94 us
  transfers between devices with their start and end apart: 2, of which 0 were waited for; matrix products, arithmetic and copies ran while one was open for 4% of the time, Pallas kernels for 0%

profile of v13, /device:TPU:0, one launch (start us, length us, event | category | flops | bytes accessed | tf_op | source)
XLA Modules:
  0.0 239.4 jit_solution(1031875355021959331)
XLA Ops:
  0.7 1.5 concatenate.49.refs_4_
  2.2 76.0 %shard_map.254 = (bf16[8,96,2304]{2,1,0:T(8,128)(2,1)}, bf16[8,96,768]{2,1,0:T(8,128)(2,1)}, bf16[8,96,3072]{2,1,0:T(8,128)(2,1)}, bf16[8,384,768]{2,1,0:T(8,128)(2,1)}, bf16[8,1,1152]{2,1,0:T(2,128)(2,1)}) custom-call(bf16[96,2304]{1,0:T(8,128)(2,1)} %bitcast.102, bf16[96,768]{1,0:T(8,128)(2,1)} %bitcast.104, bf16[96,3072]{1,0:T(8,128)(2,1)} %bitcast.100, ...), custom_call_target="tpu_custom_call" | custom-call | tf_op jit(solution)/shard_map/pallas_call | solution.py:329
  78.2 0.8 copy.76
  79.1 0.7 slice_convert_fusion.2
  80.8 0.9 constant_dynamic-update-slice_fusion.9
  81.7 2.7 %fusion = bf16[128,2304]{1,0:T(8,128)(2,1)S(1)} fusion(bf16[128,768]{1,0:T(8,128)(2,1)S(1)} %get-tuple-element.50, bf16[768,2304]{1,0:T(8,128)(2,1)} %bitcast.81, f32[2304]{0:T(1024)S(1)} %pad_maximum_fusion.6), kind=kOutput, calls=%fused_computation.3 | convolution fusion | flops 453574656 | bytes 4334592 | tf_op jit(solution)/shard_map/dot_general | solution.py:47
  85.9 0.4 copy-done.1
  86.3 0.4 fusion.42
  87.0 0.7 constant_dynamic-update-slice_fusion.8
  87.7 0.8 constant_dynamic-update-slice_fusion.7
  88.6 4.9 %constant_dynamic-update-slice_fusion.6 = (bf16[128,12288]{1,0:T(8,128)(2,1)}, bf16[128,3072]{1,0:T(8,128)(2,1)}, f32[128,3072]{1,0:T(8,128)S(1)}) fusion(bf16[128,12288]{1,0:T(8,128)(2,1)} %get-tuple-element.47, f32[3072]{0:T(1024)S(1)} %reshape.303, bf16[128,768]{1,0:T(8,128)(2,1)S(1)} %get-tuple-element.48, bf16[768,3072]{1,0:T(8,128)(2,1)} %bitcast.73), kind=kOutput, calls=%fused_computation.79 | convolution fusion | flops 607911936 | bytes 8073216 | tf_op jit(solution)/shard_map/dot_general | solution.py:69
  93.5 5.0 %convert_reduce_fusion = (f32[3072]{0:T(1024)}, bf16[128,3072]{1,0:T(8,128)(2,1)S(1)}) fusion(f32[128,3072]{1,0:T(8,128)S(1)} %get-tuple-element.82, bf16[3072,768]{1,0:T(8,128)(2,1)} %bitcast.79, bf16[128,768]{1,0:T(8,128)(2,1)S(1)} %copy-done.6), kind=kOutput, calls=%fused_computation.15 | convolution fusion | flops 612627456 | bytes 7286784 | tf_op jit(solution)/shard_map/td,fd->tf/dot_general | solution.py:100
  98.6 2.3 multiply_reduce_fusion.1
  100.9 1.5 convert_reduce_fusion.4
  102.4 1.2 convolution_convert_fusion.1
  103.6 1.8 copy.53
  105.4 2.0 convolution_convert_fusion
  107.4 1.3 multiply_reduce_fusion
  110.4 0.7 constant_dynamic-update-slice_fusion.5
  111.1 0.7 constant_dynamic-update-slice_fusion.4
  111.8 0.7 constant_dynamic-update-slice_fusion.3
  112.5 0.7 constant_dynamic-update-slice_fusion.2
  113.3 1.0 constant_dynamic-update-slice_fusion.1
  114.2 0.7 constant_dynamic-update-slice_fusion
  115.0 0.4 collective-permute-start
  115.7 4.1 %fusion.27 = (f32[768]{0:T(1024)S(1)}, f32[128]{0:T(128)S(1)}, f32[128]{0:T(128)S(1)}, f32[768]{0:T(1024)S(1)}, f32[128,768]{1,0:T(8,128)}) fusion(bf16[128,768]{1,0:T(8,128)(2,1)S(1)} %copy-done, f32[128]{0:T(128)S(1)} %copy-done.34, f32[128]{0:T(128)S(1)} %copy-done.32, f32[768]{0:T(1024)S(1)} %reshape.298, bf16[768,2304]{1,0:T(8,128)(2,1)} %bitcast.82, ...), kind=kOutput, calls=%fused_computation.55 | convolution fusion | flops 455735552 | bytes 4729856 | tf_op jit(solution)/shard_map/te,ce->tc/dot_general | solution.py:138
  120.6 4.1 %fusion.11 = bf16[128,768]{1,0:T(8,128)(2,1)} fusion(f32[128,768]{1,0:T(8,128)S(1)} %get-tuple-element.81, bf16[128,3072]{1,0:T(8,128)(2,1)S(1)} %copy-done.2, bf16[3072,768]{1,0:T(8,128)(2,1)} %bitcast.80, f32[768]{0:T(1024)S(1)} %reshape.304), kind=kOutput, calls=%fused_computation.27 | convolution fusion | flops 604274688 | bytes 6097920 | tf_op jit(solution)/shard_map/dot_general | solution.py:72
  124.7 0.9 fusion.26
  125.7 0.6 reshape.297.refs_8_
  126.3 1.1 slice.163
  127.4 1.1 pad_maximum_fusion.1.refs_4_
  128.5 1.5 fusion.36
  130.0 1.3 pad_maximum_fusion.refs_6_
  131.2 1.4 fusion.35
  132.6 0.8 pad_maximum_fusion.4.refs_7_
  133.4 0.8 pad_maximum_fusion.3.refs_5_
  134.3 0.9 copy.67
  135.2 0.9 copy.66
  136.2 0.9 copy.64
  137.2 1.6 copy.73
  138.8 91.7 %shard_map.255 = (f32[96,2304]{1,0:T(8,128)}, f32[96,768]{1,0:T(8,128)}, f32[96,3072]{1,0:T(8,128)}, f32[384,768]{1,0:T(8,128)}, f32[1,1152]{1,0:T(1,128)}) custom-call(bf16[8,96,256]{2,1,0:T(8,128)(2,1)} %bitcast.93, bf16[8,96,256]{2,1,0:T(8,128)(2,1)} %bitcast.92, bf16[8,96,256]{2,1,0:T(8,128)(2,1)} %bitcast.91, bf16[8,384,256]{2,1,0:T(8,128)(2,1)} %bitcast.72, ...), custom_call_target="tpu_custom_call" | custom-call | tf_op jit(solution)/shard_map/pallas_call | solution.py:560
  230.5 1.4 slice.140
  231.9 1.3 slice.144
  233.2 1.4 fusion.40
  234.6 2.1 copy.90
  236.7 0.7 copy.91
  237.4 1.0 copy.92
  238.4 1.0 copy.93
  (137 shorter events, 5.6 us)
Async XLA Ops:
  0.6 79.2 %copy-start = (bf16[128,768]{1,0:T(8,128)(2,1)S(1)}, bf16[128,768]{1,0:T(8,128)(2,1)}, u32[]{:S(2)}) copy-start(bf16[128,768]{1,0:T(8,128)(2,1)} %param.15) | copy-start | bytes 589828
  0.7 79.5 %copy-start.35 = (s32[128]{0:T(128)S(1)}, s32[128]{0:T(128)}, u32[]{:S(2)}) copy-start(s32[128]{0:T(128)} %param.16) | copy-start | bytes 1540
  79.9 4.5 %copy-start.31 = (f32[128]{0:T(128)}, f32[128]{0:T(128)S(1)}, u32[]{:S(2)}) copy-start(f32[128]{0:T(128)S(1)} %broadcast_multiply_fusion.5) | copy-start | bytes 1540
  80.2 4.3 %copy-start.33 = (f32[128]{0:T(128)}, f32[128]{0:T(128)S(1)}, u32[]{:S(2)}) copy-start(f32[128]{0:T(128)S(1)} %add_rsqrt_fusion.1) | copy-start | bytes 1540
  81.7 2.8 %copy-start.4 = (bf16[128,768]{1,0:T(8,128)(2,1)}, bf16[128,768]{1,0:T(8,128)(2,1)S(1)}, u32[]{:S(2)}) copy-start(bf16[128,768]{1,0:T(8,128)(2,1)S(1)} %get-tuple-element.50) | copy-start | bytes 589828
  84.6 1.1 copy-start.9
  84.8 0.9 copy-start.11
  85.0 0.8 copy-start.15
  85.0 1.3 copy-start.1
  85.9 2.7 %copy-start.13 = (bf16[128,768]{1,0:T(8,128)(2,1)}, bf16[128,768]{1,0:T(8,128)(2,1)S(1)}, u32[]{:S(2)}) copy-start(bf16[128,768]{1,0:T(8,128)(2,1)S(1)} %copy.60) | copy-start | bytes 589828
  88.6 5.0 %copy-start.21 = (bf16[128,768]{1,0:T(8,128)(2,1)}, bf16[128,768]{1,0:T(8,128)(2,1)S(1)}, u32[]{:S(2)}) copy-start(bf16[128,768]{1,0:T(8,128)(2,1)S(1)} %get-tuple-element.48) | copy-start | bytes 589828
  88.6 5.0 %copy-start.6 = (bf16[128,768]{1,0:T(8,128)(2,1)S(1)}, bf16[128,768]{1,0:T(8,128)(2,1)}, u32[]{:S(2)}) copy-start(bf16[128,768]{1,0:T(8,128)(2,1)} %param.17) | copy-start | bytes 589828
  88.6 10.0 %slice-start = ((s8[4718592]{0:T(1024)(128)(4,1)}), s8[4194304]{0:T(1024)(128)(4,1)S(1)}, s32[]{:S(2)}) async-start(s8[4718592]{0:T(1024)(128)(4,1)} %bitcast.74), calls=%async_computation | async-start | bytes 8388608
  93.5 5.0 %slice-start.1 = ((s8[4718592]{0:T(1024)(128)(4,1)}), s8[524288]{0:T(1024)(128)(4,1)S(1)}, s32[]{:S(2)}) async-start(s8[4718592]{0:T(1024)(128)(4,1)} %bitcast.74), calls=%async_computation.1 | async-start | bytes 1048576
  103.6 3.8 %copy-start.16 = (bf16[128,768]{0,1:T(8,128)(2,1)S(1)}, bf16[128,768]{0,1:T(8,128)(2,1)}, u32[]{:S(2)}) copy-start(bf16[128,768]{0,1:T(8,128)(2,1)} %copy-done.15) | copy-start | bytes 589828
  107.4 1.5 copy-start.12
  108.7 0.9 copy-start.10
  108.9 1.0 copy-start.20
  110.3 3.9 %copy-start.7 = (bf16[128,768]{1,0:T(8,128)(2,1)S(1)}, bf16[128,768]{1,0:T(8,128)(2,1)}, u32[]{:S(2)}) copy-start(bf16[128,768]{1,0:T(8,128)(2,1)} %param.17) | copy-start | bytes 589828
  111.1 4.3 %copy-start.30 = (f32[3072]{0:T(1024)S(1)}, f32[3072]{0:T(1024)}, u32[]{:S(2)}) copy-start(f32[3072]{0:T(1024)} %get-tuple-element.87) | copy-start | bytes 36868
  111.1 4.3 %copy-start.26 = (f32[768]{0:T(1024)S(1)}, f32[768]{0:T(1024)}, u32[]{:S(2)}) copy-start(f32[768]{0:T(1024)} %get-tuple-element.34) | copy-start | bytes 9220
  111.1 4.4 %copy-start.28 = (f32[768]{0:T(1024)S(1)}, f32[768]{0:T(1024)}, u32[]{:S(2)}) copy-start(f32[768]{0:T(1024)} %get-tuple-element.42) | copy-start | bytes 9220
  111.1 4.5 %copy-start.27 = (f32[768]{0:T(1024)S(1)}, f32[768]{0:T(1024)}, u32[]{:S(2)}) copy-start(f32[768]{0:T(1024)} %get-tuple-element.61) | copy-start | bytes 9220
  111.1 4.6 %copy-start.25 = (f32[768]{0:T(1024)S(1)}, f32[768]{0:T(1024)}, u32[]{:S(2)}) copy-start(f32[768]{0:T(1024)} %get-tuple-element.40) | copy-start | bytes 9220
  111.1 4.6 %copy-start.32 = (f32[128]{0:T(128)S(1)}, f32[128]{0:T(128)}, u32[]{:S(2)}) copy-start(f32[128]{0:T(128)} %copy-done.31) | copy-start | bytes 1540
  111.1 4.6 %copy-start.34 = (f32[128]{0:T(128)S(1)}, f32[128]{0:T(128)}, u32[]{:S(2)}) copy-start(f32[128]{0:T(128)} %copy-done.33) | copy-start | bytes 1540
  115.0 11.3 %collective-permute-start = (bf16[128,12288]{1,0:T(8,128)(2,1)}, bf16[128,12288]{1,0:T(8,128)(2,1)}, u32[]{:S(2)}, u32[]{:S(2)}) collective-permute-start(bf16[128,12288]{1,0:T(8,128)(2,1)} %constant_dynamic-update-slice_fusion), channel_id=1, source_target_pairs={{0,8},{8,0},{16,24},{24,16},{1,9},{9,1},{17,25},{25,17},{2,10},{10... | collective-permute-start | bytes 9437192 | tf_op jit(solution)/shard_map/ppermute | solution.py:593
  115.7 4.8 %copy-start.29 = (f32[8,96]{1,0:T(8,128)S(1)}, f32[8,96]{1,0:T(8,128)}, u32[]{:S(2)}) copy-start(f32[8,96]{1,0:T(8,128)} %get-tuple-element.62) | copy-start | bytes 9220
  115.7 4.9 %copy-start.2 = (bf16[128,3072]{1,0:T(8,128)(2,1)S(1)}, bf16[128,3072]{1,0:T(8,128)(2,1)}, u32[]{:S(2)}) copy-start(bf16[128,3072]{1,0:T(8,128)(2,1)} %get-tuple-element.46) | copy-start | bytes 2359300
  120.4 5.3 %collective-permute-start.1 = (f32[8,1152]{1,0:T(8,128)S(1)}, f32[8,1152]{1,0:T(8,128)S(1)}, u32[]{:S(2)}, u32[]{:S(2)}) collective-permute-start(f32[8,1152]{1,0:T(8,128)S(1)} %concatenate.64), channel_id=1, source_target_pairs={{0,8},{8,0},{16,24},{24,16},{1,9},{9,1},{17,25},{25,17},{2,10},{10... | collective-permute-start | bytes 110600 | tf_op jit(solution)/shard_map/ppermute | solution.py:593
  120.6 4.1 %copy-start.17 = (f32[128,768]{1,0:T(8,128)S(1)}, f32[128,768]{1,0:T(8,128)}, u32[]{:S(2)}) copy-start(f32[128,768]{1,0:T(8,128)} %get-tuple-element.44) | copy-start | bytes 1179652
  120.6 4.1 %copy-start.23 = (f32[128,768]{1,0:T(8,128)S(1)}, f32[128,768]{1,0:T(8,128)}, u32[]{:S(2)}) copy-start(f32[128,768]{1,0:T(8,128)} %get-tuple-element.86) | copy-start | bytes 1179652
  131.2 1.4 copy-start.8
  131.2 3.0 %copy-start.22 = (bf16[128,768]{1,0:T(8,128)(2,1)S(1)}, bf16[128,768]{1,0:T(8,128)(2,1)}, u32[]{:S(2)}) copy-start(bf16[128,768]{1,0:T(8,128)(2,1)} %copy-done.21) | copy-start | bytes 589828
  132.6 2.5 %copy-start.14 = (bf16[128,768]{1,0:T(8,128)(2,1)S(1)}, bf16[128,768]{1,0:T(8,128)(2,1)}, u32[]{:S(2)}) copy-start(bf16[128,768]{1,0:T(8,128)(2,1)} %copy-done.13) | copy-start | bytes 589828
  134.2 1.9 copy-start.5
  135.2 1.9 copy-start.3
  230.5 6.2 %copy-start.24 = (f32[96,768]{1,0:T(8,128)S(1)}, f32[96,768]{1,0:T(8,128)}, u32[]{:S(2)}) copy-start(f32[96,768]{1,0:T(8,128)} %get-tuple-element.31) | copy-start | bytes 884740
  230.5 6.9 %copy-start.19 = (f32[96,3072]{1,0:T(8,128)S(1)}, f32[96,3072]{1,0:T(8,128)}, u32[]{:S(2)}) copy-start(f32[96,3072]{1,0:T(8,128)} %get-tuple-element.32) | copy-start | bytes 3538948
  236.7 1.7 copy-start.18

commit v14 on v13

--- a/solution.py
+++ b/solution.py
@@ -184,13 +184,19 @@
 CHAIN_LAG = 0
 
 
-X_ONLY = (2, 3)
-
-
-def gather_kernel(n, count, *refs):
+def gather_kernel(n, count, parts, plane_only, first_core, *refs):
     local = refs[:count]
     full = refs[count : 2 * count]
     ring_send, ring_recv, pair_send, pair_recv, x_send, x_recv, relay_send, relay_recv = refs[2 * count :]
+    count = len(parts)
+
+    def lview(w):
+        array, row, rows = parts[w]
+        return local[array] if rows is None else local[array].at[pl.ds(row, rows)]
+
+    def fview(w, pos):
+        array, row, rows = parts[w]
+        return full[array].at[pos] if rows is None else full[array].at[pos, pl.ds(row, rows)]
     rep = lax.axis_index("rep")
     shard = lax.axis_index("shard")
     core = rep % 2
@@ -218,26 +224,25 @@
 
     def core_carries(k, w, which_core):
         if split_last and k == steps:
-            return (which_core == 0) == (w in FIRST_CORE_HALF)
+            return (which_core == 0) == (w in first_core)
         return True
 
     def plane_carries(w, which_plane):
-        if w == X_ONLY[0]:
-            return which_plane == 0
-        if w == X_ONLY[1]:
-            return which_plane == 1
+        for only, sole in enumerate(plane_only):
+            if w in sole:
+                return which_plane == only
         return True
 
     def ring_in(k, w):
         return both(plane_carries(w, plane), core_carries(k, w, core))
 
     def x_out(k, w):
-        if w not in X_ONLY:
+        if not any(w in sole for sole in plane_only):
             return False
         return both(plane_carries(w, plane), core_carries(k, w, core))
 
     def x_in(k, w):
-        if w not in X_ONLY:
+        if not any(w in sole for sole in plane_only):
             return False
         return both(plane_carries(w, 1 - plane), core_carries(k, w, core))
 
@@ -245,7 +250,7 @@
         return both(plane_carries(w, plane), core_carries(k, w, 1 - core))
 
     def partner_x_in(k, w):
-        if w not in X_ONLY:
+        if not any(w in sole for sole in plane_only):
             return False
         return both(plane_carries(w, 1 - plane), core_carries(k, w, 1 - core))
 
@@ -267,24 +272,24 @@
 
     def ring_copy(k, w):
         src_pos = here - step_dir * (k - 1)
-        src = local[w] if k == 1 else full[w].at[slot(src_pos)]
-        return remote(src, full[w].at[slot(src_pos)], ring_send.at[k - 1, w], ring_recv.at[k - 1, w], target)
+        src = lview(w) if k == 1 else fview(w, slot(src_pos))
+        return remote(src, fview(w, slot(src_pos)), ring_send.at[k - 1, w], ring_recv.at[k - 1, w], target)
 
     def incoming_ring(k, w):
         pos = slot(here - step_dir * k)
-        return remote(full[w].at[pos], full[w].at[pos], ring_send.at[k - 1, w], ring_recv.at[k - 1, w], source)
+        return remote(fview(w, pos), fview(w, pos), ring_send.at[k - 1, w], ring_recv.at[k - 1, w], source)
 
     def pair_copy(k, w, pos):
-        src = local[w] if k == 0 else full[w].at[slot(pos)]
-        return remote(src, full[w].at[slot(pos)], pair_send.at[k, w], pair_recv.at[k, w], partner)
+        src = lview(w) if k == 0 else fview(w, slot(pos))
+        return remote(src, fview(w, slot(pos)), pair_send.at[k, w], pair_recv.at[k, w], partner)
 
     def x_copy(k, w):
         pos = slot(here - step_dir * k)
-        return remote(full[w].at[pos], full[w].at[pos], x_send.at[k - 1, w], x_recv.at[k - 1, w], x_partner)
+        return remote(fview(w, pos), fview(w, pos), x_send.at[k - 1, w], x_recv.at[k - 1, w], x_partner)
 
     def relay_copy(k, w, pos):
         pos = slot(pos)
-        return remote(full[w].at[pos], full[w].at[pos], relay_send.at[k - 1, w], relay_recv.at[k - 1, w], partner)
+        return remote(fview(w, pos), fview(w, pos), relay_send.at[k - 1, w], relay_recv.at[k - 1, w], partner)
 
     for w in range(count):
         pair_copy(0, w, here).start()
@@ -325,21 +330,32 @@
 def gather_weights(locals_, n):
     count = len(locals_)
     steps = n // 2
+    rows = locals_[2].shape[0]
+    if n == 8 and rows % 32 == 0:
+        half = rows // 2
+        parts = ((0, 0, None), (1, 0, None), (2, 0, half), (2, half, half), (3, 0, None), (4, 0, None))
+        plane_only = ((0,), (1, 2))
+        first_core = (1, 4)
+    else:
+        parts = tuple((a, 0, None) for a in range(count))
+        plane_only = ((),)
+        first_core = FIRST_CORE_HALF
+    pieces = len(parts)
     dma = pltpu.SemaphoreType.DMA
     return pl.pallas_call(
-        functools.partial(gather_kernel, n, count),
+        functools.partial(gather_kernel, n, count, parts, plane_only, first_core),
         out_shape=[jax.ShapeDtypeStruct((n,) + a.shape, a.dtype) for a in locals_],
         in_specs=[pl.BlockSpec(memory_space=pl.ANY)] * count,
         out_specs=[pl.BlockSpec(memory_space=pl.ANY)] * count,
         scratch_shapes=[
-            dma((steps, count)),
-            dma((steps, count)),
-            dma((steps + 1, count)),
-            dma((steps + 1, count)),
-            dma((steps, count)),
-            dma((steps, count)),
-            dma((steps, count)),
-            dma((steps, count)),
+            dma((steps, pieces)),
+            dma((steps, pieces)),
+            dma((steps + 1, pieces)),
+            dma((steps + 1, pieces)),
+            dma((steps, pieces)),
+            dma((steps, pieces)),
+            dma((steps, pieces)),
+            dma((steps, pieces)),
         ],
         compiler_params=pltpu.CompilerParams(collective_id=0, has_side_effects=True),
     )(*locals_)

time: 240 us -> 228 us (0.950)
  Pallas kernels: 168 us -> 156 us
    pallas_call x1, Pallas kernels: 76 us -> 62.9 us  [gather_weights(): pl.pallas_call(functools.partial(gather_kernel, n, count, parts, plane_on...]
  transfers between devices with their start and end apart: 2 -> 2, of which waited for: 0 -> 0; matrix products, arithmetic and copies ran while one was open for 4% -> 5% of each run, Pallas kernels for 0% -> 0%
where the time goes in v14:
time: 228 us
  Pallas kernels  156 us (68%)
  local copies, waits for them, and re-layouts  30.7 us (13%)
  matrix products  29.1 us (13%)
  other arithmetic  10.1 us (4%)
    pallas_call x1, Pallas kernels, reduce_gradients(): pl.pallas_call(functools.partial(reduce_kernel, n, count, mm), out_shape=...  92.9 us
    pallas_call x1, Pallas kernels, gather_weights(): pl.pallas_call(functools.partial(gather_kernel, n, count, parts, plane_on...  62.9 us
    unnamed x87, local copies, waits for them, and re-layouts  11.1 us
    dot_general x1, matrix products, layer_backward(): jnp.einsum('td,fd->tf', proj_in, proj_weight, preferred_element_type=jnp....  5.01 us
    dot_general x1, matrix products, layer_forward(): jnp.dot(second_low, fc_weight, preferred_element_type=jnp.float32) + fc_bias  4.94 us
  transfers between devices with their start and end apart: 2, of which 0 were waited for; matrix products, arithmetic and copies ran while one was open for 5% of the time, Pallas kernels for 0%

profile of v14, /device:TPU:0, one launch (start us, length us, event | category | flops | bytes accessed | tf_op | source)
XLA Modules:
  0.0 227.6 jit_solution(6715234587558477181)
XLA Ops:
  0.7 1.5 concatenate.49.refs_4_
  2.2 62.9 %shard_map.254 = (bf16[8,96,2304]{2,1,0:T(8,128)(2,1)}, bf16[8,96,768]{2,1,0:T(8,128)(2,1)}, bf16[8,96,3072]{2,1,0:T(8,128)(2,1)}, bf16[8,384,768]{2,1,0:T(8,128)(2,1)}, bf16[8,1,1152]{2,1,0:T(2,128)(2,1)}) custom-call(bf16[96,2304]{1,0:T(8,128)(2,1)} %bitcast.102, bf16[96,768]{1,0:T(8,128)(2,1)} %bitcast.104, bf16[96,3072]{1,0:T(8,128)(2,1)} %bitcast.100, ...), custom_call_target="tpu_custom_call" | custom-call | tf_op jit(solution)/shard_map/pallas_call | solution.py:345
  65.1 0.8 copy.76
  66.0 0.7 slice_convert_fusion.2
  67.7 0.9 constant_dynamic-update-slice_fusion.9
  68.6 2.7 %fusion = bf16[128,2304]{1,0:T(8,128)(2,1)S(1)} fusion(bf16[128,768]{1,0:T(8,128)(2,1)S(1)} %get-tuple-element.50, bf16[768,2304]{1,0:T(8,128)(2,1)} %bitcast.81, f32[2304]{0:T(1024)S(1)} %pad_maximum_fusion.6), kind=kOutput, calls=%fused_computation.3 | convolution fusion | flops 453574656 | bytes 4334592 | tf_op jit(solution)/shard_map/dot_general | solution.py:47
  72.8 0.4 copy-done.1
  73.2 0.4 fusion.42
  73.9 0.7 constant_dynamic-update-slice_fusion.8
  74.6 0.8 constant_dynamic-update-slice_fusion.7
  75.5 4.9 %constant_dynamic-update-slice_fusion.6 = (bf16[128,12288]{1,0:T(8,128)(2,1)}, bf16[128,3072]{1,0:T(8,128)(2,1)}, f32[128,3072]{1,0:T(8,128)S(1)}) fusion(bf16[128,12288]{1,0:T(8,128)(2,1)} %get-tuple-element.47, f32[3072]{0:T(1024)S(1)} %reshape.303, bf16[128,768]{1,0:T(8,128)(2,1)S(1)} %get-tuple-element.48, bf16[768,3072]{1,0:T(8,128)(2,1)} %bitcast.73), kind=kOutput, calls=%fused_computation.79 | convolution fusion | flops 607911936 | bytes 8073216 | tf_op jit(solution)/shard_map/dot_general | solution.py:69
  80.4 5.0 %convert_reduce_fusion = (f32[3072]{0:T(1024)}, bf16[128,3072]{1,0:T(8,128)(2,1)S(1)}) fusion(f32[128,3072]{1,0:T(8,128)S(1)} %get-tuple-element.82, bf16[3072,768]{1,0:T(8,128)(2,1)} %bitcast.79, bf16[128,768]{1,0:T(8,128)(2,1)S(1)} %copy-done.6), kind=kOutput, calls=%fused_computation.15 | convolution fusion | flops 612627456 | bytes 7286784 | tf_op jit(solution)/shard_map/td,fd->tf/dot_general | solution.py:100
  85.4 2.3 %multiply_reduce_fusion.1 = (f32[768]{0:T(1024)}, f32[128]{0:T(128)S(1)}, f32[128]{0:T(128)S(1)}, f32[768]{0:T(1024)}, f32[128,768]{1,0:T(8,128)S(1)}) fusion(f32[128,768]{1,0:T(8,128)S(1)} %get-tuple-element.81, f32[128]{0:T(128)S(1)} %add_rsqrt_fusion, f32[128]{0:T(128)S(1)} %broadcast_multiply_fusion.4, f32[768]{0:T(1024)S(1)} %reshape.301, ...), kind=kOutput, calls=%fused_computation.62 | convolution fusion | flops 604862720 | bytes 6302720 | tf_op jit(solution)/shard_map/tf,df->td/dot_general | solution.py:104
  87.8 1.5 convert_reduce_fusion.4
  89.3 1.2 convolution_convert_fusion.1
  90.5 1.8 copy.53
  92.3 2.0 convolution_convert_fusion
  94.3 1.3 multiply_reduce_fusion
  97.3 0.7 constant_dynamic-update-slice_fusion.5
  98.0 0.7 constant_dynamic-update-slice_fusion.4
  98.7 0.7 constant_dynamic-update-slice_fusion.3
  99.4 0.7 constant_dynamic-update-slice_fusion.2
  100.2 1.0 constant_dynamic-update-slice_fusion.1
  101.1 0.7 constant_dynamic-update-slice_fusion
  101.8 0.5 collective-permute-start
  102.6 4.1 %fusion.27 = (f32[768]{0:T(1024)S(1)}, f32[128]{0:T(128)S(1)}, f32[128]{0:T(128)S(1)}, f32[768]{0:T(1024)S(1)}, f32[128,768]{1,0:T(8,128)}) fusion(bf16[128,768]{1,0:T(8,128)(2,1)S(1)} %copy-done, f32[128]{0:T(128)S(1)} %copy-done.34, f32[128]{0:T(128)S(1)} %copy-done.32, f32[768]{0:T(1024)S(1)} %reshape.298, bf16[768,2304]{1,0:T(8,128)(2,1)} %bitcast.82, ...), kind=kOutput, calls=%fused_computation.55 | convolution fusion | flops 455735552 | bytes 4729856 | tf_op jit(solution)/shard_map/te,ce->tc/dot_general | solution.py:138
  107.5 3.9 %fusion.11 = bf16[128,768]{1,0:T(8,128)(2,1)} fusion(f32[128,768]{1,0:T(8,128)S(1)} %get-tuple-element.81, bf16[128,3072]{1,0:T(8,128)(2,1)S(1)} %copy-done.2, bf16[3072,768]{1,0:T(8,128)(2,1)} %bitcast.80, f32[768]{0:T(1024)S(1)} %reshape.304), kind=kOutput, calls=%fused_computation.27 | convolution fusion | flops 604274688 | bytes 6097920 | tf_op jit(solution)/shard_map/dot_general | solution.py:72
  111.4 0.9 fusion.26
  112.3 0.6 reshape.297.refs_8_
  113.0 1.3 slice.163
  114.3 1.1 pad_maximum_fusion.1.refs_4_
  115.4 1.5 fusion.36
  116.8 1.3 pad_maximum_fusion.refs_6_
  118.1 1.4 fusion.35
  119.5 0.8 pad_maximum_fusion.4.refs_7_
  120.3 0.8 pad_maximum_fusion.3.refs_5_
  121.1 0.9 copy.67
  122.1 0.9 copy.66
  123.0 0.9 copy.64
  124.1 1.6 copy.73
  125.6 92.9 %shard_map.255 = (f32[96,2304]{1,0:T(8,128)}, f32[96,768]{1,0:T(8,128)}, f32[96,3072]{1,0:T(8,128)}, f32[384,768]{1,0:T(8,128)}, f32[1,1152]{1,0:T(1,128)}) custom-call(bf16[8,96,256]{2,1,0:T(8,128)(2,1)} %bitcast.93, bf16[8,96,256]{2,1,0:T(8,128)(2,1)} %bitcast.92, bf16[8,96,256]{2,1,0:T(8,128)(2,1)} %bitcast.91, bf16[8,384,256]{2,1,0:T(8,128)(2,1)} %bitcast.72, ...), custom_call_target="tpu_custom_call" | custom-call | tf_op jit(solution)/shard_map/pallas_call | solution.py:576
  218.6 1.4 slice.140
  220.0 1.3 slice.144
  221.3 1.4 fusion.40
  222.7 2.1 copy.90
  224.8 0.7 copy.91
  225.5 1.0 copy.92
  226.6 1.0 copy.93
  (137 shorter events, 5.6 us)
Async XLA Ops:
  0.6 66.1 %copy-start = (bf16[128,768]{1,0:T(8,128)(2,1)S(1)}, bf16[128,768]{1,0:T(8,128)(2,1)}, u32[]{:S(2)}) copy-start(bf16[128,768]{1,0:T(8,128)(2,1)} %param.15) | copy-start | bytes 589828
  0.7 66.4 %copy-start.35 = (s32[128]{0:T(128)S(1)}, s32[128]{0:T(128)}, u32[]{:S(2)}) copy-start(s32[128]{0:T(128)} %param.16) | copy-start | bytes 1540
  66.8 4.5 %copy-start.31 = (f32[128]{0:T(128)}, f32[128]{0:T(128)S(1)}, u32[]{:S(2)}) copy-start(f32[128]{0:T(128)S(1)} %broadcast_multiply_fusion.5) | copy-start | bytes 1540
  67.1 4.3 %copy-start.33 = (f32[128]{0:T(128)}, f32[128]{0:T(128)S(1)}, u32[]{:S(2)}) copy-start(f32[128]{0:T(128)S(1)} %add_rsqrt_fusion.1) | copy-start | bytes 1540
  68.6 2.8 %copy-start.4 = (bf16[128,768]{1,0:T(8,128)(2,1)}, bf16[128,768]{1,0:T(8,128)(2,1)S(1)}, u32[]{:S(2)}) copy-start(bf16[128,768]{1,0:T(8,128)(2,1)S(1)} %get-tuple-element.50) | copy-start | bytes 589828
  71.5 1.1 copy-start.9
  71.7 0.9 copy-start.11
  71.9 0.8 copy-start.15
  71.9 1.3 copy-start.1
  72.8 2.7 %copy-start.13 = (bf16[128,768]{1,0:T(8,128)(2,1)}, bf16[128,768]{1,0:T(8,128)(2,1)S(1)}, u32[]{:S(2)}) copy-start(bf16[128,768]{1,0:T(8,128)(2,1)S(1)} %copy.60) | copy-start | bytes 589828
  75.5 5.0 %copy-start.21 = (bf16[128,768]{1,0:T(8,128)(2,1)}, bf16[128,768]{1,0:T(8,128)(2,1)S(1)}, u32[]{:S(2)}) copy-start(bf16[128,768]{1,0:T(8,128)(2,1)S(1)} %get-tuple-element.48) | copy-start | bytes 589828
  75.5 5.0 %copy-start.6 = (bf16[128,768]{1,0:T(8,128)(2,1)S(1)}, bf16[128,768]{1,0:T(8,128)(2,1)}, u32[]{:S(2)}) copy-start(bf16[128,768]{1,0:T(8,128)(2,1)} %param.17) | copy-start | bytes 589828
  75.5 10.0 %slice-start = ((s8[4718592]{0:T(1024)(128)(4,1)}), s8[4194304]{0:T(1024)(128)(4,1)S(1)}, s32[]{:S(2)}) async-start(s8[4718592]{0:T(1024)(128)(4,1)} %bitcast.74), calls=%async_computation | async-start | bytes 8388608
  80.4 5.0 %slice-start.1 = ((s8[4718592]{0:T(1024)(128)(4,1)}), s8[524288]{0:T(1024)(128)(4,1)S(1)}, s32[]{:S(2)}) async-start(s8[4718592]{0:T(1024)(128)(4,1)} %bitcast.74), calls=%async_computation.1 | async-start | bytes 1048576
  90.5 3.8 %copy-start.16 = (bf16[128,768]{0,1:T(8,128)(2,1)S(1)}, bf16[128,768]{0,1:T(8,128)(2,1)}, u32[]{:S(2)}) copy-start(bf16[128,768]{0,1:T(8,128)(2,1)} %copy-done.15) | copy-start | bytes 589828
  94.3 1.5 copy-start.12
  95.6 0.9 copy-start.10
  95.8 1.0 copy-start.20
  97.2 3.9 %copy-start.7 = (bf16[128,768]{1,0:T(8,128)(2,1)S(1)}, bf16[128,768]{1,0:T(8,128)(2,1)}, u32[]{:S(2)}) copy-start(bf16[128,768]{1,0:T(8,128)(2,1)} %param.17) | copy-start | bytes 589828
  98.0 4.4 %copy-start.30 = (f32[3072]{0:T(1024)S(1)}, f32[3072]{0:T(1024)}, u32[]{:S(2)}) copy-start(f32[3072]{0:T(1024)} %get-tuple-element.87) | copy-start | bytes 36868
  98.0 4.4 %copy-start.26 = (f32[768]{0:T(1024)S(1)}, f32[768]{0:T(1024)}, u32[]{:S(2)}) copy-start(f32[768]{0:T(1024)} %get-tuple-element.34) | copy-start | bytes 9220
  98.0 4.4 %copy-start.28 = (f32[768]{0:T(1024)S(1)}, f32[768]{0:T(1024)}, u32[]{:S(2)}) copy-start(f32[768]{0:T(1024)} %get-tuple-element.42) | copy-start | bytes 9220
  98.0 4.5 %copy-start.27 = (f32[768]{0:T(1024)S(1)}, f32[768]{0:T(1024)}, u32[]{:S(2)}) copy-start(f32[768]{0:T(1024)} %get-tuple-element.61) | copy-start | bytes 9220
  98.0 4.6 %copy-start.25 = (f32[768]{0:T(1024)S(1)}, f32[768]{0:T(1024)}, u32[]{:S(2)}) copy-start(f32[768]{0:T(1024)} %get-tuple-element.40) | copy-start | bytes 9220
  98.0 4.6 %copy-start.32 = (f32[128]{0:T(128)S(1)}, f32[128]{0:T(128)}, u32[]{:S(2)}) copy-start(f32[128]{0:T(128)} %copy-done.31) | copy-start | bytes 1540
  98.0 4.6 %copy-start.34 = (f32[128]{0:T(128)S(1)}, f32[128]{0:T(128)}, u32[]{:S(2)}) copy-start(f32[128]{0:T(128)} %copy-done.33) | copy-start | bytes 1540
  101.8 11.1 %collective-permute-start = (bf16[128,12288]{1,0:T(8,128)(2,1)}, bf16[128,12288]{1,0:T(8,128)(2,1)}, u32[]{:S(2)}, u32[]{:S(2)}) collective-permute-start(bf16[128,12288]{1,0:T(8,128)(2,1)} %constant_dynamic-update-slice_fusion), channel_id=1, source_target_pairs={{0,8},{8,0},{16,24},{24,16},{1,9},{9,1},{17,25},{25,17},{2,10},{10... | collective-permute-start | bytes 9437192 | tf_op jit(solution)/shard_map/ppermute | solution.py:609
  102.6 4.8 %copy-start.29 = (f32[8,96]{1,0:T(8,128)S(1)}, f32[8,96]{1,0:T(8,128)}, u32[]{:S(2)}) copy-start(f32[8,96]{1,0:T(8,128)} %get-tuple-element.62) | copy-start | bytes 9220
  102.6 4.9 %copy-start.2 = (bf16[128,3072]{1,0:T(8,128)(2,1)S(1)}, bf16[128,3072]{1,0:T(8,128)(2,1)}, u32[]{:S(2)}) copy-start(bf16[128,3072]{1,0:T(8,128)(2,1)} %get-tuple-element.46) | copy-start | bytes 2359300
  107.3 5.1 %collective-permute-start.1 = (f32[8,1152]{1,0:T(8,128)S(1)}, f32[8,1152]{1,0:T(8,128)S(1)}, u32[]{:S(2)}, u32[]{:S(2)}) collective-permute-start(f32[8,1152]{1,0:T(8,128)S(1)} %concatenate.64), channel_id=1, source_target_pairs={{0,8},{8,0},{16,24},{24,16},{1,9},{9,1},{17,25},{25,17},{2,10},{10... | collective-permute-start | bytes 110600 | tf_op jit(solution)/shard_map/ppermute | solution.py:609
  107.5 3.9 %copy-start.17 = (f32[128,768]{1,0:T(8,128)S(1)}, f32[128,768]{1,0:T(8,128)}, u32[]{:S(2)}) copy-start(f32[128,768]{1,0:T(8,128)} %get-tuple-element.44) | copy-start | bytes 1179652
  107.5 3.9 %copy-start.23 = (f32[128,768]{1,0:T(8,128)S(1)}, f32[128,768]{1,0:T(8,128)}, u32[]{:S(2)}) copy-start(f32[128,768]{1,0:T(8,128)} %get-tuple-element.86) | copy-start | bytes 1179652
  118.1 1.4 copy-start.8
  118.1 3.0 %copy-start.22 = (bf16[128,768]{1,0:T(8,128)(2,1)S(1)}, bf16[128,768]{1,0:T(8,128)(2,1)}, u32[]{:S(2)}) copy-start(bf16[128,768]{1,0:T(8,128)(2,1)} %copy-done.21) | copy-start | bytes 589828
  119.5 2.5 %copy-start.14 = (bf16[128,768]{1,0:T(8,128)(2,1)S(1)}, bf16[128,768]{1,0:T(8,128)(2,1)}, u32[]{:S(2)}) copy-start(bf16[128,768]{1,0:T(8,128)(2,1)} %copy-done.13) | copy-start | bytes 589828
  121.1 1.9 copy-start.5
  122.1 1.9 copy-start.3
  218.6 6.2 %copy-start.24 = (f32[96,768]{1,0:T(8,128)S(1)}, f32[96,768]{1,0:T(8,128)}, u32[]{:S(2)}) copy-start(f32[96,768]{1,0:T(8,128)} %get-tuple-element.31) | copy-start | bytes 884740
  218.6 6.9 %copy-start.19 = (f32[96,3072]{1,0:T(8,128)S(1)}, f32[96,3072]{1,0:T(8,128)}, u32[]{:S(2)}) copy-start(f32[96,3072]{1,0:T(8,128)} %get-tuple-element.32) | copy-start | bytes 3538948
  224.8 1.7 copy-start.18

commit v15 on v14

--- a/solution.py
+++ b/solution.py
@@ -376,8 +376,10 @@
 def reduce_kernel(n, count, mm, *refs):
     xt = refs[:mm]
     dy = refs[mm : 2 * mm]
-    contrib = (None,) * mm + refs[2 * mm : mm + count]
-    refs = refs[mm + count :]
+    xtp = refs[2 * mm : 3 * mm]
+    dyp = refs[3 * mm : 4 * mm]
+    contrib = (None,) * mm + refs[4 * mm : 3 * mm + count]
+    refs = refs[3 * mm + count :]
     out = refs[:count]
     land, send, other, own, xland, stage, xsend = (refs[count + i * count : count + (i + 1) * count] for i in range(7))
     (load_sem, own_sem, ring_send, ring_recv, pair_send, pair_recv, x_send, x_recv, back_send, back_recv) = refs[
@@ -442,7 +444,9 @@
 
         def body(i, carry):
             window = pl.ds(pl.multiple_of(i * width, width), width)
-            dst[:, window] = jnp.dot(xt[w][block], dy[w][:, window], preferred_element_type=jnp.float32)
+            dst[:, window] = jnp.dot(
+                xt[w][block], dy[w][:, window], preferred_element_type=jnp.float32
+            ) + jnp.dot(xtp[w][block], dyp[w][:, window], preferred_element_type=jnp.float32)
             return carry
 
         lax.fori_loop(0, dy[w].shape[1] // width, body, 0)
@@ -569,14 +573,14 @@
     mm = len(pairs_t)
     count = mm + len(contribs)
     steps = n // 2
-    blocks = [(xt.shape[1], dy.shape[1]) for xt, dy in pairs_t] + [c.shape[1:] for c in contribs]
+    blocks = [(xt.shape[1], dy.shape[1]) for xt, dy, _, _ in pairs_t] + [c.shape[1:] for c in contribs]
     ring_types = [jnp.bfloat16] * mm + [jnp.float32] * len(contribs)
     vmem = lambda shape, dtype=jnp.float32: pltpu.VMEM(shape, dtype)
     dma = pltpu.SemaphoreType.DMA
     return pl.pallas_call(
         functools.partial(reduce_kernel, n, count, mm),
         out_shape=[jax.ShapeDtypeStruct(b, jnp.float32) for b in blocks],
-        in_specs=[pl.BlockSpec(memory_space=pltpu.VMEM)] * (2 * mm)
+        in_specs=[pl.BlockSpec(memory_space=pltpu.VMEM)] * (4 * mm)
         + [pl.BlockSpec(memory_space=pl.ANY)] * len(contribs),
         out_specs=[pl.BlockSpec(memory_space=pltpu.VMEM)] * count,
         scratch_shapes=[vmem((steps,) + b, t) for b, t in zip(blocks, ring_types)]
@@ -601,7 +605,7 @@
         compiler_params=pltpu.CompilerParams(
             collective_id=1, has_side_effects=True, vmem_limit_bytes=62 * 1024 * 1024
         ),
-    )(*[xt for xt, _ in pairs_t], *[dy for _, dy in pairs_t], *contribs)
+    )(*[p[0] for p in pairs_t], *[p[1] for p in pairs_t], *[p[2] for p in pairs_t], *[p[3] for p in pairs_t], *contribs)
 
 
 def swap_core(value):
@@ -680,22 +684,13 @@
     upstream = to_float(cotangent)
     input_grad, small_grads, pairs = layer_backward(upstream, saved, small, weights)
 
-    outgoing = jnp.concatenate([x for x, _ in pairs] + [dy for _, dy in pairs], axis=1)
-    incoming = swap_core(outgoing)
     small_mine = jnp.concatenate([g.reshape(shard, -1) for g in small_grads], axis=1)
     small_theirs = swap_core(small_mine)
     small_chip = jnp.where(core == 0, small_mine + small_theirs, small_theirs + small_mine)
-    start = 0
-    partner_x = []
-    for x, _ in pairs:
-        partner_x.append(incoming[:, start : start + x.shape[1]])
-        start += x.shape[1]
     pairs_t = []
-    for (x, dy), px in zip(pairs, partner_x):
-        pdy = incoming[:, start : start + dy.shape[1]]
-        start += dy.shape[1]
-        rows_t = jnp.concatenate([x, px], axis=0).T
-        pairs_t.append((rows_t.reshape(shard, -1, rows_t.shape[1]), jnp.concatenate([dy, pdy], axis=0)))
+    for x, dy in pairs:
+        rows_t = x.T.reshape(shard, -1, x.shape[0])
+        pairs_t.append((rows_t, dy, swap_core(rows_t), swap_core(dy)))
     totals = reduce_gradients(pairs_t, [small_chip.reshape(shard, 1, -1)], shard)
     small_share = totals[4]
     owned = [t[None] for t in totals[:4]]

time: 228 us -> 220 us (0.965)
  local copies, waits for them, and re-layouts: 30.7 us -> 22.7 us
  matrix products: 29.1 us -> 26.3 us
    slice x3 -> x0, local copies, waits for them, and re-layouts: 4.14 us -> none  [per_device(): pdy = incoming[:, start:start + dy.shape[1]]]
    concatenate x4 -> x0, other arithmetic: 3.92 us -> none  [per_device(): jnp.concatenate([dy, pdy], axis=0)]
    unnamed x87 -> x107, local copies, waits for them, and re-layouts: 11.1 us -> 8.08 us
    reduce_sum x1, other arithmetic: 0.1 us -> 2.61 us  [layer_backward(): column_sums = jnp.sum(to_float(joined_grad), axis=0)]
    transpose x3 -> x2, local copies, waits for them, and re-layouts: 2.77 us -> 0.32 us  [per_device(): rows_t = x.T.reshape(shard, -1, x.shape[0])]
  transfers between devices with their start and end apart: 2 -> 9, of which waited for: 0 -> 2; matrix products, arithmetic and copies ran while one was open for 5% -> 14% of each run, Pallas kernels for 0% -> 0%
where the time goes in v15:
time: 220 us; the launch traced here: 219 us
  Pallas kernels  156 us (71%)
  matrix products  26.3 us (12%)
  local copies, waits for them, and re-layouts  22.7 us (10%)
  other arithmetic  9.34 us (4%)
  starting transfers between devices  2.57 us (1%)
    pallas_call x1, Pallas kernels, reduce_gradients(): pl.pallas_call(functools.partial(reduce_kernel, n, count, mm), out_shape=...  93.1 us
    pallas_call x1, Pallas kernels, gather_weights(): pl.pallas_call(functools.partial(gather_kernel, n, count, parts, plane_on...  62.9 us
    unnamed x107, local copies, waits for them, and re-layouts  8.08 us
    dot_general x1, matrix products, layer_forward(): jnp.dot(second_low, fc_weight, preferred_element_type=jnp.float32) + fc_bias  5.01 us
    dot_general x1, matrix products, layer_forward(): jnp.dot(hidden_low, proj_weight, preferred_element_type=jnp.float32)  4.93 us
  transfers between devices with their start and end apart: 9, of which 2 were waited for; matrix products, arithmetic and copies ran while one was open for 14% of the time, Pallas kernels for 0%

profile of v15, /device:TPU:0, one launch (start us, length us, event | category | flops | bytes accessed | tf_op | source)
XLA Modules:
  0.0 219.3 jit_solution(11632489533165012981)
XLA Ops:
  0.7 1.5 concatenate.21.refs_4_
  2.2 62.9 %shard_map.254 = (bf16[8,96,2304]{2,1,0:T(8,128)(2,1)}, bf16[8,96,768]{2,1,0:T(8,128)(2,1)}, bf16[8,96,3072]{2,1,0:T(8,128)(2,1)}, bf16[8,384,768]{2,1,0:T(8,128)(2,1)}, bf16[8,1,1152]{2,1,0:T(2,128)(2,1)}) custom-call(bf16[96,2304]{1,0:T(8,128)(2,1)} %bitcast.104, bf16[96,768]{1,0:T(8,128)(2,1)} %bitcast.106, bf16[96,3072]{1,0:T(8,128)(2,1)} %bitcast.102, ...), custom_call_target="tpu_custom_call" | custom-call | tf_op jit(solution)/shard_map/pallas_call | solution.py:345
  65.1 0.8 copy.72
  65.9 0.7 slice_convert_fusion.2
  67.4 2.7 %fusion = bf16[128,2304]{1,0:T(8,128)(2,1)S(1)} fusion(bf16[768,2304]{1,0:T(8,128)(2,1)} %bitcast.71, f32[2304]{0:T(1024)S(1)} %pad_maximum_fusion.1, bf16[128,768]{1,0:T(8,128)(2,1)S(1)} %copy-done.1, f32[768]{0:T(1024)S(1)} %reshape.299, f32[768]{0:T(1024)S(1)} %reshape.298, f32[128]{0:T(128)S(1)} %add_rsqrt_fusion.1, f32[128]{0:T(128)S(1)} %broadcast_multiply_fusion.5), kind=kOutput, calls=%fused_computation.3 | convolution fusion | flops 454164480 | bytes 4341760 | tf_op jit(solution)/shard_map/dot_general | solution.py:47
  70.9 0.3 fusion.55
  71.6 0.2 convolution_convert_fusion.2
  71.8 0.3 copy-done.6
  72.2 0.4 fusion.56
  72.9 5.0 %fusion.15 = (bf16[3072,128]{0,1:T(8,128)(2,1)}, f32[128,3072]{1,0:T(8,128)S(1)}) fusion(f32[3072]{0:T(1024)S(1)} %reshape.303, bf16[768,3072]{1,0:T(8,128)(2,1)} %bitcast.73, f32[128,768]{1,0:T(8,128)S(1)} %get-tuple-element.72, f32[768]{0:T(1024)S(1)} %reshape.302, f32[768]{0:T(1024)S(1)} %reshape.301, f32[128]{0:T(128)S(1)} %add_rsqrt_fusion, ...), kind=kOutput, calls=%fused_computation.21 | convolution fusion | flops 608403456 | bytes 7490560 | tf_op jit(solution)/shard_map/dot_general | solution.py:69
  77.9 3.5 %convert_reduce_fusion = (f32[3072]{0:T(1024)}, bf16[128,3072]{1,0:T(8,128)(2,1)}) fusion(f32[128,3072]{1,0:T(8,128)S(1)} %get-tuple-element.76, bf16[3072,768]{1,0:T(8,128)(2,1)S(1)} %bitcast.111, bf16[128,768]{1,0:T(8,128)(2,1)S(1)} %copy-done.21), kind=kOutput, calls=%fused_computation.22 | convolution fusion | flops 612627456 | bytes 7286784 | tf_op jit(solution)/shard_map/td,fd->tf/dot_general | solution.py:100
  81.4 0.5 collective-permute-start.6
  81.9 2.8 %fusion.57 = f32[128,768]{1,0:T(8,128)S(1)} fusion(bf16[128,3072]{1,0:T(8,128)(2,1)} %get-tuple-element.78.refs_6_, bf16[768,3072]{1,0:T(8,128)(2,1)S(1)} %bitcast.76), kind=kOutput, calls=%fused_computation.109 | convolution fusion | flops 603979776 | bytes 5898240 | tf_op jit(solution)/shard_map/tf,df->td/dot_general | solution.py:104
  84.8 0.9 multiply_reduce_fusion.1
  85.7 1.6 convert_reduce_fusion.4
  87.2 0.7 copy-done.12
  87.9 0.5 convolution_convert_fusion.1
  88.6 1.1 convolution_convert_fusion
  89.7 0.3 multiply_reduce_fusion
  90.2 0.4 copy-done.15
  90.6 1.0 fusion.21
  91.7 0.9 fusion.20
  92.6 1.7 copy.60
  94.3 1.7 copy.59
  96.1 1.7 copy.58
  97.8 2.6 %convert_reduce_fusion.1 = (f32[2304]{0:T(1024)}, bf16[128,2304]{1,0:T(8,128)(2,1)}) fusion(bf16[128,768]{1,0:T(8,128)(2,1)} %copy.60, bf16[128,768]{1,0:T(8,128)(2,1)} %copy.59, bf16[128,768]{1,0:T(8,128)(2,1)} %copy.58), kind=kLoop, calls=%fused_computation.32 | loop fusion | flops 2356992 | bytes 1188864 | tf_op jit(solution)/shard_map/reduce_sum | solution.py:136
  100.5 2.4 %fusion.58 = f32[128,768]{1,0:T(8,128)S(1)} fusion(bf16[128,2304]{1,0:T(8,128)(2,1)} %get-tuple-element.46.refs_4_, bf16[768,2304]{1,0:T(8,128)(2,1)S(1)} %bitcast.72), kind=kOutput, calls=%fused_computation.110 | convolution fusion | flops 452984832 | bytes 4521984 | tf_op jit(solution)/shard_map/te,ce->tc/dot_general | solution.py:138
  103.0 0.8 fusion.39
  104.0 0.5 collective-permute-start
  104.5 0.4 copy.69
  105.7 0.7 concatenate.27
  106.4 0.4 collective-permute-start.8
  107.0 4.9 %fusion.19 = bf16[128,768]{1,0:T(8,128)(2,1)} fusion(f32[128,768]{1,0:T(8,128)S(1)} %copy-done.5, bf16[3072,768]{1,0:T(8,128)(2,1)} %bitcast.110, f32[128,3072]{1,0:T(8,128)} %copy-done.48, f32[768]{0:T(1024)S(1)} %reshape.304), kind=kOutput, calls=%fused_computation.33 | convolution fusion | flops 607813632 | bytes 6884352 | tf_op jit(solution)/shard_map/dot_general | solution.py:72
  112.3 0.4 collective-permute-start.2
  112.7 0.9 collective-permute-done.1.refs_9_
  113.9 0.3 collective-permute-start.7
  114.2 0.9 fusion.38
  115.2 0.8 add.133
  116.0 0.6 reshape.297.refs_16_
  116.6 0.7 copy-done.32
  117.4 93.1 %shard_map.255 = (f32[96,2304]{1,0:T(8,128)}, f32[96,768]{1,0:T(8,128)}, f32[96,3072]{1,0:T(8,128)}, f32[384,768]{1,0:T(8,128)}, f32[1,1152]{1,0:T(1,128)}) custom-call(bf16[8,96,128]{2,1,0:T(8,128)(2,1)} %bitcast.96, bf16[8,96,128]{2,1,0:T(8,128)(2,1)} %bitcast.82, bf16[8,96,128]{2,1,0:T(8,128)(2,1)} %bitcast.98, bf16[8,384,128]{2,1,0:T(8,128)(2,1)} %bitcast.80, ...), custom_call_target="tpu_custom_call" | custom-call | tf_op jit(solution)/shard_map/pallas_call | solution.py:580
  210.5 1.4 fusion.54
  211.9 1.3 slice.108
  213.1 1.3 slice.112
  214.4 2.1 copy.77
  216.6 0.7 copy.78
  217.3 1.0 copy.79
  218.3 1.0 copy.80
  (157 shorter events, 4.4 us)
Async XLA Ops:
  0.6 66.4 %copy-start.1 = (bf16[128,768]{1,0:T(8,128)(2,1)S(1)}, bf16[128,768]{1,0:T(8,128)(2,1)}, u32[]{:S(2)}) copy-start(bf16[128,768]{1,0:T(8,128)(2,1)} %param.15) | copy-start | bytes 589828
  67.2 3.0 %copy-start.38 = (f32[128]{0:T(128)}, f32[128]{0:T(128)S(1)}, u32[]{:S(2)}) copy-start(f32[128]{0:T(128)S(1)} %broadcast_multiply_fusion.5) | copy-start | bytes 1540
  67.4 2.7 %copy-start.41 = (f32[128]{0:T(128)}, f32[128]{0:T(128)S(1)}, u32[]{:S(2)}) copy-start(f32[128]{0:T(128)S(1)} %add_rsqrt_fusion.1) | copy-start | bytes 1540
  72.2 5.7 %copy-start.47 = (bf16[8,384,768]{2,1,0:T(8,128)(2,1)S(1)}, bf16[8,384,768]{2,1,0:T(8,128)(2,1)}, u32[]{:S(2)}) copy-start(bf16[8,384,768]{2,1,0:T(8,128)(2,1)} %get-tuple-element.28) | copy-start | bytes 14155780
  72.6 13.0 %copy-start.4 = (f32[128,768]{1,0:T(8,128)}, f32[128,768]{1,0:T(8,128)S(1)}, u32[]{:S(2)}) copy-start(f32[128,768]{1,0:T(8,128)S(1)} %get-tuple-element.72) | copy-start | bytes 1179652
  72.9 5.0 %copy-start.21 = (bf16[128,768]{1,0:T(8,128)(2,1)S(1)}, bf16[128,768]{1,0:T(8,128)(2,1)}, u32[]{:S(2)}) copy-start(bf16[128,768]{1,0:T(8,128)(2,1)} %refs_7_) | copy-start | bytes 589828
  72.9 9.0 %slice-start = ((s8[4718592]{0:T(1024)(128)(4,1)}), s8[4194304]{0:T(1024)(128)(4,1)S(1)}, s32[]{:S(2)}) async-start(s8[4718592]{0:T(1024)(128)(4,1)} %bitcast.74), calls=%async_computation | async-start | bytes 8388608
  77.9 3.5 %copy-start.48 = (f32[128,3072]{1,0:T(8,128)}, f32[128,3072]{1,0:T(8,128)S(1)}, u32[]{:S(2)}) copy-start(f32[128,3072]{1,0:T(8,128)S(1)} %get-tuple-element.76) | copy-start | bytes 4718596
  77.9 4.0 %slice-start.1 = ((s8[4718592]{0:T(1024)(128)(4,1)}), s8[524288]{0:T(1024)(128)(4,1)S(1)}, s32[]{:S(2)}) async-start(s8[4718592]{0:T(1024)(128)(4,1)} %bitcast.74), calls=%async_computation.1 | async-start | bytes 1048576
  81.4 35.9 %collective-permute-start.6 = (bf16[128,3072]{1,0:T(8,128)(2,1)}, bf16[128,3072]{1,0:T(8,128)(2,1)}, u32[]{:S(2)}, u32[]{:S(2)}) collective-permute-start(bf16[128,3072]{1,0:T(8,128)(2,1)} %get-tuple-element.78.refs_6_), channel_id=1, source_target_pairs={{0,8},{8,0},{16,24},{24,16},{1,9},{9,1},{17,25},{25,17},{2,10},{10... | collective-permute-start | bytes 2359304 | tf_op jit(solution)/shard_map/ppermute | solution.py:613
  90.6 9.9 %copy-start = (bf16[8,96,2304]{2,1,0:T(8,128)(2,1)S(1)}, bf16[8,96,2304]{2,1,0:T(8,128)(2,1)}, u32[]{:S(2)}) copy-start(bf16[8,96,2304]{2,1,0:T(8,128)(2,1)} %get-tuple-element.25) | copy-start | bytes 10616836
  100.4 2.5 %copy-start.2 = (bf16[128,768]{1,0:T(8,128)(2,1)S(1)}, bf16[128,768]{1,0:T(8,128)(2,1)}, u32[]{:S(2)}) copy-start(bf16[128,768]{1,0:T(8,128)(2,1)} %param.15) | copy-start | bytes 589828
  100.4 2.5 %copy-start.39 = (f32[128]{0:T(128)S(1)}, f32[128]{0:T(128)}, u32[]{:S(2)}) copy-start(f32[128]{0:T(128)} %copy-done.38) | copy-start | bytes 1540
  100.4 2.5 %copy-start.42 = (f32[128]{0:T(128)S(1)}, f32[128]{0:T(128)}, u32[]{:S(2)}) copy-start(f32[128]{0:T(128)} %copy-done.41) | copy-start | bytes 1540
  100.4 16.2 %collective-permute-start.4 = (bf16[128,2304]{1,0:T(8,128)(2,1)}, bf16[128,2304]{1,0:T(8,128)(2,1)}, u32[]{:S(2)}, u32[]{:S(2)}) collective-permute-start(bf16[128,2304]{1,0:T(8,128)(2,1)} %get-tuple-element.46.refs_4_), channel_id=1, source_target_pairs={{0,8},{8,0},{16,24},{24,16},{1,9},{9,1},{17,25},{25,17},{2,10},{10... | collective-permute-start | bytes 1769480 | tf_op jit(solution)/shard_map/ppermute | solution.py:613
  102.9 2.3 %copy-start.33 = (f32[2304]{0:T(1024)S(1)}, f32[2304]{0:T(1024)}, u32[]{:S(2)}) copy-start(f32[2304]{0:T(1024)} %get-tuple-element.45) | copy-start | bytes 27652
  103.0 2.4 %copy-start.35 = (f32[768]{0:T(1024)S(1)}, f32[768]{0:T(1024)}, u32[]{:S(2)}) copy-start(f32[768]{0:T(1024)} %get-tuple-element.42) | copy-start | bytes 9220
  103.0 2.6 %copy-start.37 = (f32[3072]{0:T(1024)S(1)}, f32[3072]{0:T(1024)}, u32[]{:S(2)}) copy-start(f32[3072]{0:T(1024)} %get-tuple-element.77) | copy-start | bytes 36868
  103.0 2.6 %copy-start.34 = (f32[768]{0:T(1024)S(1)}, f32[768]{0:T(1024)}, u32[]{:S(2)}) copy-start(f32[768]{0:T(1024)} %get-tuple-element.52) | copy-start | bytes 9220
  103.0 3.8 %copy-start.36 = (f32[8,96]{1,0:T(8,128)S(1)}, f32[8,96]{1,0:T(8,128)}, u32[]{:S(2)}) copy-start(f32[8,96]{1,0:T(8,128)} %get-tuple-element.53) | copy-start | bytes 9220
  103.0 3.9 %copy-start.5 = (f32[128,768]{1,0:T(8,128)S(1)}, f32[128,768]{1,0:T(8,128)}, u32[]{:S(2)}) copy-start(f32[128,768]{1,0:T(8,128)} %copy-done.4) | copy-start | bytes 1179652
  104.0 7.9 %copy-start.23 = (bf16[768,128]{1,0:T(8,128)(2,1)}, bf16[768,128]{1,0:T(8,128)(2,1)S(1)}, u32[]{:S(2)}) copy-start(bf16[768,128]{1,0:T(8,128)(2,1)S(1)} %copy.61) | copy-start | bytes 589828
  104.0 8.3 %collective-permute-start = (bf16[8,96,128]{2,1,0:T(8,128)(2,1)S(1)}, bf16[8,96,128]{2,1,0:T(8,128)(2,1)S(1)}, u32[]{:S(2)}, u32[]{:S(2)}) collective-permute-start(bf16[8,96,128]{2,1,0:T(8,128)(2,1)S(1)} %bitcast.95), channel_id=1, source_target_pairs={{0,8},{8,0},{16,24},{24,16},{1,9},{9,1},{17,25},{25,17},{2,10},{10... | collective-permute-start | bytes 589832 | tf_op jit(solution)/shard_map/ppermute | solution.py:613
  104.8 7.0 %copy-start.9 = (bf16[3072,128]{1,0:T(8,128)(2,1)}, bf16[3072,128]{1,0:T(8,128)(2,1)S(1)}, u32[]{:S(2)}) copy-start(bf16[3072,128]{1,0:T(8,128)(2,1)S(1)} %copy.69) | copy-start | bytes 2359300
  104.9 11.8 %collective-permute-start.3 = (bf16[8,384,128]{2,1,0:T(8,128)(2,1)S(1)}, bf16[8,384,128]{2,1,0:T(8,128)(2,1)}, u32[]{:S(2)}, u32[]{:S(2)}) collective-permute-start(bf16[8,384,128]{2,1,0:T(8,128)(2,1)S(1)} %bitcast.79), channel_id=1, source_target_pairs={{0,8},{8,0},{16,24},{24,16},{1,9},{9,1},{17,25},{25,17},{2,10},{10... | collective-permute-start | bytes 2359304 | tf_op jit(solution)/shard_map/ppermute | solution.py:613
  106.4 5.7 %collective-permute-start.8 = (f32[8,1152]{1,0:T(8,128)}, f32[8,1152]{1,0:T(8,128)}, u32[]{:S(2)}, u32[]{:S(2)}) collective-permute-start(f32[8,1152]{1,0:T(8,128)} %concatenate.27), channel_id=1, source_target_pairs={{0,8},{8,0},{16,24},{24,16},{1,9},{9,1},{17,25},{25,17},{2,10},{10... | collective-permute-start | bytes 110600 | tf_op jit(solution)/shard_map/ppermute | solution.py:613
  106.9 5.0 %copy-start.46 = (f32[128]{0:T(128)S(1)}, f32[128]{0:T(128)}, u32[]{:S(2)}) copy-start(f32[128]{0:T(128)} %get-tuple-element.37) | copy-start | bytes 1540
  106.9 5.1 %copy-start.26 = (bf16[768,128]{0,1:T(8,128)(2,1)S(1)}, bf16[768,128]{0,1:T(8,128)(2,1)}, u32[]{:S(2)}) copy-start(bf16[768,128]{0,1:T(8,128)(2,1)} %get-tuple-element.50) | copy-start | bytes 589828
  106.9 5.2 %copy-start.11 = (bf16[12,64,128]{2,1,0:T(8,128)(2,1)S(1)}, bf16[12,64,128]{2,1,0:T(8,128)(2,1)}, u32[]{:S(2)}) copy-start(bf16[12,64,128]{2,1,0:T(8,128)(2,1)} %copy-done.10) | copy-start | bytes 589828
  106.9 5.8 %copy-start.45 = (f32[128]{0:T(128)S(1)}, f32[128]{0:T(128)}, u32[]{:S(2)}) copy-start(f32[128]{0:T(128)} %get-tuple-element.38) | copy-start | bytes 1540
  106.9 6.7 %copy-start.13 = (bf16[128,768]{1,0:T(8,128)(2,1)S(1)}, bf16[128,768]{1,0:T(8,128)(2,1)}, u32[]{:S(2)}) copy-start(bf16[128,768]{1,0:T(8,128)(2,1)} %copy-done.12) | copy-start | bytes 589828
  106.9 7.0 %copy-start.22 = (bf16[128,768]{1,0:T(8,128)(2,1)S(1)}, bf16[128,768]{1,0:T(8,128)(2,1)}, u32[]{:S(2)}) copy-start(bf16[128,768]{1,0:T(8,128)(2,1)} %refs_7_) | copy-start | bytes 589828
  106.9 7.3 %copy-start.3 = (bf16[128,768]{1,0:T(8,128)(2,1)S(1)}, bf16[128,768]{1,0:T(8,128)(2,1)}, u32[]{:S(2)}) copy-start(bf16[128,768]{1,0:T(8,128)(2,1)} %param.15) | copy-start | bytes 589828
  106.9 7.3 %copy-start.8 = (f32[128,768]{1,0:T(8,128)S(1)}, f32[128,768]{1,0:T(8,128)}, u32[]{:S(2)}) copy-start(f32[128,768]{1,0:T(8,128)} %copy-done.7) | copy-start | bytes 1179652
  106.9 7.3 %copy-start.18 = (f32[128,768]{1,0:T(8,128)S(1)}, f32[128,768]{1,0:T(8,128)}, u32[]{:S(2)}) copy-start(f32[128,768]{1,0:T(8,128)} %get-tuple-element.44) | copy-start | bytes 1179652
  106.9 7.3 %copy-start.40 = (f32[128]{0:T(128)S(1)}, f32[128]{0:T(128)}, u32[]{:S(2)}) copy-start(f32[128]{0:T(128)} %copy-done.38) | copy-start | bytes 1540
  106.9 7.3 %copy-start.43 = (f32[128]{0:T(128)S(1)}, f32[128]{0:T(128)}, u32[]{:S(2)}) copy-start(f32[128]{0:T(128)} %copy-done.41) | copy-start | bytes 1540
  112.1 5.2 %copy-start.24 = (bf16[768,128]{1,0:T(8,128)(2,1)}, bf16[768,128]{1,0:T(8,128)(2,1)S(1)}, u32[]{:S(2)}) copy-start(bf16[768,128]{1,0:T(8,128)(2,1)S(1)} %copy.62) | copy-start | bytes 589828
  112.1 1.5 collective-permute-start.1
  112.3 5.0 %copy-start.28 = (bf16[8,96,128]{2,1,0:T(8,128)(2,1)}, bf16[8,96,128]{2,1,0:T(8,128)(2,1)S(1)}, u32[]{:S(2)}) copy-start(bf16[8,96,128]{2,1,0:T(8,128)(2,1)S(1)} %collective-permute-done.refs_8_) | copy-start | bytes 589828
  112.3 1.6 collective-permute-start.2
  113.6 3.7 %copy-start.29 = (bf16[8,96,128]{2,1,0:T(8,128)(2,1)}, bf16[8,96,128]{2,1,0:T(8,128)(2,1)S(1)}, u32[]{:S(2)}) copy-start(bf16[8,96,128]{2,1,0:T(8,128)(2,1)S(1)} %collective-permute-done.1.refs_9_) | copy-start | bytes 589828
  113.6 3.0 %collective-permute-start.5 = (bf16[128,768]{1,0:T(8,128)(2,1)S(1)}, bf16[128,768]{1,0:T(8,128)(2,1)S(1)}, u32[]{:S(2)}, u32[]{:S(2)}) collective-permute-start(bf16[128,768]{1,0:T(8,128)(2,1)S(1)} %copy-done.13), channel_id=1, source_target_pairs={{0,8},{8,0},{16,24},{24,16},{1,9},{9,1},{17,25},{25,17},{2,10},{10... | collective-permute-start | bytes 589832 | tf_op jit(solution)/shard_map/ppermute | solution.py:613
  113.9 2.7 %copy-start.30 = (bf16[8,96,128]{2,1,0:T(8,128)(2,1)}, bf16[8,96,128]{2,1,0:T(8,128)(2,1)S(1)}, u32[]{:S(2)}) copy-start(bf16[8,96,128]{2,1,0:T(8,128)(2,1)S(1)} %collective-permute-done.2.refs_10_) | copy-start | bytes 589828
  113.9 2.7 %collective-permute-start.7 = (bf16[128,768]{1,0:T(8,128)(2,1)S(1)}, bf16[128,768]{1,0:T(8,128)(2,1)S(1)}, u32[]{:S(2)}, u32[]{:S(2)}) collective-permute-start(bf16[128,768]{1,0:T(8,128)(2,1)S(1)} %copy-done.22), channel_id=1, source_target_pairs={{0,8},{8,0},{16,24},{24,16},{1,9},{9,1},{17,25},{25,17},{2,10},{10... | collective-permute-start | bytes 589832 | tf_op jit(solution)/shard_map/ppermute | solution.py:613
  210.4 6.1 %copy-start.27 = (f32[96,768]{1,0:T(8,128)S(1)}, f32[96,768]{1,0:T(8,128)}, u32[]{:S(2)}) copy-start(f32[96,768]{1,0:T(8,128)} %get-tuple-element.31) | copy-start | bytes 884740
  210.4 6.8 %copy-start.20 = (f32[96,3072]{1,0:T(8,128)S(1)}, f32[96,3072]{1,0:T(8,128)}, u32[]{:S(2)}) copy-start(f32[96,3072]{1,0:T(8,128)} %get-tuple-element.32) | copy-start | bytes 3538948
  216.6 1.7 copy-start.19
  (12 other events, 12.4 us)

commit v16 on v15

--- a/solution.py
+++ b/solution.py
@@ -113,26 +113,24 @@
     prob_grad = jnp.einsum(
         "qhd,khd->hqk", mixed_grad, saved["values_all"], preferred_element_type=jnp.float32
     )
-    value_grad = jnp.einsum(
-        "hqk,qhd->khd", saved["probs_low"], mixed_grad, preferred_element_type=jnp.float32
-    )
     attn_probs = saved["attn_probs"]
     row_delta = jnp.sum(attn_probs * prob_grad, axis=-1, keepdims=True)
     score_grad = (attn_probs * (prob_grad - row_delta)).astype(jnp.bfloat16)
     query_grad = jnp.einsum(
-        "hqk,khd->qhd", score_grad, saved["keys_all"], preferred_element_type=jnp.float32
+        "hqk,khd->hqd", score_grad, saved["keys_all"], preferred_element_type=jnp.float32
     ) * HEAD ** (-0.5)
     key_grad = jnp.einsum(
-        "hqk,qhd->khd", score_grad, saved["queries"], preferred_element_type=jnp.float32
+        "hqk,qhd->hkd", score_grad, saved["queries"], preferred_element_type=jnp.float32
     ) * HEAD ** (-0.5)
-    joined_grad = jnp.concatenate(
-        [
-            query_grad.reshape(row_count, width_all),
-            key_grad.reshape(row_count, width_all),
-            value_grad.reshape(row_count, width_all),
-        ],
-        axis=1,
-    ).astype(jnp.bfloat16)
+    value_grad = jnp.einsum(
+        "hqk,qhd->hkd", saved["probs_low"], mixed_grad, preferred_element_type=jnp.float32
+    )
+    joined_grad = (
+        jnp.stack([query_grad, key_grad, value_grad])
+        .transpose(2, 0, 1, 3)
+        .reshape(row_count, 3 * width_all)
+        .astype(jnp.bfloat16)
+    )
     column_sums = jnp.sum(to_float(joined_grad), axis=0)
     grad_qv_b = jnp.concatenate([column_sums[:width_all], column_sums[2 * width_all :]])
     first_grad = jnp.einsum(

time: 220 us -> 214 us (0.973)
  matrix products: 26.3 us -> 21.6 us
    reshape x3 -> x0, local copies, waits for them, and re-layouts: 5.23 us -> none  [the longest x1 1.75 us: layer_backward(): value_grad.reshape(row_count, width_all)]
    reduce_sum x1, other arithmetic: 2.61 us -> 0.38 us  [layer_backward(): column_sums = jnp.sum(to_float(joined_grad), axis=0)]
    unnamed x107 -> x95, local copies, waits for them, and re-layouts: 8.08 us -> 9.43 us
  transfers between devices with their start and end apart: 9 -> 9, of which waited for: 2 -> 2; matrix products, arithmetic and copies ran while one was open for 14% -> 12% of each run, Pallas kernels for 0% -> 0%
where the time goes in v16:
time: 214 us
  Pallas kernels  156 us (73%)
  local copies, waits for them, and re-layouts  23.6 us (11%)
  matrix products  21.6 us (10%)
  other arithmetic  8.33 us (4%)
  starting transfers between devices  2.56 us (1%)
    pallas_call x1, Pallas kernels, reduce_gradients(): pl.pallas_call(functools.partial(reduce_kernel, n, count, mm), out_shape=...  93 us
    pallas_call x1, Pallas kernels, gather_weights(): pl.pallas_call(functools.partial(gather_kernel, n, count, parts, plane_on...  62.9 us
    unnamed x95, local copies, waits for them, and re-layouts  9.43 us
    dot_general x1, matrix products, layer_forward(): jnp.dot(second_low, fc_weight, preferred_element_type=jnp.float32) + fc_bias  4.89 us
    dot_general x1, matrix products, layer_forward(): jnp.dot(hidden_low, proj_weight, preferred_element_type=jnp.float32)  4.8 us
  transfers between devices with their start and end apart: 9, of which 2 were waited for; matrix products, arithmetic and copies ran while one was open for 12% of the time, Pallas kernels for 0%

profile of v16, /device:TPU:0, one launch (start us, length us, event | category | flops | bytes accessed | tf_op | source)
XLA Modules:
  0.0 213.7 jit_solution(3026305453932701042)
XLA Ops:
  0.7 1.5 concatenate.13.refs_4_
  2.2 62.9 %shard_map.254 = (bf16[8,96,2304]{2,1,0:T(8,128)(2,1)}, bf16[8,96,768]{2,1,0:T(8,128)(2,1)}, bf16[8,96,3072]{2,1,0:T(8,128)(2,1)}, bf16[8,384,768]{2,1,0:T(8,128)(2,1)}, bf16[8,1,1152]{2,1,0:T(2,128)(2,1)}) custom-call(bf16[96,2304]{1,0:T(8,128)(2,1)} %bitcast.102, bf16[96,768]{1,0:T(8,128)(2,1)} %bitcast.104, bf16[96,3072]{1,0:T(8,128)(2,1)} %bitcast.100, ...), custom_call_target="tpu_custom_call" | custom-call | tf_op jit(solution)/shard_map/pallas_call | solution.py:343
  65.1 0.8 copy.69
  65.9 0.7 slice_convert_fusion.2
  67.9 2.7 %fusion = bf16[128,2304]{1,0:T(8,128)(2,1)S(1)} fusion(bf16[768,2304]{1,0:T(8,128)(2,1)} %bitcast.72, f32[2304]{0:T(1024)S(1)} %pad_maximum_fusion, bf16[128,768]{1,0:T(8,128)(2,1)S(1)} %copy-done.1, f32[768]{0:T(1024)S(1)} %reshape.280, f32[768]{0:T(1024)S(1)} %reshape.279, f32[128]{0:T(128)S(1)} %add_rsqrt_fusion.1, f32[128]{0:T(128)S(1)} %broadcast_multiply_fusion.5), kind=kOutput, calls=%fused_computation.3 | convolution fusion | flops 454164480 | bytes 4341760 | tf_op jit(solution)/shard_map/dot_general | solution.py:47
  71.4 0.3 fusion.55
  72.3 0.3 copy-done.2
  72.7 0.4 fusion.56
  73.3 4.9 %fusion.15 = (bf16[3072,128]{0,1:T(8,128)(2,1)}, f32[128,3072]{1,0:T(8,128)S(1)}) fusion(f32[3072]{0:T(1024)S(1)} %reshape.284, bf16[768,3072]{1,0:T(8,128)(2,1)} %bitcast.76, f32[128,768]{1,0:T(8,128)S(1)} %get-tuple-element.72, f32[768]{0:T(1024)S(1)} %reshape.283, f32[768]{0:T(1024)S(1)} %reshape.282, f32[128]{0:T(128)S(1)} %add_rsqrt_fusion, ...), kind=kOutput, calls=%fused_computation.21 | convolution fusion | flops 608403456 | bytes 7490560 | tf_op jit(solution)/shard_map/dot_general | solution.py:69
  78.2 2.6 %convert_reduce_fusion = (f32[3072]{0:T(1024)}, bf16[128,3072]{1,0:T(8,128)(2,1)S(1)}) fusion(f32[128,3072]{1,0:T(8,128)S(1)} %get-tuple-element.76, bf16[3072,768]{1,0:T(8,128)(2,1)S(1)} %bitcast.109, bf16[128,768]{1,0:T(8,128)(2,1)S(1)} %copy-done.17), kind=kOutput, calls=%fused_computation.22 | convolution fusion | flops 612627456 | bytes 7286784 | tf_op jit(solution)/shard_map/td,fd->tf/dot_general | solution.py:100
  80.9 0.5 collective-permute-start.6
  81.4 1.7 fusion.57
  83.1 1.5 multiply_reduce_fusion.1
  84.6 1.5 convert_reduce_fusion.4
  86.1 0.7 copy-done.6
  86.8 1.2 convolution_convert_fusion
  88.1 1.1 copy.52
  89.2 0.4 convolution_bitcast_fusion.1
  89.6 0.3 multiply_reduce_fusion
  90.1 0.4 copy-done.9
  90.5 0.4 fusion.19
  91.1 0.4 convert_reduce_fusion.1
  91.5 0.6 copy-done
  92.1 1.3 fusion.58
  93.4 0.8 fusion.39
  94.3 0.8 copy.56
  95.1 1.5 copy.66
  96.7 0.5 collective-permute-start.3
  97.2 1.1 copy.61.refs_4_
  98.9 0.7 concatenate.16
  99.6 0.5 collective-permute-start.8
  100.2 4.8 %fusion.21 = bf16[128,768]{1,0:T(8,128)(2,1)} fusion(f32[128,768]{1,0:T(8,128)S(1)} %get-tuple-element.72, bf16[3072,768]{1,0:T(8,128)(2,1)} %bitcast.108, f32[128,3072]{1,0:T(8,128)} %copy-done.42, f32[768]{0:T(1024)S(1)} %reshape.285), kind=kOutput, calls=%fused_computation.37 | convolution fusion | flops 607813632 | bytes 6884352 | tf_op jit(solution)/shard_map/dot_general | solution.py:72
  105.0 1.1 copy.57
  106.2 0.5 collective-permute-start.2
  106.7 0.7 broadcast_multiply_fusion.1
  108.2 0.4 copy-done.22
  108.6 0.9 fusion.38
  109.5 0.8 add.133
  110.3 0.6 reshape.278.refs_16_
  111.0 0.6 copy-done.23
  111.7 93.0 %shard_map.255 = (f32[96,2304]{1,0:T(8,128)}, f32[96,768]{1,0:T(8,128)}, f32[96,3072]{1,0:T(8,128)}, f32[384,768]{1,0:T(8,128)}, f32[1,1152]{1,0:T(1,128)}) custom-call(bf16[8,96,128]{2,1,0:T(8,128)(2,1)} %bitcast.21.refs_0_, bf16[8,96,128]{2,1,0:T(8,128)(2,1)} %bitcast.86, bf16[8,96,128]{2,1,0:T(8,128)(2,1)} %bitcast.99, bf16[8,384,128]{2,1,0:T(8,128)(2,1)} %bitcast.83, ...), custom_call_target="tpu_custom_call" | custom-call | tf_op jit(solution)/shard_map/pallas_call | solution.py:578
  204.8 1.4 fusion.54
  206.2 1.3 slice.104
  207.5 1.3 slice.108
  208.8 2.1 copy.74
  210.9 0.7 copy.75
  211.6 1.0 copy.76
  212.7 1.0 copy.77
  (143 shorter events, 5.2 us)
Async XLA Ops:
  0.6 66.4 %copy-start.1 = (bf16[128,768]{1,0:T(8,128)(2,1)S(1)}, bf16[128,768]{1,0:T(8,128)(2,1)}, u32[]{:S(2)}) copy-start(bf16[128,768]{1,0:T(8,128)(2,1)} %param.15) | copy-start | bytes 589828
  70.8 1.4 copy-start.12
  71.0 1.3 copy-start.8
  71.3 1.0 copy-start.10
  71.4 1.3 copy-start.2
  72.0 1.4 copy-start.31
  72.3 33.8 %copy-start.5 = (bf16[12,64,128]{2,1,0:T(8,128)(2,1)}, bf16[12,64,128]{2,1,0:T(8,128)(2,1)S(1)}, u32[]{:S(2)}) copy-start(bf16[12,64,128]{2,1,0:T(8,128)(2,1)S(1)} %convolution_convert_fusion.1) | copy-start | bytes 589828
  72.6 5.6 %copy-start.41 = (bf16[8,384,768]{2,1,0:T(8,128)(2,1)S(1)}, bf16[8,384,768]{2,1,0:T(8,128)(2,1)}, u32[]{:S(2)}) copy-start(bf16[8,384,768]{2,1,0:T(8,128)(2,1)} %get-tuple-element.28) | copy-start | bytes 14155780
  73.3 4.9 %copy-start.17 = (bf16[128,768]{1,0:T(8,128)(2,1)S(1)}, bf16[128,768]{1,0:T(8,128)(2,1)}, u32[]{:S(2)}) copy-start(bf16[128,768]{1,0:T(8,128)(2,1)} %refs_7_) | copy-start | bytes 589828
  73.3 8.0 %slice-start = ((s8[4718592]{0:T(1024)(128)(4,1)}), s8[4194304]{0:T(1024)(128)(4,1)S(1)}, s32[]{:S(2)}) async-start(s8[4718592]{0:T(1024)(128)(4,1)} %bitcast.77), calls=%async_computation | async-start | bytes 8388608
  78.2 2.7 %copy-start.42 = (f32[128,3072]{1,0:T(8,128)}, f32[128,3072]{1,0:T(8,128)S(1)}, u32[]{:S(2)}) copy-start(f32[128,3072]{1,0:T(8,128)S(1)} %get-tuple-element.76) | copy-start | bytes 4718596
  78.2 3.1 %slice-start.1 = ((s8[4718592]{0:T(1024)(128)(4,1)}), s8[524288]{0:T(1024)(128)(4,1)S(1)}, s32[]{:S(2)}) async-start(s8[4718592]{0:T(1024)(128)(4,1)} %bitcast.77), calls=%async_computation.1 | async-start | bytes 1048576
  80.9 2.2 %copy-start.4 = (bf16[128,3072]{1,0:T(8,128)(2,1)}, bf16[128,3072]{1,0:T(8,128)(2,1)S(1)}, u32[]{:S(2)}) copy-start(bf16[128,3072]{1,0:T(8,128)(2,1)S(1)} %get-tuple-element.78.refs_6_) | copy-start | bytes 2359300
  80.9 2.2 %copy-start.32 = (f32[768]{0:T(1024)S(1)}, f32[768]{0:T(1024)}, u32[]{:S(2)}) copy-start(f32[768]{0:T(1024)} %copy-done.31) | copy-start | bytes 9220
  80.9 30.8 %collective-permute-start.6 = (bf16[128,3072]{1,0:T(8,128)(2,1)S(1)}, bf16[128,3072]{1,0:T(8,128)(2,1)}, u32[]{:S(2)}, u32[]{:S(2)}) collective-permute-start(bf16[128,3072]{1,0:T(8,128)(2,1)S(1)} %get-tuple-element.78.refs_6_), channel_id=1, source_target_pairs={{0,8},{8,0},{16,24},{24,16},{1,9},{9,1},{17,25},{25,17},{2,10},{10... | collective-permute-start | bytes 2359304 | tf_op jit(solution)/shard_map/ppermute | solution.py:611
  88.1 1.5 copy-start.13
  89.6 0.9 copy-start.9
  89.9 1.0 copy-start.11
  89.9 2.1 copy-start
  92.1 1.3 copy-start.26
  92.1 1.3 copy-start.36
  92.1 1.3 copy-start.38
  94.2 4.4 %copy-start.30 = (f32[768]{0:T(1024)S(1)}, f32[768]{0:T(1024)}, u32[]{:S(2)}) copy-start(f32[768]{0:T(1024)} %get-tuple-element.42) | copy-start | bytes 9220
  94.2 4.4 %copy-start.28 = (f32[768]{0:T(1024)S(1)}, f32[768]{0:T(1024)}, u32[]{:S(2)}) copy-start(f32[768]{0:T(1024)} %get-tuple-element.34) | copy-start | bytes 9220
  94.2 4.5 %copy-start.27 = (f32[768]{0:T(1024)S(1)}, f32[768]{0:T(1024)}, u32[]{:S(2)}) copy-start(f32[768]{0:T(1024)} %get-tuple-element.40) | copy-start | bytes 9220
  94.2 4.6 %copy-start.34 = (f32[3072]{0:T(1024)S(1)}, f32[3072]{0:T(1024)}, u32[]{:S(2)}) copy-start(f32[3072]{0:T(1024)} %get-tuple-element.77) | copy-start | bytes 36868
  94.2 4.6 %copy-start.29 = (f32[768]{0:T(1024)S(1)}, f32[768]{0:T(1024)}, u32[]{:S(2)}) copy-start(f32[768]{0:T(1024)} %get-tuple-element.52) | copy-start | bytes 9220
  95.1 5.0 %copy-start.33 = (f32[8,96]{1,0:T(8,128)S(1)}, f32[8,96]{1,0:T(8,128)}, u32[]{:S(2)}) copy-start(f32[8,96]{1,0:T(8,128)} %get-tuple-element.55) | copy-start | bytes 9220
  95.1 11.2 %collective-permute-start = (bf16[8,96,128]{2,1,0:T(8,128)(2,1)}, bf16[8,96,128]{2,1,0:T(8,128)(2,1)}, u32[]{:S(2)}, u32[]{:S(2)}) collective-permute-start(bf16[8,96,128]{2,1,0:T(8,128)(2,1)} %bitcast.21.refs_0_), channel_id=1, source_target_pairs={{0,8},{8,0},{16,24},{24,16},{1,9},{9,1},{17,25},{25,17},{2,10},{10... | collective-permute-start | bytes 589832 | tf_op jit(solution)/shard_map/ppermute | solution.py:611
  96.6 8.3 %copy-start.3 = (bf16[3072,128]{1,0:T(8,128)(2,1)}, bf16[3072,128]{1,0:T(8,128)(2,1)S(1)}, u32[]{:S(2)}) copy-start(bf16[3072,128]{1,0:T(8,128)(2,1)S(1)} %copy.66) | copy-start | bytes 2359300
  96.7 14.3 %collective-permute-start.3 = (bf16[8,384,128]{2,1,0:T(8,128)(2,1)S(1)}, bf16[8,384,128]{2,1,0:T(8,128)(2,1)}, u32[]{:S(2)}, u32[]{:S(2)}) collective-permute-start(bf16[8,384,128]{2,1,0:T(8,128)(2,1)S(1)} %bitcast.82), channel_id=1, source_target_pairs={{0,8},{8,0},{16,24},{24,16},{1,9},{9,1},{17,25},{25,17},{2,10},{10... | collective-permute-start | bytes 2359304 | tf_op jit(solution)/shard_map/ppermute | solution.py:611
  98.2 12.7 %collective-permute-start.4 = (bf16[128,2304]{1,0:T(8,128)(2,1)}, bf16[128,2304]{1,0:T(8,128)(2,1)}, u32[]{:S(2)}, u32[]{:S(2)}) collective-permute-start(bf16[128,2304]{1,0:T(8,128)(2,1)} %copy.61.refs_4_), channel_id=1, source_target_pairs={{0,8},{8,0},{16,24},{24,16},{1,9},{9,1},{17,25},{25,17},{2,10},{10... | collective-permute-start | bytes 1769480 | tf_op jit(solution)/shard_map/ppermute | solution.py:611
  99.6 6.5 %collective-permute-start.8 = (f32[8,1152]{1,0:T(8,128)}, f32[8,1152]{1,0:T(8,128)}, u32[]{:S(2)}, u32[]{:S(2)}) collective-permute-start(f32[8,1152]{1,0:T(8,128)} %concatenate.16), channel_id=1, source_target_pairs={{0,8},{8,0},{16,24},{24,16},{1,9},{9,1},{17,25},{25,17},{2,10},{10... | collective-permute-start | bytes 110600 | tf_op jit(solution)/shard_map/ppermute | solution.py:611
  100.1 4.8 %copy-start.40 = (f32[128]{0:T(128)S(1)}, f32[128]{0:T(128)}, u32[]{:S(2)}) copy-start(f32[128]{0:T(128)} %get-tuple-element.37) | copy-start | bytes 1540
  100.1 7.5 %copy-start.7 = (bf16[128,768]{1,0:T(8,128)(2,1)S(1)}, bf16[128,768]{1,0:T(8,128)(2,1)}, u32[]{:S(2)}) copy-start(bf16[128,768]{1,0:T(8,128)(2,1)} %copy-done.6) | copy-start | bytes 589828
  100.2 7.7 %copy-start.18 = (bf16[128,768]{1,0:T(8,128)(2,1)S(1)}, bf16[128,768]{1,0:T(8,128)(2,1)}, u32[]{:S(2)}) copy-start(bf16[128,768]{1,0:T(8,128)(2,1)} %refs_7_) | copy-start | bytes 589828
  100.2 8.4 %copy-start.14 = (f32[128,768]{1,0:T(8,128)S(1)}, f32[128,768]{1,0:T(8,128)}, u32[]{:S(2)}) copy-start(f32[128,768]{1,0:T(8,128)} %get-tuple-element.44) | copy-start | bytes 1179652
  106.1 4.9 %copy-start.19 = (bf16[768,128]{1,0:T(8,128)(2,1)}, bf16[768,128]{1,0:T(8,128)(2,1)S(1)}, u32[]{:S(2)}) copy-start(bf16[768,128]{1,0:T(8,128)(2,1)S(1)} %copy.57) | copy-start | bytes 589828
  106.1 1.5 collective-permute-start.1
  106.2 1.7 collective-permute-start.2
  107.6 3.4 %copy-start.21 = (bf16[8,96,128]{2,1,0:T(8,128)(2,1)}, bf16[8,96,128]{2,1,0:T(8,128)(2,1)S(1)}, u32[]{:S(2)}) copy-start(bf16[8,96,128]{2,1,0:T(8,128)(2,1)S(1)} %collective-permute-done.1.refs_9_) | copy-start | bytes 589828
  107.6 3.3 %collective-permute-start.5 = (bf16[128,768]{1,0:T(8,128)(2,1)S(1)}, bf16[128,768]{1,0:T(8,128)(2,1)S(1)}, u32[]{:S(2)}, u32[]{:S(2)}) collective-permute-start(bf16[128,768]{1,0:T(8,128)(2,1)S(1)} %copy-done.7), channel_id=1, source_target_pairs={{0,8},{8,0},{16,24},{24,16},{1,9},{9,1},{17,25},{25,17},{2,10},{10... | collective-permute-start | bytes 589832 | tf_op jit(solution)/shard_map/ppermute | solution.py:611
  107.9 0.7 copy-start.22
  107.9 3.1 %collective-permute-start.7 = (bf16[128,768]{1,0:T(8,128)(2,1)S(1)}, bf16[128,768]{1,0:T(8,128)(2,1)S(1)}, u32[]{:S(2)}, u32[]{:S(2)}) collective-permute-start(bf16[128,768]{1,0:T(8,128)(2,1)S(1)} %copy-done.18), channel_id=1, source_target_pairs={{0,8},{8,0},{16,24},{24,16},{1,9},{9,1},{17,25},{25,17},{2,10},{10... | collective-permute-start | bytes 589832 | tf_op jit(solution)/shard_map/ppermute | solution.py:611
  111.0 0.7 copy-start.24
  204.8 6.2 %copy-start.20 = (f32[96,768]{1,0:T(8,128)S(1)}, f32[96,768]{1,0:T(8,128)}, u32[]{:S(2)}) copy-start(f32[96,768]{1,0:T(8,128)} %get-tuple-element.31) | copy-start | bytes 884740
  204.8 6.9 %copy-start.16 = (f32[96,3072]{1,0:T(8,128)S(1)}, f32[96,3072]{1,0:T(8,128)}, u32[]{:S(2)}) copy-start(f32[96,3072]{1,0:T(8,128)} %get-tuple-element.32) | copy-start | bytes 3538948
  210.9 1.7 copy-start.15
  (6 other events, 3.6 us)

commit v17 on v16

--- a/solution.py
+++ b/solution.py
@@ -344,7 +344,7 @@
         functools.partial(gather_kernel, n, count, parts, plane_only, first_core),
         out_shape=[jax.ShapeDtypeStruct((n,) + a.shape, a.dtype) for a in locals_],
         in_specs=[pl.BlockSpec(memory_space=pl.ANY)] * count,
-        out_specs=[pl.BlockSpec(memory_space=pl.ANY)] * count,
+        out_specs=[pl.BlockSpec(memory_space=pltpu.VMEM)] * count,
         scratch_shapes=[
             dma((steps, pieces)),
             dma((steps, pieces)),
@@ -355,7 +355,9 @@
             dma((steps, pieces)),
             dma((steps, pieces)),
         ],
-        compiler_params=pltpu.CompilerParams(collective_id=0, has_side_effects=True),
+        compiler_params=pltpu.CompilerParams(
+            collective_id=0, has_side_effects=True, vmem_limit_bytes=40 * 1024 * 1024
+        ),
     )(*locals_)
 
 

time: 214 us -> 242 us (1.13)
  local copies, waits for them, and re-layouts: 23.6 us -> 39.3 us
  matrix products: 21.6 us -> 28.1 us
  other arithmetic: 8.33 us -> 12.1 us
    unnamed x95 -> x129, local copies, waits for them, and re-layouts: 9.43 us -> 15.2 us
    convert_element_type x7, local copies, waits for them, and re-layouts: 0.44 us -> 4.97 us  [to_float(): return value.astype(jnp.float32)]
  transfers between devices with their start and end apart: 9 -> 9, of which waited for: 2 -> 2; matrix products, arithmetic and copies ran while one was open for 12% -> 11% of each run, Pallas kernels for 0% -> 0%
where the time goes in v17:
time: 242 us; the launch traced here: 241 us
  Pallas kernels  157 us (65%)
  local copies, waits for them, and re-layouts  39.3 us (16%)
  matrix products  28.1 us (12%)
  other arithmetic  12.1 us (5%)
  starting transfers between devices  2.62 us (1%)
    pallas_call x1, Pallas kernels, reduce_gradients(): pl.pallas_call(functools.partial(reduce_kernel, n, count, mm), out_shape=...  93 us
    pallas_call x1, Pallas kernels, gather_weights(): pl.pallas_call(functools.partial(gather_kernel, n, count, parts, plane_on...  64.1 us
    unnamed x129, local copies, waits for them, and re-layouts  15.2 us
    convert_element_type x7, local copies, waits for them, and re-layouts, to_float(): return value.astype(jnp.float32)  4.97 us
    dot_general x1, matrix products, layer_forward(): jnp.dot(hidden_low, proj_weight, preferred_element_type=jnp.float32)  4.85 us
  transfers between devices with their start and end apart: 9, of which 2 were waited for; matrix products, arithmetic and copies ran while one was open for 11% of the time, Pallas kernels for 0%

profile of v17, /device:TPU:0, one launch (start us, length us, event | category | flops | bytes accessed | tf_op | source)
XLA Modules:
  0.0 241.0 jit_solution(2979604158323205743)
XLA Ops:
  0.6 0.9 concatenate.13.refs_4_
  1.5 1.1 copy-done.3
  2.6 1.1 copy-done.4
  3.7 1.0 copy-done.5
  4.7 0.9 copy-done.6
  5.6 64.1 %shard_map.254 = (bf16[8,96,2304]{2,1,0:T(8,128)(2,1)S(1)}, bf16[8,96,768]{2,1,0:T(8,128)(2,1)S(1)}, bf16[8,96,3072]{2,1,0:T(8,128)(2,1)S(1)}, bf16[8,384,768]{2,1,0:T(8,128)(2,1)}, bf16[8,1,1152]{2,1,0:T(2,128)(2,1)S(1)}) custom-call(bf16[96,2304]{1,0:T(8,128)(2,1)S(1)} %bitcast.82, bf16[96,768]{1,0:T(8,128)(2,1)S(1)} %bitcast.83, ...), custom_call_target="tpu_custom_call" | custom-call | tf_op jit(solution)/shard_map/pallas_call | solution.py:343
  69.7 2.2 copy-done
  71.9 1.0 copy-done.1
  74.3 1.3 reshape.281
  76.3 0.8 slice.89
  77.0 1.4 slice.87
  78.5 0.8 reshape.279
  79.2 1.0 convert_reduce_fusion.2
  80.3 1.1 fusion.40
  82.1 1.6 fusion
  83.8 0.8 fusion.51
  84.6 1.7 copy.48
  86.4 1.7 copy.49
  88.1 1.7 copy.50
  89.9 1.4 fusion.55
  91.3 0.9 copy-done.7
  92.3 1.3 reshape.284
  94.3 0.7 reshape.282
  95.0 1.6 convolution_convert_fusion.1
  96.7 1.5 fusion.56
  98.5 4.7 %fusion.15 = (bf16[3072,128]{0,1:T(8,128)(2,1)}, f32[128,3072]{1,0:T(8,128)S(1)}) fusion(f32[3072]{0:T(1024)S(1)} %copy-done.49, bf16[768,3072]{1,0:T(8,128)(2,1)} %bitcast.74, f32[128,768]{1,0:T(8,128)S(1)} %get-tuple-element.72, f32[768]{0:T(1024)S(1)} %copy-done.45, f32[768]{0:T(1024)S(1)} %reshape.282, f32[128]{0:T(128)S(1)} %add_rsqrt_fusion, ...), kind=kOutput, calls=%fused_computation.21 | convolution fusion | flops 608403456 | bytes 7490560 | tf_op jit(solution)/shard_map/dot_general | solution.py:69
  103.1 3.5 %convert_reduce_fusion = (f32[3072]{0:T(1024)}, bf16[128,3072]{1,0:T(8,128)(2,1)}) fusion(f32[128,3072]{1,0:T(8,128)S(1)} %get-tuple-element.76, bf16[3072,768]{1,0:T(8,128)(2,1)S(1)} %bitcast.111, bf16[128,768]{1,0:T(8,128)(2,1)S(1)} %copy-done.28), kind=kOutput, calls=%fused_computation.22 | convolution fusion | flops 612627456 | bytes 7286784 | tf_op jit(solution)/shard_map/td,fd->tf/dot_general | solution.py:100
  107.2 2.8 %fusion.57 = f32[128,768]{1,0:T(8,128)S(1)} fusion(bf16[128,3072]{1,0:T(8,128)(2,1)} %get-tuple-element.78.refs_6_, bf16[768,3072]{1,0:T(8,128)(2,1)S(1)} %bitcast.77), kind=kOutput, calls=%fused_computation.109 | convolution fusion | flops 603979776 | bytes 5898240 | tf_op jit(solution)/shard_map/tf,df->td/dot_general | solution.py:104
  110.0 1.5 multiply_reduce_fusion.1
  111.5 1.6 convert_reduce_fusion.4
  113.7 1.2 convolution_convert_fusion
  114.9 1.7 copy.52
  116.7 1.6 convolution_bitcast_fusion.1
  118.3 1.4 multiply_reduce_fusion
  120.9 1.0 convert_reduce_fusion.1
  121.9 1.3 fusion.58
  123.3 0.8 fusion.39
  127.7 4.9 %fusion.21 = bf16[128,768]{1,0:T(8,128)(2,1)} fusion(f32[128,768]{1,0:T(8,128)S(1)} %copy-done.12, bf16[3072,768]{1,0:T(8,128)(2,1)} %bitcast.110, f32[128,3072]{1,0:T(8,128)} %copy-done.59, f32[768]{0:T(1024)S(1)} %reshape.285), kind=kOutput, calls=%fused_computation.37 | convolution fusion | flops 607813632 | bytes 6884352 | tf_op jit(solution)/shard_map/dot_general | solution.py:72
  132.6 1.1 copy.57
  135.9 0.9 fusion.38
  136.9 0.8 add.133
  139.0 93.0 %shard_map.255 = (f32[96,2304]{1,0:T(8,128)}, f32[96,768]{1,0:T(8,128)}, f32[96,3072]{1,0:T(8,128)}, f32[384,768]{1,0:T(8,128)}, f32[1,1152]{1,0:T(1,128)}) custom-call(bf16[8,96,128]{2,1,0:T(8,128)(2,1)} %bitcast.103, bf16[8,96,128]{2,1,0:T(8,128)(2,1)} %bitcast.89, bf16[8,96,128]{2,1,0:T(8,128)(2,1)} %bitcast.105, bf16[8,384,128]{2,1,0:T(8,128)(2,1)} %bitcast.87, ...), custom_call_target="tpu_custom_call" | custom-call | tf_op jit(solution)/shard_map/pallas_call | solution.py:580
  232.1 1.4 fusion.54
  233.5 1.3 slice.104
  234.8 1.3 slice.108
  236.1 2.1 copy.74
  239.0 1.0 copy.76
  240.0 1.0 copy.77
  (177 shorter events, 14.0 us)
Async XLA Ops:
  69.7 2.2 copy-start
  78.5 5.3 %copy-start.39 = (f32[768]{0:T(1024)}, f32[768]{0:T(1024)S(1)}, u32[]{:S(2)}) copy-start(f32[768]{0:T(1024)S(1)} %reshape.280) | copy-start | bytes 9220
  80.3 3.5 %copy-start.50 = (f32[128]{0:T(128)}, f32[128]{0:T(128)S(1)}, u32[]{:S(2)}) copy-start(f32[128]{0:T(128)S(1)} %broadcast_multiply_fusion.5) | copy-start | bytes 1540
  81.4 2.4 copy-start.53
  83.8 6.1 %copy-start.56 = (s32[128]{0:T(128)S(1)}, s32[128]{0:T(128)}, u32[]{:S(2)}) copy-start(s32[128]{0:T(128)} %param.16) | copy-start | bytes 1540
  95.0 3.4 %copy-start.45 = (f32[768]{0:T(1024)S(1)}, f32[768]{0:T(1024)}, u32[]{:S(2)}) copy-start(f32[768]{0:T(1024)} %reshape.283) | copy-start | bytes 9220
  95.0 3.4 %copy-start.49 = (f32[3072]{0:T(1024)S(1)}, f32[3072]{0:T(1024)}, u32[]{:S(2)}) copy-start(f32[3072]{0:T(1024)} %reshape.284) | copy-start | bytes 36868
  96.6 1.8 copy-start.19
  96.6 6.5 %copy-start.58 = (bf16[8,384,768]{2,1,0:T(8,128)(2,1)S(1)}, bf16[8,384,768]{2,1,0:T(8,128)(2,1)}, u32[]{:S(2)}) copy-start(bf16[8,384,768]{2,1,0:T(8,128)(2,1)} %get-tuple-element.28) | copy-start | bytes 14155780
  98.2 13.3 %copy-start.11 = (f32[128,768]{1,0:T(8,128)}, f32[128,768]{1,0:T(8,128)S(1)}, u32[]{:S(2)}) copy-start(f32[128,768]{1,0:T(8,128)S(1)} %get-tuple-element.72) | copy-start | bytes 1179652
  98.4 4.7 %copy-start.28 = (bf16[128,768]{1,0:T(8,128)(2,1)S(1)}, bf16[128,768]{1,0:T(8,128)(2,1)}, u32[]{:S(2)}) copy-start(bf16[128,768]{1,0:T(8,128)(2,1)} %refs_7_) | copy-start | bytes 589828
  98.4 8.7 %slice-start = ((s8[4718592]{0:T(1024)(128)(4,1)}), s8[4194304]{0:T(1024)(128)(4,1)S(1)}, s32[]{:S(2)}) async-start(s8[4718592]{0:T(1024)(128)(4,1)} %bitcast.75), calls=%async_computation | async-start | bytes 8388608
  103.1 3.5 %copy-start.59 = (f32[128,3072]{1,0:T(8,128)}, f32[128,3072]{1,0:T(8,128)S(1)}, u32[]{:S(2)}) copy-start(f32[128,3072]{1,0:T(8,128)S(1)} %get-tuple-element.76) | copy-start | bytes 4718596
  103.1 4.0 %slice-start.1 = ((s8[4718592]{0:T(1024)(128)(4,1)}), s8[524288]{0:T(1024)(128)(4,1)S(1)}, s32[]{:S(2)}) async-start(s8[4718592]{0:T(1024)(128)(4,1)} %bitcast.75), calls=%async_computation.1 | async-start | bytes 1048576
  106.7 32.3 %collective-permute-start.6 = (bf16[128,3072]{1,0:T(8,128)(2,1)}, bf16[128,3072]{1,0:T(8,128)(2,1)}, u32[]{:S(2)}, u32[]{:S(2)}) collective-permute-start(bf16[128,3072]{1,0:T(8,128)(2,1)} %get-tuple-element.78.refs_6_), channel_id=1, source_target_pairs={{0,8},{8,0},{16,24},{24,16},{1,9},{9,1},{17,25},{25,17},{2,10},{10... | collective-permute-start | bytes 2359304 | tf_op jit(solution)/shard_map/ppermute | solution.py:613
  124.1 1.7 copy-start.46
  124.1 2.2 copy-start.41
  124.2 8.3 %copy-start.30 = (bf16[768,128]{1,0:T(8,128)(2,1)}, bf16[768,128]{1,0:T(8,128)(2,1)S(1)}, u32[]{:S(2)}) copy-start(bf16[768,128]{1,0:T(8,128)(2,1)S(1)} %copy.56) | copy-start | bytes 589828
  124.3 1.9 copy-start.44
  124.3 1.9 copy-start.42
  124.3 2.1 copy-start.48
  124.3 2.1 copy-start.43
  124.3 3.2 %copy-start.47 = (f32[8,96]{1,0:T(8,128)S(1)}, f32[8,96]{1,0:T(8,128)}, u32[]{:S(2)}) copy-start(f32[8,96]{1,0:T(8,128)} %get-tuple-element.55) | copy-start | bytes 9220
  124.3 3.3 %copy-start.12 = (f32[128,768]{1,0:T(8,128)S(1)}, f32[128,768]{1,0:T(8,128)}, u32[]{:S(2)}) copy-start(f32[128,768]{1,0:T(8,128)} %copy-done.11) | copy-start | bytes 1179652
  124.3 9.6 %collective-permute-start = (bf16[8,96,128]{2,1,0:T(8,128)(2,1)S(1)}, bf16[8,96,128]{2,1,0:T(8,128)(2,1)}, u32[]{:S(2)}, u32[]{:S(2)}) collective-permute-start(bf16[8,96,128]{2,1,0:T(8,128)(2,1)S(1)} %bitcast.102), channel_id=1, source_target_pairs={{0,8},{8,0},{16,24},{24,16},{1,9},{9,1},{17,25},{25,17},{2,10},{10... | collective-permute-start | bytes 589832 | tf_op jit(solution)/shard_map/ppermute | solution.py:613
  124.9 7.7 %copy-start.17 = (bf16[3072,128]{1,0:T(8,128)(2,1)}, bf16[3072,128]{1,0:T(8,128)(2,1)S(1)}, u32[]{:S(2)}) copy-start(bf16[3072,128]{1,0:T(8,128)(2,1)S(1)} %copy.66) | copy-start | bytes 2359300
  124.9 13.4 %collective-permute-start.3 = (bf16[8,384,128]{2,1,0:T(8,128)(2,1)S(1)}, bf16[8,384,128]{2,1,0:T(8,128)(2,1)}, u32[]{:S(2)}, u32[]{:S(2)}) collective-permute-start(bf16[8,384,128]{2,1,0:T(8,128)(2,1)S(1)} %bitcast.86), channel_id=1, source_target_pairs={{0,8},{8,0},{16,24},{24,16},{1,9},{9,1},{17,25},{25,17},{2,10},{10... | collective-permute-start | bytes 2359304 | tf_op jit(solution)/shard_map/ppermute | solution.py:613
  125.6 7.0 %copy-start.18 = (bf16[128,2304]{1,0:T(8,128)(2,1)}, bf16[128,2304]{1,0:T(8,128)(2,1)S(1)}, u32[]{:S(2)}) copy-start(bf16[128,2304]{1,0:T(8,128)(2,1)S(1)} %copy.61.refs_4_) | copy-start | bytes 1769476
  125.6 12.7 %collective-permute-start.4 = (bf16[128,2304]{1,0:T(8,128)(2,1)S(1)}, bf16[128,2304]{1,0:T(8,128)(2,1)}, u32[]{:S(2)}, u32[]{:S(2)}) collective-permute-start(bf16[128,2304]{1,0:T(8,128)(2,1)S(1)} %copy.61.refs_4_), channel_id=1, source_target_pairs={{0,8},{8,0},{16,24},{24,16},{1,9},{9,1},{17,25},{25,17},{2,10},{10... | collective-permute-start | bytes 1769480 | tf_op jit(solution)/shard_map/ppermute | solution.py:613
  127.2 6.5 %collective-permute-start.8 = (f32[8,1152]{1,0:T(8,128)}, f32[8,1152]{1,0:T(8,128)}, u32[]{:S(2)}, u32[]{:S(2)}) collective-permute-start(f32[8,1152]{1,0:T(8,128)} %concatenate.16), channel_id=1, source_target_pairs={{0,8},{8,0},{16,24},{24,16},{1,9},{9,1},{17,25},{25,17},{2,10},{10... | collective-permute-start | bytes 110600 | tf_op jit(solution)/shard_map/ppermute | solution.py:613
  127.6 4.9 %copy-start.57 = (f32[128]{0:T(128)S(1)}, f32[128]{0:T(128)}, u32[]{:S(2)}) copy-start(f32[128]{0:T(128)} %get-tuple-element.37) | copy-start | bytes 1540
  127.6 6.1 %copy-start.20 = (bf16[12,64,128]{2,1,0:T(8,128)(2,1)S(1)}, bf16[12,64,128]{2,1,0:T(8,128)(2,1)}, u32[]{:S(2)}) copy-start(bf16[12,64,128]{2,1,0:T(8,128)(2,1)} %copy-done.19) | copy-start | bytes 589828
  127.6 7.6 %copy-start.22 = (bf16[128,768]{1,0:T(8,128)(2,1)S(1)}, bf16[128,768]{1,0:T(8,128)(2,1)}, u32[]{:S(2)}) copy-start(bf16[128,768]{1,0:T(8,128)(2,1)} %copy-done.21) | copy-start | bytes 589828
  127.6 7.9 %copy-start.29 = (bf16[128,768]{1,0:T(8,128)(2,1)S(1)}, bf16[128,768]{1,0:T(8,128)(2,1)}, u32[]{:S(2)}) copy-start(bf16[128,768]{1,0:T(8,128)(2,1)} %refs_7_) | copy-start | bytes 589828
  127.7 8.2 %copy-start.10 = (bf16[128,768]{1,0:T(8,128)(2,1)S(1)}, bf16[128,768]{1,0:T(8,128)(2,1)}, u32[]{:S(2)}) copy-start(bf16[128,768]{1,0:T(8,128)(2,1)} %param.15) | copy-start | bytes 589828
  127.7 8.2 %copy-start.16 = (f32[128,768]{1,0:T(8,128)S(1)}, f32[128,768]{1,0:T(8,128)}, u32[]{:S(2)}) copy-start(f32[128,768]{1,0:T(8,128)} %copy-done.15) | copy-start | bytes 1179652
  127.7 8.2 %copy-start.25 = (f32[128,768]{1,0:T(8,128)S(1)}, f32[128,768]{1,0:T(8,128)}, u32[]{:S(2)}) copy-start(f32[128,768]{1,0:T(8,128)} %get-tuple-element.44) | copy-start | bytes 1179652
  127.7 8.2 %copy-start.52 = (f32[128]{0:T(128)S(1)}, f32[128]{0:T(128)}, u32[]{:S(2)}) copy-start(f32[128]{0:T(128)} %copy-done.50) | copy-start | bytes 1540
  127.7 8.2 %copy-start.55 = (f32[128]{0:T(128)S(1)}, f32[128]{0:T(128)}, u32[]{:S(2)}) copy-start(f32[128]{0:T(128)} %copy-done.53) | copy-start | bytes 1540
  133.7 5.3 %copy-start.31 = (bf16[768,128]{1,0:T(8,128)(2,1)}, bf16[768,128]{1,0:T(8,128)(2,1)S(1)}, u32[]{:S(2)}) copy-start(bf16[768,128]{1,0:T(8,128)(2,1)S(1)} %copy.57) | copy-start | bytes 589828
  133.7 1.5 collective-permute-start.1
  133.9 1.6 collective-permute-start.2
  135.2 3.0 %collective-permute-start.5 = (bf16[128,768]{1,0:T(8,128)(2,1)S(1)}, bf16[128,768]{1,0:T(8,128)(2,1)S(1)}, u32[]{:S(2)}, u32[]{:S(2)}) collective-permute-start(bf16[128,768]{1,0:T(8,128)(2,1)S(1)} %copy-done.22), channel_id=1, source_target_pairs={{0,8},{8,0},{16,24},{24,16},{1,9},{9,1},{17,25},{25,17},{2,10},{10... | collective-permute-start | bytes 589832 | tf_op jit(solution)/shard_map/ppermute | solution.py:613
  135.5 3.5 %copy-start.35 = (bf16[8,96,128]{2,1,0:T(8,128)(2,1)}, bf16[8,96,128]{2,1,0:T(8,128)(2,1)S(1)}, u32[]{:S(2)}) copy-start(bf16[8,96,128]{2,1,0:T(8,128)(2,1)S(1)} %collective-permute-done.2.refs_10_) | copy-start | bytes 589828
  135.5 2.8 %collective-permute-start.7 = (bf16[128,768]{1,0:T(8,128)(2,1)S(1)}, bf16[128,768]{1,0:T(8,128)(2,1)S(1)}, u32[]{:S(2)}, u32[]{:S(2)}) collective-permute-start(bf16[128,768]{1,0:T(8,128)(2,1)S(1)} %copy-done.29), channel_id=1, source_target_pairs={{0,8},{8,0},{16,24},{24,16},{1,9},{9,1},{17,25},{25,17},{2,10},{10... | collective-permute-start | bytes 589832 | tf_op jit(solution)/shard_map/ppermute | solution.py:613
  232.1 6.2 %copy-start.33 = (f32[96,768]{1,0:T(8,128)S(1)}, f32[96,768]{1,0:T(8,128)}, u32[]{:S(2)}) copy-start(f32[96,768]{1,0:T(8,128)} %get-tuple-element.31) | copy-start | bytes 884740
  232.1 6.9 %copy-start.27 = (f32[96,3072]{1,0:T(8,128)S(1)}, f32[96,3072]{1,0:T(8,128)}, u32[]{:S(2)}) copy-start(f32[96,3072]{1,0:T(8,128)} %get-tuple-element.32) | copy-start | bytes 3538948
  238.3 1.7 copy-start.26
  (23 other events, 26.4 us)

commit v18 on v16

--- a/solution.py
+++ b/solution.py
@@ -68,9 +68,6 @@
     second_low = second_norm.astype(jnp.bfloat16)
     hidden_pre = jnp.dot(second_low, fc_weight, preferred_element_type=jnp.float32) + fc_bias
     hidden_low = jax.nn.gelu(hidden_pre, approximate=True).astype(jnp.bfloat16)
-    result = (
-        after_attn + jnp.dot(hidden_low, proj_weight, preferred_element_type=jnp.float32) + proj_bias
-    )
     return dict(
         normed_one=normed_one,
         inverse_one=inverse_one,
@@ -86,7 +83,7 @@
         second_low=second_low,
         hidden_pre=hidden_pre,
         hidden_low=hidden_low,
-        result=result,
+        after_attn=after_attn,
     )
 
 
@@ -378,11 +375,16 @@
     dyp = refs[3 * mm : 4 * mm]
     contrib = (None,) * mm + refs[4 * mm : 3 * mm + count]
     refs = refs[3 * mm + count :]
+    hidden, residual, bias, weight = refs[:4]
+    refs = refs[4:]
     out = refs[:count]
-    land, send, other, own, xland, stage, xsend = (refs[count + i * count : count + (i + 1) * count] for i in range(7))
+    tokens = refs[count]
+    refs = refs[count + 1 :]
+    land, send, other, own, xland, stage, xsend = (refs[i * count : (i + 1) * count] for i in range(7))
     (load_sem, own_sem, ring_send, ring_recv, pair_send, pair_recv, x_send, x_recv, back_send, back_recv) = refs[
-        8 * count :
+        7 * count : 7 * count + 10
     ]
+    weight_vmem, weight_sem = refs[7 * count + 10 :]
     rep = lax.axis_index("rep")
     shard = lax.axis_index("shard")
     core = rep % 2
@@ -449,6 +451,8 @@
 
         lax.fori_loop(0, dy[w].shape[1] // width, body, 0)
 
+    weight_copy = pltpu.make_async_copy(weight, weight_vmem, weight_sem)
+    weight_copy.start()
     for w in range(mm, count):
         load_own(w).start()
     for k in range(1, steps + 1):
@@ -546,6 +550,17 @@
         for w in by_rank:
             if steps + CHAIN_LAG * rank[w] == t:
                 arrive(w)
+        if t == 0:
+            weight_copy.wait()
+            width = 256
+
+            def project(i, carry):
+                window = pl.ds(pl.multiple_of(i * width, width), width)
+                product = jnp.dot(hidden[...], weight_vmem[:, window], preferred_element_type=jnp.float32)
+                tokens[:, window] = (residual[:, window] + product + bias[:, window]).astype(tokens.dtype)
+                return carry
+
+            lax.fori_loop(0, weight_vmem.shape[1] // width, project, 0)
     for w in range(count):
         pl.when(owner(w))(lambda w=w: total(w))
 
@@ -567,7 +582,7 @@
             guarded(carried(k, w), lambda k=k, w=w: ring_copy(k, w, target).wait_send())
 
 
-def reduce_gradients(pairs_t, contribs, n):
+def reduce_gradients(pairs_t, contribs, head, n):
     mm = len(pairs_t)
     count = mm + len(contribs)
     steps = n // 2
@@ -577,10 +592,13 @@
     dma = pltpu.SemaphoreType.DMA
     return pl.pallas_call(
         functools.partial(reduce_kernel, n, count, mm),
-        out_shape=[jax.ShapeDtypeStruct(b, jnp.float32) for b in blocks],
+        out_shape=[jax.ShapeDtypeStruct(b, jnp.float32) for b in blocks]
+        + [jax.ShapeDtypeStruct(head[1].shape, jnp.bfloat16)],
         in_specs=[pl.BlockSpec(memory_space=pltpu.VMEM)] * (4 * mm)
-        + [pl.BlockSpec(memory_space=pl.ANY)] * len(contribs),
-        out_specs=[pl.BlockSpec(memory_space=pltpu.VMEM)] * count,
+        + [pl.BlockSpec(memory_space=pl.ANY)] * len(contribs)
+        + [pl.BlockSpec(memory_space=pltpu.VMEM)] * 3
+        + [pl.BlockSpec(memory_space=pl.ANY)],
+        out_specs=[pl.BlockSpec(memory_space=pltpu.VMEM)] * (count + 1),
         scratch_shapes=[vmem((steps,) + b, t) for b, t in zip(blocks, ring_types)]
         + [vmem((steps,) + b, t) for b, t in zip(blocks, ring_types)]
         + [vmem(b, t) for b, t in zip(blocks, ring_types)]
@@ -599,11 +617,13 @@
             dma((count,)),
             dma((count,)),
             dma((count,)),
+            pltpu.VMEM(head[3].shape, head[3].dtype),
+            dma(()),
         ],
         compiler_params=pltpu.CompilerParams(
             collective_id=1, has_side_effects=True, vmem_limit_bytes=62 * 1024 * 1024
         ),
-    )(*[p[0] for p in pairs_t], *[p[1] for p in pairs_t], *[p[2] for p in pairs_t], *[p[3] for p in pairs_t], *contribs)
+    )(*[p[0] for p in pairs_t], *[p[1] for p in pairs_t], *[p[2] for p in pairs_t], *[p[3] for p in pairs_t], *contribs, *head)
 
 
 def swap_core(value):
@@ -678,7 +698,6 @@
 
     residual = to_float(tokens)
     saved = layer_forward(residual, allowed, small, weights)
-    out_tokens = saved["result"].astype(jnp.bfloat16)
     upstream = to_float(cotangent)
     input_grad, small_grads, pairs = layer_backward(upstream, saved, small, weights)
 
@@ -689,7 +708,8 @@
     for x, dy in pairs:
         rows_t = x.T.reshape(shard, -1, x.shape[0])
         pairs_t.append((rows_t, dy, swap_core(rows_t), swap_core(dy)))
-    totals = reduce_gradients(pairs_t, [small_chip.reshape(shard, 1, -1)], shard)
+    head = (saved["hidden_low"], saved["after_attn"], small[7].reshape(1, -1), weights[3])
+    *totals, out_tokens = reduce_gradients(pairs_t, [small_chip.reshape(shard, 1, -1)], head, shard)
     small_share = totals[4]
     owned = [t[None] for t in totals[:4]]
     small_owned = []

time: 214 us -> 211 us (0.986)
  local copies, waits for them, and re-layouts: 23.6 us -> 20.8 us
    dot_general x1 -> x0, matrix products: 4.8 us -> none  [layer_forward(): jnp.dot(hidden_low, proj_weight, preferred_element_type=jnp.float32)]
    dot_general x1, matrix products: 2.64 us -> 5.54 us  [layer_backward(): jnp.einsum('td,fd->tf', proj_in, proj_weight, preferred_element_type=jnp....]
    convert_element_type x0 -> x1, other arithmetic: none -> 2.78 us  [layer_forward(): hidden_low = jax.nn.gelu(hidden_pre, approximate=True).astype(jnp.bfloat16)]
    reduce_sum x2 -> x0, other arithmetic: 2.3 us -> none  [norm_back(): jnp.sum(upstream * normed, axis=0)]
    unnamed x95 -> x100, local copies, waits for them, and re-layouts: 9.43 us -> 10.4 us
  transfers between devices with their start and end apart: 9 -> 9, of which waited for: 2 -> 1; matrix products, arithmetic and copies ran while one was open for 12% -> 6% of each run, Pallas kernels for 0% -> 0%
where the time goes in v18:
time: 211 us
  Pallas kernels  156 us (74%)
  local copies, waits for them, and re-layouts  20.8 us (10%)
  matrix products  20.5 us (10%)
  other arithmetic  8.38 us (4%)
  starting transfers between devices  2.7 us (1%)
    pallas_call x1, Pallas kernels, reduce_gradients(): pl.pallas_call(functools.partial(reduce_kernel, n, count, mm), out_shape=...  93.5 us
    pallas_call x1, Pallas kernels, gather_weights(): pl.pallas_call(functools.partial(gather_kernel, n, count, parts, plane_on...  62.9 us
    unnamed x100, local copies, waits for them, and re-layouts  10.4 us
    dot_general x1, matrix products, layer_backward(): jnp.einsum('td,fd->tf', proj_in, proj_weight, preferred_element_type=jnp....  5.54 us
    dot_general x1, matrix products, layer_forward(): jnp.dot(second_low, fc_weight, preferred_element_type=jnp.float32) + fc_bias  4.66 us
  transfers between devices with their start and end apart: 9, of which 1 were waited for; matrix products, arithmetic and copies ran while one was open for 6% of the time, Pallas kernels for 0%

profile of v18, /device:TPU:0, one launch (start us, length us, event | category | flops | bytes accessed | tf_op | source)
XLA Modules:
  0.0 210.8 jit_solution(1033059911618956756)
XLA Ops:
  0.7 1.5 concatenate.13.refs_4_
  2.2 62.9 %shard_map.254 = (bf16[8,96,2304]{2,1,0:T(8,128)(2,1)}, bf16[8,96,768]{2,1,0:T(8,128)(2,1)}, bf16[8,96,3072]{2,1,0:T(8,128)(2,1)}, bf16[8,384,768]{2,1,0:T(8,128)(2,1)}, bf16[8,1,1152]{2,1,0:T(2,128)(2,1)}) custom-call(bf16[96,2304]{1,0:T(8,128)(2,1)} %bitcast.105, bf16[96,768]{1,0:T(8,128)(2,1)} %bitcast.107, bf16[96,3072]{1,0:T(8,128)(2,1)} %bitcast.103, ...), custom_call_target="tpu_custom_call" | custom-call | tf_op jit(solution)/shard_map/pallas_call | solution.py:340
  65.1 0.8 copy.69
  65.9 0.7 slice_convert_fusion.2
  67.6 0.2 copy-done.38
  67.8 2.7 %fusion = bf16[128,2304]{1,0:T(8,128)(2,1)S(1)} fusion(bf16[768,2304]{1,0:T(8,128)(2,1)} %bitcast.71, f32[2304]{0:T(1024)S(1)} %pad_maximum_fusion, bf16[128,768]{1,0:T(8,128)(2,1)S(1)} %copy-done.2, f32[768]{0:T(1024)S(1)} %reshape.286, f32[768]{0:T(1024)S(1)} %reshape.285, f32[128]{0:T(128)S(1)} %add_rsqrt_fusion.1, f32[128]{0:T(128)S(1)} %broadcast_multiply_fusion.5), kind=kOutput, calls=%fused_computation.3 | convolution fusion | flops 454164480 | bytes 4341760 | tf_op jit(solution)/shard_map/dot_general | solution.py:47
  70.9 0.3 copy-done.42
  71.3 0.3 fusion.45
  72.0 0.2 convolution_convert_fusion.1
  72.3 0.3 copy-done.3
  72.6 0.4 fusion.46
  73.4 4.7 %fusion.15 = (bf16[3072,128]{0,1:T(8,128)(2,1)}, f32[128,3072]{1,0:T(8,128)S(1)}) fusion(f32[3072]{0:T(1024)S(1)} %reshape.290, bf16[768,3072]{1,0:T(8,128)(2,1)} %bitcast.77, f32[128,768]{1,0:T(8,128)S(1)} %get-tuple-element.75.refs_18_, f32[768]{0:T(1024)S(1)} %reshape.289, f32[768]{0:T(1024)S(1)} %reshape.288, f32[128]{0:T(128)S(1)} %add_rsqrt_fusion, ...), kind=kOutput, calls=%fused_computation.21 | convolution fusion | flops 608403456 | bytes 7490560 | tf_op jit(solution)/shard_map/dot_general | solution.py:69
  78.2 5.5 %convert_reduce_fusion = (f32[3072]{0:T(1024)}, bf16[128,3072]{1,0:T(8,128)(2,1)S(1)}) fusion(f32[128,3072]{1,0:T(8,128)S(1)} %get-tuple-element.81, bf16[3072,768]{1,0:T(8,128)(2,1)} %bitcast.75, bf16[128,768]{1,0:T(8,128)(2,1)S(1)} %copy-done.21), kind=kOutput, calls=%fused_computation.23 | convolution fusion | flops 612627456 | bytes 7286784 | tf_op jit(solution)/shard_map/td,fd->tf/dot_general | solution.py:97
  83.8 2.3 %multiply_reduce_fusion.1 = (f32[768]{0:T(1024)}, f32[128]{0:T(128)S(1)}, f32[128]{0:T(128)S(1)}, f32[768]{0:T(1024)}, f32[128,768]{1,0:T(8,128)S(1)}) fusion(f32[128,768]{1,0:T(8,128)S(1)} %get-tuple-element.75.refs_18_, f32[128]{0:T(128)S(1)} %copy-done.44, f32[128]{0:T(128)S(1)} %copy-done.41, f32[768]{0:T(1024)S(1)} %reshape.288, ...), kind=kOutput, calls=%fused_computation.60 | convolution fusion | flops 604862720 | bytes 6302720 | tf_op jit(solution)/shard_map/tf,df->td/dot_general | solution.py:101
  86.1 1.7 convert_reduce_fusion.4
  87.8 0.5 collective-permute-start.5
  88.3 1.5 convolution_convert_fusion
  89.9 0.3 multiply_reduce_fusion
  90.4 0.4 copy-done.8
  90.8 0.2 fusion.18
  91.1 0.4 fusion.19
  91.5 0.4 convolution_bitcast_fusion.1
  91.9 0.4 convert_reduce_fusion.1
  92.2 0.6 copy-done
  92.9 1.5 fusion.30
  94.4 1.0 fusion.33
  96.0 0.5 collective-permute-start.2
  97.1 0.7 concatenate.16
  97.9 0.4 collective-permute-start.6
  98.3 0.4 copy.66
  98.7 0.7 collective-permute-done.8
  99.5 0.4 copy.61.refs_4_
  99.9 0.4 collective-permute-start.7
  100.5 0.3 collective-permute-start.1
  100.9 2.8 %multiply_convert_fusion.refs_17_ = bf16[128,3072]{1,0:T(8,128)(2,1)} fusion(f32[128,3072]{1,0:T(8,128)} %copy-done.13), kind=kLoop, calls=%fused_computation.22 | loop fusion | flops 3538944 | bytes 2359296 | tf_op jit(solution)/shard_map/convert_element_type | solution.py:70
  103.7 0.7 reshape.291.refs_19_
  104.3 0.8 add.118
  105.1 0.6 reshape.284.refs_16_
  105.8 0.9 copy-done.22
  106.7 93.5 %shard_map.255 = (f32[96,2304]{1,0:T(8,128)}, f32[96,768]{1,0:T(8,128)}, f32[96,3072]{1,0:T(8,128)}, f32[384,768]{1,0:T(8,128)}, f32[1,1152]{1,0:T(1,128)}, /*index=5*/bf16[128,768]{1,0:T(8,128)(2,1)}) custom-call(bf16[8,96,128]{2,1,0:T(8,128)(2,1)} %bitcast.100, bf16[8,96,128]{2,1,0:T(8,128)(2,1)} %bitcast.90, bf16[8,96,128]{2,1,0:T(8,128)(2,1)} %bitcast.102, ...), custom_call_target="tpu_custom_call" | custom-call | tf_op jit(solution)/shard_map/pallas_call | solution.py:593
  200.3 1.4 fusion.44
  201.7 1.3 slice.108
  203.0 1.3 slice.104
  204.3 1.6 copy.75
  206.0 2.1 %copy.76 = f32[1,96,2304]{2,1,0:T(8,128)} copy(f32[1,96,2304]{2,1,0:T(8,128)} %bitcast.98) | data formatting | bytes 1769472
  208.1 0.7 copy.77
  208.8 1.0 copy.78
  209.8 1.0 copy.79
  (146 shorter events, 4.3 us)
Async XLA Ops:
  0.6 66.3 %copy-start.2 = (bf16[128,768]{1,0:T(8,128)(2,1)S(1)}, bf16[128,768]{1,0:T(8,128)(2,1)}, u32[]{:S(2)}) copy-start(bf16[128,768]{1,0:T(8,128)(2,1)} %param.15) | copy-start | bytes 589828
  71.2 1.1 copy-start.7
  71.3 1.3 copy-start.3
  71.9 1.1 copy-start.11
  72.3 5.8 %copy-start.9 = (bf16[12,64,128]{2,1,0:T(8,128)(2,1)}, bf16[12,64,128]{2,1,0:T(8,128)(2,1)S(1)}, u32[]{:S(2)}) copy-start(bf16[12,64,128]{2,1,0:T(8,128)(2,1)S(1)} %convolution_convert_fusion.1) | copy-start | bytes 589828
  73.0 13.1 %copy-start.1 = (f32[128,768]{1,0:T(8,128)}, f32[128,768]{1,0:T(8,128)S(1)}, u32[]{:S(2)}) copy-start(f32[128,768]{1,0:T(8,128)S(1)} %get-tuple-element.75.refs_18_) | copy-start | bytes 1179652
  73.0 5.1 %copy-start.40 = (f32[128]{0:T(128)}, f32[128]{0:T(128)S(1)}, u32[]{:S(2)}) copy-start(f32[128]{0:T(128)S(1)} %broadcast_multiply_fusion.4) | copy-start | bytes 1540
  73.3 4.8 %copy-start.43 = (f32[128]{0:T(128)}, f32[128]{0:T(128)S(1)}, u32[]{:S(2)}) copy-start(f32[128]{0:T(128)S(1)} %add_rsqrt_fusion) | copy-start | bytes 1540
  73.4 4.7 %copy-start.32 = (f32[768]{0:T(1024)}, f32[768]{0:T(1024)S(1)}, u32[]{:S(2)}) copy-start(f32[768]{0:T(1024)S(1)} %reshape.289) | copy-start | bytes 9220
  73.4 4.7 %copy-start.21 = (bf16[128,768]{1,0:T(8,128)(2,1)S(1)}, bf16[128,768]{1,0:T(8,128)(2,1)}, u32[]{:S(2)}) copy-start(bf16[128,768]{1,0:T(8,128)(2,1)} %refs_7_) | copy-start | bytes 589828
  73.4 10.3 %slice-start = ((s8[4718592]{0:T(1024)(128)(4,1)}), s8[4194304]{0:T(1024)(128)(4,1)S(1)}, s32[]{:S(2)}) async-start(s8[4718592]{0:T(1024)(128)(4,1)} %bitcast.78), calls=%async_computation | async-start | bytes 8388608
  78.1 5.6 %copy-start.13 = (f32[128,3072]{1,0:T(8,128)}, f32[128,3072]{1,0:T(8,128)S(1)}, u32[]{:S(2)}) copy-start(f32[128,3072]{1,0:T(8,128)S(1)} %get-tuple-element.81) | copy-start | bytes 4718596
  78.1 5.6 %slice-start.1 = ((s8[4718592]{0:T(1024)(128)(4,1)}), s8[524288]{0:T(1024)(128)(4,1)S(1)}, s32[]{:S(2)}) async-start(s8[4718592]{0:T(1024)(128)(4,1)} %bitcast.78), calls=%async_computation.1 | async-start | bytes 1048576
  78.1 5.6 %copy-start.41 = (f32[128]{0:T(128)S(1)}, f32[128]{0:T(128)}, u32[]{:S(2)}) copy-start(f32[128]{0:T(128)} %copy-done.40) | copy-start | bytes 1540
  78.2 5.6 %copy-start.44 = (f32[128]{0:T(128)S(1)}, f32[128]{0:T(128)}, u32[]{:S(2)}) copy-start(f32[128]{0:T(128)} %copy-done.43) | copy-start | bytes 1540
  83.7 14.1 %copy-start.4 = (bf16[128,3072]{1,0:T(8,128)(2,1)}, bf16[128,3072]{1,0:T(8,128)(2,1)S(1)}, u32[]{:S(2)}) copy-start(bf16[128,3072]{1,0:T(8,128)(2,1)S(1)} %get-tuple-element.83.refs_6_) | copy-start | bytes 2359300
  83.7 2.3 %copy-start.33 = (f32[768]{0:T(1024)S(1)}, f32[768]{0:T(1024)}, u32[]{:S(2)}) copy-start(f32[768]{0:T(1024)} %copy-done.32) | copy-start | bytes 9220
  87.8 2.1 copy-start.12
  87.8 12.7 %collective-permute-start.5 = (bf16[128,768]{1,0:T(8,128)(2,1)}, bf16[128,768]{1,0:T(8,128)(2,1)}, u32[]{:S(2)}, u32[]{:S(2)}) collective-permute-start(bf16[128,768]{1,0:T(8,128)(2,1)} %get-tuple-element.45.refs_5_), channel_id=1, source_target_pairs={{0,8},{8,0},{16,24},{24,16},{1,9},{9,1},{17,25},{25,17},{2,10},{10... | collective-permute-start | bytes 589832 | tf_op jit(solution)/shard_map/ppermute | solution.py:631
  90.8 2.0 copy-start
  91.1 1.8 copy-start.37
  91.1 1.8 copy-start.39
  92.8 1.6 copy-start.14
  92.9 1.6 copy-start.27
  94.3 1.4 copy-start.18
  94.3 2.4 %copy-start.31 = (f32[768]{0:T(1024)S(1)}, f32[768]{0:T(1024)}, u32[]{:S(2)}) copy-start(f32[768]{0:T(1024)} %get-tuple-element.44) | copy-start | bytes 9220
  94.4 2.5 %copy-start.30 = (f32[768]{0:T(1024)S(1)}, f32[768]{0:T(1024)}, u32[]{:S(2)}) copy-start(f32[768]{0:T(1024)} %get-tuple-element.55) | copy-start | bytes 9220
  94.4 2.5 %copy-start.29 = (f32[768]{0:T(1024)S(1)}, f32[768]{0:T(1024)}, u32[]{:S(2)}) copy-start(f32[768]{0:T(1024)} %get-tuple-element.36) | copy-start | bytes 9220
  94.4 2.6 %copy-start.28 = (f32[768]{0:T(1024)S(1)}, f32[768]{0:T(1024)}, u32[]{:S(2)}) copy-start(f32[768]{0:T(1024)} %get-tuple-element.43) | copy-start | bytes 9220
  94.4 2.7 %copy-start.35 = (f32[3072]{0:T(1024)S(1)}, f32[3072]{0:T(1024)}, u32[]{:S(2)}) copy-start(f32[3072]{0:T(1024)} %get-tuple-element.82) | copy-start | bytes 36868
  94.4 3.9 %copy-start.17 = (bf16[3072,128]{0,1:T(8,128)(2,1)S(1)}, bf16[3072,128]{0,1:T(8,128)(2,1)}, u32[]{:S(2)}) copy-start(bf16[3072,128]{0,1:T(8,128)(2,1)} %get-tuple-element.80) | copy-start | bytes 2359300
  95.6 4.3 %copy-start.19 = (bf16[768,128]{1,0:T(8,128)(2,1)}, bf16[768,128]{1,0:T(8,128)(2,1)S(1)}, u32[]{:S(2)}) copy-start(bf16[768,128]{1,0:T(8,128)(2,1)S(1)} %copy.48) | copy-start | bytes 589828
  95.6 4.3 %collective-permute-start = (bf16[8,96,128]{2,1,0:T(8,128)(2,1)S(1)}, bf16[8,96,128]{2,1,0:T(8,128)(2,1)}, u32[]{:S(2)}, u32[]{:S(2)}) collective-permute-start(bf16[8,96,128]{2,1,0:T(8,128)(2,1)S(1)} %bitcast.99), channel_id=1, source_target_pairs={{0,8},{8,0},{16,24},{24,16},{1,9},{9,1},{17,25},{25,17},{2,10},{10... | collective-permute-start | bytes 589832 | tf_op jit(solution)/shard_map/ppermute | solution.py:631
  95.9 7.7 %copy-start.20 = (bf16[768,128]{1,0:T(8,128)(2,1)}, bf16[768,128]{1,0:T(8,128)(2,1)S(1)}, u32[]{:S(2)}) copy-start(bf16[768,128]{1,0:T(8,128)(2,1)S(1)} %copy.53) | copy-start | bytes 589828
  95.9 4.6 %copy-start.10 = (bf16[12,64,128]{2,1,0:T(8,128)(2,1)S(1)}, bf16[12,64,128]{2,1,0:T(8,128)(2,1)}, u32[]{:S(2)}) copy-start(bf16[12,64,128]{2,1,0:T(8,128)(2,1)} %copy-done.9) | copy-start | bytes 589828
  96.0 4.4 %collective-permute-start.2 = (bf16[8,96,128]{2,1,0:T(8,128)(2,1)S(1)}, bf16[8,96,128]{2,1,0:T(8,128)(2,1)}, u32[]{:S(2)}, u32[]{:S(2)}) collective-permute-start(bf16[8,96,128]{2,1,0:T(8,128)(2,1)S(1)} %bitcast.101), channel_id=1, source_target_pairs={{0,8},{8,0},{16,24},{24,16},{1,9},{9,1},{17,25},{25,17},{2,10},{10... | collective-permute-start | bytes 589832 | tf_op jit(solution)/shard_map/ppermute | solution.py:631
  97.8 1.6 collective-permute-start.8
  97.9 8.0 %collective-permute-start.6 = (bf16[128,3072]{1,0:T(8,128)(2,1)S(1)}, bf16[128,3072]{1,0:T(8,128)(2,1)}, u32[]{:S(2)}, u32[]{:S(2)}) collective-permute-start(bf16[128,3072]{1,0:T(8,128)(2,1)S(1)} %get-tuple-element.83.refs_6_), channel_id=1, source_target_pairs={{0,8},{8,0},{16,24},{24,16},{1,9},{9,1},{17,25},{25,17},{2,10},{10... | collective-permute-start | bytes 2359304 | tf_op jit(solution)/shard_map/ppermute | solution.py:631
  98.7 5.0 %copy-start.5 = (bf16[3072,128]{1,0:T(8,128)(2,1)}, bf16[3072,128]{1,0:T(8,128)(2,1)S(1)}, u32[]{:S(2)}) copy-start(bf16[3072,128]{1,0:T(8,128)(2,1)S(1)} %copy.66) | copy-start | bytes 2359300
  99.3 4.3 %copy-start.34 = (f32[8,96]{1,0:T(8,128)S(1)}, f32[8,96]{1,0:T(8,128)}, u32[]{:S(2)}) copy-start(f32[8,96]{1,0:T(8,128)} %get-tuple-element.58) | copy-start | bytes 9220
  99.3 7.4 %collective-permute-start.3 = (bf16[8,384,128]{2,1,0:T(8,128)(2,1)S(1)}, bf16[8,384,128]{2,1,0:T(8,128)(2,1)}, u32[]{:S(2)}, u32[]{:S(2)}) collective-permute-start(bf16[8,384,128]{2,1,0:T(8,128)(2,1)S(1)} %bitcast.83), channel_id=1, source_target_pairs={{0,8},{8,0},{16,24},{24,16},{1,9},{9,1},{17,25},{25,17},{2,10},{10... | collective-permute-start | bytes 2359304 | tf_op jit(solution)/shard_map/ppermute | solution.py:631
  99.9 5.9 %copy-start.6 = (bf16[128,2304]{1,0:T(8,128)(2,1)}, bf16[128,2304]{1,0:T(8,128)(2,1)S(1)}, u32[]{:S(2)}) copy-start(bf16[128,2304]{1,0:T(8,128)(2,1)S(1)} %copy.61.refs_4_) | copy-start | bytes 1769476
  99.9 5.8 %collective-permute-start.7 = (bf16[128,768]{1,0:T(8,128)(2,1)}, bf16[128,768]{1,0:T(8,128)(2,1)S(1)}, u32[]{:S(2)}, u32[]{:S(2)}) collective-permute-start(bf16[128,768]{1,0:T(8,128)(2,1)} %refs_7_), channel_id=1, source_target_pairs={{0,8},{8,0},{16,24},{24,16},{1,9},{9,1},{17,25},{25,17},{2,10},{10... | collective-permute-start | bytes 589832 | tf_op jit(solution)/shard_map/ppermute | solution.py:631
  100.4 5.4 %collective-permute-start.4 = (bf16[128,2304]{1,0:T(8,128)(2,1)S(1)}, bf16[128,2304]{1,0:T(8,128)(2,1)S(1)}, u32[]{:S(2)}, u32[]{:S(2)}) collective-permute-start(bf16[128,2304]{1,0:T(8,128)(2,1)S(1)} %copy.61.refs_4_), channel_id=1, source_target_pairs={{0,8},{8,0},{16,24},{24,16},{1,9},{9,1},{17,25},{25,17},{2,10},{10... | collective-permute-start | bytes 1769480 | tf_op jit(solution)/shard_map/ppermute | solution.py:631
  100.5 5.2 %collective-permute-start.1 = (bf16[8,96,128]{2,1,0:T(8,128)(2,1)S(1)}, bf16[8,96,128]{2,1,0:T(8,128)(2,1)S(1)}, u32[]{:S(2)}, u32[]{:S(2)}) collective-permute-start(bf16[8,96,128]{2,1,0:T(8,128)(2,1)S(1)} %bitcast.91), channel_id=1, source_target_pairs={{0,8},{8,0},{16,24},{24,16},{1,9},{9,1},{17,25},{25,17},{2,10},{10... | collective-permute-start | bytes 589832 | tf_op jit(solution)/shard_map/ppermute | solution.py:631
  200.3 7.8 %copy-start.23 = (f32[96,768]{1,0:T(8,128)S(1)}, f32[96,768]{1,0:T(8,128)}, u32[]{:S(2)}) copy-start(f32[96,768]{1,0:T(8,128)} %get-tuple-element.33) | copy-start | bytes 884740
  200.3 8.5 %copy-start.16 = (f32[96,3072]{1,0:T(8,128)S(1)}, f32[96,3072]{1,0:T(8,128)}, u32[]{:S(2)}) copy-start(f32[96,3072]{1,0:T(8,128)} %get-tuple-element.34) | copy-start | bytes 3538948
  208.1 1.7 copy-start.15
  (8 other events, 6.0 us)

commit v19 on v18

--- a/solution.py
+++ b/solution.py
@@ -516,13 +516,12 @@
 
             @pl.when(core == 0)
             def _():
-                add_into(own[w], [own[w], mine, other[w]])
+                add_into(xsend[w], [own[w], mine, other[w]])
 
             @pl.when(core == 1)
             def _():
-                add_into(own[w], [own[w], other[w], mine])
-
-            add_into(xsend[w], [own[w]])
+                add_into(xsend[w], [own[w], other[w], mine])
+
             x_copy(w).start()
 
         pl.when(owner(w))(plane)

time: 211 us -> 211 us (level)
  no operation moved by 1% of the time
where the time goes in v19:
time: 211 us
  Pallas kernels  156 us (74%)
  local copies, waits for them, and re-layouts  20.8 us (10%)
  matrix products  20.5 us (10%)
  other arithmetic  8.38 us (4%)
  starting transfers between devices  2.7 us (1%)
    pallas_call x1, Pallas kernels, reduce_gradients(): pl.pallas_call(functools.partial(reduce_kernel, n, count, mm), out_shape=...  93.4 us
    pallas_call x1, Pallas kernels, gather_weights(): pl.pallas_call(functools.partial(gather_kernel, n, count, parts, plane_on...  62.9 us
    unnamed x100, local copies, waits for them, and re-layouts  10.4 us
    dot_general x1, matrix products, layer_backward(): jnp.einsum('td,fd->tf', proj_in, proj_weight, preferred_element_type=jnp....  5.54 us
    dot_general x1, matrix products, layer_forward(): jnp.dot(second_low, fc_weight, preferred_element_type=jnp.float32) + fc_bias  4.66 us
  transfers between devices with their start and end apart: 9, of which 1 were waited for; matrix products, arithmetic and copies ran while one was open for 6% of the time, Pallas kernels for 0%

profile of v19, /device:TPU:0, one launch (start us, length us, event | category | flops | bytes accessed | tf_op | source)
XLA Modules:
  0.0 210.7 jit_solution(13878205358736459602)
XLA Ops:
  0.7 1.5 concatenate.13.refs_4_
  2.2 62.9 %shard_map.254 = (bf16[8,96,2304]{2,1,0:T(8,128)(2,1)}, bf16[8,96,768]{2,1,0:T(8,128)(2,1)}, bf16[8,96,3072]{2,1,0:T(8,128)(2,1)}, bf16[8,384,768]{2,1,0:T(8,128)(2,1)}, bf16[8,1,1152]{2,1,0:T(2,128)(2,1)}) custom-call(bf16[96,2304]{1,0:T(8,128)(2,1)} %bitcast.105, bf16[96,768]{1,0:T(8,128)(2,1)} %bitcast.107, bf16[96,3072]{1,0:T(8,128)(2,1)} %bitcast.103, ...), custom_call_target="tpu_custom_call" | custom-call | tf_op jit(solution)/shard_map/pallas_call | solution.py:340
  65.1 0.8 copy.69
  65.9 0.7 slice_convert_fusion.2
  67.6 0.2 copy-done.38
  67.8 2.7 %fusion = bf16[128,2304]{1,0:T(8,128)(2,1)S(1)} fusion(bf16[768,2304]{1,0:T(8,128)(2,1)} %bitcast.71, f32[2304]{0:T(1024)S(1)} %pad_maximum_fusion, bf16[128,768]{1,0:T(8,128)(2,1)S(1)} %copy-done.2, f32[768]{0:T(1024)S(1)} %reshape.286, f32[768]{0:T(1024)S(1)} %reshape.285, f32[128]{0:T(128)S(1)} %add_rsqrt_fusion.1, f32[128]{0:T(128)S(1)} %broadcast_multiply_fusion.5), kind=kOutput, calls=%fused_computation.3 | convolution fusion | flops 454164480 | bytes 4341760 | tf_op jit(solution)/shard_map/dot_general | solution.py:47
  70.9 0.3 copy-done.42
  71.3 0.3 fusion.45
  72.0 0.2 convolution_convert_fusion.1
  72.3 0.3 copy-done.3
  72.6 0.4 fusion.46
  73.4 4.7 %fusion.15 = (bf16[3072,128]{0,1:T(8,128)(2,1)}, f32[128,3072]{1,0:T(8,128)S(1)}) fusion(f32[3072]{0:T(1024)S(1)} %reshape.290, bf16[768,3072]{1,0:T(8,128)(2,1)} %bitcast.77, f32[128,768]{1,0:T(8,128)S(1)} %get-tuple-element.75.refs_18_, f32[768]{0:T(1024)S(1)} %reshape.289, f32[768]{0:T(1024)S(1)} %reshape.288, f32[128]{0:T(128)S(1)} %add_rsqrt_fusion, ...), kind=kOutput, calls=%fused_computation.21 | convolution fusion | flops 608403456 | bytes 7490560 | tf_op jit(solution)/shard_map/dot_general | solution.py:69
  78.2 5.5 %convert_reduce_fusion = (f32[3072]{0:T(1024)}, bf16[128,3072]{1,0:T(8,128)(2,1)S(1)}) fusion(f32[128,3072]{1,0:T(8,128)S(1)} %get-tuple-element.81, bf16[3072,768]{1,0:T(8,128)(2,1)} %bitcast.75, bf16[128,768]{1,0:T(8,128)(2,1)S(1)} %copy-done.21), kind=kOutput, calls=%fused_computation.23 | convolution fusion | flops 612627456 | bytes 7286784 | tf_op jit(solution)/shard_map/td,fd->tf/dot_general | solution.py:97
  83.8 2.3 %multiply_reduce_fusion.1 = (f32[768]{0:T(1024)}, f32[128]{0:T(128)S(1)}, f32[128]{0:T(128)S(1)}, f32[768]{0:T(1024)}, f32[128,768]{1,0:T(8,128)S(1)}) fusion(f32[128,768]{1,0:T(8,128)S(1)} %get-tuple-element.75.refs_18_, f32[128]{0:T(128)S(1)} %copy-done.44, f32[128]{0:T(128)S(1)} %copy-done.41, f32[768]{0:T(1024)S(1)} %reshape.288, ...), kind=kOutput, calls=%fused_computation.60 | convolution fusion | flops 604862720 | bytes 6302720 | tf_op jit(solution)/shard_map/tf,df->td/dot_general | solution.py:101
  86.1 1.7 convert_reduce_fusion.4
  87.8 0.5 collective-permute-start.5
  88.3 1.5 convolution_convert_fusion
  89.9 0.3 multiply_reduce_fusion
  90.4 0.4 copy-done.8
  90.8 0.2 fusion.18
  91.1 0.4 fusion.19
  91.5 0.4 convolution_bitcast_fusion.1
  91.9 0.4 convert_reduce_fusion.1
  92.2 0.6 copy-done
  92.9 1.5 fusion.30
  94.4 1.0 fusion.33
  96.0 0.5 collective-permute-start.2
  97.1 0.7 concatenate.16
  97.9 0.4 collective-permute-start.6
  98.3 0.4 copy.66
  98.7 0.7 collective-permute-done.8
  99.5 0.4 copy.61.refs_4_
  99.9 0.4 collective-permute-start.7
  100.5 0.3 collective-permute-start.1
  100.9 2.8 %multiply_convert_fusion.refs_17_ = bf16[128,3072]{1,0:T(8,128)(2,1)} fusion(f32[128,3072]{1,0:T(8,128)} %copy-done.13), kind=kLoop, calls=%fused_computation.22 | loop fusion | flops 3538944 | bytes 2359296 | tf_op jit(solution)/shard_map/convert_element_type | solution.py:70
  103.7 0.7 reshape.291.refs_19_
  104.3 0.8 add.118
  105.1 0.6 reshape.284.refs_16_
  105.8 0.9 copy-done.22
  106.7 93.4 %shard_map.255 = (f32[96,2304]{1,0:T(8,128)}, f32[96,768]{1,0:T(8,128)}, f32[96,3072]{1,0:T(8,128)}, f32[384,768]{1,0:T(8,128)}, f32[1,1152]{1,0:T(1,128)}, /*index=5*/bf16[128,768]{1,0:T(8,128)(2,1)}) custom-call(bf16[8,96,128]{2,1,0:T(8,128)(2,1)} %bitcast.100, bf16[8,96,128]{2,1,0:T(8,128)(2,1)} %bitcast.90, bf16[8,96,128]{2,1,0:T(8,128)(2,1)} %bitcast.102, ...), custom_call_target="tpu_custom_call" | custom-call | tf_op jit(solution)/shard_map/pallas_call | solution.py:592
  200.2 1.4 fusion.44
  201.6 1.3 slice.108
  202.9 1.3 slice.104
  204.2 1.6 copy.75
  205.8 2.1 %copy.76 = f32[1,96,2304]{2,1,0:T(8,128)} copy(f32[1,96,2304]{2,1,0:T(8,128)} %bitcast.98) | data formatting | bytes 1769472
  208.0 0.7 copy.77
  208.7 1.0 copy.78
  209.7 1.0 copy.79
  (146 shorter events, 4.3 us)
Async XLA Ops:
  0.6 66.3 %copy-start.2 = (bf16[128,768]{1,0:T(8,128)(2,1)S(1)}, bf16[128,768]{1,0:T(8,128)(2,1)}, u32[]{:S(2)}) copy-start(bf16[128,768]{1,0:T(8,128)(2,1)} %param.15) | copy-start | bytes 589828
  71.2 1.1 copy-start.7
  71.3 1.3 copy-start.3
  71.9 1.1 copy-start.11
  72.3 5.8 %copy-start.9 = (bf16[12,64,128]{2,1,0:T(8,128)(2,1)}, bf16[12,64,128]{2,1,0:T(8,128)(2,1)S(1)}, u32[]{:S(2)}) copy-start(bf16[12,64,128]{2,1,0:T(8,128)(2,1)S(1)} %convolution_convert_fusion.1) | copy-start | bytes 589828
  73.0 13.1 %copy-start.1 = (f32[128,768]{1,0:T(8,128)}, f32[128,768]{1,0:T(8,128)S(1)}, u32[]{:S(2)}) copy-start(f32[128,768]{1,0:T(8,128)S(1)} %get-tuple-element.75.refs_18_) | copy-start | bytes 1179652
  73.0 5.1 %copy-start.40 = (f32[128]{0:T(128)}, f32[128]{0:T(128)S(1)}, u32[]{:S(2)}) copy-start(f32[128]{0:T(128)S(1)} %broadcast_multiply_fusion.4) | copy-start | bytes 1540
  73.3 4.8 %copy-start.43 = (f32[128]{0:T(128)}, f32[128]{0:T(128)S(1)}, u32[]{:S(2)}) copy-start(f32[128]{0:T(128)S(1)} %add_rsqrt_fusion) | copy-start | bytes 1540
  73.4 4.7 %copy-start.32 = (f32[768]{0:T(1024)}, f32[768]{0:T(1024)S(1)}, u32[]{:S(2)}) copy-start(f32[768]{0:T(1024)S(1)} %reshape.289) | copy-start | bytes 9220
  73.4 4.7 %copy-start.21 = (bf16[128,768]{1,0:T(8,128)(2,1)S(1)}, bf16[128,768]{1,0:T(8,128)(2,1)}, u32[]{:S(2)}) copy-start(bf16[128,768]{1,0:T(8,128)(2,1)} %refs_7_) | copy-start | bytes 589828
  73.4 10.3 %slice-start = ((s8[4718592]{0:T(1024)(128)(4,1)}), s8[4194304]{0:T(1024)(128)(4,1)S(1)}, s32[]{:S(2)}) async-start(s8[4718592]{0:T(1024)(128)(4,1)} %bitcast.78), calls=%async_computation | async-start | bytes 8388608
  78.1 5.6 %copy-start.13 = (f32[128,3072]{1,0:T(8,128)}, f32[128,3072]{1,0:T(8,128)S(1)}, u32[]{:S(2)}) copy-start(f32[128,3072]{1,0:T(8,128)S(1)} %get-tuple-element.81) | copy-start | bytes 4718596
  78.1 5.6 %slice-start.1 = ((s8[4718592]{0:T(1024)(128)(4,1)}), s8[524288]{0:T(1024)(128)(4,1)S(1)}, s32[]{:S(2)}) async-start(s8[4718592]{0:T(1024)(128)(4,1)} %bitcast.78), calls=%async_computation.1 | async-start | bytes 1048576
  78.1 5.6 %copy-start.41 = (f32[128]{0:T(128)S(1)}, f32[128]{0:T(128)}, u32[]{:S(2)}) copy-start(f32[128]{0:T(128)} %copy-done.40) | copy-start | bytes 1540
  78.2 5.6 %copy-start.44 = (f32[128]{0:T(128)S(1)}, f32[128]{0:T(128)}, u32[]{:S(2)}) copy-start(f32[128]{0:T(128)} %copy-done.43) | copy-start | bytes 1540
  83.7 14.1 %copy-start.4 = (bf16[128,3072]{1,0:T(8,128)(2,1)}, bf16[128,3072]{1,0:T(8,128)(2,1)S(1)}, u32[]{:S(2)}) copy-start(bf16[128,3072]{1,0:T(8,128)(2,1)S(1)} %get-tuple-element.83.refs_6_) | copy-start | bytes 2359300
  83.7 2.3 %copy-start.33 = (f32[768]{0:T(1024)S(1)}, f32[768]{0:T(1024)}, u32[]{:S(2)}) copy-start(f32[768]{0:T(1024)} %copy-done.32) | copy-start | bytes 9220
  87.8 2.1 copy-start.12
  87.8 12.7 %collective-permute-start.5 = (bf16[128,768]{1,0:T(8,128)(2,1)}, bf16[128,768]{1,0:T(8,128)(2,1)}, u32[]{:S(2)}, u32[]{:S(2)}) collective-permute-start(bf16[128,768]{1,0:T(8,128)(2,1)} %get-tuple-element.45.refs_5_), channel_id=1, source_target_pairs={{0,8},{8,0},{16,24},{24,16},{1,9},{9,1},{17,25},{25,17},{2,10},{10... | collective-permute-start | bytes 589832 | tf_op jit(solution)/shard_map/ppermute | solution.py:630
  90.8 2.0 copy-start
  91.1 1.8 copy-start.37
  91.1 1.8 copy-start.39
  92.8 1.6 copy-start.14
  92.9 1.6 copy-start.27
  94.3 1.4 copy-start.18
  94.3 2.4 %copy-start.31 = (f32[768]{0:T(1024)S(1)}, f32[768]{0:T(1024)}, u32[]{:S(2)}) copy-start(f32[768]{0:T(1024)} %get-tuple-element.44) | copy-start | bytes 9220
  94.4 2.5 %copy-start.30 = (f32[768]{0:T(1024)S(1)}, f32[768]{0:T(1024)}, u32[]{:S(2)}) copy-start(f32[768]{0:T(1024)} %get-tuple-element.55) | copy-start | bytes 9220
  94.4 2.5 %copy-start.29 = (f32[768]{0:T(1024)S(1)}, f32[768]{0:T(1024)}, u32[]{:S(2)}) copy-start(f32[768]{0:T(1024)} %get-tuple-element.36) | copy-start | bytes 9220
  94.4 2.6 %copy-start.28 = (f32[768]{0:T(1024)S(1)}, f32[768]{0:T(1024)}, u32[]{:S(2)}) copy-start(f32[768]{0:T(1024)} %get-tuple-element.43) | copy-start | bytes 9220
  94.4 2.7 %copy-start.35 = (f32[3072]{0:T(1024)S(1)}, f32[3072]{0:T(1024)}, u32[]{:S(2)}) copy-start(f32[3072]{0:T(1024)} %get-tuple-element.82) | copy-start | bytes 36868
  94.4 3.9 %copy-start.17 = (bf16[3072,128]{0,1:T(8,128)(2,1)S(1)}, bf16[3072,128]{0,1:T(8,128)(2,1)}, u32[]{:S(2)}) copy-start(bf16[3072,128]{0,1:T(8,128)(2,1)} %get-tuple-element.80) | copy-start | bytes 2359300
  95.6 4.3 %copy-start.19 = (bf16[768,128]{1,0:T(8,128)(2,1)}, bf16[768,128]{1,0:T(8,128)(2,1)S(1)}, u32[]{:S(2)}) copy-start(bf16[768,128]{1,0:T(8,128)(2,1)S(1)} %copy.48) | copy-start | bytes 589828
  95.6 4.3 %collective-permute-start = (bf16[8,96,128]{2,1,0:T(8,128)(2,1)S(1)}, bf16[8,96,128]{2,1,0:T(8,128)(2,1)}, u32[]{:S(2)}, u32[]{:S(2)}) collective-permute-start(bf16[8,96,128]{2,1,0:T(8,128)(2,1)S(1)} %bitcast.99), channel_id=1, source_target_pairs={{0,8},{8,0},{16,24},{24,16},{1,9},{9,1},{17,25},{25,17},{2,10},{10... | collective-permute-start | bytes 589832 | tf_op jit(solution)/shard_map/ppermute | solution.py:630
  95.9 7.7 %copy-start.20 = (bf16[768,128]{1,0:T(8,128)(2,1)}, bf16[768,128]{1,0:T(8,128)(2,1)S(1)}, u32[]{:S(2)}) copy-start(bf16[768,128]{1,0:T(8,128)(2,1)S(1)} %copy.53) | copy-start | bytes 589828
  95.9 4.6 %copy-start.10 = (bf16[12,64,128]{2,1,0:T(8,128)(2,1)S(1)}, bf16[12,64,128]{2,1,0:T(8,128)(2,1)}, u32[]{:S(2)}) copy-start(bf16[12,64,128]{2,1,0:T(8,128)(2,1)} %copy-done.9) | copy-start | bytes 589828
  96.0 4.4 %collective-permute-start.2 = (bf16[8,96,128]{2,1,0:T(8,128)(2,1)S(1)}, bf16[8,96,128]{2,1,0:T(8,128)(2,1)}, u32[]{:S(2)}, u32[]{:S(2)}) collective-permute-start(bf16[8,96,128]{2,1,0:T(8,128)(2,1)S(1)} %bitcast.101), channel_id=1, source_target_pairs={{0,8},{8,0},{16,24},{24,16},{1,9},{9,1},{17,25},{25,17},{2,10},{10... | collective-permute-start | bytes 589832 | tf_op jit(solution)/shard_map/ppermute | solution.py:630
  97.8 1.6 collective-permute-start.8
  97.9 8.0 %collective-permute-start.6 = (bf16[128,3072]{1,0:T(8,128)(2,1)S(1)}, bf16[128,3072]{1,0:T(8,128)(2,1)}, u32[]{:S(2)}, u32[]{:S(2)}) collective-permute-start(bf16[128,3072]{1,0:T(8,128)(2,1)S(1)} %get-tuple-element.83.refs_6_), channel_id=1, source_target_pairs={{0,8},{8,0},{16,24},{24,16},{1,9},{9,1},{17,25},{25,17},{2,10},{10... | collective-permute-start | bytes 2359304 | tf_op jit(solution)/shard_map/ppermute | solution.py:630
  98.7 5.0 %copy-start.5 = (bf16[3072,128]{1,0:T(8,128)(2,1)}, bf16[3072,128]{1,0:T(8,128)(2,1)S(1)}, u32[]{:S(2)}) copy-start(bf16[3072,128]{1,0:T(8,128)(2,1)S(1)} %copy.66) | copy-start | bytes 2359300
  99.3 4.3 %copy-start.34 = (f32[8,96]{1,0:T(8,128)S(1)}, f32[8,96]{1,0:T(8,128)}, u32[]{:S(2)}) copy-start(f32[8,96]{1,0:T(8,128)} %get-tuple-element.58) | copy-start | bytes 9220
  99.3 7.4 %collective-permute-start.3 = (bf16[8,384,128]{2,1,0:T(8,128)(2,1)S(1)}, bf16[8,384,128]{2,1,0:T(8,128)(2,1)}, u32[]{:S(2)}, u32[]{:S(2)}) collective-permute-start(bf16[8,384,128]{2,1,0:T(8,128)(2,1)S(1)} %bitcast.83), channel_id=1, source_target_pairs={{0,8},{8,0},{16,24},{24,16},{1,9},{9,1},{17,25},{25,17},{2,10},{10... | collective-permute-start | bytes 2359304 | tf_op jit(solution)/shard_map/ppermute | solution.py:630
  99.9 5.9 %copy-start.6 = (bf16[128,2304]{1,0:T(8,128)(2,1)}, bf16[128,2304]{1,0:T(8,128)(2,1)S(1)}, u32[]{:S(2)}) copy-start(bf16[128,2304]{1,0:T(8,128)(2,1)S(1)} %copy.61.refs_4_) | copy-start | bytes 1769476
  99.9 5.8 %collective-permute-start.7 = (bf16[128,768]{1,0:T(8,128)(2,1)}, bf16[128,768]{1,0:T(8,128)(2,1)S(1)}, u32[]{:S(2)}, u32[]{:S(2)}) collective-permute-start(bf16[128,768]{1,0:T(8,128)(2,1)} %refs_7_), channel_id=1, source_target_pairs={{0,8},{8,0},{16,24},{24,16},{1,9},{9,1},{17,25},{25,17},{2,10},{10... | collective-permute-start | bytes 589832 | tf_op jit(solution)/shard_map/ppermute | solution.py:630
  100.4 5.4 %collective-permute-start.4 = (bf16[128,2304]{1,0:T(8,128)(2,1)S(1)}, bf16[128,2304]{1,0:T(8,128)(2,1)S(1)}, u32[]{:S(2)}, u32[]{:S(2)}) collective-permute-start(bf16[128,2304]{1,0:T(8,128)(2,1)S(1)} %copy.61.refs_4_), channel_id=1, source_target_pairs={{0,8},{8,0},{16,24},{24,16},{1,9},{9,1},{17,25},{25,17},{2,10},{10... | collective-permute-start | bytes 1769480 | tf_op jit(solution)/shard_map/ppermute | solution.py:630
  100.5 5.2 %collective-permute-start.1 = (bf16[8,96,128]{2,1,0:T(8,128)(2,1)S(1)}, bf16[8,96,128]{2,1,0:T(8,128)(2,1)S(1)}, u32[]{:S(2)}, u32[]{:S(2)}) collective-permute-start(bf16[8,96,128]{2,1,0:T(8,128)(2,1)S(1)} %bitcast.91), channel_id=1, source_target_pairs={{0,8},{8,0},{16,24},{24,16},{1,9},{9,1},{17,25},{25,17},{2,10},{10... | collective-permute-start | bytes 589832 | tf_op jit(solution)/shard_map/ppermute | solution.py:630
  200.1 7.8 %copy-start.23 = (f32[96,768]{1,0:T(8,128)S(1)}, f32[96,768]{1,0:T(8,128)}, u32[]{:S(2)}) copy-start(f32[96,768]{1,0:T(8,128)} %get-tuple-element.33) | copy-start | bytes 884740
  200.1 8.5 %copy-start.16 = (f32[96,3072]{1,0:T(8,128)S(1)}, f32[96,3072]{1,0:T(8,128)}, u32[]{:S(2)}) copy-start(f32[96,3072]{1,0:T(8,128)} %get-tuple-element.34) | copy-start | bytes 3538948
  208.0 1.7 copy-start.15
  (8 other events, 6.0 us)

commit v20 on v19

--- a/solution.py
+++ b/solution.py
@@ -175,7 +175,7 @@
 FIRST_CORE_HALF = (0, 3)
 
 
-CHAIN_RANK = (2, 3, 0, 1, 4)
+CHAIN_RANK = (0, 1, 2, 3, 4)
 CHAIN_LAG = 0
 
 
@@ -329,8 +329,8 @@
     if n == 8 and rows % 32 == 0:
         half = rows // 2
         parts = ((0, 0, None), (1, 0, None), (2, 0, half), (2, half, half), (3, 0, None), (4, 0, None))
-        plane_only = ((0,), (1, 2))
-        first_core = (1, 4)
+        plane_only = ((0, 1), (2, 3))
+        first_core = (0, 4)
     else:
         parts = tuple((a, 0, None) for a in range(count))
         plane_only = ((),)

time: 211 us -> 210 us (level)
    pallas_call x1, Pallas kernels: 62.9 us -> 60.4 us  [gather_weights(): pl.pallas_call(functools.partial(gather_kernel, n, count, parts, plane_on...]
where the time goes in v20:
time: 210 us; the launch traced here: 209 us
  Pallas kernels  155 us (74%)
  local copies, waits for them, and re-layouts  20.8 us (10%)
  matrix products  20.5 us (10%)
  other arithmetic  8.38 us (4%)
  starting transfers between devices  2.28 us (1%)
    pallas_call x1, Pallas kernels, reduce_gradients(): pl.pallas_call(functools.partial(reduce_kernel, n, count, mm), out_shape=...  94.9 us
    pallas_call x1, Pallas kernels, gather_weights(): pl.pallas_call(functools.partial(gather_kernel, n, count, parts, plane_on...  60.4 us
    unnamed x100, local copies, waits for them, and re-layouts  10.4 us
    dot_general x1, matrix products, layer_backward(): jnp.einsum('td,fd->tf', proj_in, proj_weight, preferred_element_type=jnp....  5.54 us
    dot_general x1, matrix products, layer_forward(): jnp.dot(second_low, fc_weight, preferred_element_type=jnp.float32) + fc_bias  4.66 us
  transfers between devices with their start and end apart: 9, of which 1 were waited for; matrix products, arithmetic and copies ran while one was open for 6% of the time, Pallas kernels for 0%

profile of v20, /device:TPU:0, one launch (start us, length us, event | category | flops | bytes accessed | tf_op | source)
XLA Modules:
  0.0 209.3 jit_solution(14986094254050084752)
XLA Ops:
  0.7 1.5 concatenate.13.refs_4_
  2.2 60.4 %shard_map.254 = (bf16[8,96,2304]{2,1,0:T(8,128)(2,1)}, bf16[8,96,768]{2,1,0:T(8,128)(2,1)}, bf16[8,96,3072]{2,1,0:T(8,128)(2,1)}, bf16[8,384,768]{2,1,0:T(8,128)(2,1)}, bf16[8,1,1152]{2,1,0:T(2,128)(2,1)}) custom-call(bf16[96,2304]{1,0:T(8,128)(2,1)} %bitcast.105, bf16[96,768]{1,0:T(8,128)(2,1)} %bitcast.107, bf16[96,3072]{1,0:T(8,128)(2,1)} %bitcast.103, ...), custom_call_target="tpu_custom_call" | custom-call | tf_op jit(solution)/shard_map/pallas_call | solution.py:340
  62.6 0.8 copy.69
  63.4 0.7 slice_convert_fusion.2
  65.1 0.2 copy-done.38
  65.3 2.7 %fusion = bf16[128,2304]{1,0:T(8,128)(2,1)S(1)} fusion(bf16[768,2304]{1,0:T(8,128)(2,1)} %bitcast.71, f32[2304]{0:T(1024)S(1)} %pad_maximum_fusion, bf16[128,768]{1,0:T(8,128)(2,1)S(1)} %copy-done.2, f32[768]{0:T(1024)S(1)} %reshape.286, f32[768]{0:T(1024)S(1)} %reshape.285, f32[128]{0:T(128)S(1)} %add_rsqrt_fusion.1, f32[128]{0:T(128)S(1)} %broadcast_multiply_fusion.5), kind=kOutput, calls=%fused_computation.3 | convolution fusion | flops 454164480 | bytes 4341760 | tf_op jit(solution)/shard_map/dot_general | solution.py:47
  68.4 0.3 copy-done.42
  68.8 0.3 fusion.45
  69.5 0.2 convolution_convert_fusion.1
  69.8 0.3 copy-done.3
  70.0 0.4 fusion.46
  70.9 4.7 %fusion.15 = (bf16[3072,128]{0,1:T(8,128)(2,1)}, f32[128,3072]{1,0:T(8,128)S(1)}) fusion(f32[3072]{0:T(1024)S(1)} %reshape.290, bf16[768,3072]{1,0:T(8,128)(2,1)} %bitcast.77, f32[128,768]{1,0:T(8,128)S(1)} %get-tuple-element.75.refs_18_, f32[768]{0:T(1024)S(1)} %reshape.289, f32[768]{0:T(1024)S(1)} %reshape.288, f32[128]{0:T(128)S(1)} %add_rsqrt_fusion, ...), kind=kOutput, calls=%fused_computation.21 | convolution fusion | flops 608403456 | bytes 7490560 | tf_op jit(solution)/shard_map/dot_general | solution.py:69
  75.6 5.5 %convert_reduce_fusion = (f32[3072]{0:T(1024)}, bf16[128,3072]{1,0:T(8,128)(2,1)S(1)}) fusion(f32[128,3072]{1,0:T(8,128)S(1)} %get-tuple-element.81, bf16[3072,768]{1,0:T(8,128)(2,1)} %bitcast.75, bf16[128,768]{1,0:T(8,128)(2,1)S(1)} %copy-done.21), kind=kOutput, calls=%fused_computation.23 | convolution fusion | flops 612627456 | bytes 7286784 | tf_op jit(solution)/shard_map/td,fd->tf/dot_general | solution.py:97
  81.2 2.3 %multiply_reduce_fusion.1 = (f32[768]{0:T(1024)}, f32[128]{0:T(128)S(1)}, f32[128]{0:T(128)S(1)}, f32[768]{0:T(1024)}, f32[128,768]{1,0:T(8,128)S(1)}) fusion(f32[128,768]{1,0:T(8,128)S(1)} %get-tuple-element.75.refs_18_, f32[128]{0:T(128)S(1)} %copy-done.44, f32[128]{0:T(128)S(1)} %copy-done.41, f32[768]{0:T(1024)S(1)} %reshape.288, ...), kind=kOutput, calls=%fused_computation.60 | convolution fusion | flops 604862720 | bytes 6302720 | tf_op jit(solution)/shard_map/tf,df->td/dot_general | solution.py:101
  83.6 1.7 convert_reduce_fusion.4
  85.3 1.5 convolution_convert_fusion
  87.0 0.3 multiply_reduce_fusion
  87.6 0.4 copy-done.8
  88.0 0.2 fusion.18
  88.2 0.4 fusion.19
  88.6 0.4 convolution_bitcast_fusion.1
  89.0 0.4 convert_reduce_fusion.1
  89.4 0.6 copy-done
  90.0 1.5 fusion.30
  91.6 1.0 fusion.33
  92.7 0.5 collective-permute-start
  94.2 0.7 concatenate.16
  94.9 0.4 collective-permute-start.8
  95.4 0.4 copy.66
  95.8 0.7 collective-permute-done.8
  96.5 0.3 collective-permute-start.3
  96.9 0.4 copy.61.refs_4_
  97.3 0.2 collective-permute-start.7
  97.5 0.3 collective-permute-start.4
  98.1 2.8 %multiply_convert_fusion.refs_17_ = bf16[128,3072]{1,0:T(8,128)(2,1)} fusion(f32[128,3072]{1,0:T(8,128)} %copy-done.13), kind=kLoop, calls=%fused_computation.22 | loop fusion | flops 3538944 | bytes 2359296 | tf_op jit(solution)/shard_map/convert_element_type | solution.py:70
  100.8 0.7 reshape.291.refs_19_
  101.5 0.8 add.118
  102.3 0.6 reshape.284.refs_16_
  103.0 0.9 copy-done.22
  103.9 94.9 %shard_map.255 = (f32[96,2304]{1,0:T(8,128)}, f32[96,768]{1,0:T(8,128)}, f32[96,3072]{1,0:T(8,128)}, f32[384,768]{1,0:T(8,128)}, f32[1,1152]{1,0:T(1,128)}, /*index=5*/bf16[128,768]{1,0:T(8,128)(2,1)}) custom-call(bf16[8,96,128]{2,1,0:T(8,128)(2,1)} %bitcast.100, bf16[8,96,128]{2,1,0:T(8,128)(2,1)} %bitcast.90, bf16[8,96,128]{2,1,0:T(8,128)(2,1)} %bitcast.102, ...), custom_call_target="tpu_custom_call" | custom-call | tf_op jit(solution)/shard_map/pallas_call | solution.py:592
  198.8 1.4 fusion.44
  200.2 1.3 slice.108
  201.5 1.3 slice.104
  202.8 1.6 copy.75
  204.5 2.1 %copy.76 = f32[1,96,2304]{2,1,0:T(8,128)} copy(f32[1,96,2304]{2,1,0:T(8,128)} %bitcast.98) | data formatting | bytes 1769472
  206.6 0.7 copy.77
  207.3 1.0 copy.78
  208.3 1.0 copy.79
  (146 shorter events, 4.2 us)
Async XLA Ops:
  0.6 63.8 %copy-start.2 = (bf16[128,768]{1,0:T(8,128)(2,1)S(1)}, bf16[128,768]{1,0:T(8,128)(2,1)}, u32[]{:S(2)}) copy-start(bf16[128,768]{1,0:T(8,128)(2,1)} %param.15) | copy-start | bytes 589828
  68.7 1.1 copy-start.7
  68.8 1.3 copy-start.3
  69.4 1.1 copy-start.11
  69.8 5.8 %copy-start.9 = (bf16[12,64,128]{2,1,0:T(8,128)(2,1)}, bf16[12,64,128]{2,1,0:T(8,128)(2,1)S(1)}, u32[]{:S(2)}) copy-start(bf16[12,64,128]{2,1,0:T(8,128)(2,1)S(1)} %convolution_convert_fusion.1) | copy-start | bytes 589828
  70.5 13.1 %copy-start.1 = (f32[128,768]{1,0:T(8,128)}, f32[128,768]{1,0:T(8,128)S(1)}, u32[]{:S(2)}) copy-start(f32[128,768]{1,0:T(8,128)S(1)} %get-tuple-element.75.refs_18_) | copy-start | bytes 1179652
  70.5 5.1 %copy-start.40 = (f32[128]{0:T(128)}, f32[128]{0:T(128)S(1)}, u32[]{:S(2)}) copy-start(f32[128]{0:T(128)S(1)} %broadcast_multiply_fusion.4) | copy-start | bytes 1540
  70.7 4.8 %copy-start.43 = (f32[128]{0:T(128)}, f32[128]{0:T(128)S(1)}, u32[]{:S(2)}) copy-start(f32[128]{0:T(128)S(1)} %add_rsqrt_fusion) | copy-start | bytes 1540
  70.9 4.7 %copy-start.32 = (f32[768]{0:T(1024)}, f32[768]{0:T(1024)S(1)}, u32[]{:S(2)}) copy-start(f32[768]{0:T(1024)S(1)} %reshape.289) | copy-start | bytes 9220
  70.9 4.7 %copy-start.21 = (bf16[128,768]{1,0:T(8,128)(2,1)S(1)}, bf16[128,768]{1,0:T(8,128)(2,1)}, u32[]{:S(2)}) copy-start(bf16[128,768]{1,0:T(8,128)(2,1)} %refs_7_) | copy-start | bytes 589828
  70.9 10.3 %slice-start = ((s8[4718592]{0:T(1024)(128)(4,1)}), s8[4194304]{0:T(1024)(128)(4,1)S(1)}, s32[]{:S(2)}) async-start(s8[4718592]{0:T(1024)(128)(4,1)} %bitcast.78), calls=%async_computation | async-start | bytes 8388608
  75.6 5.6 %copy-start.13 = (f32[128,3072]{1,0:T(8,128)}, f32[128,3072]{1,0:T(8,128)S(1)}, u32[]{:S(2)}) copy-start(f32[128,3072]{1,0:T(8,128)S(1)} %get-tuple-element.81) | copy-start | bytes 4718596
  75.6 5.6 %slice-start.1 = ((s8[4718592]{0:T(1024)(128)(4,1)}), s8[524288]{0:T(1024)(128)(4,1)S(1)}, s32[]{:S(2)}) async-start(s8[4718592]{0:T(1024)(128)(4,1)} %bitcast.78), calls=%async_computation.1 | async-start | bytes 1048576
  75.6 5.6 %copy-start.41 = (f32[128]{0:T(128)S(1)}, f32[128]{0:T(128)}, u32[]{:S(2)}) copy-start(f32[128]{0:T(128)} %copy-done.40) | copy-start | bytes 1540
  75.6 5.6 %copy-start.44 = (f32[128]{0:T(128)S(1)}, f32[128]{0:T(128)}, u32[]{:S(2)}) copy-start(f32[128]{0:T(128)} %copy-done.43) | copy-start | bytes 1540
  81.2 14.1 %copy-start.4 = (bf16[128,3072]{1,0:T(8,128)(2,1)}, bf16[128,3072]{1,0:T(8,128)(2,1)S(1)}, u32[]{:S(2)}) copy-start(bf16[128,3072]{1,0:T(8,128)(2,1)S(1)} %get-tuple-element.83.refs_6_) | copy-start | bytes 2359300
  81.2 2.3 %copy-start.33 = (f32[768]{0:T(1024)S(1)}, f32[768]{0:T(1024)}, u32[]{:S(2)}) copy-start(f32[768]{0:T(1024)} %copy-done.32) | copy-start | bytes 9220
  85.3 1.7 copy-start.12
  85.3 12.6 %collective-permute-start.5 = (bf16[128,768]{1,0:T(8,128)(2,1)}, bf16[128,768]{1,0:T(8,128)(2,1)}, u32[]{:S(2)}, u32[]{:S(2)}) collective-permute-start(bf16[128,768]{1,0:T(8,128)(2,1)} %get-tuple-element.45.refs_5_), channel_id=1, source_target_pairs={{0,8},{8,0},{16,24},{24,16},{1,9},{9,1},{17,25},{25,17},{2,10},{10... | collective-permute-start | bytes 589832 | tf_op jit(solution)/shard_map/ppermute | solution.py:630
  88.0 2.0 copy-start
  88.2 1.8 copy-start.37
  88.2 1.8 copy-start.39
  90.0 1.6 copy-start.14
  90.0 1.6 copy-start.27
  91.4 1.8 copy-start.18
  91.5 2.4 %copy-start.31 = (f32[768]{0:T(1024)S(1)}, f32[768]{0:T(1024)}, u32[]{:S(2)}) copy-start(f32[768]{0:T(1024)} %get-tuple-element.44) | copy-start | bytes 9220
  91.5 2.5 %copy-start.30 = (f32[768]{0:T(1024)S(1)}, f32[768]{0:T(1024)}, u32[]{:S(2)}) copy-start(f32[768]{0:T(1024)} %get-tuple-element.55) | copy-start | bytes 9220
  91.5 2.5 %copy-start.29 = (f32[768]{0:T(1024)S(1)}, f32[768]{0:T(1024)}, u32[]{:S(2)}) copy-start(f32[768]{0:T(1024)} %get-tuple-element.36) | copy-start | bytes 9220
  91.5 2.6 %copy-start.28 = (f32[768]{0:T(1024)S(1)}, f32[768]{0:T(1024)}, u32[]{:S(2)}) copy-start(f32[768]{0:T(1024)} %get-tuple-element.43) | copy-start | bytes 9220
  91.5 2.7 %copy-start.35 = (f32[3072]{0:T(1024)S(1)}, f32[3072]{0:T(1024)}, u32[]{:S(2)}) copy-start(f32[3072]{0:T(1024)} %get-tuple-element.82) | copy-start | bytes 36868
  91.5 3.9 %copy-start.17 = (bf16[3072,128]{0,1:T(8,128)(2,1)S(1)}, bf16[3072,128]{0,1:T(8,128)(2,1)}, u32[]{:S(2)}) copy-start(bf16[3072,128]{0,1:T(8,128)(2,1)} %get-tuple-element.80) | copy-start | bytes 2359300
  92.7 4.6 %copy-start.19 = (bf16[768,128]{1,0:T(8,128)(2,1)}, bf16[768,128]{1,0:T(8,128)(2,1)S(1)}, u32[]{:S(2)}) copy-start(bf16[768,128]{1,0:T(8,128)(2,1)S(1)} %copy.48) | copy-start | bytes 589828
  92.7 4.6 %collective-permute-start = (bf16[8,96,128]{2,1,0:T(8,128)(2,1)S(1)}, bf16[8,96,128]{2,1,0:T(8,128)(2,1)}, u32[]{:S(2)}, u32[]{:S(2)}) collective-permute-start(bf16[8,96,128]{2,1,0:T(8,128)(2,1)S(1)} %bitcast.99), channel_id=1, source_target_pairs={{0,8},{8,0},{16,24},{24,16},{1,9},{9,1},{17,25},{25,17},{2,10},{10... | collective-permute-start | bytes 589832 | tf_op jit(solution)/shard_map/ppermute | solution.py:630
  93.4 7.5 %copy-start.20 = (bf16[768,128]{1,0:T(8,128)(2,1)}, bf16[768,128]{1,0:T(8,128)(2,1)S(1)}, u32[]{:S(2)}) copy-start(bf16[768,128]{1,0:T(8,128)(2,1)S(1)} %copy.53) | copy-start | bytes 589828
  93.4 4.5 %copy-start.10 = (bf16[12,64,128]{2,1,0:T(8,128)(2,1)S(1)}, bf16[12,64,128]{2,1,0:T(8,128)(2,1)}, u32[]{:S(2)}) copy-start(bf16[12,64,128]{2,1,0:T(8,128)(2,1)} %copy-done.9) | copy-start | bytes 589828
  93.4 4.1 %collective-permute-start.2 = (bf16[8,96,128]{2,1,0:T(8,128)(2,1)S(1)}, bf16[8,96,128]{2,1,0:T(8,128)(2,1)}, u32[]{:S(2)}, u32[]{:S(2)}) collective-permute-start(bf16[8,96,128]{2,1,0:T(8,128)(2,1)S(1)} %bitcast.101), channel_id=1, source_target_pairs={{0,8},{8,0},{16,24},{24,16},{1,9},{9,1},{17,25},{25,17},{2,10},{10... | collective-permute-start | bytes 589832 | tf_op jit(solution)/shard_map/ppermute | solution.py:630
  94.9 1.6 collective-permute-start.8
  95.3 7.7 %collective-permute-start.6 = (bf16[128,3072]{1,0:T(8,128)(2,1)S(1)}, bf16[128,3072]{1,0:T(8,128)(2,1)}, u32[]{:S(2)}, u32[]{:S(2)}) collective-permute-start(bf16[128,3072]{1,0:T(8,128)(2,1)S(1)} %get-tuple-element.83.refs_6_), channel_id=1, source_target_pairs={{0,8},{8,0},{16,24},{24,16},{1,9},{9,1},{17,25},{25,17},{2,10},{10... | collective-permute-start | bytes 2359304 | tf_op jit(solution)/shard_map/ppermute | solution.py:630
  95.8 5.1 %copy-start.5 = (bf16[3072,128]{1,0:T(8,128)(2,1)}, bf16[3072,128]{1,0:T(8,128)(2,1)S(1)}, u32[]{:S(2)}) copy-start(bf16[3072,128]{1,0:T(8,128)(2,1)S(1)} %copy.66) | copy-start | bytes 2359300
  96.5 4.3 %copy-start.34 = (f32[8,96]{1,0:T(8,128)S(1)}, f32[8,96]{1,0:T(8,128)}, u32[]{:S(2)}) copy-start(f32[8,96]{1,0:T(8,128)} %get-tuple-element.58) | copy-start | bytes 9220
  96.5 7.4 %collective-permute-start.3 = (bf16[8,384,128]{2,1,0:T(8,128)(2,1)S(1)}, bf16[8,384,128]{2,1,0:T(8,128)(2,1)}, u32[]{:S(2)}, u32[]{:S(2)}) collective-permute-start(bf16[8,384,128]{2,1,0:T(8,128)(2,1)S(1)} %bitcast.83), channel_id=1, source_target_pairs={{0,8},{8,0},{16,24},{24,16},{1,9},{9,1},{17,25},{25,17},{2,10},{10... | collective-permute-start | bytes 2359304 | tf_op jit(solution)/shard_map/ppermute | solution.py:630
  97.3 5.7 %copy-start.6 = (bf16[128,2304]{1,0:T(8,128)(2,1)}, bf16[128,2304]{1,0:T(8,128)(2,1)S(1)}, u32[]{:S(2)}) copy-start(bf16[128,2304]{1,0:T(8,128)(2,1)S(1)} %copy.61.refs_4_) | copy-start | bytes 1769476
  97.3 5.6 %collective-permute-start.7 = (bf16[128,768]{1,0:T(8,128)(2,1)}, bf16[128,768]{1,0:T(8,128)(2,1)S(1)}, u32[]{:S(2)}, u32[]{:S(2)}) collective-permute-start(bf16[128,768]{1,0:T(8,128)(2,1)} %refs_7_), channel_id=1, source_target_pairs={{0,8},{8,0},{16,24},{24,16},{1,9},{9,1},{17,25},{25,17},{2,10},{10... | collective-permute-start | bytes 589832 | tf_op jit(solution)/shard_map/ppermute | solution.py:630
  97.5 5.4 %collective-permute-start.4 = (bf16[128,2304]{1,0:T(8,128)(2,1)S(1)}, bf16[128,2304]{1,0:T(8,128)(2,1)S(1)}, u32[]{:S(2)}, u32[]{:S(2)}) collective-permute-start(bf16[128,2304]{1,0:T(8,128)(2,1)S(1)} %copy.61.refs_4_), channel_id=1, source_target_pairs={{0,8},{8,0},{16,24},{24,16},{1,9},{9,1},{17,25},{25,17},{2,10},{10... | collective-permute-start | bytes 1769480 | tf_op jit(solution)/shard_map/ppermute | solution.py:630
  97.9 5.1 %collective-permute-start.1 = (bf16[8,96,128]{2,1,0:T(8,128)(2,1)S(1)}, bf16[8,96,128]{2,1,0:T(8,128)(2,1)S(1)}, u32[]{:S(2)}, u32[]{:S(2)}) collective-permute-start(bf16[8,96,128]{2,1,0:T(8,128)(2,1)S(1)} %bitcast.91), channel_id=1, source_target_pairs={{0,8},{8,0},{16,24},{24,16},{1,9},{9,1},{17,25},{25,17},{2,10},{10... | collective-permute-start | bytes 589832 | tf_op jit(solution)/shard_map/ppermute | solution.py:630
  198.8 7.8 %copy-start.23 = (f32[96,768]{1,0:T(8,128)S(1)}, f32[96,768]{1,0:T(8,128)}, u32[]{:S(2)}) copy-start(f32[96,768]{1,0:T(8,128)} %get-tuple-element.33) | copy-start | bytes 884740
  198.8 8.5 %copy-start.16 = (f32[96,3072]{1,0:T(8,128)S(1)}, f32[96,3072]{1,0:T(8,128)}, u32[]{:S(2)}) copy-start(f32[96,3072]{1,0:T(8,128)} %get-tuple-element.34) | copy-start | bytes 3538948
  206.6 1.7 copy-start.15
  (8 other events, 6.0 us)

commit v21 on v20

--- a/solution.py
+++ b/solution.py
@@ -175,7 +175,7 @@
 FIRST_CORE_HALF = (0, 3)
 
 
-CHAIN_RANK = (0, 1, 2, 3, 4)
+CHAIN_RANK = (2, 3, 0, 1, 4)
 CHAIN_LAG = 0
 
 

time: 210 us -> 211 us (level)
  no operation moved by 1% of the time
where the time goes in v21:
time: 211 us; the launch traced here: 210 us
  Pallas kernels  156 us (74%)
  local copies, waits for them, and re-layouts  20.8 us (10%)
  matrix products  20.5 us (10%)
  other arithmetic  8.38 us (4%)
  starting transfers between devices  2.28 us (1%)
    pallas_call x1, Pallas kernels, reduce_gradients(): pl.pallas_call(functools.partial(reduce_kernel, n, count, mm), out_shape=...  95.6 us
    pallas_call x1, Pallas kernels, gather_weights(): pl.pallas_call(functools.partial(gather_kernel, n, count, parts, plane_on...  60.4 us
    unnamed x100, local copies, waits for them, and re-layouts  10.4 us
    dot_general x1, matrix products, layer_backward(): jnp.einsum('td,fd->tf', proj_in, proj_weight, preferred_element_type=jnp....  5.54 us
    dot_general x1, matrix products, layer_forward(): jnp.dot(second_low, fc_weight, preferred_element_type=jnp.float32) + fc_bias  4.66 us
  transfers between devices with their start and end apart: 9, of which 1 were waited for; matrix products, arithmetic and copies ran while one was open for 6% of the time, Pallas kernels for 0%

profile of v21, /device:TPU:0, one launch (start us, length us, event | category | flops | bytes accessed | tf_op | source)
XLA Modules:
  0.0 210.1 jit_solution(3383247234859509397)
XLA Ops:
  0.7 1.5 concatenate.13.refs_4_
  2.2 60.4 %shard_map.254 = (bf16[8,96,2304]{2,1,0:T(8,128)(2,1)}, bf16[8,96,768]{2,1,0:T(8,128)(2,1)}, bf16[8,96,3072]{2,1,0:T(8,128)(2,1)}, bf16[8,384,768]{2,1,0:T(8,128)(2,1)}, bf16[8,1,1152]{2,1,0:T(2,128)(2,1)}) custom-call(bf16[96,2304]{1,0:T(8,128)(2,1)} %bitcast.105, bf16[96,768]{1,0:T(8,128)(2,1)} %bitcast.107, bf16[96,3072]{1,0:T(8,128)(2,1)} %bitcast.103, ...), custom_call_target="tpu_custom_call" | custom-call | tf_op jit(solution)/shard_map/pallas_call | solution.py:340
  62.6 0.8 copy.69
  63.4 0.7 slice_convert_fusion.2
  65.1 0.2 copy-done.38
  65.3 2.7 %fusion = bf16[128,2304]{1,0:T(8,128)(2,1)S(1)} fusion(bf16[768,2304]{1,0:T(8,128)(2,1)} %bitcast.71, f32[2304]{0:T(1024)S(1)} %pad_maximum_fusion, bf16[128,768]{1,0:T(8,128)(2,1)S(1)} %copy-done.2, f32[768]{0:T(1024)S(1)} %reshape.286, f32[768]{0:T(1024)S(1)} %reshape.285, f32[128]{0:T(128)S(1)} %add_rsqrt_fusion.1, f32[128]{0:T(128)S(1)} %broadcast_multiply_fusion.5), kind=kOutput, calls=%fused_computation.3 | convolution fusion | flops 454164480 | bytes 4341760 | tf_op jit(solution)/shard_map/dot_general | solution.py:47
  68.4 0.3 copy-done.42
  68.8 0.3 fusion.45
  69.5 0.2 convolution_convert_fusion.1
  69.8 0.3 copy-done.3
  70.0 0.4 fusion.46
  70.9 4.7 %fusion.15 = (bf16[3072,128]{0,1:T(8,128)(2,1)}, f32[128,3072]{1,0:T(8,128)S(1)}) fusion(f32[3072]{0:T(1024)S(1)} %reshape.290, bf16[768,3072]{1,0:T(8,128)(2,1)} %bitcast.77, f32[128,768]{1,0:T(8,128)S(1)} %get-tuple-element.75.refs_18_, f32[768]{0:T(1024)S(1)} %reshape.289, f32[768]{0:T(1024)S(1)} %reshape.288, f32[128]{0:T(128)S(1)} %add_rsqrt_fusion, ...), kind=kOutput, calls=%fused_computation.21 | convolution fusion | flops 608403456 | bytes 7490560 | tf_op jit(solution)/shard_map/dot_general | solution.py:69
  75.6 5.5 %convert_reduce_fusion = (f32[3072]{0:T(1024)}, bf16[128,3072]{1,0:T(8,128)(2,1)S(1)}) fusion(f32[128,3072]{1,0:T(8,128)S(1)} %get-tuple-element.81, bf16[3072,768]{1,0:T(8,128)(2,1)} %bitcast.75, bf16[128,768]{1,0:T(8,128)(2,1)S(1)} %copy-done.21), kind=kOutput, calls=%fused_computation.23 | convolution fusion | flops 612627456 | bytes 7286784 | tf_op jit(solution)/shard_map/td,fd->tf/dot_general | solution.py:97
  81.2 2.3 %multiply_reduce_fusion.1 = (f32[768]{0:T(1024)}, f32[128]{0:T(128)S(1)}, f32[128]{0:T(128)S(1)}, f32[768]{0:T(1024)}, f32[128,768]{1,0:T(8,128)S(1)}) fusion(f32[128,768]{1,0:T(8,128)S(1)} %get-tuple-element.75.refs_18_, f32[128]{0:T(128)S(1)} %copy-done.44, f32[128]{0:T(128)S(1)} %copy-done.41, f32[768]{0:T(1024)S(1)} %reshape.288, ...), kind=kOutput, calls=%fused_computation.60 | convolution fusion | flops 604862720 | bytes 6302720 | tf_op jit(solution)/shard_map/tf,df->td/dot_general | solution.py:101
  83.6 1.7 convert_reduce_fusion.4
  85.3 1.5 convolution_convert_fusion
  87.0 0.3 multiply_reduce_fusion
  87.6 0.4 copy-done.8
  88.0 0.2 fusion.18
  88.2 0.4 fusion.19
  88.6 0.4 convolution_bitcast_fusion.1
  89.0 0.4 convert_reduce_fusion.1
  89.4 0.6 copy-done
  90.0 1.5 fusion.30
  91.6 1.0 fusion.33
  92.7 0.5 collective-permute-start
  94.2 0.7 concatenate.16
  94.9 0.4 collective-permute-start.8
  95.4 0.4 copy.66
  95.8 0.7 collective-permute-done.8
  96.5 0.3 collective-permute-start.3
  96.9 0.4 copy.61.refs_4_
  97.3 0.2 collective-permute-start.7
  97.5 0.3 collective-permute-start.4
  98.1 2.8 %multiply_convert_fusion.refs_17_ = bf16[128,3072]{1,0:T(8,128)(2,1)} fusion(f32[128,3072]{1,0:T(8,128)} %copy-done.13), kind=kLoop, calls=%fused_computation.22 | loop fusion | flops 3538944 | bytes 2359296 | tf_op jit(solution)/shard_map/convert_element_type | solution.py:70
  100.8 0.7 reshape.291.refs_19_
  101.5 0.8 add.118
  102.3 0.6 reshape.284.refs_16_
  103.0 0.9 copy-done.22
  103.9 95.6 %shard_map.255 = (f32[96,2304]{1,0:T(8,128)}, f32[96,768]{1,0:T(8,128)}, f32[96,3072]{1,0:T(8,128)}, f32[384,768]{1,0:T(8,128)}, f32[1,1152]{1,0:T(1,128)}, /*index=5*/bf16[128,768]{1,0:T(8,128)(2,1)}) custom-call(bf16[8,96,128]{2,1,0:T(8,128)(2,1)} %bitcast.100, bf16[8,96,128]{2,1,0:T(8,128)(2,1)} %bitcast.90, bf16[8,96,128]{2,1,0:T(8,128)(2,1)} %bitcast.102, ...), custom_call_target="tpu_custom_call" | custom-call | tf_op jit(solution)/shard_map/pallas_call | solution.py:592
  199.6 1.4 fusion.44
  201.0 1.3 slice.108
  202.3 1.3 slice.104
  203.6 1.6 copy.75
  205.2 2.1 %copy.76 = f32[1,96,2304]{2,1,0:T(8,128)} copy(f32[1,96,2304]{2,1,0:T(8,128)} %bitcast.98) | data formatting | bytes 1769472
  207.4 0.7 copy.77
  208.1 1.0 copy.78
  209.1 1.0 copy.79
  (146 shorter events, 4.2 us)
Async XLA Ops:
  0.6 63.8 %copy-start.2 = (bf16[128,768]{1,0:T(8,128)(2,1)S(1)}, bf16[128,768]{1,0:T(8,128)(2,1)}, u32[]{:S(2)}) copy-start(bf16[128,768]{1,0:T(8,128)(2,1)} %param.15) | copy-start | bytes 589828
  68.7 1.1 copy-start.7
  68.8 1.3 copy-start.3
  69.4 1.1 copy-start.11
  69.8 5.8 %copy-start.9 = (bf16[12,64,128]{2,1,0:T(8,128)(2,1)}, bf16[12,64,128]{2,1,0:T(8,128)(2,1)S(1)}, u32[]{:S(2)}) copy-start(bf16[12,64,128]{2,1,0:T(8,128)(2,1)S(1)} %convolution_convert_fusion.1) | copy-start | bytes 589828
  70.5 13.1 %copy-start.1 = (f32[128,768]{1,0:T(8,128)}, f32[128,768]{1,0:T(8,128)S(1)}, u32[]{:S(2)}) copy-start(f32[128,768]{1,0:T(8,128)S(1)} %get-tuple-element.75.refs_18_) | copy-start | bytes 1179652
  70.5 5.1 %copy-start.40 = (f32[128]{0:T(128)}, f32[128]{0:T(128)S(1)}, u32[]{:S(2)}) copy-start(f32[128]{0:T(128)S(1)} %broadcast_multiply_fusion.4) | copy-start | bytes 1540
  70.7 4.8 %copy-start.43 = (f32[128]{0:T(128)}, f32[128]{0:T(128)S(1)}, u32[]{:S(2)}) copy-start(f32[128]{0:T(128)S(1)} %add_rsqrt_fusion) | copy-start | bytes 1540
  70.9 4.7 %copy-start.32 = (f32[768]{0:T(1024)}, f32[768]{0:T(1024)S(1)}, u32[]{:S(2)}) copy-start(f32[768]{0:T(1024)S(1)} %reshape.289) | copy-start | bytes 9220
  70.9 4.7 %copy-start.21 = (bf16[128,768]{1,0:T(8,128)(2,1)S(1)}, bf16[128,768]{1,0:T(8,128)(2,1)}, u32[]{:S(2)}) copy-start(bf16[128,768]{1,0:T(8,128)(2,1)} %refs_7_) | copy-start | bytes 589828
  70.9 10.3 %slice-start = ((s8[4718592]{0:T(1024)(128)(4,1)}), s8[4194304]{0:T(1024)(128)(4,1)S(1)}, s32[]{:S(2)}) async-start(s8[4718592]{0:T(1024)(128)(4,1)} %bitcast.78), calls=%async_computation | async-start | bytes 8388608
  75.6 5.6 %copy-start.13 = (f32[128,3072]{1,0:T(8,128)}, f32[128,3072]{1,0:T(8,128)S(1)}, u32[]{:S(2)}) copy-start(f32[128,3072]{1,0:T(8,128)S(1)} %get-tuple-element.81) | copy-start | bytes 4718596
  75.6 5.6 %slice-start.1 = ((s8[4718592]{0:T(1024)(128)(4,1)}), s8[524288]{0:T(1024)(128)(4,1)S(1)}, s32[]{:S(2)}) async-start(s8[4718592]{0:T(1024)(128)(4,1)} %bitcast.78), calls=%async_computation.1 | async-start | bytes 1048576
  75.6 5.6 %copy-start.41 = (f32[128]{0:T(128)S(1)}, f32[128]{0:T(128)}, u32[]{:S(2)}) copy-start(f32[128]{0:T(128)} %copy-done.40) | copy-start | bytes 1540
  75.6 5.6 %copy-start.44 = (f32[128]{0:T(128)S(1)}, f32[128]{0:T(128)}, u32[]{:S(2)}) copy-start(f32[128]{0:T(128)} %copy-done.43) | copy-start | bytes 1540
  81.2 14.1 %copy-start.4 = (bf16[128,3072]{1,0:T(8,128)(2,1)}, bf16[128,3072]{1,0:T(8,128)(2,1)S(1)}, u32[]{:S(2)}) copy-start(bf16[128,3072]{1,0:T(8,128)(2,1)S(1)} %get-tuple-element.83.refs_6_) | copy-start | bytes 2359300
  81.2 2.3 %copy-start.33 = (f32[768]{0:T(1024)S(1)}, f32[768]{0:T(1024)}, u32[]{:S(2)}) copy-start(f32[768]{0:T(1024)} %copy-done.32) | copy-start | bytes 9220
  85.3 1.7 copy-start.12
  85.3 12.6 %collective-permute-start.5 = (bf16[128,768]{1,0:T(8,128)(2,1)}, bf16[128,768]{1,0:T(8,128)(2,1)}, u32[]{:S(2)}, u32[]{:S(2)}) collective-permute-start(bf16[128,768]{1,0:T(8,128)(2,1)} %get-tuple-element.45.refs_5_), channel_id=1, source_target_pairs={{0,8},{8,0},{16,24},{24,16},{1,9},{9,1},{17,25},{25,17},{2,10},{10... | collective-permute-start | bytes 589832 | tf_op jit(solution)/shard_map/ppermute | solution.py:630
  88.0 2.0 copy-start
  88.2 1.8 copy-start.37
  88.2 1.8 copy-start.39
  90.0 1.6 copy-start.14
  90.0 1.6 copy-start.27
  91.4 1.8 copy-start.18
  91.5 2.4 %copy-start.31 = (f32[768]{0:T(1024)S(1)}, f32[768]{0:T(1024)}, u32[]{:S(2)}) copy-start(f32[768]{0:T(1024)} %get-tuple-element.44) | copy-start | bytes 9220
  91.5 2.5 %copy-start.30 = (f32[768]{0:T(1024)S(1)}, f32[768]{0:T(1024)}, u32[]{:S(2)}) copy-start(f32[768]{0:T(1024)} %get-tuple-element.55) | copy-start | bytes 9220
  91.5 2.5 %copy-start.29 = (f32[768]{0:T(1024)S(1)}, f32[768]{0:T(1024)}, u32[]{:S(2)}) copy-start(f32[768]{0:T(1024)} %get-tuple-element.36) | copy-start | bytes 9220
  91.5 2.6 %copy-start.28 = (f32[768]{0:T(1024)S(1)}, f32[768]{0:T(1024)}, u32[]{:S(2)}) copy-start(f32[768]{0:T(1024)} %get-tuple-element.43) | copy-start | bytes 9220
  91.5 2.7 %copy-start.35 = (f32[3072]{0:T(1024)S(1)}, f32[3072]{0:T(1024)}, u32[]{:S(2)}) copy-start(f32[3072]{0:T(1024)} %get-tuple-element.82) | copy-start | bytes 36868
  91.5 3.9 %copy-start.17 = (bf16[3072,128]{0,1:T(8,128)(2,1)S(1)}, bf16[3072,128]{0,1:T(8,128)(2,1)}, u32[]{:S(2)}) copy-start(bf16[3072,128]{0,1:T(8,128)(2,1)} %get-tuple-element.80) | copy-start | bytes 2359300
  92.7 4.6 %copy-start.19 = (bf16[768,128]{1,0:T(8,128)(2,1)}, bf16[768,128]{1,0:T(8,128)(2,1)S(1)}, u32[]{:S(2)}) copy-start(bf16[768,128]{1,0:T(8,128)(2,1)S(1)} %copy.48) | copy-start | bytes 589828
  92.7 4.6 %collective-permute-start = (bf16[8,96,128]{2,1,0:T(8,128)(2,1)S(1)}, bf16[8,96,128]{2,1,0:T(8,128)(2,1)}, u32[]{:S(2)}, u32[]{:S(2)}) collective-permute-start(bf16[8,96,128]{2,1,0:T(8,128)(2,1)S(1)} %bitcast.99), channel_id=1, source_target_pairs={{0,8},{8,0},{16,24},{24,16},{1,9},{9,1},{17,25},{25,17},{2,10},{10... | collective-permute-start | bytes 589832 | tf_op jit(solution)/shard_map/ppermute | solution.py:630
  93.4 7.5 %copy-start.20 = (bf16[768,128]{1,0:T(8,128)(2,1)}, bf16[768,128]{1,0:T(8,128)(2,1)S(1)}, u32[]{:S(2)}) copy-start(bf16[768,128]{1,0:T(8,128)(2,1)S(1)} %copy.53) | copy-start | bytes 589828
  93.4 4.5 %copy-start.10 = (bf16[12,64,128]{2,1,0:T(8,128)(2,1)S(1)}, bf16[12,64,128]{2,1,0:T(8,128)(2,1)}, u32[]{:S(2)}) copy-start(bf16[12,64,128]{2,1,0:T(8,128)(2,1)} %copy-done.9) | copy-start | bytes 589828
  93.4 4.1 %collective-permute-start.2 = (bf16[8,96,128]{2,1,0:T(8,128)(2,1)S(1)}, bf16[8,96,128]{2,1,0:T(8,128)(2,1)}, u32[]{:S(2)}, u32[]{:S(2)}) collective-permute-start(bf16[8,96,128]{2,1,0:T(8,128)(2,1)S(1)} %bitcast.101), channel_id=1, source_target_pairs={{0,8},{8,0},{16,24},{24,16},{1,9},{9,1},{17,25},{25,17},{2,10},{10... | collective-permute-start | bytes 589832 | tf_op jit(solution)/shard_map/ppermute | solution.py:630
  94.9 1.6 collective-permute-start.8
  95.3 7.7 %collective-permute-start.6 = (bf16[128,3072]{1,0:T(8,128)(2,1)S(1)}, bf16[128,3072]{1,0:T(8,128)(2,1)}, u32[]{:S(2)}, u32[]{:S(2)}) collective-permute-start(bf16[128,3072]{1,0:T(8,128)(2,1)S(1)} %get-tuple-element.83.refs_6_), channel_id=1, source_target_pairs={{0,8},{8,0},{16,24},{24,16},{1,9},{9,1},{17,25},{25,17},{2,10},{10... | collective-permute-start | bytes 2359304 | tf_op jit(solution)/shard_map/ppermute | solution.py:630
  95.8 5.1 %copy-start.5 = (bf16[3072,128]{1,0:T(8,128)(2,1)}, bf16[3072,128]{1,0:T(8,128)(2,1)S(1)}, u32[]{:S(2)}) copy-start(bf16[3072,128]{1,0:T(8,128)(2,1)S(1)} %copy.66) | copy-start | bytes 2359300
  96.5 4.3 %copy-start.34 = (f32[8,96]{1,0:T(8,128)S(1)}, f32[8,96]{1,0:T(8,128)}, u32[]{:S(2)}) copy-start(f32[8,96]{1,0:T(8,128)} %get-tuple-element.58) | copy-start | bytes 9220
  96.5 7.4 %collective-permute-start.3 = (bf16[8,384,128]{2,1,0:T(8,128)(2,1)S(1)}, bf16[8,384,128]{2,1,0:T(8,128)(2,1)}, u32[]{:S(2)}, u32[]{:S(2)}) collective-permute-start(bf16[8,384,128]{2,1,0:T(8,128)(2,1)S(1)} %bitcast.83), channel_id=1, source_target_pairs={{0,8},{8,0},{16,24},{24,16},{1,9},{9,1},{17,25},{25,17},{2,10},{10... | collective-permute-start | bytes 2359304 | tf_op jit(solution)/shard_map/ppermute | solution.py:630
  97.3 5.7 %copy-start.6 = (bf16[128,2304]{1,0:T(8,128)(2,1)}, bf16[128,2304]{1,0:T(8,128)(2,1)S(1)}, u32[]{:S(2)}) copy-start(bf16[128,2304]{1,0:T(8,128)(2,1)S(1)} %copy.61.refs_4_) | copy-start | bytes 1769476
  97.3 5.6 %collective-permute-start.7 = (bf16[128,768]{1,0:T(8,128)(2,1)}, bf16[128,768]{1,0:T(8,128)(2,1)S(1)}, u32[]{:S(2)}, u32[]{:S(2)}) collective-permute-start(bf16[128,768]{1,0:T(8,128)(2,1)} %refs_7_), channel_id=1, source_target_pairs={{0,8},{8,0},{16,24},{24,16},{1,9},{9,1},{17,25},{25,17},{2,10},{10... | collective-permute-start | bytes 589832 | tf_op jit(solution)/shard_map/ppermute | solution.py:630
  97.5 5.4 %collective-permute-start.4 = (bf16[128,2304]{1,0:T(8,128)(2,1)S(1)}, bf16[128,2304]{1,0:T(8,128)(2,1)S(1)}, u32[]{:S(2)}, u32[]{:S(2)}) collective-permute-start(bf16[128,2304]{1,0:T(8,128)(2,1)S(1)} %copy.61.refs_4_), channel_id=1, source_target_pairs={{0,8},{8,0},{16,24},{24,16},{1,9},{9,1},{17,25},{25,17},{2,10},{10... | collective-permute-start | bytes 1769480 | tf_op jit(solution)/shard_map/ppermute | solution.py:630
  97.9 5.1 %collective-permute-start.1 = (bf16[8,96,128]{2,1,0:T(8,128)(2,1)S(1)}, bf16[8,96,128]{2,1,0:T(8,128)(2,1)S(1)}, u32[]{:S(2)}, u32[]{:S(2)}) collective-permute-start(bf16[8,96,128]{2,1,0:T(8,128)(2,1)S(1)} %bitcast.91), channel_id=1, source_target_pairs={{0,8},{8,0},{16,24},{24,16},{1,9},{9,1},{17,25},{25,17},{2,10},{10... | collective-permute-start | bytes 589832 | tf_op jit(solution)/shard_map/ppermute | solution.py:630
  199.5 7.8 %copy-start.23 = (f32[96,768]{1,0:T(8,128)S(1)}, f32[96,768]{1,0:T(8,128)}, u32[]{:S(2)}) copy-start(f32[96,768]{1,0:T(8,128)} %get-tuple-element.33) | copy-start | bytes 884740
  199.5 8.5 %copy-start.16 = (f32[96,3072]{1,0:T(8,128)S(1)}, f32[96,3072]{1,0:T(8,128)}, u32[]{:S(2)}) copy-start(f32[96,3072]{1,0:T(8,128)} %get-tuple-element.34) | copy-start | bytes 3538948
  207.4 1.7 copy-start.15
  (8 other events, 6.0 us)

commit v22 on v20

--- a/solution.py
+++ b/solution.py
@@ -328,7 +328,8 @@
     rows = locals_[2].shape[0]
     if n == 8 and rows % 32 == 0:
         half = rows // 2
-        parts = ((0, 0, None), (1, 0, None), (2, 0, half), (2, half, half), (3, 0, None), (4, 0, None))
+        parts = ((0, 0, None), (1, 0, None), (2, 0, half), (2, half, half), (3, 0, None))
+        parts = parts + tuple((a, 0, None) for a in range(4, count))
         plane_only = ((0, 1), (2, 3))
         first_core = (0, 4)
     else:
@@ -682,18 +683,9 @@
         proj_weight[layer_index],
     )
     rows_local = local_weights[0].shape[0]
-    small_row = jnp.concatenate(small_local, axis=1)
-    fulls = gather_weights(list(local_weights) + [small_row], shard)
+    fulls = gather_weights(list(local_weights) + list(small_local), shard)
     weights = tuple(f.reshape(-1, f.shape[-1]) for f in fulls[:4])
-    halves = [take_half(w, core, 1) for w in local_weights]
-    half_widths = [h.size // rows_local for h in halves]
-    packed_all = fulls[4].reshape(shard, -1)
-    small = []
-    start = 0
-    for width in widths:
-        small.append(to_float(packed_all[:, start : start + width].reshape(-1)))
-        start += width
-    small = tuple(small)
+    small = tuple(to_float(f.reshape(-1)) for f in fulls[4:])
 
     residual = to_float(tokens)
     saved = layer_forward(residual, allowed, small, weights)

time: 210 us -> 212 us (level)
  Pallas kernels: 155 us -> 158 us
    pallas_call x1, Pallas kernels: 60.4 us -> 62.7 us  [gather_weights(): pl.pallas_call(functools.partial(gather_kernel, n, count, parts, plane_on...]
    unnamed x100 -> x101, local copies, waits for them, and re-layouts: 10.4 us -> 9.2 us
  transfers between devices with their start and end apart: 9 -> 9, of which waited for: 1 -> 0; matrix products, arithmetic and copies ran while one was open for 6% -> 7% of each run, Pallas kernels for 0% -> 0%
where the time goes in v22:
time: 212 us; the launch traced here: 211 us
  Pallas kernels  158 us (75%)
  matrix products  20.5 us (10%)
  local copies, waits for them, and re-layouts  19.3 us (9%)
  other arithmetic  9.84 us (5%)
  starting transfers between devices  2.3 us (1%)
    pallas_call x1, Pallas kernels, reduce_gradients(): pl.pallas_call(functools.partial(reduce_kernel, n, count, mm), out_shape=...  95 us
    pallas_call x1, Pallas kernels, gather_weights(): pl.pallas_call(functools.partial(gather_kernel, n, count, parts, plane_on...  62.7 us
    unnamed x101, local copies, waits for them, and re-layouts  9.2 us
    dot_general x1, matrix products, layer_backward(): jnp.einsum('td,fd->tf', proj_in, proj_weight, preferred_element_type=jnp....  5.54 us
    dot_general x1, matrix products, layer_forward(): jnp.dot(second_low, fc_weight, preferred_element_type=jnp.float32) + fc_bias  4.68 us
  transfers between devices with their start and end apart: 9, of which 0 were waited for; matrix products, arithmetic and copies ran while one was open for 7% of the time, Pallas kernels for 0%

profile of v22, /device:TPU:0, one launch (start us, length us, event | category | flops | bytes accessed | tf_op | source)
XLA Modules:
  0.0 211.1 jit_solution(2352827410413543446)
XLA Ops:
  0.7 62.7 %shard_map.254 = (bf16[8,96,2304]{2,1,0:T(8,128)(2,1)}, bf16[8,96,768]{2,1,0:T(8,128)(2,1)}, bf16[8,96,3072]{2,1,0:T(8,128)(2,1)}, bf16[8,384,768]{2,1,0:T(8,128...) custom-call(bf16[96,2304]{1,0:T(8,128)(2,1)} %bitcast.103, ...), custom_call_target="tpu_custom_call" | custom-call | tf_op jit(solution)/shard_map/pallas_call | solution.py:341
  63.4 0.7 convert_element_type.148
  64.3 0.7 convert_reduce_fusion.8
  65.1 0.7 convert_reduce_fusion.10
  66.0 0.2 fusion.34
  66.2 2.7 %fusion = bf16[128,2304]{1,0:T(8,128)(2,1)S(1)} fusion(bf16[768,2304]{1,0:T(8,128)(2,1)} %bitcast.69, f32[2304]{0:T(1024)S(1)} %pad_maximum_fusion, bf16[128,768]{1,0:T(8,128)(2,1)S(1)} %copy-done.2, f32[768]{0:T(1024)S(1)} %reshape.282, f32[768]{0:T(1024)S(1)} %reshape.281, f32[128]{0:T(128)S(1)} %add_rsqrt_fusion.1, f32[128]{0:T(128)S(1)} %broadcast_multiply_fusion.5), kind=kOutput, calls=%fused_computation.3 | convolution fusion | flops 454164480 | bytes 4341760 | tf_op jit(solution)/shard_map/dot_general | solution.py:47
  69.3 0.3 copy-done.43
  69.7 0.3 fusion.44
  70.4 0.2 convolution_convert_fusion.1
  70.7 0.3 copy-done.11
  71.0 0.4 fusion.45
  71.5 0.2 multiply_reduce_fusion.3
  72.0 4.7 %fusion.15 = (bf16[3072,128]{0,1:T(8,128)(2,1)}, f32[128,3072]{1,0:T(8,128)S(1)}) fusion(f32[3072]{0:T(1024)S(1)} %bitcast.106, bf16[768,3072]{1,0:T(8,128)(2,1)} %bitcast.75, f32[128,768]{1,0:T(8,128)S(1)} %get-tuple-element.83.refs_18_, f32[768]{0:T(1024)S(1)} %reshape.285, f32[768]{0:T(1024)S(1)} %reshape.284, f32[128]{0:T(128)S(1)} %add_rsqrt_fusion, ...), kind=kOutput, calls=%fused_computation.21 | convolution fusion | flops 608403456 | bytes 7490560 | tf_op jit(solution)/shard_map/dot_general | solution.py:69
  76.7 5.5 %convert_reduce_fusion = (f32[3072]{0:T(1024)}, bf16[128,3072]{1,0:T(8,128)(2,1)S(1)}) fusion(f32[128,3072]{1,0:T(8,128)S(1)} %get-tuple-element.89, bf16[3072,768]{1,0:T(8,128)(2,1)} %bitcast.73, bf16[128,768]{1,0:T(8,128)(2,1)S(1)} %copy-done.21), kind=kOutput, calls=%fused_computation.23 | convolution fusion | flops 612627456 | bytes 7286784 | tf_op jit(solution)/shard_map/td,fd->tf/dot_general | solution.py:97
  82.3 2.3 %multiply_reduce_fusion.1 = (f32[768]{0:T(1024)}, f32[128]{0:T(128)S(1)}, f32[128]{0:T(128)S(1)}, f32[768]{0:T(1024)}, f32[128,768]{1,0:T(8,128)S(1)}) fusion(f32[128,768]{1,0:T(8,128)S(1)} %get-tuple-element.83.refs_18_, f32[128]{0:T(128)S(1)} %copy-done.45, f32[128]{0:T(128)S(1)} %copy-done.39, f32[768]{0:T(1024)S(1)} %reshape.284, ...), kind=kOutput, calls=%fused_computation.60 | convolution fusion | flops 604862720 | bytes 6302720 | tf_op jit(solution)/shard_map/tf,df->td/dot_general | solution.py:101
  84.7 1.7 convert_reduce_fusion.4
  86.4 1.5 convolution_convert_fusion
  88.1 0.3 multiply_reduce_fusion
  88.4 0.2 multiply_convert_fusion.1
  88.6 0.4 copy-done.8
  89.0 0.2 fusion.18
  89.3 0.4 fusion.19
  89.6 0.4 convolution_bitcast_fusion.1
  90.0 0.4 convert_reduce_fusion.1
  90.4 0.6 copy-done
  91.0 1.5 fusion.30
  92.6 1.0 fusion.33
  93.8 0.5 collective-permute-start
  95.2 0.7 concatenate.12
  95.9 0.5 collective-permute-start.8
  96.4 0.2 copy.61.refs_4_
  96.7 1.7 copy.66
  98.5 0.5 collective-permute-start.7
  99.1 0.4 collective-permute-start.3
  99.6 2.9 %multiply_convert_fusion.refs_17_ = bf16[128,3072]{1,0:T(8,128)(2,1)} fusion(f32[128,3072]{1,0:T(8,128)} %copy-done.13), kind=kLoop, calls=%fused_computation.22 | loop fusion | flops 3538944 | bytes 2359296 | tf_op jit(solution)/shard_map/convert_element_type | solution.py:70
  102.5 0.7 reshape.287.refs_19_
  103.2 0.8 add.118
  104.0 0.6 reshape.280.refs_16_
  104.6 0.9 copy-done.17
  105.6 95.0 %shard_map.255 = (f32[96,2304]{1,0:T(8,128)}, f32[96,768]{1,0:T(8,128)}, f32[96,3072]{1,0:T(8,128)}, f32[384,768]{1,0:T(8,128)}, f32[1,1152]{1,0:T(1,128)}, /*index=5*/bf16[128,768]{1,0:T(8,128)(2,1)}) custom-call(bf16[8,96,128]{2,1,0:T(8,128)(2,1)} %bitcast.98, bf16[8,96,128]{2,1,0:T(8,128)(2,1)} %bitcast.88, bf16[8,96,128]{2,1,0:T(8,128)(2,1)} %bitcast.100, ...), custom_call_target="tpu_custom_call" | custom-call | tf_op jit(solution)/shard_map/pallas_call | solution.py:593
  200.6 1.4 fusion.43
  202.0 1.3 slice.76
  203.3 1.3 slice.72
  204.6 1.6 copy.72
  206.2 2.1 %copy.73 = f32[1,96,2304]{2,1,0:T(8,128)} copy(f32[1,96,2304]{2,1,0:T(8,128)} %bitcast.96) | data formatting | bytes 1769472
  208.3 0.7 copy.74
  209.0 1.0 copy.75
  210.0 1.0 copy.76
  (149 shorter events, 3.1 us)
Async XLA Ops:
  0.7 65.2 %copy-start.2 = (bf16[128,768]{1,0:T(8,128)(2,1)S(1)}, bf16[128,768]{1,0:T(8,128)(2,1)}, u32[]{:S(2)}) copy-start(bf16[128,768]{1,0:T(8,128)(2,1)} %param.15) | copy-start | bytes 589828
  66.0 3.0 %copy-start.34 = (f32[128]{0:T(128)}, f32[128]{0:T(128)S(1)}, u32[]{:S(2)}) copy-start(f32[128]{0:T(128)S(1)} %broadcast_multiply_fusion.5) | copy-start | bytes 1540
  66.2 2.8 %copy-start.36 = (f32[128]{0:T(128)}, f32[128]{0:T(128)S(1)}, u32[]{:S(2)}) copy-start(f32[128]{0:T(128)S(1)} %add_rsqrt_fusion.1) | copy-start | bytes 1540
  69.7 1.3 copy-start.3
  70.4 1.5 copy-start.33
  70.7 6.0 %copy-start.9 = (bf16[12,64,128]{2,1,0:T(8,128)(2,1)}, bf16[12,64,128]{2,1,0:T(8,128)(2,1)S(1)}, u32[]{:S(2)}) copy-start(bf16[12,64,128]{2,1,0:T(8,128)(2,1)S(1)} %convolution_convert_fusion.1) | copy-start | bytes 589828
  71.5 13.2 %copy-start.1 = (f32[128,768]{1,0:T(8,128)}, f32[128,768]{1,0:T(8,128)S(1)}, u32[]{:S(2)}) copy-start(f32[128,768]{1,0:T(8,128)S(1)} %get-tuple-element.83.refs_18_) | copy-start | bytes 1179652
  71.5 5.2 %copy-start.38 = (f32[128]{0:T(128)}, f32[128]{0:T(128)S(1)}, u32[]{:S(2)}) copy-start(f32[128]{0:T(128)S(1)} %broadcast_multiply_fusion.4) | copy-start | bytes 1540
  71.7 4.9 %copy-start.44 = (f32[128]{0:T(128)}, f32[128]{0:T(128)S(1)}, u32[]{:S(2)}) copy-start(f32[128]{0:T(128)S(1)} %add_rsqrt_fusion) | copy-start | bytes 1540
  71.9 4.7 %copy-start.30 = (f32[768]{0:T(1024)}, f32[768]{0:T(1024)S(1)}, u32[]{:S(2)}) copy-start(f32[768]{0:T(1024)S(1)} %reshape.285) | copy-start | bytes 9220
  72.0 4.7 %copy-start.21 = (bf16[128,768]{1,0:T(8,128)(2,1)S(1)}, bf16[128,768]{1,0:T(8,128)(2,1)}, u32[]{:S(2)}) copy-start(bf16[128,768]{1,0:T(8,128)(2,1)} %refs_7_.2) | copy-start | bytes 589828
  72.0 10.3 %slice-start = ((s8[4718592]{0:T(1024)(128)(4,1)}), s8[4194304]{0:T(1024)(128)(4,1)S(1)}, s32[]{:S(2)}) async-start(s8[4718592]{0:T(1024)(128)(4,1)} %bitcast.76), calls=%async_computation | async-start | bytes 8388608
  76.7 5.6 %copy-start.13 = (f32[128,3072]{1,0:T(8,128)}, f32[128,3072]{1,0:T(8,128)S(1)}, u32[]{:S(2)}) copy-start(f32[128,3072]{1,0:T(8,128)S(1)} %get-tuple-element.89) | copy-start | bytes 4718596
  76.7 5.6 %slice-start.1 = ((s8[4718592]{0:T(1024)(128)(4,1)}), s8[524288]{0:T(1024)(128)(4,1)S(1)}, s32[]{:S(2)}) async-start(s8[4718592]{0:T(1024)(128)(4,1)} %bitcast.76), calls=%async_computation.1 | async-start | bytes 1048576
  76.7 5.6 %copy-start.39 = (f32[128]{0:T(128)S(1)}, f32[128]{0:T(128)}, u32[]{:S(2)}) copy-start(f32[128]{0:T(128)} %copy-done.38) | copy-start | bytes 1540
  76.7 5.6 %copy-start.45 = (f32[128]{0:T(128)S(1)}, f32[128]{0:T(128)}, u32[]{:S(2)}) copy-start(f32[128]{0:T(128)} %copy-done.44) | copy-start | bytes 1540
  82.3 14.1 %copy-start.4 = (bf16[128,3072]{1,0:T(8,128)(2,1)}, bf16[128,3072]{1,0:T(8,128)(2,1)S(1)}, u32[]{:S(2)}) copy-start(bf16[128,3072]{1,0:T(8,128)(2,1)S(1)} %get-tuple-element.91.refs_6_) | copy-start | bytes 2359300
  82.3 2.4 %copy-start.31 = (f32[768]{0:T(1024)S(1)}, f32[768]{0:T(1024)}, u32[]{:S(2)}) copy-start(f32[768]{0:T(1024)} %copy-done.30) | copy-start | bytes 9220
  86.4 1.7 copy-start.12
  86.4 13.1 %collective-permute-start.5 = (bf16[128,768]{1,0:T(8,128)(2,1)}, bf16[128,768]{1,0:T(8,128)(2,1)}, u32[]{:S(2)}, u32[]{:S(2)}) collective-permute-start(bf16[128,768]{1,0:T(8,128)(2,1)} %get-tuple-element.61.refs_5_), channel_id=1, source_target_pairs={{0,8},{8,0},{16,24},{24,16},{1,9},{9,1},{17,25},{25,17},{2,10},{10... | collective-permute-start | bytes 589832 | tf_op jit(solution)/shard_map/ppermute | solution.py:631
  89.0 2.0 copy-start
  89.2 1.8 copy-start.35
  89.2 1.8 copy-start.37
  91.0 1.6 copy-start.14
  91.0 1.6 copy-start.25
  92.5 1.8 copy-start.18
  92.5 2.4 %copy-start.29 = (f32[768]{0:T(1024)S(1)}, f32[768]{0:T(1024)}, u32[]{:S(2)}) copy-start(f32[768]{0:T(1024)} %get-tuple-element.60) | copy-start | bytes 9220
  92.5 2.4 %copy-start.28 = (f32[768]{0:T(1024)S(1)}, f32[768]{0:T(1024)}, u32[]{:S(2)}) copy-start(f32[768]{0:T(1024)} %get-tuple-element.71) | copy-start | bytes 9220
  92.5 2.5 %copy-start.27 = (f32[768]{0:T(1024)S(1)}, f32[768]{0:T(1024)}, u32[]{:S(2)}) copy-start(f32[768]{0:T(1024)} %get-tuple-element.50) | copy-start | bytes 9220
  92.5 2.6 %copy-start.26 = (f32[768]{0:T(1024)S(1)}, f32[768]{0:T(1024)}, u32[]{:S(2)}) copy-start(f32[768]{0:T(1024)} %get-tuple-element.57) | copy-start | bytes 9220
  92.5 2.6 %copy-start.32 = (f32[3072]{0:T(1024)S(1)}, f32[3072]{0:T(1024)}, u32[]{:S(2)}) copy-start(f32[3072]{0:T(1024)} %get-tuple-element.90) | copy-start | bytes 36868
  93.7 4.7 %copy-start.19 = (bf16[768,128]{1,0:T(8,128)(2,1)}, bf16[768,128]{1,0:T(8,128)(2,1)S(1)}, u32[]{:S(2)}) copy-start(bf16[768,128]{1,0:T(8,128)(2,1)S(1)} %copy.48) | copy-start | bytes 589828
  93.8 5.2 %collective-permute-start = (bf16[8,96,128]{2,1,0:T(8,128)(2,1)S(1)}, bf16[8,96,128]{2,1,0:T(8,128)(2,1)}, u32[]{:S(2)}, u32[]{:S(2)}) collective-permute-start(bf16[8,96,128]{2,1,0:T(8,128)(2,1)S(1)} %bitcast.97), channel_id=1, source_target_pairs={{0,8},{8,0},{16,24},{24,16},{1,9},{9,1},{17,25},{25,17},{2,10},{10... | collective-permute-start | bytes 589832 | tf_op jit(solution)/shard_map/ppermute | solution.py:631
  94.5 8.0 %copy-start.20 = (bf16[768,128]{1,0:T(8,128)(2,1)}, bf16[768,128]{1,0:T(8,128)(2,1)S(1)}, u32[]{:S(2)}) copy-start(bf16[768,128]{1,0:T(8,128)(2,1)S(1)} %copy.53) | copy-start | bytes 589828
  94.5 5.1 %copy-start.10 = (bf16[12,64,128]{2,1,0:T(8,128)(2,1)S(1)}, bf16[12,64,128]{2,1,0:T(8,128)(2,1)}, u32[]{:S(2)}) copy-start(bf16[12,64,128]{2,1,0:T(8,128)(2,1)} %copy-done.9) | copy-start | bytes 589828
  94.5 4.6 %collective-permute-start.2 = (bf16[8,96,128]{2,1,0:T(8,128)(2,1)S(1)}, bf16[8,96,128]{2,1,0:T(8,128)(2,1)}, u32[]{:S(2)}, u32[]{:S(2)}) collective-permute-start(bf16[8,96,128]{2,1,0:T(8,128)(2,1)S(1)} %bitcast.99), channel_id=1, source_target_pairs={{0,8},{8,0},{16,24},{24,16},{1,9},{9,1},{17,25},{25,17},{2,10},{10... | collective-permute-start | bytes 589832 | tf_op jit(solution)/shard_map/ppermute | solution.py:631
  95.9 2.5 %collective-permute-start.8 = (f32[8,1152]{1,0:T(8,128)}, f32[8,1152]{1,0:T(8,128)}, u32[]{:S(2)}, u32[]{:S(2)}) collective-permute-start(f32[8,1152]{1,0:T(8,128)} %concatenate.12), channel_id=1, source_target_pairs={{0,8},{8,0},{16,24},{24,16},{1,9},{9,1},{17,25},{25,17},{2,10},{10... | collective-permute-start | bytes 110600 | tf_op jit(solution)/shard_map/ppermute | solution.py:631
  96.4 8.2 %collective-permute-start.6 = (bf16[128,3072]{1,0:T(8,128)(2,1)S(1)}, bf16[128,3072]{1,0:T(8,128)(2,1)S(1)}, u32[]{:S(2)}, u32[]{:S(2)}) collective-permute-start(bf16[128,3072]{1,0:T(8,128)(2,1)S(1)} %get-tuple-element.91.refs_6_), channel_id=1, source_target_pairs={{0,8},{8,0},{16,24},{24,16},{1,9},{9,1},{17,25},{25,17},{2,10},{10... | collective-permute-start | bytes 2359304 | tf_op jit(solution)/shard_map/ppermute | solution.py:631
  96.7 5.8 %copy-start.6 = (bf16[128,2304]{1,0:T(8,128)(2,1)}, bf16[128,2304]{1,0:T(8,128)(2,1)S(1)}, u32[]{:S(2)}) copy-start(bf16[128,2304]{1,0:T(8,128)(2,1)S(1)} %copy.61.refs_4_) | copy-start | bytes 1769476
  98.4 7.1 %copy-start.5 = (bf16[3072,128]{1,0:T(8,128)(2,1)}, bf16[3072,128]{1,0:T(8,128)(2,1)S(1)}, u32[]{:S(2)}) copy-start(bf16[3072,128]{1,0:T(8,128)(2,1)S(1)} %copy.66) | copy-start | bytes 2359300
  98.4 4.0 %copy-start.40 = (bf16[8,1,96]{2,1,0:T(2,128)(2,1)S(1)}, bf16[8,1,96]{2,1,0:T(2,128)(2,1)}, u32[]{:S(2)}) copy-start(bf16[8,1,96]{2,1,0:T(2,128)(2,1)} %get-tuple-element.43) | copy-start | bytes 4612
  98.5 6.2 %collective-permute-start.7 = (bf16[128,768]{1,0:T(8,128)(2,1)}, bf16[128,768]{1,0:T(8,128)(2,1)}, u32[]{:S(2)}, u32[]{:S(2)}) collective-permute-start(bf16[128,768]{1,0:T(8,128)(2,1)} %refs_7_.2), channel_id=1, source_target_pairs={{0,8},{8,0},{16,24},{24,16},{1,9},{9,1},{17,25},{25,17},{2,10},{10... | collective-permute-start | bytes 589832 | tf_op jit(solution)/shard_map/ppermute | solution.py:631
  99.0 5.6 %collective-permute-start.4 = (bf16[128,2304]{1,0:T(8,128)(2,1)S(1)}, bf16[128,2304]{1,0:T(8,128)(2,1)}, u32[]{:S(2)}, u32[]{:S(2)}) collective-permute-start(bf16[128,2304]{1,0:T(8,128)(2,1)S(1)} %copy.61.refs_4_), channel_id=1, source_target_pairs={{0,8},{8,0},{16,24},{24,16},{1,9},{9,1},{17,25},{25,17},{2,10},{10... | collective-permute-start | bytes 1769480 | tf_op jit(solution)/shard_map/ppermute | solution.py:631
  99.1 6.5 %collective-permute-start.3 = (bf16[8,384,128]{2,1,0:T(8,128)(2,1)S(1)}, bf16[8,384,128]{2,1,0:T(8,128)(2,1)}, u32[]{:S(2)}, u32[]{:S(2)}) collective-permute-start(bf16[8,384,128]{2,1,0:T(8,128)(2,1)S(1)} %bitcast.81), channel_id=1, source_target_pairs={{0,8},{8,0},{16,24},{24,16},{1,9},{9,1},{17,25},{25,17},{2,10},{10... | collective-permute-start | bytes 2359304 | tf_op jit(solution)/shard_map/ppermute | solution.py:631
  99.5 5.1 %collective-permute-start.1 = (bf16[8,96,128]{2,1,0:T(8,128)(2,1)S(1)}, bf16[8,96,128]{2,1,0:T(8,128)(2,1)S(1)}, u32[]{:S(2)}, u32[]{:S(2)}) collective-permute-start(bf16[8,96,128]{2,1,0:T(8,128)(2,1)S(1)} %bitcast.89), channel_id=1, source_target_pairs={{0,8},{8,0},{16,24},{24,16},{1,9},{9,1},{17,25},{25,17},{2,10},{10... | collective-permute-start | bytes 589832 | tf_op jit(solution)/shard_map/ppermute | solution.py:631
  200.6 7.8 %copy-start.22 = (f32[96,768]{1,0:T(8,128)S(1)}, f32[96,768]{1,0:T(8,128)}, u32[]{:S(2)}) copy-start(f32[96,768]{1,0:T(8,128)} %get-tuple-element.47) | copy-start | bytes 884740
  200.6 8.5 %copy-start.16 = (f32[96,3072]{1,0:T(8,128)S(1)}, f32[96,3072]{1,0:T(8,128)}, u32[]{:S(2)}) copy-start(f32[96,3072]{1,0:T(8,128)} %get-tuple-element.48) | copy-start | bytes 3538948
  208.3 1.7 copy-start.15
  (9 other events, 9.0 us)

commit v23 on v20

--- a/solution.py
+++ b/solution.py
@@ -375,8 +375,8 @@
     dyp = refs[3 * mm : 4 * mm]
     contrib = (None,) * mm + refs[4 * mm : 3 * mm + count]
     refs = refs[3 * mm + count :]
-    hidden, residual, bias, weight = refs[:4]
-    refs = refs[4:]
+    residual, bias, weight = refs[:3]
+    refs = refs[3:]
     out = refs[:count]
     tokens = refs[count]
     refs = refs[count + 1 :]
@@ -553,9 +553,19 @@
             weight_copy.wait()
             width = 256
 
+            depth = xt[mm - 1].shape[1]
+
             def project(i, carry):
                 window = pl.ds(pl.multiple_of(i * width, width), width)
-                product = jnp.dot(hidden[...], weight_vmem[:, window], preferred_element_type=jnp.float32)
+                product = None
+                for j in range(n):
+                    part = lax.dot_general(
+                        xt[mm - 1][j],
+                        weight_vmem[j * depth : (j + 1) * depth, window],
+                        (((0,), (0,)), ((), ())),
+                        preferred_element_type=jnp.float32,
+                    )
+                    product = part if product is None else product + part
                 tokens[:, window] = (residual[:, window] + product + bias[:, window]).astype(tokens.dtype)
                 return carry
 
@@ -592,10 +602,10 @@
     return pl.pallas_call(
         functools.partial(reduce_kernel, n, count, mm),
         out_shape=[jax.ShapeDtypeStruct(b, jnp.float32) for b in blocks]
-        + [jax.ShapeDtypeStruct(head[1].shape, jnp.bfloat16)],
+        + [jax.ShapeDtypeStruct(head[0].shape, jnp.bfloat16)],
         in_specs=[pl.BlockSpec(memory_space=pltpu.VMEM)] * (4 * mm)
         + [pl.BlockSpec(memory_space=pl.ANY)] * len(contribs)
-        + [pl.BlockSpec(memory_space=pltpu.VMEM)] * 3
+        + [pl.BlockSpec(memory_space=pltpu.VMEM)] * 2
         + [pl.BlockSpec(memory_space=pl.ANY)],
         out_specs=[pl.BlockSpec(memory_space=pltpu.VMEM)] * (count + 1),
         scratch_shapes=[vmem((steps,) + b, t) for b, t in zip(blocks, ring_types)]
@@ -616,7 +626,7 @@
             dma((count,)),
             dma((count,)),
             dma((count,)),
-            pltpu.VMEM(head[3].shape, head[3].dtype),
+            pltpu.VMEM(head[2].shape, head[2].dtype),
             dma(()),
         ],
         compiler_params=pltpu.CompilerParams(
@@ -707,7 +717,7 @@
     for x, dy in pairs:
         rows_t = x.T.reshape(shard, -1, x.shape[0])
         pairs_t.append((rows_t, dy, swap_core(rows_t), swap_core(dy)))
-    head = (saved["hidden_low"], saved["after_attn"], small[7].reshape(1, -1), weights[3])
+    head = (saved["after_attn"], small[7].reshape(1, -1), weights[3])
     *totals, out_tokens = reduce_gradients(pairs_t, [small_chip.reshape(shard, 1, -1)], head, shard)
     small_share = totals[4]
     owned = [t[None] for t in totals[:4]]

time: 210 us -> 211 us (level)
  other arithmetic: 8.38 us -> 4.75 us
  local copies, waits for them, and re-layouts: 20.8 us -> 23.7 us
    convert_element_type x1 -> x0, other arithmetic: 2.78 us -> none  [layer_forward(): hidden_low = jax.nn.gelu(hidden_pre, approximate=True).astype(jnp.bfloat16)]
    dot_general x1, matrix products: 2.32 us -> 4.75 us  [layer_backward(): jnp.einsum('tf,df->td', pre_grad, fc_weight, preferred_element_type=jnp.f...]
    reshape x1, local copies, waits for them, and re-layouts: 0.37 us -> 2.55 us  [per_device(): rows_t = x.T.reshape(shard, -1, x.shape[0])]
    unnamed x100 -> x102, local copies, waits for them, and re-layouts: 10.4 us -> 11.9 us
  transfers between devices with their start and end apart: 9 -> 9, of which waited for: 1 -> 3; matrix products, arithmetic and copies ran while one was open for 6% -> 8% of each run, Pallas kernels for 0% -> 0%
where the time goes in v23:
time: 211 us; the launch traced here: 210 us
  Pallas kernels  155 us (73%)
  local copies, waits for them, and re-layouts  23.7 us (11%)
  matrix products  21.3 us (10%)
  other arithmetic  4.75 us (2%)
  starting transfers between devices  2.58 us (1%)
    pallas_call x1, Pallas kernels, reduce_gradients(): pl.pallas_call(functools.partial(reduce_kernel, n, count, mm), out_shape=...  94.4 us
    pallas_call x1, Pallas kernels, gather_weights(): pl.pallas_call(functools.partial(gather_kernel, n, count, parts, plane_on...  60.4 us
    unnamed x102, local copies, waits for them, and re-layouts  11.9 us
    dot_general x1, matrix products, layer_backward(): jnp.einsum('td,fd->tf', proj_in, proj_weight, preferred_element_type=jnp....  4.96 us
    dot_general x1, matrix products, layer_backward(): jnp.einsum('tf,df->td', pre_grad, fc_weight, preferred_element_type=jnp.f...  4.75 us
    dot_general x1, matrix products, layer_forward(): jnp.dot(second_low, fc_weight, preferred_element_type=jnp.float32) + fc_bias  4.55 us
  transfers between devices with their start and end apart: 9, of which 3 were waited for; matrix products, arithmetic and copies ran while one was open for 8% of the time, Pallas kernels for 0%

profile of v23, /device:TPU:0, one launch (start us, length us, event | category | flops | bytes accessed | tf_op | source)
XLA Modules:
  0.0 210.1 jit_solution(12401174841927103326)
XLA Ops:
  0.7 1.5 concatenate.13.refs_4_
  2.2 60.4 %shard_map.254 = (bf16[8,96,2304]{2,1,0:T(8,128)(2,1)}, bf16[8,96,768]{2,1,0:T(8,128)(2,1)}, bf16[8,96,3072]{2,1,0:T(8,128)(2,1)}, bf16[8,384,768]{2,1,0:T(8,128)(2,1)}, bf16[8,1,1152]{2,1,0:T(2,128)(2,1)}) custom-call(bf16[96,2304]{1,0:T(8,128)(2,1)} %bitcast.103, bf16[96,768]{1,0:T(8,128)(2,1)} %bitcast.105, bf16[96,3072]{1,0:T(8,128)(2,1)} %bitcast.101, ...), custom_call_target="tpu_custom_call" | custom-call | tf_op jit(solution)/shard_map/pallas_call | solution.py:340
  62.6 0.8 copy.69
  63.4 0.7 slice_convert_fusion.2
  65.3 2.7 %fusion = bf16[128,2304]{1,0:T(8,128)(2,1)S(1)} fusion(bf16[768,2304]{1,0:T(8,128)(2,1)} %bitcast.71, f32[2304]{0:T(1024)S(1)} %pad_maximum_fusion, bf16[128,768]{1,0:T(8,128)(2,1)S(1)} %copy-done.2, f32[768]{0:T(1024)S(1)} %reshape.286, f32[768]{0:T(1024)S(1)} %reshape.285, f32[128]{0:T(128)S(1)} %add_rsqrt_fusion.1, f32[128]{0:T(128)S(1)} %broadcast_multiply_fusion.5), kind=kOutput, calls=%fused_computation.3 | convolution fusion | flops 454164480 | bytes 4341760 | tf_op jit(solution)/shard_map/dot_general | solution.py:47
  68.4 0.3 copy-done.45
  68.8 0.3 fusion.45
  69.8 0.3 copy-done.10
  70.1 0.3 copy-done.8
  70.5 0.4 fusion.46
  71.3 4.5 %fusion.15 = (bf16[3072,128]{0,1:T(8,128)(2,1)}, f32[128,3072]{1,0:T(8,128)S(1)}) fusion(f32[3072]{0:T(1024)S(1)} %reshape.290, bf16[768,3072]{1,0:T(8,128)(2,1)} %bitcast.77, f32[128,768]{1,0:T(8,128)S(1)} %get-tuple-element.75.refs_17_, f32[768]{0:T(1024)S(1)} %reshape.289, f32[768]{0:T(1024)S(1)} %reshape.288, f32[128]{0:T(128)S(1)} %add_rsqrt_fusion, ...), kind=kOutput, calls=%fused_computation.21 | convolution fusion | flops 608403456 | bytes 7490560 | tf_op jit(solution)/shard_map/dot_general | solution.py:69
  75.9 5.0 %convert_reduce_fusion = (f32[3072]{0:T(1024)}, bf16[128,3072]{1,0:T(8,128)(2,1)S(1)}) fusion(f32[128,3072]{1,0:T(8,128)S(1)} %get-tuple-element.81, bf16[3072,768]{1,0:T(8,128)(2,1)} %bitcast.75, bf16[128,768]{1,0:T(8,128)(2,1)S(1)} %copy-done.20), kind=kOutput, calls=%fused_computation.22 | convolution fusion | flops 612627456 | bytes 7286784 | tf_op jit(solution)/shard_map/td,fd->tf/dot_general | solution.py:97
  80.9 2.5 %copy.66 = bf16[3072,128]{1,0:T(8,128)(2,1)} copy(bf16[3072,128]{0,1:T(8,128)(2,1)} %get-tuple-element.80) | data formatting | bytes 1572864 | tf_op jit(solution)/shard_map/reshape | solution.py:718
  83.4 0.3 collective-permute-start.3
  83.7 4.8 %multiply_reduce_fusion.1 = (f32[768]{0:T(1024)}, f32[128]{0:T(128)S(1)}, f32[128]{0:T(128)S(1)}, f32[768]{0:T(1024)}, f32[128,768]{1,0:T(8,128)S(1)}) fusion(f32[128,768]{1,0:T(8,128)S(1)} %get-tuple-element.75.refs_17_, f32[128]{0:T(128)} %copy-done.46, f32[128]{0:T(128)} %copy-done.43, f32[768]{0:T(1024)S(1)} %reshape.288, ...), kind=kOutput, calls=%fused_computation.59 | convolution fusion | flops 604862720 | bytes 6302720 | tf_op jit(solution)/shard_map/tf,df->td/dot_general | solution.py:101
  88.5 1.7 convert_reduce_fusion.4
  90.2 0.7 copy-done.12
  90.9 0.5 convolution_convert_fusion
  91.6 0.3 multiply_reduce_fusion
  92.1 0.4 copy-done.7
  92.8 0.4 fusion.19
  93.1 0.4 convolution_bitcast_fusion.1
  93.5 0.4 convert_reduce_fusion.1
  93.9 0.6 copy-done
  94.5 1.5 fusion.30
  96.1 1.0 fusion.33
  97.3 0.4 collective-permute-start
  97.9 0.3 collective-permute-start.4
  98.9 0.4 collective-permute-start.8
  99.5 0.7 collective-permute-done.8
  100.2 0.3 collective-permute-start.2
  100.5 0.5 collective-permute-start.5
  101.0 0.7 collective-permute-done.2.refs_10_
  101.7 0.3 collective-permute-start.1
  102.4 0.5 copy-done.27
  102.9 0.7 reshape.291.refs_18_
  103.6 0.6 reshape.284.refs_16_
  104.3 0.6 copy-done.28
  104.9 0.3 copy-done.23
  105.2 94.4 %shard_map.255 = (f32[96,2304]{1,0:T(8,128)}, f32[96,768]{1,0:T(8,128)}, f32[96,3072]{1,0:T(8,128)}, f32[384,768]{1,0:T(8,128)}, f32[1,1152]{1,0:T(1,128)}, /*index=5*/bf16[128,768]{1,0:T(8,128)(2,1)}) custom-call(bf16[8,96,128]{2,1,0:T(8,128)(2,1)} %bitcast.98, bf16[8,96,128]{2,1,0:T(8,128)(2,1)} %bitcast.88, bf16[8,96,128]{2,1,0:T(8,128)(2,1)} %bitcast.100, ...), custom_call_target="tpu_custom_call" | custom-call | tf_op jit(solution)/shard_map/pallas_call | solution.py:602
  199.6 1.4 fusion.44
  201.0 1.3 slice.108
  202.3 1.3 slice.104
  203.6 1.6 copy.75
  205.2 2.1 %copy.76 = f32[1,96,2304]{2,1,0:T(8,128)} copy(f32[1,96,2304]{2,1,0:T(8,128)} %bitcast.96) | data formatting | bytes 1769472
  207.3 0.7 copy.77
  208.0 1.0 copy.78
  209.1 1.0 copy.79
  (146 shorter events, 5.2 us)
Async XLA Ops:
  0.6 63.8 %copy-start.2 = (bf16[128,768]{1,0:T(8,128)(2,1)S(1)}, bf16[128,768]{1,0:T(8,128)(2,1)}, u32[]{:S(2)}) copy-start(bf16[128,768]{1,0:T(8,128)(2,1)} %param.15) | copy-start | bytes 589828
  68.7 1.1 copy-start.6
  68.8 1.7 copy-start.3
  70.9 17.6 %copy-start.1 = (f32[128,768]{1,0:T(8,128)}, f32[128,768]{1,0:T(8,128)S(1)}, u32[]{:S(2)}) copy-start(f32[128,768]{1,0:T(8,128)S(1)} %get-tuple-element.75.refs_17_) | copy-start | bytes 1179652
  70.9 4.9 %copy-start.43 = (f32[128]{0:T(128)}, f32[128]{0:T(128)S(1)}, u32[]{:S(2)}) copy-start(f32[128]{0:T(128)S(1)} %broadcast_multiply_fusion.4) | copy-start | bytes 1540
  71.1 4.7 %copy-start.46 = (f32[128]{0:T(128)}, f32[128]{0:T(128)S(1)}, u32[]{:S(2)}) copy-start(f32[128]{0:T(128)S(1)} %add_rsqrt_fusion) | copy-start | bytes 1540
  71.3 4.6 %copy-start.35 = (f32[768]{0:T(1024)}, f32[768]{0:T(1024)S(1)}, u32[]{:S(2)}) copy-start(f32[768]{0:T(1024)S(1)} %reshape.289) | copy-start | bytes 9220
  71.3 4.6 %copy-start.20 = (bf16[128,768]{1,0:T(8,128)(2,1)S(1)}, bf16[128,768]{1,0:T(8,128)(2,1)}, u32[]{:S(2)}) copy-start(bf16[128,768]{1,0:T(8,128)(2,1)} %refs_7_) | copy-start | bytes 589828
  80.8 7.6 %copy-start.4 = (bf16[128,3072]{1,0:T(8,128)(2,1)}, bf16[128,3072]{1,0:T(8,128)(2,1)S(1)}, u32[]{:S(2)}) copy-start(bf16[128,3072]{1,0:T(8,128)(2,1)S(1)} %get-tuple-element.83.refs_6_) | copy-start | bytes 2359300
  80.8 23.4 %collective-permute-start.6 = (bf16[128,3072]{1,0:T(8,128)(2,1)S(1)}, bf16[128,3072]{1,0:T(8,128)(2,1)}, u32[]{:S(2)}, u32[]{:S(2)}) collective-permute-start(bf16[128,3072]{1,0:T(8,128)(2,1)S(1)} %get-tuple-element.83.refs_6_), channel_id=1, source_target_pairs={{0,8},{8,0},{16,24},{24,16},{1,9},{9,1},{17,25},{25,17},{2,10},{10... | collective-permute-start | bytes 2359304 | tf_op jit(solution)/shard_map/ppermute | solution.py:640
  83.4 5.1 %copy-start.21 = (bf16[128,768]{1,0:T(8,128)(2,1)S(1)}, bf16[128,768]{1,0:T(8,128)(2,1)}, u32[]{:S(2)}) copy-start(bf16[128,768]{1,0:T(8,128)(2,1)} %refs_7_) | copy-start | bytes 589828
  83.4 5.1 %copy-start.36 = (f32[768]{0:T(1024)S(1)}, f32[768]{0:T(1024)}, u32[]{:S(2)}) copy-start(f32[768]{0:T(1024)} %copy-done.35) | copy-start | bytes 9220
  83.4 5.1 %copy-start.44 = (f32[128]{0:T(128)S(1)}, f32[128]{0:T(128)}, u32[]{:S(2)}) copy-start(f32[128]{0:T(128)} %copy-done.43) | copy-start | bytes 1540
  83.4 5.1 %copy-start.47 = (f32[128]{0:T(128)S(1)}, f32[128]{0:T(128)}, u32[]{:S(2)}) copy-start(f32[128]{0:T(128)} %copy-done.46) | copy-start | bytes 1540
  83.4 21.4 %collective-permute-start.3 = (bf16[8,384,128]{2,1,0:T(8,128)(2,1)}, bf16[8,384,128]{2,1,0:T(8,128)(2,1)}, u32[]{:S(2)}, u32[]{:S(2)}) collective-permute-start(bf16[8,384,128]{2,1,0:T(8,128)(2,1)} %bitcast.81), channel_id=1, source_target_pairs={{0,8},{8,0},{16,24},{24,16},{1,9},{9,1},{17,25},{25,17},{2,10},{10... | collective-permute-start | bytes 2359304 | tf_op jit(solution)/shard_map/ppermute | solution.py:640
  90.2 1.4 copy-start.11
  91.6 0.9 copy-start.7
  92.5 2.0 copy-start
  92.7 1.8 copy-start.40
  92.8 1.8 copy-start.42
  94.5 1.5 copy-start.14
  94.5 1.5 copy-start.30
  96.0 2.5 %copy-start.34 = (f32[768]{0:T(1024)S(1)}, f32[768]{0:T(1024)}, u32[]{:S(2)}) copy-start(f32[768]{0:T(1024)} %get-tuple-element.44) | copy-start | bytes 9220
  96.1 2.5 %copy-start.33 = (f32[768]{0:T(1024)S(1)}, f32[768]{0:T(1024)}, u32[]{:S(2)}) copy-start(f32[768]{0:T(1024)} %get-tuple-element.55) | copy-start | bytes 9220
  96.1 2.6 %copy-start.32 = (f32[768]{0:T(1024)S(1)}, f32[768]{0:T(1024)}, u32[]{:S(2)}) copy-start(f32[768]{0:T(1024)} %get-tuple-element.36) | copy-start | bytes 9220
  96.1 2.7 %copy-start.31 = (f32[768]{0:T(1024)S(1)}, f32[768]{0:T(1024)}, u32[]{:S(2)}) copy-start(f32[768]{0:T(1024)} %get-tuple-element.43) | copy-start | bytes 9220
  96.1 3.2 %copy-start.17 = (bf16[768,128]{0,1:T(8,128)(2,1)S(1)}, bf16[768,128]{0,1:T(8,128)(2,1)}, u32[]{:S(2)}) copy-start(bf16[768,128]{0,1:T(8,128)(2,1)} %get-tuple-element.52) | copy-start | bytes 589828
  96.1 4.4 %copy-start.13 = (bf16[128,768]{1,0:T(8,128)(2,1)S(1)}, bf16[128,768]{1,0:T(8,128)(2,1)}, u32[]{:S(2)}) copy-start(bf16[128,768]{1,0:T(8,128)(2,1)} %copy-done.12) | copy-start | bytes 589828
  96.1 5.5 %copy-start.9 = (bf16[12,64,128]{2,1,0:T(8,128)(2,1)S(1)}, bf16[12,64,128]{2,1,0:T(8,128)(2,1)}, u32[]{:S(2)}) copy-start(bf16[12,64,128]{2,1,0:T(8,128)(2,1)} %copy-done.8) | copy-start | bytes 589828
  96.1 6.1 %copy-start.22 = (bf16[128,768]{1,0:T(8,128)(2,1)S(1)}, bf16[128,768]{1,0:T(8,128)(2,1)}, u32[]{:S(2)}) copy-start(bf16[128,768]{1,0:T(8,128)(2,1)} %refs_7_) | copy-start | bytes 589828
  96.1 6.8 %copy-start.37 = (f32[8,96]{1,0:T(8,128)S(1)}, f32[8,96]{1,0:T(8,128)}, u32[]{:S(2)}) copy-start(f32[8,96]{1,0:T(8,128)} %get-tuple-element.58) | copy-start | bytes 9220
  97.1 1.7 copy-start.38
  97.3 7.6 %copy-start.18 = (bf16[768,128]{1,0:T(8,128)(2,1)}, bf16[768,128]{1,0:T(8,128)(2,1)S(1)}, u32[]{:S(2)}) copy-start(bf16[768,128]{1,0:T(8,128)(2,1)S(1)} %copy.48) | copy-start | bytes 589828
  97.3 3.2 %collective-permute-start = (bf16[8,96,128]{2,1,0:T(8,128)(2,1)S(1)}, bf16[8,96,128]{2,1,0:T(8,128)(2,1)S(1)}, u32[]{:S(2)}, u32[]{:S(2)}) collective-permute-start(bf16[8,96,128]{2,1,0:T(8,128)(2,1)S(1)} %bitcast.97), channel_id=1, source_target_pairs={{0,8},{8,0},{16,24},{24,16},{1,9},{9,1},{17,25},{25,17},{2,10},{10... | collective-permute-start | bytes 589832 | tf_op jit(solution)/shard_map/ppermute | solution.py:640
  97.9 7.0 %copy-start.5 = (bf16[128,2304]{1,0:T(8,128)(2,1)}, bf16[128,2304]{1,0:T(8,128)(2,1)S(1)}, u32[]{:S(2)}) copy-start(bf16[128,2304]{1,0:T(8,128)(2,1)S(1)} %copy.61.refs_4_) | copy-start | bytes 1769476
  97.9 6.3 %collective-permute-start.4 = (bf16[128,2304]{1,0:T(8,128)(2,1)S(1)}, bf16[128,2304]{1,0:T(8,128)(2,1)S(1)}, u32[]{:S(2)}, u32[]{:S(2)}) collective-permute-start(bf16[128,2304]{1,0:T(8,128)(2,1)S(1)} %copy.61.refs_4_), channel_id=1, source_target_pairs={{0,8},{8,0},{16,24},{24,16},{1,9},{9,1},{17,25},{25,17},{2,10},{10... | collective-permute-start | bytes 1769480 | tf_op jit(solution)/shard_map/ppermute | solution.py:640
  98.9 1.3 collective-permute-start.8
  99.5 5.4 %copy-start.19 = (bf16[768,128]{1,0:T(8,128)(2,1)}, bf16[768,128]{1,0:T(8,128)(2,1)S(1)}, u32[]{:S(2)}) copy-start(bf16[768,128]{1,0:T(8,128)(2,1)S(1)} %copy.53) | copy-start | bytes 589828
  100.2 1.4 collective-permute-start.2
  100.5 3.7 %copy-start.25 = (bf16[8,96,128]{2,1,0:T(8,128)(2,1)}, bf16[8,96,128]{2,1,0:T(8,128)(2,1)S(1)}, u32[]{:S(2)}) copy-start(bf16[8,96,128]{2,1,0:T(8,128)(2,1)S(1)} %collective-permute-done.refs_8_) | copy-start | bytes 589828
  100.5 1.7 collective-permute-start.5
  101.6 3.3 %copy-start.26 = (bf16[8,96,128]{2,1,0:T(8,128)(2,1)}, bf16[8,96,128]{2,1,0:T(8,128)(2,1)S(1)}, u32[]{:S(2)}) copy-start(bf16[8,96,128]{2,1,0:T(8,128)(2,1)S(1)} %collective-permute-done.2.refs_10_) | copy-start | bytes 589828
  101.7 2.6 %collective-permute-start.1 = (bf16[8,96,128]{2,1,0:T(8,128)(2,1)S(1)}, bf16[8,96,128]{2,1,0:T(8,128)(2,1)}, u32[]{:S(2)}, u32[]{:S(2)}) collective-permute-start(bf16[8,96,128]{2,1,0:T(8,128)(2,1)S(1)} %bitcast.89), channel_id=1, source_target_pairs={{0,8},{8,0},{16,24},{24,16},{1,9},{9,1},{17,25},{25,17},{2,10},{10... | collective-permute-start | bytes 589832 | tf_op jit(solution)/shard_map/ppermute | solution.py:640
  102.2 2.0 collective-permute-start.7
  104.2 0.9 copy-start.23
  199.6 7.7 %copy-start.24 = (f32[96,768]{1,0:T(8,128)S(1)}, f32[96,768]{1,0:T(8,128)}, u32[]{:S(2)}) copy-start(f32[96,768]{1,0:T(8,128)} %get-tuple-element.33) | copy-start | bytes 884740
  199.6 8.4 %copy-start.16 = (f32[96,3072]{1,0:T(8,128)S(1)}, f32[96,3072]{1,0:T(8,128)}, u32[]{:S(2)}) copy-start(f32[96,3072]{1,0:T(8,128)} %get-tuple-element.34) | copy-start | bytes 3538948
  207.3 1.7 copy-start.15
  (9 other events, 5.7 us)
